TPU v7x, 512 devices: a whole 4x8x8 slice. The times are simulated.
512 devices in a mesh: blk: 8 (over y_lo, core), leaf: 64 (over z, y_hi, x).
Axes of the slice: x: 4, y: 8 (y_hi: 2, y_lo: 4; y = y_hi * 4 + y_lo), z: 8, core: 2. Of those that a mesh axis runs over, the one named last changes fastest.
Arguments:
- positions: float32 [3, 64, 8, 128], P(None, 'leaf', 'blk'), may hold values from 0 to 32, as said below
- panel_areas: float32 [64, 8, 128], P('leaf', 'blk'), may hold values from 0.5 to 2
- probe_cols: bfloat16 [576, 64, 8, 128], P(None, 'leaf', 'blk'), may hold values from -5 to 5
- full_sketch: bfloat16 [576, 64, 8, 128], P(None, 'leaf', 'blk'), may hold values from -3 to 3
- tree_order: int32 [64, 8, 128], P('leaf', 'blk'), may hold values from 0 to 127, each once within a row
- leaf_basis: bfloat16 [64, 8, 128, 512], P('leaf', 'blk'), may hold values from -0.1875 to 0.1875
- transfer_mats: bfloat16 [64, 3, 512, 512], P('leaf'), may hold values from -0.1875 to 0.1875
Outputs:
- offdiag_sketch: bfloat16 [576, 64, 8, 128], P(None, 'leaf', 'blk')
- nested_sketch: float32 [64, 2, 576, 512], P('leaf')
Inputs may be any that keep to these rules, and one draw needn't show every extreme that they name: `positions`: each leaf's panel centres lie on a surface patch of 32 by 32 mean panel widths. `tree_order`: along the last dimension, each row names every one of the 128 panels of its block once.
All inputs are finite; a program needn't handle non-finite values.
Results may differ from a plain program's by a relative error of at most 0.0046.
Values sent between devices are 32-bit elements; how exact they have to be, the bound alone decides.
No kernel may reach another device: no remote copies, remote signals or barrier semaphores. Data moves between devices by JAX's collectives and lax.ppermute only.
A program may use at most 64 MiB of HBM per device.

v0:
```python
import math

import jax
import jax.numpy as jnp
from jax import lax
from jax.sharding import PartitionSpec as P

inv_four_pi = 1.0 / (4.0 * math.pi)


def partner(value, axis, bit):
    mask = 2**bit
    pairs = [(source, source ^ mask) for source in range(lax.axis_size(axis))]
    return lax.ppermute(value, axis, pairs)


def kernel_tile(target_pos, target_area, source_pos, source_area):
    distance = jnp.zeros((target_pos.shape[1], source_pos.shape[1]), jnp.float32)
    for component in range(3):
        gap = target_pos[component][:, None] - source_pos[component][None, :]
        distance = distance + gap * gap
    soft = distance + 0.5 * (target_area[:, None] + source_area[None, :])
    return (inv_four_pi * lax.rsqrt(soft)).astype(jnp.bfloat16)


def target_blocks(target_pos, target_area):
    panels = target_pos.shape[1]
    block_size = min(512, panels)
    block_count = panels // block_size
    pos_blocks = jnp.transpose(target_pos.reshape(3, block_count, block_size), (1, 0, 2))
    return (pos_blocks, target_area.reshape(block_count, block_size))


def near_block(target_pos, target_area, source_pos, source_area, source_scaled):
    pos_blocks, area_blocks = target_blocks(target_pos, target_area)

    def one_block(entry):
        block_pos, block_area = entry
        kernel = kernel_tile(block_pos, block_area, source_pos, source_area)
        return lax.dot_general(
            source_scaled, kernel, (((1,), (1,)), ((), ())), preferred_element_type=jnp.float32
        )

    sums = lax.map(one_block, (pos_blocks, area_blocks))
    return jnp.transpose(sums, (1, 0, 2)).reshape(source_scaled.shape[0], target_pos.shape[1])


def project(current, level_mat):
    return jnp.dot(current, level_mat.astype(jnp.float32), precision=lax.Precision.HIGHEST)


def climb_both(sketch, probes, level_mats):
    for tree_level in range(level_mats.shape[0]):
        sketch_proj = project(sketch, level_mats[tree_level])
        probe_proj = project(probes, level_mats[tree_level])
        other_sketch, other_probe = partner((sketch_proj, probe_proj), "leaf", tree_level)
        sketch = sketch_proj + other_sketch
        probes = probe_proj + other_probe
    return (sketch, probes)


def shards(positions, panel_areas, probe_cols, full_sketch, tree_order, leaf_basis, transfer_mats):
    panels = positions.shape[3]
    probe_count = probe_cols.shape[0]
    basis_width = leaf_basis.shape[3]
    level_count = transfer_mats.shape[1]
    coords = positions.reshape(3, panels)
    area_row = panel_areas.reshape(1, panels)
    probe_flat = probe_cols.reshape(probe_count, panels)
    scaled = (area_row * probe_flat.astype(jnp.float32)).astype(jnp.bfloat16)
    sorting = tree_order.reshape(panels)
    basis_flat = leaf_basis.reshape(panels, basis_width)
    level_mats = transfer_mats.reshape(level_count, basis_width, basis_width)
    probe_part = jnp.dot(
        jnp.take(probe_flat, sorting, axis=1), basis_flat, preferred_element_type=jnp.float32
    )
    outgoing = jnp.concatenate([coords, area_row, scaled.astype(jnp.float32)], axis=0)
    piece = lax.all_gather(outgoing, "blk", axis=1, tiled=True)
    near_sum = near_block(coords, area_row[0], piece[:3], piece[3], piece[4:].astype(jnp.bfloat16))
    offdiag = (full_sketch.reshape(probe_count, panels).astype(jnp.float32) - near_sum).astype(
        jnp.bfloat16
    )
    sketch_part = jnp.dot(
        jnp.take(offdiag, sorting, axis=1), basis_flat, preferred_element_type=jnp.float32
    )
    sketch_sum, probe_sum = lax.psum((sketch_part, probe_part), "blk")
    sketch_top, probe_top = climb_both(sketch_sum, probe_sum, level_mats)
    nested = jnp.stack([sketch_top, probe_top], axis=0)[None]
    return (offdiag.reshape(probe_count, 1, 1, panels), nested)


def solution(mesh):
    in_specs = (
        P(None, "leaf", "blk", None),
        P("leaf", "blk", None),
        P(None, "leaf", "blk", None),
        P(None, "leaf", "blk", None),
        P("leaf", "blk", None),
        P("leaf", "blk", None, None),
        P("leaf", None, None, None),
    )
    out_specs = (P(None, "leaf", "blk", None), P("leaf", None, None, None))
    return jax.shard_map(shards, mesh=mesh, in_specs=in_specs, out_specs=out_specs, check_vma=False)
```

profile of v0, /device:TPU:25, one launch (start us, length us, event | category | flops | bytes accessed | tf_op | source)
XLA Modules:
  0.0 356.3 jit_solution(13410690366226778184)
XLA Ops:
  7.2 0.0 copy-start
  7.2 0.0 copy-start.6
  7.2 0.0 all-gather.2.cloned.1.call-start
  7.2 0.8 copy.15
  8.0 0.8 copy.13
  8.8 1.1 copy.14
  9.8 0.7 fusion.36
  10.6 0.0 copy-start.4
  10.6 0.9 pad_maximum_fusion
  11.5 0.0 all-gather.2.cloned.1.call-update
  11.6 0.0 all-reduce.3.cloned.1.call-start
  11.6 0.0 copy-done.6
  11.6 0.9 gather_fusion.1
  12.5 0.0 copy-done.4
  12.6 0.0 copy-done
  12.6 1.4 fusion.37
  14.0 0.0 copy-start.3
  14.0 0.0 copy-start.5
  14.0 44.9 %all-gather.2.cloned.1.call-done = f32[580,1024]{0,1:T(8,128)} async-done(((f32[580,128]{0,1:T(8,128)}), f32[580,1024]{0,1:T(8,128)}) %all-gather.2.cloned.1.call-update) | async-done | bytes 2375696 | tf_op jit(solution)/shard_map/all_gather | solution.py:78
  58.9 2.8 slice_reduce_fusion.3
  61.8 0.0 copy-done.3
  61.8 0.0 copy-done.5
  61.8 3.6 %fusion.23 = (bf16[576,1,1,128]{3,0,2,1:T(8,128)(2,1)}, f32[576,128]{1,0:T(8,128)S(1)}) fusion(bf16[576,1,1,128]{3,0,2,1:T(8,128)(2,1)S(1)} %copy-done.3, f32[1024]{0:T(1024)S(1)} %get-tuple-element.18, f32[128]{0:T(128)S(1)} %bitcast.61, f32[1024]{0:T(1024)S(1)} %get-tuple-element.19, f32[128]{0:T(128)S(1)} %get-tuple-element.31, ...), kind=kOutput, calls=%fused_computation.38 | convolution fusion | flops 152920064 | bytes 1918976 | tf_op jit(solution)/shard_map/while/body/eval_jaxpr/dot_general | solution.py:40
  65.4 0.2 copy.16
  65.6 0.9 gather_fusion
  66.5 1.4 fusion.39
  67.9 0.0 copy-start.1
  67.9 0.0 all-reduce.3.cloned.1.call-update
  67.9 87.3 %all-reduce.3.cloned.1.call-done = (f32[576,512]{1,0:T(8,128)}, f32[576,512]{1,0:T(8,128)}) async-done(((f32[576,512]{1,0:T(8,128)}, f32[576,512]{1,0:T(8,128)}), (f32[576,512]{1,0:T(8,128)}, f32[576,512]{1,0:T(8,128)})) %all-reduce.3.cloned.1.call-update) | async-done | bytes 2359312 | tf_op jit(solution)/shard_map/psum | solution.py:86
  155.2 0.0 copy-done.1
  155.2 0.0 copy-start.2
  155.2 2.5 fusion.15
  157.7 3.1 collective-permute-start
  160.8 0.0 copy-done.2
  160.8 1.1 fusion.13
  161.9 2.2 collective-permute-start.3
  164.1 23.5 %collective-permute-done = f32[576,512]{1,0:T(8,128)S(1)} collective-permute-done((f32[576,512]{1,0:T(8,128)S(1)}, f32[576,512]{1,0:T(8,128)S(1)}, u32[]{:S(2)}, u32[]{:S(2)}) %collective-permute-start) | collective-permute-done | bytes 1179680 | tf_op jit(solution)/shard_map/ppermute | solution.py:14
  187.7 1.1 fusion.7
  188.8 4.6 %collective-permute-start.1 = (f32[576,512]{1,0:T(8,128)S(1)}, f32[576,512]{1,0:T(8,128)S(1)}, u32[]{:S(2)}, u32[]{:S(2)}) collective-permute-start(f32[576,512]{1,0:T(8,128)S(1)} %fusion.7), channel_id=1, source_target_pairs={{0,2},{1,3},{2,0},{3,1},{4,6},{5,7},{6,4},{7,5},{8,10},{9,11},{10,... | collective-permute-start | bytes 3538952 | tf_op jit(solution)/shard_map/ppermute | solution.py:14
  193.4 19.6 %collective-permute-done.3 = f32[576,512]{1,0:T(8,128)S(1)} collective-permute-done((f32[576,512]{1,0:T(8,128)S(1)}, f32[576,512]{1,0:T(8,128)S(1)}, u32[]{:S(2)}, u32[]{:S(2)}) %collective-permute-start.3) | collective-permute-done | bytes 1179680 | tf_op jit(solution)/shard_map/ppermute | solution.py:14
  212.9 1.1 fusion.3
  214.1 4.6 %collective-permute-start.4 = (f32[576,512]{1,0:T(8,128)S(1)}, f32[576,512]{1,0:T(8,128)S(1)}, u32[]{:S(2)}, u32[]{:S(2)}) collective-permute-start(f32[576,512]{1,0:T(8,128)S(1)} %fusion.3), channel_id=1, source_target_pairs={{0,2},{1,3},{2,0},{3,1},{4,6},{5,7},{6,4},{7,5},{8,10},{9,11},{10,... | collective-permute-start | bytes 3538952 | tf_op jit(solution)/shard_map/ppermute | solution.py:14
  218.7 21.7 %collective-permute-done.1 = f32[576,512]{1,0:T(8,128)S(1)} collective-permute-done((f32[576,512]{1,0:T(8,128)S(1)}, f32[576,512]{1,0:T(8,128)S(1)}, u32[]{:S(2)}, u32[]{:S(2)}) %collective-permute-start.1) | collective-permute-done | bytes 1179680 | tf_op jit(solution)/shard_map/ppermute | solution.py:14
  240.3 1.1 fusion.5
  241.4 5.0 %collective-permute-start.2 = (f32[576,512]{1,0:T(8,128)S(1)}, f32[576,512]{1,0:T(8,128)S(1)}, u32[]{:S(2)}, u32[]{:S(2)}) collective-permute-start(f32[576,512]{1,0:T(8,128)S(1)} %fusion.5), channel_id=1, source_target_pairs={{0,4},{1,5},{2,6},{3,7},{4,0},{5,1},{6,2},{7,3},{8,12},{9,13},{10,... | collective-permute-start | bytes 3538952 | tf_op jit(solution)/shard_map/ppermute | solution.py:14
  246.5 17.7 %collective-permute-done.4 = f32[576,512]{1,0:T(8,128)S(1)} collective-permute-done((f32[576,512]{1,0:T(8,128)S(1)}, f32[576,512]{1,0:T(8,128)S(1)}, u32[]{:S(2)}, u32[]{:S(2)}) %collective-permute-start.4) | collective-permute-done | bytes 1179680 | tf_op jit(solution)/shard_map/ppermute | solution.py:14
  264.2 1.1 fusion.1
  265.3 5.2 %collective-permute-start.5 = (f32[576,512]{1,0:T(8,128)S(1)}, f32[576,512]{1,0:T(8,128)S(1)}, u32[]{:S(2)}, u32[]{:S(2)}) collective-permute-start(f32[576,512]{1,0:T(8,128)S(1)} %fusion.1), channel_id=1, source_target_pairs={{0,4},{1,5},{2,6},{3,7},{4,0},{5,1},{6,2},{7,3},{8,12},{9,13},{10,... | collective-permute-start | bytes 3538952 | tf_op jit(solution)/shard_map/ppermute | solution.py:14
  270.5 52.0 %collective-permute-done.2 = f32[576,512]{1,0:T(8,128)S(1)} collective-permute-done((f32[576,512]{1,0:T(8,128)S(1)}, f32[576,512]{1,0:T(8,128)S(1)}, u32[]{:S(2)}, u32[]{:S(2)}) %collective-permute-start.2) | collective-permute-done | bytes 1179680 | tf_op jit(solution)/shard_map/ppermute | solution.py:14
  322.6 0.2 add_bitcast_fusion.1
  322.8 24.8 %collective-permute-done.5 = f32[576,512]{1,0:T(8,128)S(1)} collective-permute-done((f32[576,512]{1,0:T(8,128)S(1)}, f32[576,512]{1,0:T(8,128)S(1)}, u32[]{:S(2)}, u32[]{:S(2)}) %collective-permute-start.5) | collective-permute-done | bytes 1179680 | tf_op jit(solution)/shard_map/ppermute | solution.py:14
  347.6 0.2 add_bitcast_fusion
  347.9 1.6 maximum_bitcast_fusion
  (5 shorter events, 0.1 us)
Async XLA Ops:
  7.2 5.4 %copy-start = (bf16[1,1,128,512]{3,2,1,0:T(8,128)(2,1)S(1)}, bf16[1,1,128,512]{3,2,1,0:T(8,128)(2,1)}, u32[]{:S(2)}) copy-start(bf16[1,1,128,512]{3,2,1,0:T(8,128)(2,1)} %param.14) | copy-start | bytes 393220
  7.2 4.4 %copy-start.6 = (s32[1,1,128]{2,1,0:T(1,128)S(1)}, s32[1,1,128]{2,1,0:T(1,128)}, u32[]{:S(2)}) copy-start(s32[1,1,128]{2,1,0:T(1,128)} %param.13) | copy-start | bytes 1540
  7.2 51.8 %all-gather.2.cloned.1.call-start = ((), (), s32[]{:S(2)}) async-start(), calls=%async_computation | async-start | bytes 2949120 | tf_op jit(solution)/shard_map/all_gather | solution.py:78
  10.6 1.9 copy-start.4
  11.6 143.7 %all-reduce.3.cloned.1.call-start = ((), (), s32[]{:S(2)}) async-start(), calls=%async_computation.1 | async-start | bytes 4718592 | tf_op jit(solution)/shard_map/psum | solution.py:86
  14.0 47.8 %copy-start.3 = (bf16[576,1,1,128]{3,0,2,1:T(8,128)(2,1)S(1)}, bf16[576,1,1,128]{3,0,2,1:T(8,128)(2,1)}, u32[]{:S(2)}) copy-start(bf16[576,1,1,128]{3,0,2,1:T(8,128)(2,1)} %param.12) | copy-start | bytes 442372
  14.0 47.8 %copy-start.5 = (f32[1,1,128]{2,1,0:T(1,128)S(1)}, f32[1,1,128]{2,1,0:T(1,128)}, u32[]{:S(2)}) copy-start(f32[1,1,128]{2,1,0:T(1,128)} %param.10) | copy-start | bytes 1540
  67.9 87.3 %copy-start.1 = (bf16[1,3,512,512]{3,2,1,0:T(8,128)(2,1)S(1)}, bf16[1,3,512,512]{3,2,1,0:T(8,128)(2,1)}, u32[]{:S(2)}) copy-start(bf16[1,3,512,512]{3,2,1,0:T(8,128)(2,1)} %param.15) | copy-start | bytes 4718596
  155.2 5.6 %copy-start.2 = (f32[576,512]{1,0:T(8,128)S(1)}, f32[576,512]{1,0:T(8,128)}, u32[]{:S(2)}) copy-start(f32[576,512]{1,0:T(8,128)} %get-tuple-element.28) | copy-start | bytes 3538948
  157.7 29.9 %collective-permute-start = (f32[576,512]{1,0:T(8,128)S(1)}, f32[576,512]{1,0:T(8,128)S(1)}, u32[]{:S(2)}, u32[]{:S(2)}) collective-permute-start(f32[576,512]{1,0:T(8,128)S(1)} %fusion.15), channel_id=1, source_target_pairs={{0,1},{1,0},{2,3},{3,2},{4,5},{5,4},{6,7},{7,6},{8,9},{9,8},{10,11... | collective-permute-start | bytes 3538952 | tf_op jit(solution)/shard_map/ppermute | solution.py:14
  161.9 51.0 %collective-permute-start.3 = (f32[576,512]{1,0:T(8,128)S(1)}, f32[576,512]{1,0:T(8,128)S(1)}, u32[]{:S(2)}, u32[]{:S(2)}) collective-permute-start(f32[576,512]{1,0:T(8,128)S(1)} %fusion.13), channel_id=1, source_target_pairs={{0,1},{1,0},{2,3},{3,2},{4,5},{5,4},{6,7},{7,6},{8,9},{9,8},{10,11... | collective-permute-start | bytes 3538952 | tf_op jit(solution)/shard_map/ppermute | solution.py:14
  188.8 51.6 %collective-permute-start.1 = (f32[576,512]{1,0:T(8,128)S(1)}, f32[576,512]{1,0:T(8,128)S(1)}, u32[]{:S(2)}, u32[]{:S(2)}) collective-permute-start(f32[576,512]{1,0:T(8,128)S(1)} %fusion.7), channel_id=1, source_target_pairs={{0,2},{1,3},{2,0},{3,1},{4,6},{5,7},{6,4},{7,5},{8,10},{9,11},{10,... | collective-permute-start | bytes 3538952 | tf_op jit(solution)/shard_map/ppermute | solution.py:14
  214.1 50.1 %collective-permute-start.4 = (f32[576,512]{1,0:T(8,128)S(1)}, f32[576,512]{1,0:T(8,128)S(1)}, u32[]{:S(2)}, u32[]{:S(2)}) collective-permute-start(f32[576,512]{1,0:T(8,128)S(1)} %fusion.3), channel_id=1, source_target_pairs={{0,2},{1,3},{2,0},{3,1},{4,6},{5,7},{6,4},{7,5},{8,10},{9,11},{10,... | collective-permute-start | bytes 3538952 | tf_op jit(solution)/shard_map/ppermute | solution.py:14
  241.4 81.1 %collective-permute-start.2 = (f32[576,512]{1,0:T(8,128)S(1)}, f32[576,512]{1,0:T(8,128)S(1)}, u32[]{:S(2)}, u32[]{:S(2)}) collective-permute-start(f32[576,512]{1,0:T(8,128)S(1)} %fusion.5), channel_id=1, source_target_pairs={{0,4},{1,5},{2,6},{3,7},{4,0},{5,1},{6,2},{7,3},{8,12},{9,13},{10,... | collective-permute-start | bytes 3538952 | tf_op jit(solution)/shard_map/ppermute | solution.py:14
  265.3 82.3 %collective-permute-start.5 = (f32[576,512]{1,0:T(8,128)S(1)}, f32[576,512]{1,0:T(8,128)S(1)}, u32[]{:S(2)}, u32[]{:S(2)}) collective-permute-start(f32[576,512]{1,0:T(8,128)S(1)} %fusion.1), channel_id=1, source_target_pairs={{0,4},{1,5},{2,6},{3,7},{4,0},{5,1},{6,2},{7,3},{8,12},{9,13},{10,... | collective-permute-start | bytes 3538952 | tf_op jit(solution)/shard_map/ppermute | solution.py:14
Sparse Core Ops, SparseCore 0:
  11.7 47.2 all-gather.1
  68.1 87.1 all-reduce.2
where the time goes:
time: 357 us; the launch traced here: 356 us
  waiting for transfers between devices  292 us (82%)
  starting transfers between devices  24.8 us (7%)
  matrix products  14.4 us (4%)
  between operations  14.3 us (4%)
  local copies, waits for them, and re-layouts  7.42 us (2%)
  other arithmetic  3.81 us (1%)
    ppermute x6, waiting for transfers between devices, partner(): return lax.ppermute(value, axis, pairs)  159 us
    psum x1, waiting for transfers between devices, shards(): sketch_sum, probe_sum = lax.psum((sketch_part, probe_part), 'blk')  87.3 us
    all_gather x1, waiting for transfers between devices, shards(): piece = lax.all_gather(outgoing, 'blk', axis=1, tiled=True)  44.9 us
    ppermute x6, starting transfers between devices, partner(): return lax.ppermute(value, axis, pairs)  24.7 us
    dot_general x6, matrix products, project(): jnp.dot(current, level_mat.astype(jnp.float32), precision=lax.Precision.H...  7.97 us
  transfers between devices with their start and end apart: 8, of which 8 were waited for; matrix products, arithmetic and copies ran while one was open for 2% of the time, Pallas kernels for 0%

commit v1 on v0

--- a/solution.py
+++ b/solution.py
@@ -49,14 +49,11 @@
     return jnp.dot(current, level_mat.astype(jnp.float32), precision=lax.Precision.HIGHEST)
 
 
-def climb_both(sketch, probes, level_mats):
+def climb_rows(rows, level_mats):
     for tree_level in range(level_mats.shape[0]):
-        sketch_proj = project(sketch, level_mats[tree_level])
-        probe_proj = project(probes, level_mats[tree_level])
-        other_sketch, other_probe = partner((sketch_proj, probe_proj), "leaf", tree_level)
-        sketch = sketch_proj + other_sketch
-        probes = probe_proj + other_probe
-    return (sketch, probes)
+        projected = project(rows, level_mats[tree_level])
+        rows = projected + partner(projected, "leaf", tree_level)
+    return rows
 
 
 def shards(positions, panel_areas, probe_cols, full_sketch, tree_order, leaf_basis, transfer_mats):
@@ -83,9 +80,10 @@
     sketch_part = jnp.dot(
         jnp.take(offdiag, sorting, axis=1), basis_flat, preferred_element_type=jnp.float32
     )
-    sketch_sum, probe_sum = lax.psum((sketch_part, probe_part), "blk")
-    sketch_top, probe_top = climb_both(sketch_sum, probe_sum, level_mats)
-    nested = jnp.stack([sketch_top, probe_top], axis=0)[None]
+    stacked = jnp.concatenate([sketch_part, probe_part], axis=0)
+    mine = lax.psum_scatter(stacked, "blk", scatter_dimension=0, tiled=True)
+    top = climb_rows(mine, level_mats)
+    nested = lax.all_gather(top, "blk", axis=0, tiled=True).reshape(2, probe_count, basis_width)[None]
     return (offdiag.reshape(probe_count, 1, 1, panels), nested)
 
 

time: 357 us -> 205 us (0.57)
  the two profiles are of different devices: /device:TPU:25 before, /device:TPU:1 now
where the time goes in v1:
time: 205 us; the launch traced here: 204 us
  waiting for transfers between devices  156 us (76%)
  between operations  13.9 us (7%)
  starting transfers between devices  13.1 us (6%)
  local copies, waits for them, and re-layouts  10.8 us (5%)
  matrix products  6.58 us (3%)
  other arithmetic  4.07 us (2%)
    all_gather x1, waiting for transfers between devices, shards(): lax.all_gather(top, 'blk', axis=0, tiled=True)  51.1 us
    all_gather x1, waiting for transfers between devices, shards(): piece = lax.all_gather(outgoing, 'blk', axis=1, tiled=True)  46 us
    reduce_scatter x1, waiting for transfers between devices, shards(): mine = lax.psum_scatter(stacked, 'blk', scatter_dimension=0, tiled=True)  43.7 us
    ppermute x3, waiting for transfers between devices, partner(): return lax.ppermute(value, axis, pairs)  15.1 us
    ppermute x3, starting transfers between devices, partner(): return lax.ppermute(value, axis, pairs)  13 us
    unnamed x15, local copies, waits for them, and re-layouts  5.16 us
  transfers between devices with their start and end apart: 6, of which 6 were waited for; matrix products, arithmetic and copies ran while one was open for 1% of the time, Pallas kernels for 0%

profile of v1, /device:TPU:1, one launch (start us, length us, event | category | flops | bytes accessed | tf_op | source)
XLA Modules:
  0.0 204.4 jit_solution(672302007747761482)
XLA Ops:
  7.2 0.0 copy-start
  7.2 0.0 copy-start.5
  7.2 0.0 all-gather.3.cloned.1.call-start
  7.2 0.8 copy.15
  8.0 0.8 copy.13
  8.8 0.0 copy-start.3
  8.8 1.1 copy.14
  9.9 0.7 fusion.25
  10.6 0.9 pad_maximum_fusion.1
  11.5 0.0 all-gather.3.cloned.1.call-update
  11.6 0.0 reduce-scatter.2.cloned.1.call-start
  11.6 0.0 copy-done.5
  11.6 0.9 gather_fusion.1
  12.5 0.0 copy-done.3
  12.6 0.0 copy-done
  12.6 0.0 copy-start.2
  12.6 0.0 copy-start.4
  12.6 0.4 fusion.26
  13.0 46.0 %all-gather.3.cloned.1.call-done = f32[580,1024]{0,1:T(8,128)} async-done(((f32[580,128]{0,1:T(8,128)}), f32[580,1024]{0,1:T(8,128)}) %all-gather.3.cloned.1.call-update) | async-done | bytes 2375696 | tf_op jit(solution)/shard_map/all_gather | solution.py:75
  59.0 2.9 %slice_reduce_fusion.3 = (f32[1024]{0:T(1024)S(1)}, f32[1024]{0:T(1024)S(1)}, f32[1024]{0:T(1024)S(1)}, f32[1024]{0:T(1024)S(1)}) fusion(f32[580,1024]{0,1:T(8,128)} %all-gather.3.cloned.1.call-done), kind=kLoop, calls=%fused_computation.8 | loop fusion | bytes 32768 | tf_op jit(solution)/shard_map/while/body/eval_jaxpr/slice | solution.py:20
  61.9 0.0 copy-done.2
  61.9 0.0 copy-done.4
  61.9 3.6 %fusion.10 = (bf16[576,1,1,128]{3,0,2,1:T(8,128)(2,1)}, f32[576,128]{1,0:T(8,128)S(1)}) fusion(bf16[576,1,1,128]{3,0,2,1:T(8,128)(2,1)S(1)} %copy-done.2, f32[1024]{0:T(1024)S(1)} %get-tuple-element.18, f32[128]{0:T(128)S(1)} %bitcast.50, f32[1024]{0:T(1024)S(1)} %get-tuple-element.19, f32[128]{0:T(128)S(1)} %get-tuple-element.29, ...), kind=kOutput, calls=%fused_computation.23 | convolution fusion | flops 152920064 | bytes 1918976 | tf_op jit(solution)/shard_map/while/body/eval_jaxpr/dot_general | solution.py:40
  65.6 0.2 copy.16
  65.7 0.9 gather_fusion
  66.6 0.4 fusion.28
  67.0 1.6 pad_maximum_fusion
  68.6 0.0 copy-start.1
  68.6 0.0 reduce-scatter.2.cloned.1.call-update
  68.7 0.0 all-gather.5.cloned.1.call-start
  68.7 43.7 %reduce-scatter.2.cloned.1.call-done = f32[144,512]{1,0:T(8,128)} async-done(((f32[1152,512]{1,0:T(8,128)}), f32[144,512]{1,0:T(8,128)}) %reduce-scatter.2.cloned.1.call-update) | async-done | bytes 294928 | tf_op jit(solution)/shard_map/reduce_scatter | solution.py:84
  112.4 0.0 copy-done.1
  112.4 1.4 fusion.5
  113.7 2.9 %collective-permute-start = (f32[144,512]{1,0:T(8,128)S(1)}, f32[144,512]{1,0:T(8,128)S(1)}, u32[]{:S(2)}, u32[]{:S(2)}) collective-permute-start(f32[144,512]{1,0:T(8,128)S(1)} %fusion.5), channel_id=1, source_target_pairs={{0,1},{1,0},{2,3},{3,2},{4,5},{5,4},{6,7},{7,6},{8,9},{9,8},{10,11... | collective-permute-start | bytes 884744 | tf_op jit(solution)/shard_map/ppermute | solution.py:14
  116.7 4.8 %collective-permute-done = f32[144,512]{1,0:T(8,128)S(1)} collective-permute-done((f32[144,512]{1,0:T(8,128)S(1)}, f32[144,512]{1,0:T(8,128)S(1)}, u32[]{:S(2)}, u32[]{:S(2)}) %collective-permute-start) | collective-permute-done | bytes 294944 | tf_op jit(solution)/shard_map/ppermute | solution.py:14
  121.5 0.4 fusion.3
  121.9 3.9 %collective-permute-start.1 = (f32[144,512]{1,0:T(8,128)S(1)}, f32[144,512]{1,0:T(8,128)S(1)}, u32[]{:S(2)}, u32[]{:S(2)}) collective-permute-start(f32[144,512]{1,0:T(8,128)S(1)} %fusion.3), channel_id=1, source_target_pairs={{0,2},{1,3},{2,0},{3,1},{4,6},{5,7},{6,4},{7,5},{8,10},{9,11},{10,... | collective-permute-start | bytes 884744 | tf_op jit(solution)/shard_map/ppermute | solution.py:14
  125.8 5.0 %collective-permute-done.1 = f32[144,512]{1,0:T(8,128)S(1)} collective-permute-done((f32[144,512]{1,0:T(8,128)S(1)}, f32[144,512]{1,0:T(8,128)S(1)}, u32[]{:S(2)}, u32[]{:S(2)}) %collective-permute-start.1) | collective-permute-done | bytes 294944 | tf_op jit(solution)/shard_map/ppermute | solution.py:14
  130.9 0.4 fusion.1
  131.3 6.2 %collective-permute-start.2 = (f32[144,512]{1,0:T(8,128)S(1)}, f32[144,512]{1,0:T(8,128)S(1)}, u32[]{:S(2)}, u32[]{:S(2)}) collective-permute-start(f32[144,512]{1,0:T(8,128)S(1)} %fusion.1), channel_id=1, source_target_pairs={{0,4},{1,5},{2,6},{3,7},{4,0},{5,1},{6,2},{7,3},{8,12},{9,13},{10,... | collective-permute-start | bytes 884744 | tf_op jit(solution)/shard_map/ppermute | solution.py:14
  137.5 5.2 %collective-permute-done.2 = f32[144,512]{1,0:T(8,128)S(1)} collective-permute-done((f32[144,512]{1,0:T(8,128)S(1)}, f32[144,512]{1,0:T(8,128)S(1)}, u32[]{:S(2)}, u32[]{:S(2)}) %collective-permute-start.2) | collective-permute-done | bytes 294944 | tf_op jit(solution)/shard_map/ppermute | solution.py:14
  142.7 0.8 add.62
  143.4 0.0 all-gather.5.cloned.1.call-update
  143.5 51.1 %all-gather.5.cloned.1.call-done = f32[1152,512]{1,0:T(8,128)} async-done(((f32[144,512]{1,0:T(8,128)}), f32[1152,512]{1,0:T(8,128)}) %all-gather.5.cloned.1.call-update) | async-done | bytes 2359312 | tf_op jit(solution)/shard_map/all_gather | solution.py:86
  194.6 3.3 %copy.18 = f32[1,2,576,512]{3,2,1,0:T(8,128)} copy(f32[1,2,576,512]{3,2,1,0:T(8,128)} %bitcast.46) | data formatting | bytes 4718592
  (5 shorter events, 0.1 us)
Async XLA Ops:
  7.2 5.4 %copy-start = (bf16[1,1,128,512]{3,2,1,0:T(8,128)(2,1)S(1)}, bf16[1,1,128,512]{3,2,1,0:T(8,128)(2,1)}, u32[]{:S(2)}) copy-start(bf16[1,1,128,512]{3,2,1,0:T(8,128)(2,1)} %param.14) | copy-start | bytes 393220
  7.2 4.4 %copy-start.5 = (s32[1,1,128]{2,1,0:T(1,128)S(1)}, s32[1,1,128]{2,1,0:T(1,128)}, u32[]{:S(2)}) copy-start(s32[1,1,128]{2,1,0:T(1,128)} %param.13) | copy-start | bytes 1540
  7.2 51.8 %all-gather.3.cloned.1.call-start = ((), (), s32[]{:S(2)}) async-start(), calls=%async_computation.1 | async-start | bytes 2949120 | tf_op jit(solution)/shard_map/all_gather | solution.py:75
  8.8 3.7 %copy-start.3 = (f32[3,1,1,128]{3,2,1,0:T(1,128)S(1)}, f32[3,1,1,128]{3,2,1,0:T(1,128)}, u32[]{:S(2)}) copy-start(f32[3,1,1,128]{3,2,1,0:T(1,128)} %param.9) | copy-start | bytes 4612
  11.6 100.8 %reduce-scatter.2.cloned.1.call-start = ((), (), s32[]{:S(2)}) async-start(), calls=%async_computation.2 | async-start | bytes 2654208 | tf_op jit(solution)/shard_map/reduce_scatter | solution.py:84
  12.6 49.3 %copy-start.2 = (bf16[576,1,1,128]{3,0,2,1:T(8,128)(2,1)S(1)}, bf16[576,1,1,128]{3,0,2,1:T(8,128)(2,1)}, u32[]{:S(2)}) copy-start(bf16[576,1,1,128]{3,0,2,1:T(8,128)(2,1)} %param.12) | copy-start | bytes 442372
  12.6 49.3 %copy-start.4 = (f32[1,1,128]{2,1,0:T(1,128)S(1)}, f32[1,1,128]{2,1,0:T(1,128)}, u32[]{:S(2)}) copy-start(f32[1,1,128]{2,1,0:T(1,128)} %param.10) | copy-start | bytes 1540
  68.6 43.7 %copy-start.1 = (bf16[1,3,512,512]{3,2,1,0:T(8,128)(2,1)S(1)}, bf16[1,3,512,512]{3,2,1,0:T(8,128)(2,1)}, u32[]{:S(2)}) copy-start(bf16[1,3,512,512]{3,2,1,0:T(8,128)(2,1)} %param.15) | copy-start | bytes 4718596
  68.7 125.9 %all-gather.5.cloned.1.call-start = ((), (), s32[]{:S(2)}) async-start(), calls=%async_computation.3 | async-start | bytes 2654208 | tf_op jit(solution)/shard_map/all_gather | solution.py:86
  113.7 7.8 %collective-permute-start = (f32[144,512]{1,0:T(8,128)S(1)}, f32[144,512]{1,0:T(8,128)S(1)}, u32[]{:S(2)}, u32[]{:S(2)}) collective-permute-start(f32[144,512]{1,0:T(8,128)S(1)} %fusion.5), channel_id=1, source_target_pairs={{0,1},{1,0},{2,3},{3,2},{4,5},{5,4},{6,7},{7,6},{8,9},{9,8},{10,11... | collective-permute-start | bytes 884744 | tf_op jit(solution)/shard_map/ppermute | solution.py:14
  121.9 9.0 %collective-permute-start.1 = (f32[144,512]{1,0:T(8,128)S(1)}, f32[144,512]{1,0:T(8,128)S(1)}, u32[]{:S(2)}, u32[]{:S(2)}) collective-permute-start(f32[144,512]{1,0:T(8,128)S(1)} %fusion.3), channel_id=1, source_target_pairs={{0,2},{1,3},{2,0},{3,1},{4,6},{5,7},{6,4},{7,5},{8,10},{9,11},{10,... | collective-permute-start | bytes 884744 | tf_op jit(solution)/shard_map/ppermute | solution.py:14
  131.3 11.4 %collective-permute-start.2 = (f32[144,512]{1,0:T(8,128)S(1)}, f32[144,512]{1,0:T(8,128)S(1)}, u32[]{:S(2)}, u32[]{:S(2)}) collective-permute-start(f32[144,512]{1,0:T(8,128)S(1)} %fusion.1), channel_id=1, source_target_pairs={{0,4},{1,5},{2,6},{3,7},{4,0},{5,1},{6,2},{7,3},{8,12},{9,13},{10,... | collective-permute-start | bytes 884744 | tf_op jit(solution)/shard_map/ppermute | solution.py:14
Sparse Core Ops, SparseCore 0:
  11.7 47.2 all-gather.2
  68.8 43.5 reduce-scatter.1
  143.6 50.9 all-gather.4

commit v2 on v1

--- a/solution.py
+++ b/solution.py
@@ -72,7 +72,8 @@
         jnp.take(probe_flat, sorting, axis=1), basis_flat, preferred_element_type=jnp.float32
     )
     outgoing = jnp.concatenate([coords, area_row, scaled.astype(jnp.float32)], axis=0)
-    piece = lax.all_gather(outgoing, "blk", axis=1, tiled=True)
+    piece = lax.all_gather(outgoing, "ylo", axis=1, tiled=True)
+    piece = lax.all_gather(piece, "core", axis=1, tiled=True)
     near_sum = near_block(coords, area_row[0], piece[:3], piece[3], piece[4:].astype(jnp.bfloat16))
     offdiag = (full_sketch.reshape(probe_count, panels).astype(jnp.float32) - near_sum).astype(
         jnp.bfloat16
@@ -81,21 +82,29 @@
         jnp.take(offdiag, sorting, axis=1), basis_flat, preferred_element_type=jnp.float32
     )
     stacked = jnp.concatenate([sketch_part, probe_part], axis=0)
-    mine = lax.psum_scatter(stacked, "blk", scatter_dimension=0, tiled=True)
+    mine = lax.psum_scatter(stacked, "core", scatter_dimension=0, tiled=True)
+    mine = lax.psum_scatter(mine, "ylo", scatter_dimension=0, tiled=True)
     top = climb_rows(mine, level_mats)
-    nested = lax.all_gather(top, "blk", axis=0, tiled=True).reshape(2, probe_count, basis_width)[None]
+    top = lax.all_gather(top, "ylo", axis=0, tiled=True)
+    nested = lax.all_gather(top, "core", axis=0, tiled=True).reshape(2, probe_count, basis_width)[None]
     return (offdiag.reshape(probe_count, 1, 1, panels), nested)
 
 
 def solution(mesh):
+    blk = mesh.shape["blk"]
+    devices = mesh.devices.reshape(blk // 2, 2, mesh.shape["leaf"])
+    split_mesh = jax.sharding.Mesh(devices, ("ylo", "core", "leaf"))
+    blk_axes = ("ylo", "core")
     in_specs = (
-        P(None, "leaf", "blk", None),
-        P("leaf", "blk", None),
-        P(None, "leaf", "blk", None),
-        P(None, "leaf", "blk", None),
-        P("leaf", "blk", None),
-        P("leaf", "blk", None, None),
+        P(None, "leaf", blk_axes, None),
+        P("leaf", blk_axes, None),
+        P(None, "leaf", blk_axes, None),
+        P(None, "leaf", blk_axes, None),
+        P("leaf", blk_axes, None),
+        P("leaf", blk_axes, None, None),
         P("leaf", None, None, None),
     )
-    out_specs = (P(None, "leaf", "blk", None), P("leaf", None, None, None))
-    return jax.shard_map(shards, mesh=mesh, in_specs=in_specs, out_specs=out_specs, check_vma=False)
+    out_specs = (P(None, "leaf", blk_axes, None), P("leaf", None, None, None))
+    return jax.shard_map(
+        shards, mesh=split_mesh, in_specs=in_specs, out_specs=out_specs, check_vma=False
+    )

time: 205 us -> 264 us (1.29)
  waiting for transfers between devices: 156 us -> 213 us
    all_gather x2 -> x4, waiting for transfers between devices: 97.1 us -> 128 us  [the longest x1 45.6 us: shards(): piece = lax.all_gather(outgoing, 'ylo', axis=1, tiled=True)]
    reduce_scatter x1 -> x2, waiting for transfers between devices: 43.7 us -> 59.1 us  [the longest x1 39.9 us: shards(): mine = lax.psum_scatter(mine, 'ylo', scatter_dimension=0, tiled=True)]
    ppermute x3, waiting for transfers between devices: 15.1 us -> 26.3 us  [partner(): return lax.ppermute(value, axis, pairs)]
  transfers between devices with their start and end apart: 6 -> 9, of which waited for: 6 -> 9; matrix products, arithmetic and copies ran while one was open for 1% -> 0% of each run, Pallas kernels for 0% -> 0%
where the time goes in v2:
time: 264 us; the launch traced here: 263 us
  waiting for transfers between devices  213 us (81%)
  between operations  14.3 us (5%)
  starting transfers between devices  14.2 us (5%)
  local copies, waits for them, and re-layouts  11 us (4%)
  matrix products  6.58 us (2%)
  other arithmetic  4.07 us (2%)
    all_gather x1, waiting for transfers between devices, shards(): piece = lax.all_gather(outgoing, 'ylo', axis=1, tiled=True)  45.6 us
    reduce_scatter x1, waiting for transfers between devices, shards(): mine = lax.psum_scatter(mine, 'ylo', scatter_dimension=0, tiled=True)  39.9 us
    all_gather x1, waiting for transfers between devices, shards(): top = lax.all_gather(top, 'ylo', axis=0, tiled=True)  38.9 us
    ppermute x3, waiting for transfers between devices, partner(): return lax.ppermute(value, axis, pairs)  26.3 us
    all_gather x1, waiting for transfers between devices, shards(): lax.all_gather(top, 'core', axis=0, tiled=True)  22.1 us
    all_gather x1, waiting for transfers between devices, shards(): piece = lax.all_gather(piece, 'core', axis=1, tiled=True)  21.1 us
    reduce_scatter x1, waiting for transfers between devices, shards(): mine = lax.psum_scatter(stacked, 'core', scatter_dimension=0, tiled=True)  19.3 us
    ppermute x3, starting transfers between devices, partner(): return lax.ppermute(value, axis, pairs)  14 us
  transfers between devices with their start and end apart: 9, of which 9 were waited for; matrix products, arithmetic and copies ran while one was open for 0% of the time, Pallas kernels for 0%

profile of v2, /device:TPU:1, one launch (start us, length us, event | category | flops | bytes accessed | tf_op | source)
XLA Modules:
  0.0 263.3 jit_solution(10981654303635103576)
XLA Ops:
  7.2 0.0 copy-start
  7.2 0.0 all-gather.5.cloned.1.call-start
  7.2 0.8 copy.15
  8.0 0.8 copy.13
  8.8 0.0 copy-start.5
  8.8 1.1 copy.14
  9.9 0.7 fusion.25
  10.6 0.9 pad_maximum_fusion.1
  11.5 0.0 copy-start.3
  11.5 0.0 all-gather.5.cloned.1.call-update
  11.6 0.0 all-gather.7.cloned.1.call-start
  11.6 45.6 %all-gather.5.cloned.1.call-done = f32[580,512]{0,1:T(8,128)} async-done(((f32[580,128]{0,1:T(8,128)}), f32[580,512]{0,1:T(8,128)}) %all-gather.5.cloned.1.call-update) | async-done | bytes 1187856 | tf_op jit(solution)/shard_map/all_gather | solution.py:75
  57.2 0.0 all-gather.7.cloned.1.call-update
  57.2 0.0 reduce-scatter.3.cloned.1.call-start
  57.3 0.0 copy-done.5
  57.3 0.9 gather_fusion.1
  58.2 0.0 copy-done.3
  58.2 0.0 copy-done
  58.2 0.0 copy-start.2
  58.2 0.0 copy-start.4
  58.3 0.4 fusion.26
  58.7 21.1 %all-gather.7.cloned.1.call-done = f32[580,1024]{0,1:T(8,128)} async-done(((f32[580,512]{0,1:T(8,128)}), f32[580,1024]{0,1:T(8,128)}) %all-gather.7.cloned.1.call-update) | async-done | bytes 2375696 | tf_op jit(solution)/shard_map/all_gather | solution.py:76
  79.7 3.2 %slice_reduce_fusion.3 = (f32[1024]{0:T(1024)S(1)}, f32[1024]{0:T(1024)S(1)}, f32[1024]{0:T(1024)S(1)}, f32[1024]{0:T(1024)S(1)}) fusion(f32[580,1024]{0,1:T(8,128)} %all-gather.7.cloned.1.call-done), kind=kLoop, calls=%fused_computation.8 | loop fusion | bytes 32768 | tf_op jit(solution)/shard_map/while/body/eval_jaxpr/slice | solution.py:20
  82.9 0.0 copy-done.2
  82.9 0.0 copy-done.4
  82.9 3.6 %fusion.10 = (bf16[576,1,1,128]{3,0,2,1:T(8,128)(2,1)}, f32[576,128]{1,0:T(8,128)S(1)}) fusion(bf16[576,1,1,128]{3,0,2,1:T(8,128)(2,1)S(1)} %copy-done.2, f32[1024]{0:T(1024)S(1)} %get-tuple-element.18, f32[128]{0:T(128)S(1)} %bitcast.50, f32[1024]{0:T(1024)S(1)} %get-tuple-element.19, f32[128]{0:T(128)S(1)} %get-tuple-element.29, ...), kind=kOutput, calls=%fused_computation.23 | convolution fusion | flops 152920064 | bytes 1918976 | tf_op jit(solution)/shard_map/while/body/eval_jaxpr/dot_general | solution.py:40
  86.5 0.2 copy.16
  86.7 0.9 gather_fusion
  87.6 0.4 fusion.28
  88.0 1.6 pad_maximum_fusion
  89.6 0.0 copy-start.1
  89.6 0.0 reduce-scatter.3.cloned.1.call-update
  89.6 0.0 reduce-scatter.5.cloned.1.call-start
  89.7 19.3 %reduce-scatter.3.cloned.1.call-done = f32[576,512]{1,0:T(8,128)} async-done(((f32[1152,512]{1,0:T(8,128)}), f32[576,512]{1,0:T(8,128)}) %reduce-scatter.3.cloned.1.call-update) | async-done | bytes 1179664 | tf_op jit(solution)/shard_map/reduce_scatter | solution.py:85
  108.9 0.0 reduce-scatter.5.cloned.1.call-update
  109.0 0.0 all-gather.9.cloned.1.call-start
  109.0 39.9 %reduce-scatter.5.cloned.1.call-done = f32[144,512]{1,0:T(8,128)} async-done(((f32[576,512]{1,0:T(8,128)}), f32[144,512]{1,0:T(8,128)}) %reduce-scatter.5.cloned.1.call-update) | async-done | bytes 294928 | tf_op jit(solution)/shard_map/reduce_scatter | solution.py:86
  148.9 0.0 copy-done.1
  148.9 1.4 fusion.5
  150.2 3.1 %collective-permute-start = (f32[144,512]{1,0:T(8,128)S(1)}, f32[144,512]{1,0:T(8,128)S(1)}, u32[]{:S(2)}, u32[]{:S(2)}) collective-permute-start(f32[144,512]{1,0:T(8,128)S(1)} %fusion.5), channel_id=1, source_target_pairs={{0,1},{1,0},{2,3},{3,2},{4,5},{5,4},{6,7},{7,6},{8,9},{9,8},{10,11... | collective-permute-start | bytes 884744 | tf_op jit(solution)/shard_map/ppermute | solution.py:14
  153.3 6.5 %collective-permute-done = f32[144,512]{1,0:T(8,128)S(1)} collective-permute-done((f32[144,512]{1,0:T(8,128)S(1)}, f32[144,512]{1,0:T(8,128)S(1)}, u32[]{:S(2)}, u32[]{:S(2)}) %collective-permute-start) | collective-permute-done | bytes 294944 | tf_op jit(solution)/shard_map/ppermute | solution.py:14
  159.8 0.4 fusion.3
  160.2 4.6 %collective-permute-start.1 = (f32[144,512]{1,0:T(8,128)S(1)}, f32[144,512]{1,0:T(8,128)S(1)}, u32[]{:S(2)}, u32[]{:S(2)}) collective-permute-start(f32[144,512]{1,0:T(8,128)S(1)} %fusion.3), channel_id=1, source_target_pairs={{0,2},{1,3},{2,0},{3,1},{4,6},{5,7},{6,4},{7,5},{8,10},{9,11},{10,... | collective-permute-start | bytes 884744 | tf_op jit(solution)/shard_map/ppermute | solution.py:14
  164.8 5.6 %collective-permute-done.1 = f32[144,512]{1,0:T(8,128)S(1)} collective-permute-done((f32[144,512]{1,0:T(8,128)S(1)}, f32[144,512]{1,0:T(8,128)S(1)}, u32[]{:S(2)}, u32[]{:S(2)}) %collective-permute-start.1) | collective-permute-done | bytes 294944 | tf_op jit(solution)/shard_map/ppermute | solution.py:14
  170.4 0.4 fusion.1
  170.8 6.3 %collective-permute-start.2 = (f32[144,512]{1,0:T(8,128)S(1)}, f32[144,512]{1,0:T(8,128)S(1)}, u32[]{:S(2)}, u32[]{:S(2)}) collective-permute-start(f32[144,512]{1,0:T(8,128)S(1)} %fusion.1), channel_id=1, source_target_pairs={{0,4},{1,5},{2,6},{3,7},{4,0},{5,1},{6,2},{7,3},{8,12},{9,13},{10,... | collective-permute-start | bytes 884744 | tf_op jit(solution)/shard_map/ppermute | solution.py:14
  177.1 14.2 %collective-permute-done.2 = f32[144,512]{1,0:T(8,128)S(1)} collective-permute-done((f32[144,512]{1,0:T(8,128)S(1)}, f32[144,512]{1,0:T(8,128)S(1)}, u32[]{:S(2)}, u32[]{:S(2)}) %collective-permute-start.2) | collective-permute-done | bytes 294944 | tf_op jit(solution)/shard_map/ppermute | solution.py:14
  191.4 0.8 add.64
  192.1 0.0 all-gather.9.cloned.1.call-update
  192.2 0.0 all-gather.11.cloned.1.call-start
  192.2 38.9 %all-gather.9.cloned.1.call-done = f32[576,512]{1,0:T(8,128)} async-done(((f32[144,512]{1,0:T(8,128)}), f32[576,512]{1,0:T(8,128)}) %all-gather.9.cloned.1.call-update) | async-done | bytes 1179664 | tf_op jit(solution)/shard_map/all_gather | solution.py:88
  231.1 0.0 all-gather.11.cloned.1.call-update
  231.1 22.1 %all-gather.11.cloned.1.call-done = f32[1152,512]{1,0:T(8,128)} async-done(((f32[576,512]{1,0:T(8,128)}), f32[1152,512]{1,0:T(8,128)}) %all-gather.11.cloned.1.call-update) | async-done | bytes 2359312 | tf_op jit(solution)/shard_map/all_gather | solution.py:89
  253.2 3.3 %copy.18 = f32[1,2,576,512]{3,2,1,0:T(8,128)} copy(f32[1,2,576,512]{3,2,1,0:T(8,128)} %bitcast.46) | data formatting | bytes 4718592
  (5 shorter events, 0.1 us)
Async XLA Ops:
  7.2 51.1 %copy-start = (bf16[1,1,128,512]{3,2,1,0:T(8,128)(2,1)S(1)}, bf16[1,1,128,512]{3,2,1,0:T(8,128)(2,1)}, u32[]{:S(2)}) copy-start(bf16[1,1,128,512]{3,2,1,0:T(8,128)(2,1)} %param.14) | copy-start | bytes 393220
  7.2 50.0 %all-gather.5.cloned.1.call-start = ((), (), s32[]{:S(2)}) async-start(), calls=%async_computation.2 | async-start | bytes 1638400 | tf_op jit(solution)/shard_map/all_gather | solution.py:75
  8.8 48.5 %copy-start.5 = (s32[1,1,128]{2,1,0:T(1,128)S(1)}, s32[1,1,128]{2,1,0:T(1,128)}, u32[]{:S(2)}) copy-start(s32[1,1,128]{2,1,0:T(1,128)} %param.13) | copy-start | bytes 1540
  11.5 46.7 %copy-start.3 = (f32[3,1,1,128]{3,2,1,0:T(1,128)S(1)}, f32[3,1,1,128]{3,2,1,0:T(1,128)}, u32[]{:S(2)}) copy-start(f32[3,1,1,128]{3,2,1,0:T(1,128)} %param.9) | copy-start | bytes 4612
  11.6 68.2 %all-gather.7.cloned.1.call-start = ((), (), s32[]{:S(2)}) async-start(), calls=%async_computation.3 | async-start | bytes 3932160 | tf_op jit(solution)/shard_map/all_gather | solution.py:76
  57.2 51.7 %reduce-scatter.3.cloned.1.call-start = ((), (), s32[]{:S(2)}) async-start(), calls=%async_computation.4 | async-start | bytes 3538944 | tf_op jit(solution)/shard_map/reduce_scatter | solution.py:85
  58.2 24.7 %copy-start.2 = (bf16[576,1,1,128]{3,0,2,1:T(8,128)(2,1)S(1)}, bf16[576,1,1,128]{3,0,2,1:T(8,128)(2,1)}, u32[]{:S(2)}) copy-start(bf16[576,1,1,128]{3,0,2,1:T(8,128)(2,1)} %param.12) | copy-start | bytes 442372
  58.2 24.7 %copy-start.4 = (f32[1,1,128]{2,1,0:T(1,128)S(1)}, f32[1,1,128]{2,1,0:T(1,128)}, u32[]{:S(2)}) copy-start(f32[1,1,128]{2,1,0:T(1,128)} %param.10) | copy-start | bytes 1540
  89.6 59.3 %copy-start.1 = (bf16[1,3,512,512]{3,2,1,0:T(8,128)(2,1)S(1)}, bf16[1,3,512,512]{3,2,1,0:T(8,128)(2,1)}, u32[]{:S(2)}) copy-start(bf16[1,3,512,512]{3,2,1,0:T(8,128)(2,1)} %param.15) | copy-start | bytes 4718596
  89.6 59.2 %reduce-scatter.5.cloned.1.call-start = ((), (), s32[]{:S(2)}) async-start(), calls=%async_computation.5 | async-start | bytes 1474560 | tf_op jit(solution)/shard_map/reduce_scatter | solution.py:86
  109.0 122.1 %all-gather.9.cloned.1.call-start = ((), (), s32[]{:S(2)}) async-start(), calls=%async_computation.6 | async-start | bytes 1474560 | tf_op jit(solution)/shard_map/all_gather | solution.py:88
  150.2 9.6 %collective-permute-start = (f32[144,512]{1,0:T(8,128)S(1)}, f32[144,512]{1,0:T(8,128)S(1)}, u32[]{:S(2)}, u32[]{:S(2)}) collective-permute-start(f32[144,512]{1,0:T(8,128)S(1)} %fusion.5), channel_id=1, source_target_pairs={{0,1},{1,0},{2,3},{3,2},{4,5},{5,4},{6,7},{7,6},{8,9},{9,8},{10,11... | collective-permute-start | bytes 884744 | tf_op jit(solution)/shard_map/ppermute | solution.py:14
  160.2 10.2 %collective-permute-start.1 = (f32[144,512]{1,0:T(8,128)S(1)}, f32[144,512]{1,0:T(8,128)S(1)}, u32[]{:S(2)}, u32[]{:S(2)}) collective-permute-start(f32[144,512]{1,0:T(8,128)S(1)} %fusion.3), channel_id=1, source_target_pairs={{0,2},{1,3},{2,0},{3,1},{4,6},{5,7},{6,4},{7,5},{8,10},{9,11},{10,... | collective-permute-start | bytes 884744 | tf_op jit(solution)/shard_map/ppermute | solution.py:14
  170.8 20.5 %collective-permute-start.2 = (f32[144,512]{1,0:T(8,128)S(1)}, f32[144,512]{1,0:T(8,128)S(1)}, u32[]{:S(2)}, u32[]{:S(2)}) collective-permute-start(f32[144,512]{1,0:T(8,128)S(1)} %fusion.1), channel_id=1, source_target_pairs={{0,4},{1,5},{2,6},{3,7},{4,0},{5,1},{6,2},{7,3},{8,12},{9,13},{10,... | collective-permute-start | bytes 884744 | tf_op jit(solution)/shard_map/ppermute | solution.py:14
  192.2 61.1 %all-gather.11.cloned.1.call-start = ((), (), s32[]{:S(2)}) async-start(), calls=%async_computation.7 | async-start | bytes 3538944 | tf_op jit(solution)/shard_map/all_gather | solution.py:89
Sparse Core Ops, SparseCore 0:
  11.7 45.4 all-gather.4
  59.3 20.4 all-gather.6
  89.8 19.1 reduce-scatter.2
  111.9 36.9 reduce-scatter.4
  192.3 38.7 all-gather.8
  233.3 19.9 all-gather.10

commit v3 on v2

--- a/solution.py
+++ b/solution.py
@@ -56,6 +56,55 @@
     return rows
 
 
+def swap_cores(value):
+    return lax.ppermute(value, "core", [(0, 1), (1, 0)])
+
+
+def shift_chips(value, step):
+    count = lax.axis_size("ylo")
+    return lax.ppermute(value, "ylo", [(source, (source + step) % count) for source in range(count)])
+
+
+def gather_any_order(block, axis):
+    count = lax.axis_size("ylo")
+    parts = [block] + [shift_chips(block, step) for step in range(1, count)]
+    chip_rows = jnp.concatenate(parts, axis)
+    return jnp.concatenate([chip_rows, swap_cores(chip_rows)], axis)
+
+
+def scatter_rows(value):
+    count = lax.axis_size("ylo")
+    chip = lax.axis_index("ylo")
+    core = lax.axis_index("core")
+    half = value.shape[0] // 2
+    chunk = half // count
+    width = value.shape[1]
+    own_half = lax.dynamic_slice(value, (core * half, 0), (half, width))
+    other_half = lax.dynamic_slice(value, ((1 - core) * half, 0), (half, width))
+    summed = own_half + swap_cores(other_half)
+    total = lax.dynamic_slice(summed, (chip * chunk, 0), (chunk, width))
+    for step in range(1, count):
+        target = (chip + step) % count
+        outgoing = lax.dynamic_slice(summed, (target * chunk, 0), (chunk, width))
+        total = total + shift_chips(outgoing, step)
+    return total
+
+
+def gather_rows(rows):
+    count = lax.axis_size("ylo")
+    chip = lax.axis_index("ylo")
+    core = lax.axis_index("core")
+    chunk, width = rows.shape
+    half = jnp.zeros((count * chunk, width), rows.dtype)
+    half = lax.dynamic_update_slice(half, rows, (chip * chunk, 0))
+    for step in range(1, count):
+        source = (chip + count - step) % count
+        half = lax.dynamic_update_slice(half, shift_chips(rows, step), (source * chunk, 0))
+    whole = jnp.zeros((2 * count * chunk, width), rows.dtype)
+    whole = lax.dynamic_update_slice(whole, half, (core * count * chunk, 0))
+    return lax.dynamic_update_slice(whole, swap_cores(half), ((1 - core) * count * chunk, 0))
+
+
 def shards(positions, panel_areas, probe_cols, full_sketch, tree_order, leaf_basis, transfer_mats):
     panels = positions.shape[3]
     probe_count = probe_cols.shape[0]
@@ -72,8 +121,7 @@
         jnp.take(probe_flat, sorting, axis=1), basis_flat, preferred_element_type=jnp.float32
     )
     outgoing = jnp.concatenate([coords, area_row, scaled.astype(jnp.float32)], axis=0)
-    piece = lax.all_gather(outgoing, "ylo", axis=1, tiled=True)
-    piece = lax.all_gather(piece, "core", axis=1, tiled=True)
+    piece = gather_any_order(outgoing, 1)
     near_sum = near_block(coords, area_row[0], piece[:3], piece[3], piece[4:].astype(jnp.bfloat16))
     offdiag = (full_sketch.reshape(probe_count, panels).astype(jnp.float32) - near_sum).astype(
         jnp.bfloat16
@@ -82,11 +130,9 @@
         jnp.take(offdiag, sorting, axis=1), basis_flat, preferred_element_type=jnp.float32
     )
     stacked = jnp.concatenate([sketch_part, probe_part], axis=0)
-    mine = lax.psum_scatter(stacked, "core", scatter_dimension=0, tiled=True)
-    mine = lax.psum_scatter(mine, "ylo", scatter_dimension=0, tiled=True)
+    mine = scatter_rows(stacked)
     top = climb_rows(mine, level_mats)
-    top = lax.all_gather(top, "ylo", axis=0, tiled=True)
-    nested = lax.all_gather(top, "core", axis=0, tiled=True).reshape(2, probe_count, basis_width)[None]
+    nested = gather_rows(top).reshape(2, probe_count, basis_width)[None]
     return (offdiag.reshape(probe_count, 1, 1, panels), nested)
 
 

time: 264 us -> 174 us (0.66)
  the two profiles are of different devices: /device:TPU:1 before, /device:TPU:223 now
where the time goes in v3:
time: 174 us; the launch traced here: 173 us
  waiting for transfers between devices  90.4 us (52%)
  starting transfers between devices  54.8 us (31%)
  local copies, waits for them, and re-layouts  16.2 us (9%)
  matrix products  6.07 us (3%)
  other arithmetic  4.48 us (3%)
    ppermute x9, waiting for transfers between devices, shift_chips(): lax.ppermute(value, 'ylo', [(source, (source + step) % count) for source...  64.2 us
    ppermute x9, starting transfers between devices, shift_chips(): lax.ppermute(value, 'ylo', [(source, (source + step) % count) for source...  33.3 us
    ppermute x3, waiting for transfers between devices, partner(): return lax.ppermute(value, axis, pairs)  21 us
    ppermute x3, starting transfers between devices, partner(): return lax.ppermute(value, axis, pairs)  12.9 us
    ppermute x3, starting transfers between devices, swap_cores(): return lax.ppermute(value, 'core', [(0, 1), (1, 0)])  8.61 us
    unnamed x22, local copies, waits for them, and re-layouts  7.44 us
    ppermute x3, waiting for transfers between devices, swap_cores(): return lax.ppermute(value, 'core', [(0, 1), (1, 0)])  5.17 us
  transfers between devices with their start and end apart: 15, of which 10 were waited for; matrix products, arithmetic and copies ran while one was open for 3% of the time, Pallas kernels for 0%

profile of v3, /device:TPU:223, one launch (start us, length us, event | category | flops | bytes accessed | tf_op | source)
XLA Modules:
  0.0 173.1 jit_solution(180142834288633856)
XLA Ops:
  0.6 0.0 copy-start
  0.7 1.1 copy.18
  1.8 0.8 copy.17
  2.5 0.8 copy.19
  3.3 0.7 fusion.32
  4.1 0.2 pad_maximum_fusion.1
  4.2 1.9 %collective-permute-start = (f32[580,128]{0,1:T(8,128)S(1)}, f32[580,128]{0,1:T(8,128)S(1)}, u32[]{:S(2)}, u32[]{:S(2)}) collective-permute-start(f32[580,128]{0,1:T(8,128)S(1)} %pad_maximum_fusion.1), channel_id=1, source_target_pairs={{0,128},{128,256},{256,384},{384,0},{1,129},{129,257},{257,385},{3... | collective-permute-start | bytes 890888 | tf_op jit(solution)/shard_map/ppermute | solution.py:65
  6.2 3.2 %collective-permute-start.1 = (f32[580,128]{0,1:T(8,128)S(1)}, f32[580,128]{0,1:T(8,128)S(1)}, u32[]{:S(2)}, u32[]{:S(2)}) collective-permute-start(f32[580,128]{0,1:T(8,128)S(1)} %pad_maximum_fusion.1), channel_id=1, source_target_pairs={{0,256},{128,384},{256,0},{384,128},{1,257},{129,385},{257,1},{385... | collective-permute-start | bytes 890888 | tf_op jit(solution)/shard_map/ppermute | solution.py:65
  9.4 2.1 %collective-permute-start.2 = (f32[580,128]{0,1:T(8,128)S(1)}, f32[580,128]{0,1:T(8,128)S(1)}, u32[]{:S(2)}, u32[]{:S(2)}) collective-permute-start(f32[580,128]{0,1:T(8,128)S(1)} %pad_maximum_fusion.1), channel_id=1, source_target_pairs={{0,384},{128,0},{256,128},{384,256},{1,385},{129,1},{257,129},{385... | collective-permute-start | bytes 890888 | tf_op jit(solution)/shard_map/ppermute | solution.py:65
  11.5 0.1 copy.21
  11.7 0.9 gather_fusion.1
  12.6 2.1 %collective-permute-done = f32[580,128]{0,1:T(8,128)S(1)} collective-permute-done((f32[580,128]{0,1:T(8,128)S(1)}, f32[580,128]{0,1:T(8,128)S(1)}, u32[]{:S(2)}, u32[]{:S(2)}) %collective-permute-start) | collective-permute-done | bytes 296992 | tf_op jit(solution)/shard_map/ppermute | solution.py:65
  14.7 21.0 %collective-permute-done.1 = f32[580,128]{0,1:T(8,128)S(1)} collective-permute-done((f32[580,128]{0,1:T(8,128)S(1)}, f32[580,128]{0,1:T(8,128)S(1)}, u32[]{:S(2)}, u32[]{:S(2)}) %collective-permute-start.1) | collective-permute-done | bytes 296992 | tf_op jit(solution)/shard_map/ppermute | solution.py:65
  35.7 0.2 pad_maximum_fusion
  35.9 0.0 copy-start.5
  35.9 1.4 copy.20
  37.3 3.4 %collective-permute-start.3 = (f32[580,512]{1,0:T(8,128)}, f32[580,512]{1,0:T(8,128)}, u32[]{:S(2)}, u32[]{:S(2)}) collective-permute-start(f32[580,512]{1,0:T(8,128)} %copy.20), channel_id=1, source_target_pairs={{0,64},{64,0},{1,65},{65,1},{2,66},{66,2},{3,67},{67,3},{4,68},{68... | collective-permute-start | bytes 3563528 | tf_op jit(solution)/shard_map/ppermute | solution.py:60
  40.7 0.8 constant_dynamic-update-slice_fusion.4
  41.6 0.4 fusion.33
  42.0 0.1 copy.22
  42.1 0.2 copy.23
  42.3 0.2 copy.24
  42.4 0.8 constant_dynamic-update-slice_fusion.3
  43.2 0.8 constant_dynamic-update-slice_fusion.2
  44.0 0.8 constant_dynamic-update-slice_fusion.1
  44.8 2.4 %constant_dynamic-update-slice_fusion = f32[580,1024]{1,0:T(8,128)} fusion(f32[580,1024]{1,0:T(8,128)} %constant_dynamic-update-slice_fusion.1, f32[580,512]{1,0:T(8,128)} %collective-permute-done.3), kind=kLoop, calls=%fused_computation.58 | loop fusion | bytes 2392064 | tf_op jit(solution)/shard_map/concatenate | solution.py:72
  47.2 0.9 fusion.50
  48.1 3.1 %fusion.13 = (bf16[576,1,1,128]{3,0,2,1:T(8,128)(2,1)}, f32[576,128]{1,0:T(8,128)S(1)}) fusion(bf16[576,1,1,128]{3,0,2,1:T(8,128)(2,1)S(1)} %copy-done.4, f32[1024]{0:T(1024)S(1)} %bitcast.53, f32[128]{0:T(128)S(1)} %bitcast.58, f32[1024]{0:T(1024)S(1)} %bitcast.54, f32[128]{0:T(128)S(1)} %get-tuple-element.34, f32[1024]{0:T(1024)S(1)} %bitcast.55, ...), kind=kOutput, calls=%fused_computation.26 | convolution fusion | flops 152920064 | bytes 1787904 | tf_op jit(solution)/shard_map/while/body/eval_jaxpr/dot_general | solution.py:40
  51.2 0.2 copy.25
  51.4 0.9 gather_fusion
  52.3 0.4 fusion.35
  52.7 1.5 fusion.1
  54.2 1.9 %collective-permute-start.4 = (f32[576,512]{1,0:T(8,128)}, f32[576,512]{1,0:T(8,128)}, u32[]{:S(2)}, u32[]{:S(2)}) collective-permute-start(f32[576,512]{1,0:T(8,128)} %fusion.1), channel_id=1, source_target_pairs={{0,64},{64,0},{1,65},{65,1},{2,66},{66,2},{3,67},{67,3},{4,68},{68... | collective-permute-start | bytes 3538952 | tf_op jit(solution)/shard_map/ppermute | solution.py:60
  56.2 3.1 %collective-permute-done.4 = f32[576,512]{1,0:T(8,128)} collective-permute-done((f32[576,512]{1,0:T(8,128)}, f32[576,512]{1,0:T(8,128)}, u32[]{:S(2)}, u32[]{:S(2)}) %collective-permute-start.4) | collective-permute-done | bytes 1179680 | tf_op jit(solution)/shard_map/ppermute | solution.py:60
  59.3 1.8 %fusion.3 = f32[576,512]{1,0:T(8,128)S(1)} fusion(f32[576,512]{1,0:T(8,128)} %collective-permute-done.4, s32[]{:T(128)S(6)} %select_n.52, f32[576,512]{1,0:T(8,128)S(1)} %fusion.35, f32[576,512]{1,0:T(8,128)S(1)} %fusion.33), kind=kLoop, calls=%fused_computation.11 | loop fusion | flops 589824 | bytes 4718596 | tf_op jit(solution)/shard_map/add | solution.py:84
  61.1 0.0 copy-start.1
  61.1 1.0 copy-done.1
  62.1 0.1 constant_dynamic-slice_fusion.2
  62.1 2.1 %collective-permute-start.5 = (f32[144,512]{1,0:T(8,128)S(1)}, f32[144,512]{1,0:T(8,128)S(1)}, u32[]{:S(2)}, u32[]{:S(2)}) collective-permute-start(f32[144,512]{1,0:T(8,128)S(1)} %get-tuple-element.30), channel_id=1, source_target_pairs={{0,128},{128,256},{256,384},{384,0},{1,129},{129,257},{257,385},{3... | collective-permute-start | bytes 884744 | tf_op jit(solution)/shard_map/ppermute | solution.py:65
  64.2 2.9 %collective-permute-start.6 = (f32[144,512]{1,0:T(8,128)S(1)}, f32[144,512]{1,0:T(8,128)S(1)}, u32[]{:S(2)}, u32[]{:S(2)}) collective-permute-start(f32[144,512]{1,0:T(8,128)S(1)} %get-tuple-element.32), channel_id=1, source_target_pairs={{0,256},{128,384},{256,0},{384,128},{1,257},{129,385},{257,1},{385... | collective-permute-start | bytes 884744 | tf_op jit(solution)/shard_map/ppermute | solution.py:65
  67.1 3.4 %collective-permute-start.7 = (f32[144,512]{1,0:T(8,128)S(1)}, f32[144,512]{1,0:T(8,128)S(1)}, u32[]{:S(2)}, u32[]{:S(2)}) collective-permute-start(f32[144,512]{1,0:T(8,128)S(1)} %get-tuple-element.31), channel_id=1, source_target_pairs={{0,384},{128,0},{256,128},{384,256},{1,385},{129,1},{257,129},{385... | collective-permute-start | bytes 884744 | tf_op jit(solution)/shard_map/ppermute | solution.py:65
  70.5 2.3 %collective-permute-done.5 = f32[144,512]{1,0:T(8,128)S(1)} collective-permute-done((f32[144,512]{1,0:T(8,128)S(1)}, f32[144,512]{1,0:T(8,128)S(1)}, u32[]{:S(2)}, u32[]{:S(2)}) %collective-permute-start.5) | collective-permute-done | bytes 294944 | tf_op jit(solution)/shard_map/ppermute | solution.py:65
  72.8 18.5 %collective-permute-done.6 = f32[144,512]{1,0:T(8,128)S(1)} collective-permute-done((f32[144,512]{1,0:T(8,128)S(1)}, f32[144,512]{1,0:T(8,128)S(1)}, u32[]{:S(2)}, u32[]{:S(2)}) %collective-permute-start.6) | collective-permute-done | bytes 294944 | tf_op jit(solution)/shard_map/ppermute | solution.py:65
  91.4 1.4 fusion.8
  92.8 2.5 %collective-permute-start.8 = (f32[144,512]{1,0:T(8,128)S(1)}, f32[144,512]{1,0:T(8,128)S(1)}, u32[]{:S(2)}, u32[]{:S(2)}) collective-permute-start(f32[144,512]{1,0:T(8,128)S(1)} %fusion.8), channel_id=1, source_target_pairs={{0,1},{1,0},{2,3},{3,2},{4,5},{5,4},{6,7},{7,6},{8,9},{9,8},{10,11... | collective-permute-start | bytes 884744 | tf_op jit(solution)/shard_map/ppermute | solution.py:14
  95.3 7.2 %collective-permute-done.8 = f32[144,512]{1,0:T(8,128)S(1)} collective-permute-done((f32[144,512]{1,0:T(8,128)S(1)}, f32[144,512]{1,0:T(8,128)S(1)}, u32[]{:S(2)}, u32[]{:S(2)}) %collective-permute-start.8) | collective-permute-done | bytes 294944 | tf_op jit(solution)/shard_map/ppermute | solution.py:14
  102.5 0.4 fusion.6
  102.9 3.0 %collective-permute-start.9 = (f32[144,512]{1,0:T(8,128)S(1)}, f32[144,512]{1,0:T(8,128)S(1)}, u32[]{:S(2)}, u32[]{:S(2)}) collective-permute-start(f32[144,512]{1,0:T(8,128)S(1)} %fusion.6), channel_id=1, source_target_pairs={{0,2},{1,3},{2,0},{3,1},{4,6},{5,7},{6,4},{7,5},{8,10},{9,11},{10,... | collective-permute-start | bytes 884744 | tf_op jit(solution)/shard_map/ppermute | solution.py:14
  106.0 7.3 %collective-permute-done.9 = f32[144,512]{1,0:T(8,128)S(1)} collective-permute-done((f32[144,512]{1,0:T(8,128)S(1)}, f32[144,512]{1,0:T(8,128)S(1)}, u32[]{:S(2)}, u32[]{:S(2)}) %collective-permute-start.9) | collective-permute-done | bytes 294944 | tf_op jit(solution)/shard_map/ppermute | solution.py:14
  113.2 0.4 fusion.4
  113.6 7.4 %collective-permute-start.10 = (f32[144,512]{1,0:T(8,128)S(1)}, f32[144,512]{1,0:T(8,128)S(1)}, u32[]{:S(2)}, u32[]{:S(2)}) collective-permute-start(f32[144,512]{1,0:T(8,128)S(1)} %fusion.4), channel_id=1, source_target_pairs={{0,4},{1,5},{2,6},{3,7},{4,0},{5,1},{6,2},{7,3},{8,12},{9,13},{10,... | collective-permute-start | bytes 884744 | tf_op jit(solution)/shard_map/ppermute | solution.py:14
  121.1 6.5 %collective-permute-done.10 = f32[144,512]{1,0:T(8,128)S(1)} collective-permute-done((f32[144,512]{1,0:T(8,128)S(1)}, f32[144,512]{1,0:T(8,128)S(1)}, u32[]{:S(2)}, u32[]{:S(2)}) %collective-permute-start.10) | collective-permute-done | bytes 294944 | tf_op jit(solution)/shard_map/ppermute | solution.py:14
  127.6 0.1 broadcast_in_dim.22
  127.8 1.9 %collective-permute-start.11 = (f32[144,512]{1,0:T(8,128)S(1)}, f32[144,512]{1,0:T(8,128)S(1)}, u32[]{:S(2)}, u32[]{:S(2)}) collective-permute-start(f32[144,512]{1,0:T(8,128)S(1)} %get-tuple-element.18), channel_id=1, source_target_pairs={{0,128},{128,256},{256,384},{384,0},{1,129},{129,257},{257,385},{3... | collective-permute-start | bytes 884744 | tf_op jit(solution)/shard_map/ppermute | solution.py:65
  129.7 12.4 %collective-permute-start.12 = (f32[144,512]{1,0:T(8,128)S(1)}, f32[144,512]{1,0:T(8,128)S(1)}, u32[]{:S(2)}, u32[]{:S(2)}) collective-permute-start(f32[144,512]{1,0:T(8,128)S(1)} %get-tuple-element.18), channel_id=1, source_target_pairs={{0,256},{128,384},{256,0},{384,128},{1,257},{129,385},{257,1},{385... | collective-permute-start | bytes 884744 | tf_op jit(solution)/shard_map/ppermute | solution.py:65
  142.2 3.4 %collective-permute-start.13 = (f32[144,512]{1,0:T(8,128)S(1)}, f32[144,512]{1,0:T(8,128)S(1)}, u32[]{:S(2)}, u32[]{:S(2)}) collective-permute-start(f32[144,512]{1,0:T(8,128)S(1)} %get-tuple-element.18), channel_id=1, source_target_pairs={{0,384},{128,0},{256,128},{384,256},{1,385},{129,1},{257,129},{385... | collective-permute-start | bytes 884744 | tf_op jit(solution)/shard_map/ppermute | solution.py:65
  145.6 20.2 %collective-permute-done.12 = f32[144,512]{1,0:T(8,128)S(1)} collective-permute-done((f32[144,512]{1,0:T(8,128)S(1)}, f32[144,512]{1,0:T(8,128)S(1)}, u32[]{:S(2)}, u32[]{:S(2)}) %collective-permute-start.12) | collective-permute-done | bytes 294944 | tf_op jit(solution)/shard_map/ppermute | solution.py:65
  165.9 3.3 %collective-permute-start.14 = (f32[576,512]{1,0:T(8,128)S(1)}, f32[576,512]{1,0:T(8,128)S(1)}, u32[]{:S(2)}, u32[]{:S(2)}) collective-permute-start(f32[576,512]{1,0:T(8,128)S(1)} %constant_dynamic-update-slice_fusion.7), channel_id=1, source_target_pairs={{0,64},{64,0},{1,65},{65,1},{2,66},{66,2},{3,67},{67,3},{4,68},{68... | collective-permute-start | bytes 3538952 | tf_op jit(solution)/shard_map/ppermute | solution.py:60
  169.1 0.3 broadcast_in_dim.21
  169.4 0.1 constant_dynamic-update-slice_fusion.6
  169.5 2.1 %collective-permute-done.14 = f32[576,512]{1,0:T(8,128)S(1)} collective-permute-done((f32[576,512]{1,0:T(8,128)S(1)}, f32[576,512]{1,0:T(8,128)S(1)}, u32[]{:S(2)}, u32[]{:S(2)}) %collective-permute-start.14) | collective-permute-done | bytes 1179680 | tf_op jit(solution)/shard_map/ppermute | solution.py:60
  171.6 0.1 constant_dynamic-update-slice_fusion.5
  171.7 0.0 copy-start.2
  171.7 1.4 copy-done.2
  (24 shorter events, 0.2 us)
Async XLA Ops:
  0.6 40.9 %copy-start = (bf16[1,1,128,512]{3,2,1,0:T(8,128)(2,1)S(1)}, bf16[1,1,128,512]{3,2,1,0:T(8,128)(2,1)}, u32[]{:S(2)}) copy-start(bf16[1,1,128,512]{3,2,1,0:T(8,128)(2,1)} %param.14) | copy-start | bytes 393220
  0.6 11.0 %copy-start.7 = (s32[1,1,128]{2,1,0:T(1,128)S(1)}, s32[1,1,128]{2,1,0:T(1,128)}, u32[]{:S(2)}) copy-start(s32[1,1,128]{2,1,0:T(1,128)} %param.13) | copy-start | bytes 1540
  4.2 10.5 %collective-permute-start = (f32[580,128]{0,1:T(8,128)S(1)}, f32[580,128]{0,1:T(8,128)S(1)}, u32[]{:S(2)}, u32[]{:S(2)}) collective-permute-start(f32[580,128]{0,1:T(8,128)S(1)} %pad_maximum_fusion.1), channel_id=1, source_target_pairs={{0,128},{128,256},{256,384},{384,0},{1,129},{129,257},{257,385},{3... | collective-permute-start | bytes 890888 | tf_op jit(solution)/shard_map/ppermute | solution.py:65
  6.2 29.5 %collective-permute-start.1 = (f32[580,128]{0,1:T(8,128)S(1)}, f32[580,128]{0,1:T(8,128)S(1)}, u32[]{:S(2)}, u32[]{:S(2)}) collective-permute-start(f32[580,128]{0,1:T(8,128)S(1)} %pad_maximum_fusion.1), channel_id=1, source_target_pairs={{0,256},{128,384},{256,0},{384,128},{1,257},{129,385},{257,1},{385... | collective-permute-start | bytes 890888 | tf_op jit(solution)/shard_map/ppermute | solution.py:65
  9.4 26.2 %collective-permute-start.2 = (f32[580,128]{0,1:T(8,128)S(1)}, f32[580,128]{0,1:T(8,128)S(1)}, u32[]{:S(2)}, u32[]{:S(2)}) collective-permute-start(f32[580,128]{0,1:T(8,128)S(1)} %pad_maximum_fusion.1), channel_id=1, source_target_pairs={{0,384},{128,0},{256,128},{384,256},{1,385},{129,1},{257,129},{385... | collective-permute-start | bytes 890888 | tf_op jit(solution)/shard_map/ppermute | solution.py:65
  35.9 5.7 %copy-start.5 = (f32[3,1,1,128]{3,2,1,0:T(1,128)S(1)}, f32[3,1,1,128]{3,2,1,0:T(1,128)}, u32[]{:S(2)}) copy-start(f32[3,1,1,128]{3,2,1,0:T(1,128)} %param.9) | copy-start | bytes 4612
  37.3 7.5 %collective-permute-start.3 = (f32[580,512]{1,0:T(8,128)}, f32[580,512]{1,0:T(8,128)}, u32[]{:S(2)}, u32[]{:S(2)}) collective-permute-start(f32[580,512]{1,0:T(8,128)} %copy.20), channel_id=1, source_target_pairs={{0,64},{64,0},{1,65},{65,1},{2,66},{66,2},{3,67},{67,3},{4,68},{68... | collective-permute-start | bytes 3563528 | tf_op jit(solution)/shard_map/ppermute | solution.py:60
  44.7 3.4 %copy-start.4 = (bf16[576,1,1,128]{3,0,2,1:T(8,128)(2,1)S(1)}, bf16[576,1,1,128]{3,0,2,1:T(8,128)(2,1)}, u32[]{:S(2)}) copy-start(bf16[576,1,1,128]{3,0,2,1:T(8,128)(2,1)} %param.12) | copy-start | bytes 442372
  44.8 3.4 %copy-start.6 = (f32[1,1,128]{2,1,0:T(1,128)S(1)}, f32[1,1,128]{2,1,0:T(1,128)}, u32[]{:S(2)}) copy-start(f32[1,1,128]{2,1,0:T(1,128)} %param.10) | copy-start | bytes 1540
  54.2 5.1 %collective-permute-start.4 = (f32[576,512]{1,0:T(8,128)}, f32[576,512]{1,0:T(8,128)}, u32[]{:S(2)}, u32[]{:S(2)}) collective-permute-start(f32[576,512]{1,0:T(8,128)} %fusion.1), channel_id=1, source_target_pairs={{0,64},{64,0},{1,65},{65,1},{2,66},{66,2},{3,67},{67,3},{4,68},{68... | collective-permute-start | bytes 3538952 | tf_op jit(solution)/shard_map/ppermute | solution.py:60
  61.1 1.0 copy-start.1
  62.1 29.3 %copy-start.3 = (bf16[1,3,512,512]{3,2,1,0:T(8,128)(2,1)S(1)}, bf16[1,3,512,512]{3,2,1,0:T(8,128)(2,1)}, u32[]{:S(2)}) copy-start(bf16[1,3,512,512]{3,2,1,0:T(8,128)(2,1)} %param.15) | copy-start | bytes 4718596
  62.1 10.7 %collective-permute-start.5 = (f32[144,512]{1,0:T(8,128)S(1)}, f32[144,512]{1,0:T(8,128)S(1)}, u32[]{:S(2)}, u32[]{:S(2)}) collective-permute-start(f32[144,512]{1,0:T(8,128)S(1)} %get-tuple-element.30), channel_id=1, source_target_pairs={{0,128},{128,256},{256,384},{384,0},{1,129},{129,257},{257,385},{3... | collective-permute-start | bytes 884744 | tf_op jit(solution)/shard_map/ppermute | solution.py:65
  64.2 27.2 %collective-permute-start.6 = (f32[144,512]{1,0:T(8,128)S(1)}, f32[144,512]{1,0:T(8,128)S(1)}, u32[]{:S(2)}, u32[]{:S(2)}) collective-permute-start(f32[144,512]{1,0:T(8,128)S(1)} %get-tuple-element.32), channel_id=1, source_target_pairs={{0,256},{128,384},{256,0},{384,128},{1,257},{129,385},{257,1},{385... | collective-permute-start | bytes 884744 | tf_op jit(solution)/shard_map/ppermute | solution.py:65
  67.1 24.3 %collective-permute-start.7 = (f32[144,512]{1,0:T(8,128)S(1)}, f32[144,512]{1,0:T(8,128)S(1)}, u32[]{:S(2)}, u32[]{:S(2)}) collective-permute-start(f32[144,512]{1,0:T(8,128)S(1)} %get-tuple-element.31), channel_id=1, source_target_pairs={{0,384},{128,0},{256,128},{384,256},{1,385},{129,1},{257,129},{385... | collective-permute-start | bytes 884744 | tf_op jit(solution)/shard_map/ppermute | solution.py:65
  92.8 9.7 %collective-permute-start.8 = (f32[144,512]{1,0:T(8,128)S(1)}, f32[144,512]{1,0:T(8,128)S(1)}, u32[]{:S(2)}, u32[]{:S(2)}) collective-permute-start(f32[144,512]{1,0:T(8,128)S(1)} %fusion.8), channel_id=1, source_target_pairs={{0,1},{1,0},{2,3},{3,2},{4,5},{5,4},{6,7},{7,6},{8,9},{9,8},{10,11... | collective-permute-start | bytes 884744 | tf_op jit(solution)/shard_map/ppermute | solution.py:14
  102.9 10.3 %collective-permute-start.9 = (f32[144,512]{1,0:T(8,128)S(1)}, f32[144,512]{1,0:T(8,128)S(1)}, u32[]{:S(2)}, u32[]{:S(2)}) collective-permute-start(f32[144,512]{1,0:T(8,128)S(1)} %fusion.6), channel_id=1, source_target_pairs={{0,2},{1,3},{2,0},{3,1},{4,6},{5,7},{6,4},{7,5},{8,10},{9,11},{10,... | collective-permute-start | bytes 884744 | tf_op jit(solution)/shard_map/ppermute | solution.py:14
  113.6 14.0 %collective-permute-start.10 = (f32[144,512]{1,0:T(8,128)S(1)}, f32[144,512]{1,0:T(8,128)S(1)}, u32[]{:S(2)}, u32[]{:S(2)}) collective-permute-start(f32[144,512]{1,0:T(8,128)S(1)} %fusion.4), channel_id=1, source_target_pairs={{0,4},{1,5},{2,6},{3,7},{4,0},{5,1},{6,2},{7,3},{8,12},{9,13},{10,... | collective-permute-start | bytes 884744 | tf_op jit(solution)/shard_map/ppermute | solution.py:14
  127.8 17.7 %collective-permute-start.11 = (f32[144,512]{1,0:T(8,128)S(1)}, f32[144,512]{1,0:T(8,128)S(1)}, u32[]{:S(2)}, u32[]{:S(2)}) collective-permute-start(f32[144,512]{1,0:T(8,128)S(1)} %get-tuple-element.18), channel_id=1, source_target_pairs={{0,128},{128,256},{256,384},{384,0},{1,129},{129,257},{257,385},{3... | collective-permute-start | bytes 884744 | tf_op jit(solution)/shard_map/ppermute | solution.py:65
  129.7 36.1 %collective-permute-start.12 = (f32[144,512]{1,0:T(8,128)S(1)}, f32[144,512]{1,0:T(8,128)S(1)}, u32[]{:S(2)}, u32[]{:S(2)}) collective-permute-start(f32[144,512]{1,0:T(8,128)S(1)} %get-tuple-element.18), channel_id=1, source_target_pairs={{0,256},{128,384},{256,0},{384,128},{1,257},{129,385},{257,1},{385... | collective-permute-start | bytes 884744 | tf_op jit(solution)/shard_map/ppermute | solution.py:65
  142.2 23.7 %collective-permute-start.13 = (f32[144,512]{1,0:T(8,128)S(1)}, f32[144,512]{1,0:T(8,128)S(1)}, u32[]{:S(2)}, u32[]{:S(2)}) collective-permute-start(f32[144,512]{1,0:T(8,128)S(1)} %get-tuple-element.18), channel_id=1, source_target_pairs={{0,384},{128,0},{256,128},{384,256},{1,385},{129,1},{257,129},{385... | collective-permute-start | bytes 884744 | tf_op jit(solution)/shard_map/ppermute | solution.py:65
  165.9 5.7 %collective-permute-start.14 = (f32[576,512]{1,0:T(8,128)S(1)}, f32[576,512]{1,0:T(8,128)S(1)}, u32[]{:S(2)}, u32[]{:S(2)}) collective-permute-start(f32[576,512]{1,0:T(8,128)S(1)} %constant_dynamic-update-slice_fusion.7), channel_id=1, source_target_pairs={{0,64},{64,0},{1,65},{65,1},{2,66},{66,2},{3,67},{67,3},{4,68},{68... | collective-permute-start | bytes 3538952 | tf_op jit(solution)/shard_map/ppermute | solution.py:60
  171.7 1.4 copy-start.2

commit v4 on v3

--- a/solution.py
+++ b/solution.py
@@ -129,10 +129,9 @@
     sketch_part = jnp.dot(
         jnp.take(offdiag, sorting, axis=1), basis_flat, preferred_element_type=jnp.float32
     )
-    stacked = jnp.concatenate([sketch_part, probe_part], axis=0)
-    mine = scatter_rows(stacked)
-    top = climb_rows(mine, level_mats)
-    nested = gather_rows(top).reshape(2, probe_count, basis_width)[None]
+    probe_top = gather_rows(climb_rows(scatter_rows(probe_part), level_mats))
+    sketch_top = gather_rows(climb_rows(scatter_rows(sketch_part), level_mats))
+    nested = jnp.stack([sketch_top, probe_top], axis=0)[None]
     return (offdiag.reshape(probe_count, 1, 1, panels), nested)
 
 

time: 174 us -> 171 us (0.983)
  the two profiles are of different devices: /device:TPU:223 before, /device:TPU:1 now
where the time goes in v4:
time: 171 us; the launch traced here: 170 us
  starting transfers between devices  98.2 us (57%)
  waiting for transfers between devices  40.2 us (24%)
  local copies, waits for them, and re-layouts  17.9 us (10%)
  matrix products  7.24 us (4%)
  other arithmetic  5.15 us (3%)
    ppermute x15, starting transfers between devices, shift_chips(): lax.ppermute(value, 'ylo', [(source, (source + step) % count) for source...  55.8 us
    ppermute x15, waiting for transfers between devices, shift_chips(): lax.ppermute(value, 'ylo', [(source, (source + step) % count) for source...  37.2 us
    ppermute x6, starting transfers between devices, partner(): return lax.ppermute(value, axis, pairs)  28.8 us
    ppermute x5, starting transfers between devices, swap_cores(): return lax.ppermute(value, 'core', [(0, 1), (1, 0)])  13.6 us
    unnamed x30, local copies, waits for them, and re-layouts  6.53 us
  transfers between devices with their start and end apart: 26, of which 10 were waited for; matrix products, arithmetic and copies ran while one was open for 13% of the time, Pallas kernels for 0%

profile of v4, /device:TPU:1, one launch (start us, length us, event | category | flops | bytes accessed | tf_op | source)
XLA Modules:
  0.0 169.9 jit_solution(8171242005373760891)
XLA Ops:
  0.7 1.1 copy.18
  1.8 0.8 copy.17
  2.5 0.8 copy.19
  3.3 0.7 fusion.32
  4.2 4.0 %collective-permute-start = (f32[580,128]{0,1:T(8,128)S(1)}, f32[580,128]{0,1:T(8,128)S(1)}, u32[]{:S(2)}, u32[]{:S(2)}) collective-permute-start(f32[580,128]{0,1:T(8,128)S(1)} %pad_maximum_fusion.1), channel_id=1, source_target_pairs={{0,128},{128,256},{256,384},{384,0},{1,129},{129,257},{257,385},{3... | collective-permute-start | bytes 890888 | tf_op jit(solution)/shard_map/ppermute | solution.py:65
  8.3 4.2 %collective-permute-start.1 = (f32[580,128]{0,1:T(8,128)S(1)}, f32[580,128]{0,1:T(8,128)S(1)}, u32[]{:S(2)}, u32[]{:S(2)}) collective-permute-start(f32[580,128]{0,1:T(8,128)S(1)} %pad_maximum_fusion.1), channel_id=1, source_target_pairs={{0,256},{128,384},{256,0},{384,128},{1,257},{129,385},{257,1},{385... | collective-permute-start | bytes 890888 | tf_op jit(solution)/shard_map/ppermute | solution.py:65
  12.5 3.0 %collective-permute-start.2 = (f32[580,128]{0,1:T(8,128)S(1)}, f32[580,128]{0,1:T(8,128)S(1)}, u32[]{:S(2)}, u32[]{:S(2)}) collective-permute-start(f32[580,128]{0,1:T(8,128)S(1)} %pad_maximum_fusion.1), channel_id=1, source_target_pairs={{0,384},{128,0},{256,128},{384,256},{1,385},{129,1},{257,129},{385... | collective-permute-start | bytes 890888 | tf_op jit(solution)/shard_map/ppermute | solution.py:65
  15.5 17.0 %collective-permute-done.1 = f32[580,128]{0,1:T(8,128)S(1)} collective-permute-done((f32[580,128]{0,1:T(8,128)S(1)}, f32[580,128]{0,1:T(8,128)S(1)}, u32[]{:S(2)}, u32[]{:S(2)}) %collective-permute-start.1) | collective-permute-done | bytes 296992 | tf_op jit(solution)/shard_map/ppermute | solution.py:65
  33.6 1.4 copy.20
  35.0 4.0 %collective-permute-start.3 = (f32[580,512]{1,0:T(8,128)}, f32[580,512]{1,0:T(8,128)}, u32[]{:S(2)}, u32[]{:S(2)}) collective-permute-start(f32[580,512]{1,0:T(8,128)} %copy.20), channel_id=1, source_target_pairs={{0,64},{64,0},{1,65},{65,1},{2,66},{66,2},{3,67},{67,3},{4,68},{68... | collective-permute-start | bytes 3563528 | tf_op jit(solution)/shard_map/ppermute | solution.py:60
  39.0 0.9 gather_fusion.1
  39.9 0.4 fusion.33
  40.3 0.9 constant_dynamic-slice_fusion.3
  41.2 2.0 %collective-permute-start.15 = (f32[288,512]{1,0:T(8,128)}, f32[288,512]{1,0:T(8,128)}, u32[]{:S(2)}, u32[]{:S(2)}) collective-permute-start(f32[288,512]{1,0:T(8,128)} %constant_dynamic-slice_fusion.3), channel_id=1, source_target_pairs={{0,64},{64,0},{1,65},{65,1},{2,66},{66,2},{3,67},{67,3},{4,68},{68... | collective-permute-start | bytes 1769480 | tf_op jit(solution)/shard_map/ppermute | solution.py:60
  43.5 0.8 constant_dynamic-update-slice_fusion.4
  44.7 0.7 constant_dynamic-update-slice_fusion.3
  45.4 0.8 constant_dynamic-update-slice_fusion.2
  46.2 0.8 constant_dynamic-update-slice_fusion.1
  47.0 2.5 %constant_dynamic-update-slice_fusion = f32[580,1024]{1,0:T(8,128)} fusion(f32[580,1024]{1,0:T(8,128)} %constant_dynamic-update-slice_fusion.1, f32[580,512]{1,0:T(8,128)} %collective-permute-done.3), kind=kLoop, calls=%fused_computation.73 | loop fusion | bytes 2392064 | tf_op jit(solution)/shard_map/concatenate | solution.py:72
  49.5 1.0 fusion.63
  50.4 3.1 %fusion.19 = (bf16[576,1,1,128]{3,0,2,1:T(8,128)(2,1)}, f32[576,128]{1,0:T(8,128)S(1)}) fusion(bf16[576,1,1,128]{3,0,2,1:T(8,128)(2,1)S(1)} %copy-done.8, f32[1024]{0:T(1024)S(1)} %bitcast.67, f32[128]{0:T(128)S(1)} %bitcast.72, f32[1024]{0:T(1024)S(1)} %bitcast.68, f32[128]{0:T(128)S(1)} %get-tuple-element.39, f32[1024]{0:T(1024)S(1)} %bitcast.69, ...), kind=kOutput, calls=%fused_computation.35 | convolution fusion | flops 152920064 | bytes 1787904 | tf_op jit(solution)/shard_map/while/body/eval_jaxpr/dot_general | solution.py:40
  53.7 0.9 gather_fusion
  54.6 0.4 fusion.35
  55.0 1.0 copy-done.2
  56.0 0.9 constant_dynamic-slice_fusion.7
  56.9 2.5 %collective-permute-start.4 = (f32[288,512]{1,0:T(8,128)}, f32[288,512]{1,0:T(8,128)}, u32[]{:S(2)}, u32[]{:S(2)}) collective-permute-start(f32[288,512]{1,0:T(8,128)} %constant_dynamic-slice_fusion.7), channel_id=1, source_target_pairs={{0,64},{64,0},{1,65},{65,1},{2,66},{66,2},{3,67},{67,3},{4,68},{68... | collective-permute-start | bytes 1769480 | tf_op jit(solution)/shard_map/ppermute | solution.py:60
  59.4 1.2 dynamic-slice_add_fusion
  60.6 0.8 constant_dynamic-slice_fusion.2
  61.4 7.3 %collective-permute-start.16 = (f32[72,512]{1,0:T(8,128)}, f32[72,512]{1,0:T(8,128)}, u32[]{:S(2)}, u32[]{:S(2)}) collective-permute-start(f32[72,512]{1,0:T(8,128)} %get-tuple-element.35), channel_id=1, source_target_pairs={{0,128},{128,256},{256,384},{384,0},{1,129},{129,257},{257,385},{3... | collective-permute-start | bytes 442376 | tf_op jit(solution)/shard_map/ppermute | solution.py:65
  68.7 3.3 %collective-permute-start.17 = (f32[72,512]{1,0:T(8,128)}, f32[72,512]{1,0:T(8,128)}, u32[]{:S(2)}, u32[]{:S(2)}) collective-permute-start(f32[72,512]{1,0:T(8,128)} %get-tuple-element.37), channel_id=1, source_target_pairs={{0,256},{128,384},{256,0},{384,128},{1,257},{129,385},{257,1},{385... | collective-permute-start | bytes 442376 | tf_op jit(solution)/shard_map/ppermute | solution.py:65
  72.0 2.6 %collective-permute-start.18 = (f32[72,512]{1,0:T(8,128)}, f32[72,512]{1,0:T(8,128)}, u32[]{:S(2)}, u32[]{:S(2)}) collective-permute-start(f32[72,512]{1,0:T(8,128)} %get-tuple-element.36), channel_id=1, source_target_pairs={{0,384},{128,0},{256,128},{384,256},{1,385},{129,1},{257,129},{385... | collective-permute-start | bytes 442376 | tf_op jit(solution)/shard_map/ppermute | solution.py:65
  74.7 6.2 %collective-permute-done.17 = f32[72,512]{1,0:T(8,128)} collective-permute-done((f32[72,512]{1,0:T(8,128)}, f32[72,512]{1,0:T(8,128)}, u32[]{:S(2)}, u32[]{:S(2)}) %collective-permute-start.17) | collective-permute-done | bytes 147488 | tf_op jit(solution)/shard_map/ppermute | solution.py:65
  80.8 1.4 collective-permute-done.18
  82.2 1.4 fusion.9
  83.7 3.1 %collective-permute-start.19 = (f32[72,512]{1,0:T(8,128)S(1)}, f32[72,512]{1,0:T(8,128)S(1)}, u32[]{:S(2)}, u32[]{:S(2)}) collective-permute-start(f32[72,512]{1,0:T(8,128)S(1)} %fusion.9), channel_id=1, source_target_pairs={{0,1},{1,0},{2,3},{3,2},{4,5},{5,4},{6,7},{7,6},{8,9},{9,8},{10,11... | collective-permute-start | bytes 442376 | tf_op jit(solution)/shard_map/ppermute | solution.py:14
  86.8 1.2 dynamic-slice_add_fusion.1
  88.0 4.0 %collective-permute-start.5 = (f32[72,512]{1,0:T(8,128)S(1)}, f32[72,512]{1,0:T(8,128)S(1)}, u32[]{:S(2)}, u32[]{:S(2)}) collective-permute-start(f32[72,512]{1,0:T(8,128)S(1)} %get-tuple-element.32), channel_id=1, source_target_pairs={{0,128},{128,256},{256,384},{384,0},{1,129},{129,257},{257,385},{3... | collective-permute-start | bytes 442376 | tf_op jit(solution)/shard_map/ppermute | solution.py:65
  92.0 2.7 %collective-permute-start.6 = (f32[72,512]{1,0:T(8,128)S(1)}, f32[72,512]{1,0:T(8,128)S(1)}, u32[]{:S(2)}, u32[]{:S(2)}) collective-permute-start(f32[72,512]{1,0:T(8,128)S(1)} %get-tuple-element.34), channel_id=1, source_target_pairs={{0,256},{128,384},{256,0},{384,128},{1,257},{129,385},{257,1},{385... | collective-permute-start | bytes 442376 | tf_op jit(solution)/shard_map/ppermute | solution.py:65
  94.7 3.2 %collective-permute-start.7 = (f32[72,512]{1,0:T(8,128)S(1)}, f32[72,512]{1,0:T(8,128)S(1)}, u32[]{:S(2)}, u32[]{:S(2)}) collective-permute-start(f32[72,512]{1,0:T(8,128)S(1)} %get-tuple-element.33), channel_id=1, source_target_pairs={{0,384},{128,0},{256,128},{384,256},{1,385},{129,1},{257,129},{385... | collective-permute-start | bytes 442376 | tf_op jit(solution)/shard_map/ppermute | solution.py:65
  97.9 0.4 fusion.5
  98.3 4.4 %collective-permute-start.20 = (f32[72,512]{1,0:T(8,128)S(1)}, f32[72,512]{1,0:T(8,128)S(1)}, u32[]{:S(2)}, u32[]{:S(2)}) collective-permute-start(f32[72,512]{1,0:T(8,128)S(1)} %fusion.5), channel_id=1, source_target_pairs={{0,2},{1,3},{2,0},{3,1},{4,6},{5,7},{6,4},{7,5},{8,10},{9,11},{10,... | collective-permute-start | bytes 442376 | tf_op jit(solution)/shard_map/ppermute | solution.py:14
  102.7 1.7 collective-permute-done.6
  104.4 0.4 fusion.11
  104.7 2.2 %collective-permute-start.8 = (f32[72,512]{1,0:T(8,128)S(1)}, f32[72,512]{1,0:T(8,128)S(1)}, u32[]{:S(2)}, u32[]{:S(2)}) collective-permute-start(f32[72,512]{1,0:T(8,128)S(1)} %fusion.11), channel_id=1, source_target_pairs={{0,1},{1,0},{2,3},{3,2},{4,5},{5,4},{6,7},{7,6},{8,9},{9,8},{10,11... | collective-permute-start | bytes 442376 | tf_op jit(solution)/shard_map/ppermute | solution.py:14
  106.9 0.4 fusion.1
  107.3 7.5 %collective-permute-start.21 = (f32[72,512]{1,0:T(8,128)S(1)}, f32[72,512]{1,0:T(8,128)S(1)}, u32[]{:S(2)}, u32[]{:S(2)}) collective-permute-start(f32[72,512]{1,0:T(8,128)S(1)} %fusion.1), channel_id=1, source_target_pairs={{0,4},{1,5},{2,6},{3,7},{4,0},{5,1},{6,2},{7,3},{8,12},{9,13},{10,... | collective-permute-start | bytes 442376 | tf_op jit(solution)/shard_map/ppermute | solution.py:14
  114.8 0.4 fusion.7
  115.2 4.6 %collective-permute-start.9 = (f32[72,512]{1,0:T(8,128)S(1)}, f32[72,512]{1,0:T(8,128)S(1)}, u32[]{:S(2)}, u32[]{:S(2)}) collective-permute-start(f32[72,512]{1,0:T(8,128)S(1)} %fusion.7), channel_id=1, source_target_pairs={{0,2},{1,3},{2,0},{3,1},{4,6},{5,7},{6,4},{7,5},{8,10},{9,11},{10,... | collective-permute-start | bytes 442376 | tf_op jit(solution)/shard_map/ppermute | solution.py:14
  119.9 6.5 %collective-permute-start.22 = (f32[72,512]{1,0:T(8,128)S(1)}, f32[72,512]{1,0:T(8,128)S(1)}, u32[]{:S(2)}, u32[]{:S(2)}) collective-permute-start(f32[72,512]{1,0:T(8,128)S(1)} %get-tuple-element.20), channel_id=1, source_target_pairs={{0,128},{128,256},{256,384},{384,0},{1,129},{129,257},{257,385},{3... | collective-permute-start | bytes 442376 | tf_op jit(solution)/shard_map/ppermute | solution.py:65
  126.5 0.4 fusion.3
  126.8 7.1 %collective-permute-start.10 = (f32[72,512]{1,0:T(8,128)S(1)}, f32[72,512]{1,0:T(8,128)S(1)}, u32[]{:S(2)}, u32[]{:S(2)}) collective-permute-start(f32[72,512]{1,0:T(8,128)S(1)} %fusion.3), channel_id=1, source_target_pairs={{0,4},{1,5},{2,6},{3,7},{4,0},{5,1},{6,2},{7,3},{8,12},{9,13},{10,... | collective-permute-start | bytes 442376 | tf_op jit(solution)/shard_map/ppermute | solution.py:14
  133.9 1.9 %collective-permute-start.23 = (f32[72,512]{1,0:T(8,128)S(1)}, f32[72,512]{1,0:T(8,128)S(1)}, u32[]{:S(2)}, u32[]{:S(2)}) collective-permute-start(f32[72,512]{1,0:T(8,128)S(1)} %get-tuple-element.20), channel_id=1, source_target_pairs={{0,256},{128,384},{256,0},{384,128},{1,257},{129,385},{257,1},{385... | collective-permute-start | bytes 442376 | tf_op jit(solution)/shard_map/ppermute | solution.py:65
  135.8 4.0 %collective-permute-start.24 = (f32[72,512]{1,0:T(8,128)S(1)}, f32[72,512]{1,0:T(8,128)S(1)}, u32[]{:S(2)}, u32[]{:S(2)}) collective-permute-start(f32[72,512]{1,0:T(8,128)S(1)} %get-tuple-element.20), channel_id=1, source_target_pairs={{0,384},{128,0},{256,128},{384,256},{1,385},{129,1},{257,129},{385... | collective-permute-start | bytes 442376 | tf_op jit(solution)/shard_map/ppermute | solution.py:65
  139.9 1.9 %collective-permute-done.10 = f32[72,512]{1,0:T(8,128)S(1)} collective-permute-done((f32[72,512]{1,0:T(8,128)S(1)}, f32[72,512]{1,0:T(8,128)S(1)}, u32[]{:S(2)}, u32[]{:S(2)}) %collective-permute-start.10) | collective-permute-done | bytes 147488 | tf_op jit(solution)/shard_map/ppermute | solution.py:14
  141.8 2.1 %collective-permute-start.11 = (f32[72,512]{1,0:T(8,128)S(1)}, f32[72,512]{1,0:T(8,128)S(1)}, u32[]{:S(2)}, u32[]{:S(2)}) collective-permute-start(f32[72,512]{1,0:T(8,128)S(1)} %get-tuple-element.18), channel_id=1, source_target_pairs={{0,128},{128,256},{256,384},{384,0},{1,129},{129,257},{257,385},{3... | collective-permute-start | bytes 442376 | tf_op jit(solution)/shard_map/ppermute | solution.py:65
  143.9 4.6 %collective-permute-done.23 = f32[72,512]{1,0:T(8,128)S(1)} collective-permute-done((f32[72,512]{1,0:T(8,128)S(1)}, f32[72,512]{1,0:T(8,128)S(1)}, u32[]{:S(2)}, u32[]{:S(2)}) %collective-permute-start.23) | collective-permute-done | bytes 147488 | tf_op jit(solution)/shard_map/ppermute | solution.py:65
  148.6 1.9 %collective-permute-start.12 = (f32[72,512]{1,0:T(8,128)S(1)}, f32[72,512]{1,0:T(8,128)S(1)}, u32[]{:S(2)}, u32[]{:S(2)}) collective-permute-start(f32[72,512]{1,0:T(8,128)S(1)} %get-tuple-element.18), channel_id=1, source_target_pairs={{0,256},{128,384},{256,0},{384,128},{1,257},{129,385},{257,1},{385... | collective-permute-start | bytes 442376 | tf_op jit(solution)/shard_map/ppermute | solution.py:65
  150.5 2.6 %collective-permute-start.25 = (f32[288,512]{1,0:T(8,128)S(1)}, f32[288,512]{1,0:T(8,128)S(1)}, u32[]{:S(2)}, u32[]{:S(2)}) collective-permute-start(f32[288,512]{1,0:T(8,128)S(1)} %constant_dynamic-update-slice_fusion.5), channel_id=1, source_target_pairs={{0,64},{64,0},{1,65},{65,1},{2,66},{66,2},{3,67},{67,3},{4,68},{68... | collective-permute-start | bytes 1769480 | tf_op jit(solution)/shard_map/ppermute | solution.py:60
  153.2 5.1 %collective-permute-start.13 = (f32[72,512]{1,0:T(8,128)S(1)}, f32[72,512]{1,0:T(8,128)S(1)}, u32[]{:S(2)}, u32[]{:S(2)}) collective-permute-start(f32[72,512]{1,0:T(8,128)S(1)} %get-tuple-element.18), channel_id=1, source_target_pairs={{0,384},{128,0},{256,128},{384,256},{1,385},{129,1},{257,129},{385... | collective-permute-start | bytes 442376 | tf_op jit(solution)/shard_map/ppermute | solution.py:65
  158.3 2.5 %collective-permute-done.12 = f32[72,512]{1,0:T(8,128)S(1)} collective-permute-done((f32[72,512]{1,0:T(8,128)S(1)}, f32[72,512]{1,0:T(8,128)S(1)}, u32[]{:S(2)}, u32[]{:S(2)}) %collective-permute-start.12) | collective-permute-done | bytes 147488 | tf_op jit(solution)/shard_map/ppermute | solution.py:65
  160.8 3.5 %collective-permute-done.13 = f32[72,512]{1,0:T(8,128)S(1)} collective-permute-done((f32[72,512]{1,0:T(8,128)S(1)}, f32[72,512]{1,0:T(8,128)S(1)}, u32[]{:S(2)}, u32[]{:S(2)}) %collective-permute-start.13) | collective-permute-done | bytes 147488 | tf_op jit(solution)/shard_map/ppermute | solution.py:65
  164.3 2.3 %collective-permute-start.14 = (f32[288,512]{1,0:T(8,128)S(1)}, f32[288,512]{1,0:T(8,128)S(1)}, u32[]{:S(2)}, u32[]{:S(2)}) collective-permute-start(f32[288,512]{1,0:T(8,128)S(1)} %constant_dynamic-update-slice_fusion.9), channel_id=1, source_target_pairs={{0,64},{64,0},{1,65},{65,1},{2,66},{66,2},{3,67},{67,3},{4,68},{68... | collective-permute-start | bytes 1769480 | tf_op jit(solution)/shard_map/ppermute | solution.py:60
  167.1 1.1 collective-permute-done.14
  168.3 1.6 maximum_bitcast_fusion
  (69 shorter events, 2.8 us)
Async XLA Ops:
  0.6 39.3 %copy-start = (bf16[1,1,128,512]{3,2,1,0:T(8,128)(2,1)S(1)}, bf16[1,1,128,512]{3,2,1,0:T(8,128)(2,1)}, u32[]{:S(2)}) copy-start(bf16[1,1,128,512]{3,2,1,0:T(8,128)(2,1)} %param.14) | copy-start | bytes 393220
  0.6 14.8 %copy-start.11 = (s32[1,1,128]{2,1,0:T(1,128)S(1)}, s32[1,1,128]{2,1,0:T(1,128)}, u32[]{:S(2)}) copy-start(s32[1,1,128]{2,1,0:T(1,128)} %param.13) | copy-start | bytes 1540
  4.2 11.3 %collective-permute-start = (f32[580,128]{0,1:T(8,128)S(1)}, f32[580,128]{0,1:T(8,128)S(1)}, u32[]{:S(2)}, u32[]{:S(2)}) collective-permute-start(f32[580,128]{0,1:T(8,128)S(1)} %pad_maximum_fusion.1), channel_id=1, source_target_pairs={{0,128},{128,256},{256,384},{384,0},{1,129},{129,257},{257,385},{3... | collective-permute-start | bytes 890888 | tf_op jit(solution)/shard_map/ppermute | solution.py:65
  8.3 24.3 %collective-permute-start.1 = (f32[580,128]{0,1:T(8,128)S(1)}, f32[580,128]{0,1:T(8,128)S(1)}, u32[]{:S(2)}, u32[]{:S(2)}) collective-permute-start(f32[580,128]{0,1:T(8,128)S(1)} %pad_maximum_fusion.1), channel_id=1, source_target_pairs={{0,256},{128,384},{256,0},{384,128},{1,257},{129,385},{257,1},{385... | collective-permute-start | bytes 890888 | tf_op jit(solution)/shard_map/ppermute | solution.py:65
  12.5 20.3 %collective-permute-start.2 = (f32[580,128]{0,1:T(8,128)S(1)}, f32[580,128]{0,1:T(8,128)S(1)}, u32[]{:S(2)}, u32[]{:S(2)}) collective-permute-start(f32[580,128]{0,1:T(8,128)S(1)} %pad_maximum_fusion.1), channel_id=1, source_target_pairs={{0,384},{128,0},{256,128},{384,256},{1,385},{129,1},{257,129},{385... | collective-permute-start | bytes 890888 | tf_op jit(solution)/shard_map/ppermute | solution.py:65
  32.6 0.8 copy-start.4
  32.9 0.7 copy-start.6
  35.0 12.0 %collective-permute-start.3 = (f32[580,512]{1,0:T(8,128)}, f32[580,512]{1,0:T(8,128)}, u32[]{:S(2)}, u32[]{:S(2)}) collective-permute-start(f32[580,512]{1,0:T(8,128)} %copy.20), channel_id=1, source_target_pairs={{0,64},{64,0},{1,65},{65,1},{2,66},{66,2},{3,67},{67,3},{4,68},{68... | collective-permute-start | bytes 3563528 | tf_op jit(solution)/shard_map/ppermute | solution.py:60
  40.3 3.9 %copy-start.9 = (f32[3,1,1,128]{3,2,1,0:T(1,128)S(1)}, f32[3,1,1,128]{3,2,1,0:T(1,128)}, u32[]{:S(2)}) copy-start(f32[3,1,1,128]{3,2,1,0:T(1,128)} %param.9) | copy-start | bytes 4612
  40.3 4.1 %copy-start.5 = (f32[580,128]{0,1:T(8,128)S(1)}, f32[580,128]{0,1:T(8,128)}, u32[]{:S(2)}) copy-start(f32[580,128]{0,1:T(8,128)} %copy-done.4) | copy-start | bytes 890884
  41.2 3.3 %copy-start.7 = (f32[580,128]{0,1:T(8,128)S(1)}, f32[580,128]{0,1:T(8,128)}, u32[]{:S(2)}) copy-start(f32[580,128]{0,1:T(8,128)} %copy-done.6) | copy-start | bytes 890884
  41.2 18.2 %collective-permute-start.15 = (f32[288,512]{1,0:T(8,128)}, f32[288,512]{1,0:T(8,128)}, u32[]{:S(2)}, u32[]{:S(2)}) collective-permute-start(f32[288,512]{1,0:T(8,128)} %constant_dynamic-slice_fusion.3), channel_id=1, source_target_pairs={{0,64},{64,0},{1,65},{65,1},{2,66},{66,2},{3,67},{67,3},{4,68},{68... | collective-permute-start | bytes 1769480 | tf_op jit(solution)/shard_map/ppermute | solution.py:60
  47.0 3.4 %copy-start.8 = (bf16[576,1,1,128]{3,0,2,1:T(8,128)(2,1)S(1)}, bf16[576,1,1,128]{3,0,2,1:T(8,128)(2,1)}, u32[]{:S(2)}) copy-start(bf16[576,1,1,128]{3,0,2,1:T(8,128)(2,1)} %param.12) | copy-start | bytes 442372
  47.0 3.4 %copy-start.10 = (f32[1,1,128]{2,1,0:T(1,128)S(1)}, f32[1,1,128]{2,1,0:T(1,128)}, u32[]{:S(2)}) copy-start(f32[1,1,128]{2,1,0:T(1,128)} %param.10) | copy-start | bytes 1540
  55.0 1.0 copy-start.2
  56.9 25.4 %copy-start.1 = (bf16[1,3,512,512]{3,2,1,0:T(8,128)(2,1)S(1)}, bf16[1,3,512,512]{3,2,1,0:T(8,128)(2,1)}, u32[]{:S(2)}) copy-start(bf16[1,3,512,512]{3,2,1,0:T(8,128)(2,1)} %param.15) | copy-start | bytes 4718596
  56.9 29.9 %collective-permute-start.4 = (f32[288,512]{1,0:T(8,128)}, f32[288,512]{1,0:T(8,128)}, u32[]{:S(2)}, u32[]{:S(2)}) collective-permute-start(f32[288,512]{1,0:T(8,128)} %constant_dynamic-slice_fusion.7), channel_id=1, source_target_pairs={{0,64},{64,0},{1,65},{65,1},{2,66},{66,2},{3,67},{67,3},{4,68},{68... | collective-permute-start | bytes 1769480 | tf_op jit(solution)/shard_map/ppermute | solution.py:60
  60.6 26.2 %copy-start.3 = (f32[576,512]{1,0:T(8,128)S(1)}, f32[576,512]{1,0:T(8,128)}, u32[]{:S(2)}) copy-start(f32[576,512]{1,0:T(8,128)} %copy-done.2) | copy-start | bytes 3538948
  61.4 13.3 %collective-permute-start.16 = (f32[72,512]{1,0:T(8,128)}, f32[72,512]{1,0:T(8,128)}, u32[]{:S(2)}, u32[]{:S(2)}) collective-permute-start(f32[72,512]{1,0:T(8,128)} %get-tuple-element.35), channel_id=1, source_target_pairs={{0,128},{128,256},{256,384},{384,0},{1,129},{129,257},{257,385},{3... | collective-permute-start | bytes 442376 | tf_op jit(solution)/shard_map/ppermute | solution.py:65
  68.7 12.1 %collective-permute-start.17 = (f32[72,512]{1,0:T(8,128)}, f32[72,512]{1,0:T(8,128)}, u32[]{:S(2)}, u32[]{:S(2)}) collective-permute-start(f32[72,512]{1,0:T(8,128)} %get-tuple-element.37), channel_id=1, source_target_pairs={{0,256},{128,384},{256,0},{384,128},{1,257},{129,385},{257,1},{385... | collective-permute-start | bytes 442376 | tf_op jit(solution)/shard_map/ppermute | solution.py:65
  72.0 10.2 %collective-permute-start.18 = (f32[72,512]{1,0:T(8,128)}, f32[72,512]{1,0:T(8,128)}, u32[]{:S(2)}, u32[]{:S(2)}) collective-permute-start(f32[72,512]{1,0:T(8,128)} %get-tuple-element.36), channel_id=1, source_target_pairs={{0,384},{128,0},{256,128},{384,256},{1,385},{129,1},{257,129},{385... | collective-permute-start | bytes 442376 | tf_op jit(solution)/shard_map/ppermute | solution.py:65
  83.7 14.3 %collective-permute-start.19 = (f32[72,512]{1,0:T(8,128)S(1)}, f32[72,512]{1,0:T(8,128)S(1)}, u32[]{:S(2)}, u32[]{:S(2)}) collective-permute-start(f32[72,512]{1,0:T(8,128)S(1)} %fusion.9), channel_id=1, source_target_pairs={{0,1},{1,0},{2,3},{3,2},{4,5},{5,4},{6,7},{7,6},{8,9},{9,8},{10,11... | collective-permute-start | bytes 442376 | tf_op jit(solution)/shard_map/ppermute | solution.py:14
  88.0 14.7 %collective-permute-start.5 = (f32[72,512]{1,0:T(8,128)S(1)}, f32[72,512]{1,0:T(8,128)S(1)}, u32[]{:S(2)}, u32[]{:S(2)}) collective-permute-start(f32[72,512]{1,0:T(8,128)S(1)} %get-tuple-element.32), channel_id=1, source_target_pairs={{0,128},{128,256},{256,384},{384,0},{1,129},{129,257},{257,385},{3... | collective-permute-start | bytes 442376 | tf_op jit(solution)/shard_map/ppermute | solution.py:65
  92.0 12.4 %collective-permute-start.6 = (f32[72,512]{1,0:T(8,128)S(1)}, f32[72,512]{1,0:T(8,128)S(1)}, u32[]{:S(2)}, u32[]{:S(2)}) collective-permute-start(f32[72,512]{1,0:T(8,128)S(1)} %get-tuple-element.34), channel_id=1, source_target_pairs={{0,256},{128,384},{256,0},{384,128},{1,257},{129,385},{257,1},{385... | collective-permute-start | bytes 442376 | tf_op jit(solution)/shard_map/ppermute | solution.py:65
  94.7 9.7 %collective-permute-start.7 = (f32[72,512]{1,0:T(8,128)S(1)}, f32[72,512]{1,0:T(8,128)S(1)}, u32[]{:S(2)}, u32[]{:S(2)}) collective-permute-start(f32[72,512]{1,0:T(8,128)S(1)} %get-tuple-element.33), channel_id=1, source_target_pairs={{0,384},{128,0},{256,128},{384,256},{1,385},{129,1},{257,129},{385... | collective-permute-start | bytes 442376 | tf_op jit(solution)/shard_map/ppermute | solution.py:65
  98.3 8.6 %collective-permute-start.20 = (f32[72,512]{1,0:T(8,128)S(1)}, f32[72,512]{1,0:T(8,128)S(1)}, u32[]{:S(2)}, u32[]{:S(2)}) collective-permute-start(f32[72,512]{1,0:T(8,128)S(1)} %fusion.5), channel_id=1, source_target_pairs={{0,2},{1,3},{2,0},{3,1},{4,6},{5,7},{6,4},{7,5},{8,10},{9,11},{10,... | collective-permute-start | bytes 442376 | tf_op jit(solution)/shard_map/ppermute | solution.py:14
  104.7 10.0 %collective-permute-start.8 = (f32[72,512]{1,0:T(8,128)S(1)}, f32[72,512]{1,0:T(8,128)S(1)}, u32[]{:S(2)}, u32[]{:S(2)}) collective-permute-start(f32[72,512]{1,0:T(8,128)S(1)} %fusion.11), channel_id=1, source_target_pairs={{0,1},{1,0},{2,3},{3,2},{4,5},{5,4},{6,7},{7,6},{8,9},{9,8},{10,11... | collective-permute-start | bytes 442376 | tf_op jit(solution)/shard_map/ppermute | solution.py:14
  107.3 12.5 %collective-permute-start.21 = (f32[72,512]{1,0:T(8,128)S(1)}, f32[72,512]{1,0:T(8,128)S(1)}, u32[]{:S(2)}, u32[]{:S(2)}) collective-permute-start(f32[72,512]{1,0:T(8,128)S(1)} %fusion.1), channel_id=1, source_target_pairs={{0,4},{1,5},{2,6},{3,7},{4,0},{5,1},{6,2},{7,3},{8,12},{9,13},{10,... | collective-permute-start | bytes 442376 | tf_op jit(solution)/shard_map/ppermute | solution.py:14
  115.2 11.3 %collective-permute-start.9 = (f32[72,512]{1,0:T(8,128)S(1)}, f32[72,512]{1,0:T(8,128)S(1)}, u32[]{:S(2)}, u32[]{:S(2)}) collective-permute-start(f32[72,512]{1,0:T(8,128)S(1)} %fusion.7), channel_id=1, source_target_pairs={{0,2},{1,3},{2,0},{3,1},{4,6},{5,7},{6,4},{7,5},{8,10},{9,11},{10,... | collective-permute-start | bytes 442376 | tf_op jit(solution)/shard_map/ppermute | solution.py:14
  119.9 19.9 %collective-permute-start.22 = (f32[72,512]{1,0:T(8,128)S(1)}, f32[72,512]{1,0:T(8,128)S(1)}, u32[]{:S(2)}, u32[]{:S(2)}) collective-permute-start(f32[72,512]{1,0:T(8,128)S(1)} %get-tuple-element.20), channel_id=1, source_target_pairs={{0,128},{128,256},{256,384},{384,0},{1,129},{129,257},{257,385},{3... | collective-permute-start | bytes 442376 | tf_op jit(solution)/shard_map/ppermute | solution.py:65
  126.8 14.9 %collective-permute-start.10 = (f32[72,512]{1,0:T(8,128)S(1)}, f32[72,512]{1,0:T(8,128)S(1)}, u32[]{:S(2)}, u32[]{:S(2)}) collective-permute-start(f32[72,512]{1,0:T(8,128)S(1)} %fusion.3), channel_id=1, source_target_pairs={{0,4},{1,5},{2,6},{3,7},{4,0},{5,1},{6,2},{7,3},{8,12},{9,13},{10,... | collective-permute-start | bytes 442376 | tf_op jit(solution)/shard_map/ppermute | solution.py:14
  133.9 14.7 %collective-permute-start.23 = (f32[72,512]{1,0:T(8,128)S(1)}, f32[72,512]{1,0:T(8,128)S(1)}, u32[]{:S(2)}, u32[]{:S(2)}) collective-permute-start(f32[72,512]{1,0:T(8,128)S(1)} %get-tuple-element.20), channel_id=1, source_target_pairs={{0,256},{128,384},{256,0},{384,128},{1,257},{129,385},{257,1},{385... | collective-permute-start | bytes 442376 | tf_op jit(solution)/shard_map/ppermute | solution.py:65
  135.8 14.7 %collective-permute-start.24 = (f32[72,512]{1,0:T(8,128)S(1)}, f32[72,512]{1,0:T(8,128)S(1)}, u32[]{:S(2)}, u32[]{:S(2)}) collective-permute-start(f32[72,512]{1,0:T(8,128)S(1)} %get-tuple-element.20), channel_id=1, source_target_pairs={{0,384},{128,0},{256,128},{384,256},{1,385},{129,1},{257,129},{385... | collective-permute-start | bytes 442376 | tf_op jit(solution)/shard_map/ppermute | solution.py:65
  141.8 16.4 %collective-permute-start.11 = (f32[72,512]{1,0:T(8,128)S(1)}, f32[72,512]{1,0:T(8,128)S(1)}, u32[]{:S(2)}, u32[]{:S(2)}) collective-permute-start(f32[72,512]{1,0:T(8,128)S(1)} %get-tuple-element.18), channel_id=1, source_target_pairs={{0,128},{128,256},{256,384},{384,0},{1,129},{129,257},{257,385},{3... | collective-permute-start | bytes 442376 | tf_op jit(solution)/shard_map/ppermute | solution.py:65
  148.6 12.2 %collective-permute-start.12 = (f32[72,512]{1,0:T(8,128)S(1)}, f32[72,512]{1,0:T(8,128)S(1)}, u32[]{:S(2)}, u32[]{:S(2)}) collective-permute-start(f32[72,512]{1,0:T(8,128)S(1)} %get-tuple-element.18), channel_id=1, source_target_pairs={{0,256},{128,384},{256,0},{384,128},{1,257},{129,385},{257,1},{385... | collective-permute-start | bytes 442376 | tf_op jit(solution)/shard_map/ppermute | solution.py:65
  150.5 16.3 %collective-permute-start.25 = (f32[288,512]{1,0:T(8,128)S(1)}, f32[288,512]{1,0:T(8,128)S(1)}, u32[]{:S(2)}, u32[]{:S(2)}) collective-permute-start(f32[288,512]{1,0:T(8,128)S(1)} %constant_dynamic-update-slice_fusion.5), channel_id=1, source_target_pairs={{0,64},{64,0},{1,65},{65,1},{2,66},{66,2},{3,67},{67,3},{4,68},{68... | collective-permute-start | bytes 1769480 | tf_op jit(solution)/shard_map/ppermute | solution.py:60
  153.2 11.1 %collective-permute-start.13 = (f32[72,512]{1,0:T(8,128)S(1)}, f32[72,512]{1,0:T(8,128)S(1)}, u32[]{:S(2)}, u32[]{:S(2)}) collective-permute-start(f32[72,512]{1,0:T(8,128)S(1)} %get-tuple-element.18), channel_id=1, source_target_pairs={{0,384},{128,0},{256,128},{384,256},{1,385},{129,1},{257,129},{385... | collective-permute-start | bytes 442376 | tf_op jit(solution)/shard_map/ppermute | solution.py:65
  164.3 3.9 %collective-permute-start.14 = (f32[288,512]{1,0:T(8,128)S(1)}, f32[288,512]{1,0:T(8,128)S(1)}, u32[]{:S(2)}, u32[]{:S(2)}) collective-permute-start(f32[288,512]{1,0:T(8,128)S(1)} %constant_dynamic-update-slice_fusion.9), channel_id=1, source_target_pairs={{0,64},{64,0},{1,65},{65,1},{2,66},{66,2},{3,67},{67,3},{4,68},{68... | collective-permute-start | bytes 1769480 | tf_op jit(solution)/shard_map/ppermute | solution.py:60

commit v5 on v2

--- a/solution.py
+++ b/solution.py
@@ -56,6 +56,27 @@
     return rows
 
 
+def exchange(value, axis):
+    return lax.all_to_all(value, axis, 0, 0, tiled=True)
+
+
+def gather_blocks(block, axis):
+    count = lax.axis_size(axis)
+    return exchange(jnp.concatenate([block] * count, axis=0), axis)
+
+
+def scatter_rows(value):
+    width = value.shape[1]
+    halves = exchange(value, "core").reshape(2, -1, width)
+    summed = halves[0] + halves[1]
+    count = lax.axis_size("ylo")
+    return exchange(summed, "ylo").reshape(count, -1, width).sum(axis=0)
+
+
+def gather_rows(rows):
+    return gather_blocks(gather_blocks(rows, "ylo"), "core")
+
+
 def shards(positions, panel_areas, probe_cols, full_sketch, tree_order, leaf_basis, transfer_mats):
     panels = positions.shape[3]
     probe_count = probe_cols.shape[0]
@@ -72,8 +93,9 @@
         jnp.take(probe_flat, sorting, axis=1), basis_flat, preferred_element_type=jnp.float32
     )
     outgoing = jnp.concatenate([coords, area_row, scaled.astype(jnp.float32)], axis=0)
-    piece = lax.all_gather(outgoing, "ylo", axis=1, tiled=True)
-    piece = lax.all_gather(piece, "core", axis=1, tiled=True)
+    rows_out = outgoing.shape[0]
+    stacked_blocks = gather_blocks(gather_blocks(outgoing, "ylo"), "core")
+    piece = jnp.transpose(stacked_blocks.reshape(-1, rows_out, panels), (1, 0, 2)).reshape(rows_out, -1)
     near_sum = near_block(coords, area_row[0], piece[:3], piece[3], piece[4:].astype(jnp.bfloat16))
     offdiag = (full_sketch.reshape(probe_count, panels).astype(jnp.float32) - near_sum).astype(
         jnp.bfloat16
@@ -82,11 +104,9 @@
         jnp.take(offdiag, sorting, axis=1), basis_flat, preferred_element_type=jnp.float32
     )
     stacked = jnp.concatenate([sketch_part, probe_part], axis=0)
-    mine = lax.psum_scatter(stacked, "core", scatter_dimension=0, tiled=True)
-    mine = lax.psum_scatter(mine, "ylo", scatter_dimension=0, tiled=True)
+    mine = scatter_rows(stacked)
     top = climb_rows(mine, level_mats)
-    top = lax.all_gather(top, "ylo", axis=0, tiled=True)
-    nested = lax.all_gather(top, "core", axis=0, tiled=True).reshape(2, probe_count, basis_width)[None]
+    nested = gather_rows(top).reshape(2, probe_count, basis_width)[None]
     return (offdiag.reshape(probe_count, 1, 1, panels), nested)
 
 

time: 264 us -> 172 us (0.65)
  waiting for transfers between devices: 213 us -> 48.6 us
  blocking collectives: 0 us -> 82.4 us
  between operations: 14.3 us -> 0.86 us
  starting transfers between devices: 14.2 us -> 19.7 us
    all_gather x4 -> x0, waiting for transfers between devices: 128 us -> none  [the longest x1 45.6 us: shards(): piece = lax.all_gather(outgoing, 'ylo', axis=1, tiled=True)]
    all_to_all x0 -> x5, blocking collectives: none -> 82.4 us  [exchange(): return lax.all_to_all(value, axis, 0, 0, tiled=True)]
    reduce_scatter x2 -> x0, waiting for transfers between devices: 59.1 us -> none  [the longest x1 39.9 us: shards(): mine = lax.psum_scatter(mine, 'ylo', scatter_dimension=0, tiled=True)]
    all_to_all x0 -> x1, waiting for transfers between devices: none -> 24.8 us  [exchange(): return lax.all_to_all(value, axis, 0, 0, tiled=True)]
    all_to_all x0 -> x1, starting transfers between devices: none -> 5.55 us  [exchange(): return lax.all_to_all(value, axis, 0, 0, tiled=True)]
  transfers between devices with their start and end apart: 9 -> 4, of which waited for: 9 -> 4; matrix products, arithmetic and copies ran while one was open for 0% -> 1% of each run, Pallas kernels for 0% -> 0%
where the time goes in v5:
time: 172 us
  blocking collectives  82.4 us (48%)
  waiting for transfers between devices  48.6 us (28%)
  starting transfers between devices  19.7 us (11%)
  local copies, waits for them, and re-layouts  11.9 us (7%)
  matrix products  6.14 us (4%)
  other arithmetic  2 us (1%)
    all_to_all x5, blocking collectives, exchange(): return lax.all_to_all(value, axis, 0, 0, tiled=True)  82.4 us
    all_to_all x1, waiting for transfers between devices, exchange(): return lax.all_to_all(value, axis, 0, 0, tiled=True)  24.8 us
    ppermute x3, waiting for transfers between devices, partner(): return lax.ppermute(value, axis, pairs)  23.8 us
    ppermute x3, starting transfers between devices, partner(): return lax.ppermute(value, axis, pairs)  14.2 us
    all_to_all x1, starting transfers between devices, exchange(): return lax.all_to_all(value, axis, 0, 0, tiled=True)  5.55 us
  transfers between devices with their start and end apart: 4, of which 4 were waited for; matrix products, arithmetic and copies ran while one was open for 1% of the time, Pallas kernels for 0%

profile of v5, /device:TPU:1, one launch (start us, length us, event | category | flops | bytes accessed | tf_op | source)
XLA Modules:
  0.0 171.6 jit_solution(13415725266278831422)
XLA Ops:
  0.6 0.0 copy-start
  0.6 1.1 copy.17
  1.7 0.8 copy.16
  2.5 0.8 copy.18
  3.3 0.7 fusion.28
  4.0 0.9 concatenate.17
  5.0 0.9 reshape.120
  5.8 1.5 copy.25
  7.3 0.0 copy-start.6
  7.4 0.0 copy-start.4
  7.4 5.6 %all-to-all-start = ((f32[4,580,128]{2,1,0:T(8,128)}), f32[4,580,128]{2,1,0:T(8,128)S(1)}, u32[]{:S(2)}, u32[]{:S(2)}) async-start(f32[4,580,128]{2,1,0:T(8,128)} %copy.25), calls=%async_computation | async-start | bytes 2392064 | tf_op jit(solution)/shard_map/all_to_all | solution.py:60
  12.9 0.0 copy-done.6
  12.9 0.9 gather_fusion.1
  13.8 0.0 copy-done.4
  13.8 0.0 copy-done
  13.9 1.4 fusion.29
  15.3 24.8 %all-to-all-done = f32[4,580,128]{2,1,0:T(8,128)S(1)} async-done(((f32[4,580,128]{2,1,0:T(8,128)}), f32[4,580,128]{2,1,0:T(8,128)S(1)}, u32[]{:S(2)}, u32[]{:S(2)}) %all-to-all-start) | async-done | bytes 1187872 | tf_op jit(solution)/shard_map/all_to_all | solution.py:60
  40.1 0.1 all_to_all.40
  40.2 0.2 pad_maximum_fusion
  40.3 7.9 %all_to_all.57 = f32[2,2320,128]{2,1,0:T(8,128)S(1)} all-to-all(f32[2,2320,128]{2,1,0:T(8,128)S(1)} %bitcast.68), channel_id=1, replica_groups=mesh['ylo'=4,'core'=2,'leaf'=64] {'core'}, dimensions={0} | all-to-all | bytes 4751360 | tf_op jit(solution)/shard_map/all_to_all | solution.py:60
  48.2 0.0 copy-start.3
  48.2 0.0 copy-start.5
  48.2 1.5 reshape.94
  49.8 1.0 fusion.45
  50.7 0.0 copy-done.3
  50.7 0.0 copy-done.5
  50.7 3.1 %fusion.13 = (bf16[576,1,1,128]{3,0,2,1:T(8,128)(2,1)}, f32[576,128]{1,0:T(8,128)S(1)}) fusion(bf16[576,1,1,128]{3,0,2,1:T(8,128)(2,1)S(1)} %copy-done.3, f32[1024]{0:T(1024)S(1)} %bitcast.82, f32[128]{0:T(128)S(1)} %bitcast.87, f32[1024]{0:T(1024)S(1)} %bitcast.83, f32[128]{0:T(128)S(1)} %get-tuple-element.29, f32[1024]{0:T(1024)S(1)} %bitcast.84, ...), kind=kOutput, calls=%fused_computation.25 | convolution fusion | flops 152920064 | bytes 1787904 | tf_op jit(solution)/shard_map/while/body/eval_jaxpr/dot_general | solution.py:40
  53.8 0.2 copy.24
  54.0 0.0 copy-start.1
  54.0 0.9 gather_fusion
  54.9 0.4 fusion.31
  55.3 0.0 copy-done.1
  55.3 0.2 pad_maximum_fusion.1
  55.5 5.6 %all_to_all.58 = f32[2,576,512]{2,1,0:T(8,128)S(1)} all-to-all(f32[2,576,512]{2,1,0:T(8,128)S(1)} %bitcast.69), channel_id=1, replica_groups=mesh['ylo'=4,'core'=2,'leaf'=64] {'core'}, dimensions={0} | all-to-all | bytes 4718592 | tf_op jit(solution)/shard_map/all_to_all | solution.py:60
  61.2 0.2 slice_add_fusion
  61.4 0.0 copy-start.2
  61.4 30.7 %all_to_all.59 = f32[4,144,512]{2,1,0:T(8,128)S(1)} all-to-all(f32[4,144,512]{2,1,0:T(8,128)S(1)} %bitcast.72), channel_id=1, replica_groups=mesh['ylo'=4,'core'=2,'leaf'=64] {'ylo'}, dimensions={0} | all-to-all | bytes 2359296 | tf_op jit(solution)/shard_map/all_to_all | solution.py:60
  92.1 0.1 reduce_sum.9
  92.3 0.0 copy-done.2
  92.3 0.4 fusion.8
  92.7 3.1 %collective-permute-start = (f32[144,512]{1,0:T(8,128)S(1)}, f32[144,512]{1,0:T(8,128)S(1)}, u32[]{:S(2)}, u32[]{:S(2)}) collective-permute-start(f32[144,512]{1,0:T(8,128)S(1)} %fusion.8), channel_id=1, source_target_pairs={{0,1},{1,0},{2,3},{3,2},{4,5},{5,4},{6,7},{7,6},{8,9},{9,8},{10,11... | collective-permute-start | bytes 884744 | tf_op jit(solution)/shard_map/ppermute | solution.py:14
  95.8 5.9 %collective-permute-done = f32[144,512]{1,0:T(8,128)S(1)} collective-permute-done((f32[144,512]{1,0:T(8,128)S(1)}, f32[144,512]{1,0:T(8,128)S(1)}, u32[]{:S(2)}, u32[]{:S(2)}) %collective-permute-start) | collective-permute-done | bytes 294944 | tf_op jit(solution)/shard_map/ppermute | solution.py:14
  101.8 0.4 fusion.6
  102.2 4.7 %collective-permute-start.1 = (f32[144,512]{1,0:T(8,128)S(1)}, f32[144,512]{1,0:T(8,128)S(1)}, u32[]{:S(2)}, u32[]{:S(2)}) collective-permute-start(f32[144,512]{1,0:T(8,128)S(1)} %fusion.6), channel_id=1, source_target_pairs={{0,2},{1,3},{2,0},{3,1},{4,6},{5,7},{6,4},{7,5},{8,10},{9,11},{10,... | collective-permute-start | bytes 884744 | tf_op jit(solution)/shard_map/ppermute | solution.py:14
  106.8 5.0 %collective-permute-done.1 = f32[144,512]{1,0:T(8,128)S(1)} collective-permute-done((f32[144,512]{1,0:T(8,128)S(1)}, f32[144,512]{1,0:T(8,128)S(1)}, u32[]{:S(2)}, u32[]{:S(2)}) %collective-permute-start.1) | collective-permute-done | bytes 294944 | tf_op jit(solution)/shard_map/ppermute | solution.py:14
  111.8 0.4 fusion.4
  112.2 6.4 %collective-permute-start.2 = (f32[144,512]{1,0:T(8,128)S(1)}, f32[144,512]{1,0:T(8,128)S(1)}, u32[]{:S(2)}, u32[]{:S(2)}) collective-permute-start(f32[144,512]{1,0:T(8,128)S(1)} %fusion.4), channel_id=1, source_target_pairs={{0,4},{1,5},{2,6},{3,7},{4,0},{5,1},{6,2},{7,3},{8,12},{9,13},{10,... | collective-permute-start | bytes 884744 | tf_op jit(solution)/shard_map/ppermute | solution.py:14
  118.7 12.9 %collective-permute-done.2 = f32[144,512]{1,0:T(8,128)S(1)} collective-permute-done((f32[144,512]{1,0:T(8,128)S(1)}, f32[144,512]{1,0:T(8,128)S(1)}, u32[]{:S(2)}, u32[]{:S(2)}) %collective-permute-start.2) | collective-permute-done | bytes 294944 | tf_op jit(solution)/shard_map/ppermute | solution.py:14
  131.6 0.1 pad_maximum_fusion.3
  131.7 30.9 %all_to_all.60 = f32[4,144,512]{2,1,0:T(8,128)S(1)} all-to-all(f32[4,144,512]{2,1,0:T(8,128)S(1)} %bitcast.74), channel_id=1, replica_groups=mesh['ylo'=4,'core'=2,'leaf'=64] {'ylo'}, dimensions={0} | all-to-all | bytes 2359296 | tf_op jit(solution)/shard_map/all_to_all | solution.py:60
  162.7 0.3 pad_maximum_fusion.2
  163.0 7.2 %all_to_all.61 = f32[2,576,512]{2,1,0:T(8,128)S(1)} all-to-all(f32[2,576,512]{2,1,0:T(8,128)S(1)} %bitcast.71), channel_id=1, replica_groups=mesh['ylo'=4,'core'=2,'leaf'=64] {'core'}, dimensions={0} | all-to-all | bytes 4718592 | tf_op jit(solution)/shard_map/all_to_all | solution.py:60
  170.2 1.4 copy.34
  (6 shorter events, 0.1 us)
Async XLA Ops:
  0.6 13.2 %copy-start = (bf16[1,1,128,512]{3,2,1,0:T(8,128)(2,1)S(1)}, bf16[1,1,128,512]{3,2,1,0:T(8,128)(2,1)}, u32[]{:S(2)}) copy-start(bf16[1,1,128,512]{3,2,1,0:T(8,128)(2,1)} %param.14) | copy-start | bytes 393220
  7.3 5.6 %copy-start.6 = (s32[1,1,128]{2,1,0:T(1,128)S(1)}, s32[1,1,128]{2,1,0:T(1,128)}, u32[]{:S(2)}) copy-start(s32[1,1,128]{2,1,0:T(1,128)} %param.13) | copy-start | bytes 1540
  7.4 6.5 %copy-start.4 = (f32[3,1,1,128]{3,2,1,0:T(1,128)S(1)}, f32[3,1,1,128]{3,2,1,0:T(1,128)}, u32[]{:S(2)}) copy-start(f32[3,1,1,128]{3,2,1,0:T(1,128)} %param.9) | copy-start | bytes 4612
  7.4 32.7 %all-to-all-start = ((f32[4,580,128]{2,1,0:T(8,128)}), f32[4,580,128]{2,1,0:T(8,128)S(1)}, u32[]{:S(2)}, u32[]{:S(2)}) async-start(f32[4,580,128]{2,1,0:T(8,128)} %copy.25), calls=%async_computation | async-start | bytes 2392064 | tf_op jit(solution)/shard_map/all_to_all | solution.py:60
  48.2 2.5 %copy-start.3 = (bf16[576,1,1,128]{3,0,2,1:T(8,128)(2,1)S(1)}, bf16[576,1,1,128]{3,0,2,1:T(8,128)(2,1)}, u32[]{:S(2)}) copy-start(bf16[576,1,1,128]{3,0,2,1:T(8,128)(2,1)} %param.12) | copy-start | bytes 442372
  48.2 2.5 %copy-start.5 = (f32[1,1,128]{2,1,0:T(1,128)S(1)}, f32[1,1,128]{2,1,0:T(1,128)}, u32[]{:S(2)}) copy-start(f32[1,1,128]{2,1,0:T(1,128)} %param.10) | copy-start | bytes 1540
  54.0 1.3 copy-start.1
  61.4 30.9 %copy-start.2 = (bf16[1,3,512,512]{3,2,1,0:T(8,128)(2,1)S(1)}, bf16[1,3,512,512]{3,2,1,0:T(8,128)(2,1)}, u32[]{:S(2)}) copy-start(bf16[1,3,512,512]{3,2,1,0:T(8,128)(2,1)} %param.15) | copy-start | bytes 4718596
  92.7 9.1 %collective-permute-start = (f32[144,512]{1,0:T(8,128)S(1)}, f32[144,512]{1,0:T(8,128)S(1)}, u32[]{:S(2)}, u32[]{:S(2)}) collective-permute-start(f32[144,512]{1,0:T(8,128)S(1)} %fusion.8), channel_id=1, source_target_pairs={{0,1},{1,0},{2,3},{3,2},{4,5},{5,4},{6,7},{7,6},{8,9},{9,8},{10,11... | collective-permute-start | bytes 884744 | tf_op jit(solution)/shard_map/ppermute | solution.py:14
  102.2 9.7 %collective-permute-start.1 = (f32[144,512]{1,0:T(8,128)S(1)}, f32[144,512]{1,0:T(8,128)S(1)}, u32[]{:S(2)}, u32[]{:S(2)}) collective-permute-start(f32[144,512]{1,0:T(8,128)S(1)} %fusion.6), channel_id=1, source_target_pairs={{0,2},{1,3},{2,0},{3,1},{4,6},{5,7},{6,4},{7,5},{8,10},{9,11},{10,... | collective-permute-start | bytes 884744 | tf_op jit(solution)/shard_map/ppermute | solution.py:14
  112.2 19.3 %collective-permute-start.2 = (f32[144,512]{1,0:T(8,128)S(1)}, f32[144,512]{1,0:T(8,128)S(1)}, u32[]{:S(2)}, u32[]{:S(2)}) collective-permute-start(f32[144,512]{1,0:T(8,128)S(1)} %fusion.4), channel_id=1, source_target_pairs={{0,4},{1,5},{2,6},{3,7},{4,0},{5,1},{6,2},{7,3},{8,12},{9,13},{10,... | collective-permute-start | bytes 884744 | tf_op jit(solution)/shard_map/ppermute | solution.py:14

commit v6 on v5

--- a/solution.py
+++ b/solution.py
@@ -85,28 +85,44 @@
     coords = positions.reshape(3, panels)
     area_row = panel_areas.reshape(1, panels)
     probe_flat = probe_cols.reshape(probe_count, panels)
+    sketch_flat = full_sketch.reshape(probe_count, panels)
     scaled = (area_row * probe_flat.astype(jnp.float32)).astype(jnp.bfloat16)
     sorting = tree_order.reshape(panels)
     basis_flat = leaf_basis.reshape(panels, basis_width)
     level_mats = transfer_mats.reshape(level_count, basis_width, basis_width)
-    probe_part = jnp.dot(
-        jnp.take(probe_flat, sorting, axis=1), basis_flat, preferred_element_type=jnp.float32
-    )
-    outgoing = jnp.concatenate([coords, area_row, scaled.astype(jnp.float32)], axis=0)
-    rows_out = outgoing.shape[0]
-    stacked_blocks = gather_blocks(gather_blocks(outgoing, "ylo"), "core")
-    piece = jnp.transpose(stacked_blocks.reshape(-1, rows_out, panels), (1, 0, 2)).reshape(rows_out, -1)
-    near_sum = near_block(coords, area_row[0], piece[:3], piece[3], piece[4:].astype(jnp.bfloat16))
-    offdiag = (full_sketch.reshape(probe_count, panels).astype(jnp.float32) - near_sum).astype(
-        jnp.bfloat16
-    )
-    sketch_part = jnp.dot(
-        jnp.take(offdiag, sorting, axis=1), basis_flat, preferred_element_type=jnp.float32
-    )
-    stacked = jnp.concatenate([sketch_part, probe_part], axis=0)
-    mine = scatter_rows(stacked)
-    top = climb_rows(mine, level_mats)
-    nested = gather_rows(top).reshape(2, probe_count, basis_width)[None]
+    geometry = jnp.concatenate([coords, area_row], axis=0)
+    geometry_rows = geometry.shape[0]
+    chunk_count = 2
+    chunk = probe_count // chunk_count
+    offdiag_chunks, sketch_chunks, probe_chunks = [], [], []
+    for index in range(chunk_count):
+        rows = slice(index * chunk, (index + 1) * chunk)
+        scaled_rows = scaled[rows].astype(jnp.float32)
+        outgoing = jnp.concatenate([geometry, scaled_rows], axis=0)
+        width_out = outgoing.shape[0]
+        blocks = gather_rows(outgoing)
+        piece = jnp.transpose(blocks.reshape(-1, width_out, panels), (1, 0, 2)).reshape(width_out, -1)
+        source_geometry = piece[:geometry_rows]
+        piece = piece[geometry_rows:]
+        near_sum = near_block(
+            coords, area_row[0], source_geometry[:3], source_geometry[3], piece.astype(jnp.bfloat16)
+        )
+        offdiag = (sketch_flat[rows].astype(jnp.float32) - near_sum).astype(jnp.bfloat16)
+        sketch_part = jnp.dot(
+            jnp.take(offdiag, sorting, axis=1), basis_flat, preferred_element_type=jnp.float32
+        )
+        probe_part = jnp.dot(
+            jnp.take(probe_flat[rows], sorting, axis=1), basis_flat, preferred_element_type=jnp.float32
+        )
+        stacked = jnp.concatenate([sketch_part, probe_part], axis=0)
+        top = gather_rows(climb_rows(scatter_rows(stacked), level_mats))
+        offdiag_chunks.append(offdiag)
+        sketch_chunks.append(top[:chunk])
+        probe_chunks.append(top[chunk:])
+    offdiag = jnp.concatenate(offdiag_chunks, axis=0)
+    nested = jnp.stack(
+        [jnp.concatenate(sketch_chunks, axis=0), jnp.concatenate(probe_chunks, axis=0)], axis=0
+    )[None]
     return (offdiag.reshape(probe_count, 1, 1, panels), nested)
 
 

time: 172 us -> 187 us (1.087)
  blocking collectives: 82.4 us -> 9.34 us
  starting transfers between devices: 19.7 us -> 81.5 us
  other arithmetic: 2 us -> 13 us
  waiting for transfers between devices: 48.6 us -> 56.3 us
  local copies, waits for them, and re-layouts: 11.9 us -> 15.6 us
  matrix products: 6.14 us -> 8.99 us
    all_to_all x5 -> x1, blocking collectives: 82.4 us -> 9.34 us  [exchange(): return lax.all_to_all(value, axis, 0, 0, tiled=True)]
    all_to_all x1 -> x11, starting transfers between devices: 5.55 us -> 53.2 us  [exchange(): return lax.all_to_all(value, axis, 0, 0, tiled=True)]
    all_to_all x1 -> x11, waiting for transfers between devices: 24.8 us -> 46.9 us  [exchange(): return lax.all_to_all(value, axis, 0, 0, tiled=True)]
    ppermute x3 -> x6, waiting for transfers between devices: 23.8 us -> 9.42 us  [partner(): return lax.ppermute(value, axis, pairs)]
    ppermute x3 -> x6, starting transfers between devices: 14.2 us -> 28.3 us  [partner(): return lax.ppermute(value, axis, pairs)]
    concatenate x3 -> x6, other arithmetic: 0.61 us -> 5.31 us  [gather_blocks(): return exchange(jnp.concatenate([block] * count, axis=0), axis)]
    concatenate x1 -> x2, local copies, waits for them, and re-layouts: 0.92 us -> 3.94 us  [gather_blocks(): return exchange(jnp.concatenate([block] * count, axis=0), axis)]
    unnamed x17 -> x23, local copies, waits for them, and re-layouts: 3.33 us -> 1.05 us
  transfers between devices with their start and end apart: 4 -> 17, of which waited for: 4 -> 13; matrix products, arithmetic and copies ran while one was open for 1% -> 15% of each run, Pallas kernels for 0% -> 0%
where the time goes in v6:
time: 187 us; the launch traced here: 186 us
  starting transfers between devices  81.5 us (44%)
  waiting for transfers between devices  56.3 us (30%)
  local copies, waits for them, and re-layouts  15.6 us (8%)
  other arithmetic  13 us (7%)
  blocking collectives  9.34 us (5%)
  matrix products  8.99 us (5%)
    all_to_all x11, starting transfers between devices, exchange(): return lax.all_to_all(value, axis, 0, 0, tiled=True)  53.2 us
    all_to_all x11, waiting for transfers between devices, exchange(): return lax.all_to_all(value, axis, 0, 0, tiled=True)  46.9 us
    ppermute x6, starting transfers between devices, partner(): return lax.ppermute(value, axis, pairs)  28.3 us
    ppermute x6, waiting for transfers between devices, partner(): return lax.ppermute(value, axis, pairs)  9.42 us
    all_to_all x1, blocking collectives, exchange(): return lax.all_to_all(value, axis, 0, 0, tiled=True)  9.34 us
    concatenate x6, other arithmetic, gather_blocks(): return exchange(jnp.concatenate([block] * count, axis=0), axis)  5.31 us
    concatenate x2, local copies, waits for them, and re-layouts, gather_blocks(): return exchange(jnp.concatenate([block] * count, axis=0), axis)  3.94 us
  transfers between devices with their start and end apart: 17, of which 13 were waited for; matrix products, arithmetic and copies ran while one was open for 15% of the time, Pallas kernels for 0%

profile of v6, /device:TPU:1, one launch (start us, length us, event | category | flops | bytes accessed | tf_op | source)
XLA Modules:
  0.0 185.6 jit_solution(5415344122225186198)
XLA Ops:
  0.6 0.7 copy.33
  1.4 0.9 fusion.26
  2.3 3.3 %concatenate.48 = f32[1168,128]{1,0:T(8,128)S(1)} concatenate(f32[3,128]{1,0:T(4,128)S(1)} %bitcast.128, f32[1,128]{1,0:T(1,128)} %bitcast.137, f32[288,128]{1,0:T(8,128)S(1)} %get-tuple-element.60, f32[3,128]{1,0:T(4,128)S(1)} %bitcast.129, f32[1,128]{1,0:T(1,128)} %bitcast.138, f32[288,128]{1,0:T(8,128)S(1)} %get-tuple-element.60, f32[3,128]{1,0:T(4,128)S(1)} %bitcast.130, ...), dimensions={0} | concatenate | bytes 1196032 | tf_op jit(solution)/shard_map/concatenate | solution.py:65
  5.6 0.9 all_to_all.81
  6.5 5.4 %all-to-all-start.2 = ((f32[4,292,128]{2,1,0:T(8,128)}), f32[4,292,128]{2,1,0:T(8,128)S(1)}, u32[]{:S(2)}, u32[]{:S(2)}) async-start(f32[4,292,128]{2,1,0:T(8,128)} %all_to_all.81), calls=%async_computation.2 | async-start | bytes 1212416 | tf_op jit(solution)/shard_map/all_to_all | solution.py:60
  12.2 0.9 gather_fusion.1
  13.1 0.9 gather_fusion.3
  13.9 0.7 concatenate.46
  14.6 0.9 all_to_all.76
  15.5 1.2 fusion.51
  17.0 7.0 %all-to-all-done.2 = f32[4,292,128]{2,1,0:T(8,128)S(1)} async-done(((f32[4,292,128]{2,1,0:T(8,128)}), f32[4,292,128]{2,1,0:T(8,128)S(1)}, u32[]{:S(2)}, u32[]{:S(2)}) %all-to-all-start.2) | async-done | bytes 598048 | tf_op jit(solution)/shard_map/all_to_all | solution.py:60
  24.2 9.3 %all_to_all.114 = f32[2,1168,128]{2,1,0:T(8,128)S(1)} all-to-all(f32[2,1168,128]{2,1,0:T(8,128)S(1)} %bitcast.118), channel_id=1, replica_groups=mesh['ylo'=4,'core'=2,'leaf'=64] {'core'}, dimensions={0} | all-to-all | bytes 2392064 | tf_op jit(solution)/shard_map/all_to_all | solution.py:60
  33.5 3.6 %all-to-all-start = ((f32[4,292,128]{2,1,0:T(8,128)}), f32[4,292,128]{2,1,0:T(8,128)S(1)}, u32[]{:S(2)}, u32[]{:S(2)}) async-start(f32[4,292,128]{2,1,0:T(8,128)} %all_to_all.76), calls=%async_computation | async-start | bytes 1212416 | tf_op jit(solution)/shard_map/all_to_all | solution.py:60
  37.2 1.1 reshape.149
  38.3 1.0 fusion.84
  39.2 1.9 %fusion.1 = bf16[288,128]{1,0:T(8,128)(2,1)S(1)} fusion(f32[1024]{0:T(1024)S(1)} %bitcast.152, f32[1024]{0:T(1024)S(1)} %bitcast.153, f32[1024]{0:T(1024)S(1)} %bitcast.154, f32[1024]{0:T(1024)S(1)} %bitcast.151, f32[128]{0:T(128)S(1)} %bitcast.145, f32[128]{0:T(128)S(1)} %get-tuple-element.62, f32[128]{0:T(128)S(1)} %get-tuple-element.63, ...), kind=kOutput, calls=%fused_computation.18 | convolution fusion | flops 77312000 | bytes 755712 | tf_op jit(solution)/shard_map/while/body/eval_jaxpr/dot_general | solution.py:40
  41.2 0.9 gather_fusion.2
  42.1 1.2 fusion.53
  43.3 9.8 %all-to-all-done = f32[4,292,128]{2,1,0:T(8,128)S(1)} async-done(((f32[4,292,128]{2,1,0:T(8,128)}), f32[4,292,128]{2,1,0:T(8,128)S(1)}, u32[]{:S(2)}, u32[]{:S(2)}) %all-to-all-start) | async-done | bytes 598048 | tf_op jit(solution)/shard_map/all_to_all | solution.py:60
  53.2 1.1 pad_maximum_fusion
  54.3 4.9 %all-to-all-start.1 = ((f32[2,1168,128]{2,1,0:T(8,128)}), f32[2,1168,128]{2,1,0:T(8,128)S(1)}, u32[]{:S(2)}, u32[]{:S(2)}) async-start(f32[2,1168,128]{2,1,0:T(8,128)} %bitcast.4), calls=%async_computation.1 | async-start | bytes 2392064 | tf_op jit(solution)/shard_map/all_to_all | solution.py:60
  59.2 1.1 pad_maximum_fusion.4
  60.3 0.7 all-to-all-done.1
  61.0 4.0 %all-to-all-start.8 = ((f32[2,288,512]{2,1,0:T(8,128)}), f32[2,288,512]{2,1,0:T(8,128)S(1)}, u32[]{:S(2)}, u32[]{:S(2)}) async-start(f32[2,288,512]{2,1,0:T(8,128)} %bitcast.119), calls=%async_computation.8 | async-start | bytes 2359296 | tf_op jit(solution)/shard_map/all_to_all | solution.py:60
  65.0 1.1 reshape.148
  66.1 1.0 fusion.83
  67.1 1.9 fusion
  69.0 0.9 gather_fusion
  70.3 1.1 pad_maximum_fusion.2
  71.4 3.6 %all-to-all-start.4 = ((f32[2,288,512]{2,1,0:T(8,128)}), f32[2,288,512]{2,1,0:T(8,128)S(1)}, u32[]{:S(2)}, u32[]{:S(2)}) async-start(f32[2,288,512]{2,1,0:T(8,128)} %bitcast.121), calls=%async_computation.4 | async-start | bytes 2359296 | tf_op jit(solution)/shard_map/all_to_all | solution.py:60
  75.0 0.9 slice_add_fusion
  75.9 0.9 all-to-all-done.4
  76.8 3.5 %all-to-all-start.9 = ((f32[4,72,512]{2,1,0:T(8,128)}), f32[4,72,512]{2,1,0:T(8,128)S(1)}, u32[]{:S(2)}, u32[]{:S(2)}) async-start(f32[4,72,512]{2,1,0:T(8,128)} %bitcast.39), calls=%async_computation.9 | async-start | bytes 1179648 | tf_op jit(solution)/shard_map/all_to_all | solution.py:60
  80.3 0.9 slice_add_fusion.1
  81.2 14.7 %all-to-all-done.9 = f32[4,72,512]{2,1,0:T(8,128)S(1)} async-done(((f32[4,72,512]{2,1,0:T(8,128)}), f32[4,72,512]{2,1,0:T(8,128)S(1)}, u32[]{:S(2)}, u32[]{:S(2)}) %all-to-all-start.9) | async-done | bytes 589856 | tf_op jit(solution)/shard_map/all_to_all | solution.py:60
  95.9 3.5 %all-to-all-start.5 = ((f32[4,72,512]{2,1,0:T(8,128)}), f32[4,72,512]{2,1,0:T(8,128)S(1)}, u32[]{:S(2)}, u32[]{:S(2)}) async-start(f32[4,72,512]{2,1,0:T(8,128)} %bitcast.27), calls=%async_computation.5 | async-start | bytes 1179648 | tf_op jit(solution)/shard_map/all_to_all | solution.py:60
  99.4 0.4 fusion.16
  99.8 3.1 %collective-permute-start.3 = (f32[72,512]{1,0:T(8,128)S(1)}, f32[72,512]{1,0:T(8,128)S(1)}, u32[]{:S(2)}, u32[]{:S(2)}) collective-permute-start(f32[72,512]{1,0:T(8,128)S(1)} %fusion.16), channel_id=1, source_target_pairs={{0,1},{1,0},{2,3},{3,2},{4,5},{5,4},{6,7},{7,6},{8,9},{9,8},{10,11... | collective-permute-start | bytes 442376 | tf_op jit(solution)/shard_map/ppermute | solution.py:14
  103.0 3.0 %collective-permute-done.3 = f32[72,512]{1,0:T(8,128)S(1)} collective-permute-done((f32[72,512]{1,0:T(8,128)S(1)}, f32[72,512]{1,0:T(8,128)S(1)}, u32[]{:S(2)}, u32[]{:S(2)}) %collective-permute-start.3) | collective-permute-done | bytes 147488 | tf_op jit(solution)/shard_map/ppermute | solution.py:14
  106.0 0.4 fusion.12
  106.4 4.7 %collective-permute-start.4 = (f32[72,512]{1,0:T(8,128)S(1)}, f32[72,512]{1,0:T(8,128)S(1)}, u32[]{:S(2)}, u32[]{:S(2)}) collective-permute-start(f32[72,512]{1,0:T(8,128)S(1)} %fusion.12), channel_id=1, source_target_pairs={{0,2},{1,3},{2,0},{3,1},{4,6},{5,7},{6,4},{7,5},{8,10},{9,11},{10,... | collective-permute-start | bytes 442376 | tf_op jit(solution)/shard_map/ppermute | solution.py:14
  111.0 3.7 %all-to-all-done.5 = f32[4,72,512]{2,1,0:T(8,128)S(1)} async-done(((f32[4,72,512]{2,1,0:T(8,128)}), f32[4,72,512]{2,1,0:T(8,128)S(1)}, u32[]{:S(2)}, u32[]{:S(2)}) %all-to-all-start.5) | async-done | bytes 589856 | tf_op jit(solution)/shard_map/all_to_all | solution.py:60
  114.8 0.4 fusion.8
  115.2 6.3 %collective-permute-start.5 = (f32[72,512]{1,0:T(8,128)S(1)}, f32[72,512]{1,0:T(8,128)S(1)}, u32[]{:S(2)}, u32[]{:S(2)}) collective-permute-start(f32[72,512]{1,0:T(8,128)S(1)} %fusion.8), channel_id=1, source_target_pairs={{0,4},{1,5},{2,6},{3,7},{4,0},{5,1},{6,2},{7,3},{8,12},{9,13},{10,... | collective-permute-start | bytes 442376 | tf_op jit(solution)/shard_map/ppermute | solution.py:14
  121.5 0.4 fusion.18
  121.9 3.1 %collective-permute-start = (f32[72,512]{1,0:T(8,128)S(1)}, f32[72,512]{1,0:T(8,128)S(1)}, u32[]{:S(2)}, u32[]{:S(2)}) collective-permute-start(f32[72,512]{1,0:T(8,128)S(1)} %fusion.18), channel_id=1, source_target_pairs={{0,1},{1,0},{2,3},{3,2},{4,5},{5,4},{6,7},{7,6},{8,9},{9,8},{10,11... | collective-permute-start | bytes 442376 | tf_op jit(solution)/shard_map/ppermute | solution.py:14
  125.1 0.9 pad_maximum_fusion.7
  126.0 4.1 %all-to-all-start.10 = ((f32[4,72,512]{2,1,0:T(8,128)}), f32[4,72,512]{2,1,0:T(8,128)S(1)}, u32[]{:S(2)}, u32[]{:S(2)}) async-start(f32[4,72,512]{2,1,0:T(8,128)} %bitcast.40), calls=%async_computation.10 | async-start | bytes 1179648 | tf_op jit(solution)/shard_map/all_to_all | solution.py:60
  130.5 4.7 %collective-permute-start.1 = (f32[72,512]{1,0:T(8,128)S(1)}, f32[72,512]{1,0:T(8,128)S(1)}, u32[]{:S(2)}, u32[]{:S(2)}) collective-permute-start(f32[72,512]{1,0:T(8,128)S(1)} %fusion.14), channel_id=1, source_target_pairs={{0,2},{1,3},{2,0},{3,1},{4,6},{5,7},{6,4},{7,5},{8,10},{9,11},{10,... | collective-permute-start | bytes 442376 | tf_op jit(solution)/shard_map/ppermute | solution.py:14
  135.1 2.7 %collective-permute-done.1 = f32[72,512]{1,0:T(8,128)S(1)} collective-permute-done((f32[72,512]{1,0:T(8,128)S(1)}, f32[72,512]{1,0:T(8,128)S(1)}, u32[]{:S(2)}, u32[]{:S(2)}) %collective-permute-start.1) | collective-permute-done | bytes 147488 | tf_op jit(solution)/shard_map/ppermute | solution.py:14
  138.2 6.4 %collective-permute-start.2 = (f32[72,512]{1,0:T(8,128)S(1)}, f32[72,512]{1,0:T(8,128)S(1)}, u32[]{:S(2)}, u32[]{:S(2)}) collective-permute-start(f32[72,512]{1,0:T(8,128)S(1)} %fusion.10), channel_id=1, source_target_pairs={{0,4},{1,5},{2,6},{3,7},{4,0},{5,1},{6,2},{7,3},{8,12},{9,13},{10,... | collective-permute-start | bytes 442376 | tf_op jit(solution)/shard_map/ppermute | solution.py:14
  144.6 3.6 %collective-permute-done.2 = f32[72,512]{1,0:T(8,128)S(1)} collective-permute-done((f32[72,512]{1,0:T(8,128)S(1)}, f32[72,512]{1,0:T(8,128)S(1)}, u32[]{:S(2)}, u32[]{:S(2)}) %collective-permute-start.2) | collective-permute-done | bytes 147488 | tf_op jit(solution)/shard_map/ppermute | solution.py:14
  148.2 0.9 pad_maximum_fusion.6
  149.1 6.5 %all-to-all-start.6 = ((f32[4,72,512]{2,1,0:T(8,128)}), f32[4,72,512]{2,1,0:T(8,128)S(1)}, u32[]{:S(2)}, u32[]{:S(2)}) async-start(f32[4,72,512]{2,1,0:T(8,128)} %bitcast.31), calls=%async_computation.6 | async-start | bytes 1179648 | tf_op jit(solution)/shard_map/all_to_all | solution.py:60
  155.6 0.7 maximum_bitcast_fusion.3
  156.3 1.2 pad_maximum_fusion.5
  157.4 8.4 %all-to-all-done.6 = f32[4,72,512]{2,1,0:T(8,128)S(1)} async-done(((f32[4,72,512]{2,1,0:T(8,128)}), f32[4,72,512]{2,1,0:T(8,128)S(1)}, u32[]{:S(2)}, u32[]{:S(2)}) %all-to-all-start.6) | async-done | bytes 589856 | tf_op jit(solution)/shard_map/all_to_all | solution.py:60
  165.8 10.2 %all-to-all-start.11 = ((f32[2,288,512]{2,1,0:T(8,128)}), f32[2,288,512]{2,1,0:T(8,128)S(1)}, u32[]{:S(2)}, u32[]{:S(2)}) async-start(f32[2,288,512]{2,1,0:T(8,128)} %bitcast.42), calls=%async_computation.11 | async-start | bytes 2359296 | tf_op jit(solution)/shard_map/all_to_all | solution.py:60
  176.1 1.2 pad_maximum_fusion.3
  177.2 0.7 all-to-all-done.11
  177.9 4.0 %all-to-all-start.7 = ((f32[2,288,512]{2,1,0:T(8,128)}), f32[2,288,512]{2,1,0:T(8,128)S(1)}, u32[]{:S(2)}, u32[]{:S(2)}) async-start(f32[2,288,512]{2,1,0:T(8,128)} %bitcast.120), calls=%async_computation.7 | async-start | bytes 2359296 | tf_op jit(solution)/shard_map/all_to_all | solution.py:60
  181.9 0.9 slice_bitcast_fusion.2
  182.8 0.9 all-to-all-done.7
  184.0 1.6 maximum_bitcast_fusion
  (48 shorter events, 2.7 us)
Async XLA Ops:
  0.6 14.9 %copy-start = (bf16[1,1,128,512]{3,2,1,0:T(8,128)(2,1)S(1)}, bf16[1,1,128,512]{3,2,1,0:T(8,128)(2,1)}, u32[]{:S(2)}) copy-start(bf16[1,1,128,512]{3,2,1,0:T(8,128)(2,1)} %param.14) | copy-start | bytes 393220
  5.6 6.3 %copy-start.5 = (bf16[576,1,1,128]{3,0,2,1:T(8,128)(2,1)S(1)}, bf16[576,1,1,128]{3,0,2,1:T(8,128)(2,1)}, u32[]{:S(2)}) copy-start(bf16[576,1,1,128]{3,0,2,1:T(8,128)(2,1)} %param.11) | copy-start | bytes 442372
  5.6 6.3 %copy-start.9 = (s32[1,1,128]{2,1,0:T(1,128)S(1)}, s32[1,1,128]{2,1,0:T(1,128)}, u32[]{:S(2)}) copy-start(s32[1,1,128]{2,1,0:T(1,128)} %param.13) | copy-start | bytes 1540
  6.5 17.6 %all-to-all-start.2 = ((f32[4,292,128]{2,1,0:T(8,128)}), f32[4,292,128]{2,1,0:T(8,128)S(1)}, u32[]{:S(2)}, u32[]{:S(2)}) async-start(f32[4,292,128]{2,1,0:T(8,128)} %all_to_all.81), calls=%async_computation.2 | async-start | bytes 1212416 | tf_op jit(solution)/shard_map/all_to_all | solution.py:60
  11.9 2.0 %copy-start.6 = (f32[1,1,128]{2,1,0:T(1,128)S(1)}, f32[1,1,128]{2,1,0:T(1,128)}, u32[]{:S(2)}) copy-start(f32[1,1,128]{2,1,0:T(1,128)} %param.10) | copy-start | bytes 1540
  33.5 3.6 %copy-start.7 = (f32[3,1,1,128]{3,2,1,0:T(1,128)S(1)}, f32[3,1,1,128]{3,2,1,0:T(1,128)}, u32[]{:S(2)}) copy-start(f32[3,1,1,128]{3,2,1,0:T(1,128)} %param.9) | copy-start | bytes 4612
  33.5 19.6 %all-to-all-start = ((f32[4,292,128]{2,1,0:T(8,128)}), f32[4,292,128]{2,1,0:T(8,128)S(1)}, u32[]{:S(2)}, u32[]{:S(2)}) async-start(f32[4,292,128]{2,1,0:T(8,128)} %all_to_all.76), calls=%async_computation | async-start | bytes 1212416 | tf_op jit(solution)/shard_map/all_to_all | solution.py:60
  37.2 2.1 %copy-start.8 = (bf16[576,1,1,128]{3,0,2,1:T(8,128)(2,1)S(1)}, bf16[576,1,1,128]{3,0,2,1:T(8,128)(2,1)}, u32[]{:S(2)}) copy-start(bf16[576,1,1,128]{3,0,2,1:T(8,128)(2,1)} %param.12) | copy-start | bytes 442372
  54.2 4.9 %copy-start.3 = (f32[288,512]{1,0:T(8,128)S(1)}, f32[288,512]{1,0:T(8,128)}, u32[]{:S(2)}) copy-start(f32[288,512]{1,0:T(8,128)} %fusion.51) | copy-start | bytes 1769476
  54.3 4.9 %copy-start.4 = (f32[288,512]{1,0:T(8,128)S(1)}, f32[288,512]{1,0:T(8,128)}, u32[]{:S(2)}) copy-start(f32[288,512]{1,0:T(8,128)} %fusion.53) | copy-start | bytes 1769476
  54.3 6.8 %all-to-all-start.1 = ((f32[2,1168,128]{2,1,0:T(8,128)}), f32[2,1168,128]{2,1,0:T(8,128)S(1)}, u32[]{:S(2)}, u32[]{:S(2)}) async-start(f32[2,1168,128]{2,1,0:T(8,128)} %bitcast.4), calls=%async_computation.1 | async-start | bytes 2392064 | tf_op jit(solution)/shard_map/all_to_all | solution.py:60
  61.0 10.3 %all-to-all-start.8 = ((f32[2,288,512]{2,1,0:T(8,128)}), f32[2,288,512]{2,1,0:T(8,128)S(1)}, u32[]{:S(2)}, u32[]{:S(2)}) async-start(f32[2,288,512]{2,1,0:T(8,128)} %bitcast.119), calls=%async_computation.8 | async-start | bytes 2359296 | tf_op jit(solution)/shard_map/all_to_all | solution.py:60
  71.4 5.4 %all-to-all-start.4 = ((f32[2,288,512]{2,1,0:T(8,128)}), f32[2,288,512]{2,1,0:T(8,128)S(1)}, u32[]{:S(2)}, u32[]{:S(2)}) async-start(f32[2,288,512]{2,1,0:T(8,128)} %bitcast.121), calls=%async_computation.4 | async-start | bytes 2359296 | tf_op jit(solution)/shard_map/all_to_all | solution.py:60
  76.8 19.1 %all-to-all-start.9 = ((f32[4,72,512]{2,1,0:T(8,128)}), f32[4,72,512]{2,1,0:T(8,128)S(1)}, u32[]{:S(2)}, u32[]{:S(2)}) async-start(f32[4,72,512]{2,1,0:T(8,128)} %bitcast.39), calls=%async_computation.9 | async-start | bytes 1179648 | tf_op jit(solution)/shard_map/all_to_all | solution.py:60
  81.2 18.2 %copy-start.1 = (bf16[1,3,512,512]{3,2,1,0:T(8,128)(2,1)S(1)}, bf16[1,3,512,512]{3,2,1,0:T(8,128)(2,1)}, u32[]{:S(2)}) copy-start(bf16[1,3,512,512]{3,2,1,0:T(8,128)(2,1)} %param.15) | copy-start | bytes 4718596
  95.9 18.8 %all-to-all-start.5 = ((f32[4,72,512]{2,1,0:T(8,128)}), f32[4,72,512]{2,1,0:T(8,128)S(1)}, u32[]{:S(2)}, u32[]{:S(2)}) async-start(f32[4,72,512]{2,1,0:T(8,128)} %bitcast.27), calls=%async_computation.5 | async-start | bytes 1179648 | tf_op jit(solution)/shard_map/all_to_all | solution.py:60
  99.8 6.2 %collective-permute-start.3 = (f32[72,512]{1,0:T(8,128)S(1)}, f32[72,512]{1,0:T(8,128)S(1)}, u32[]{:S(2)}, u32[]{:S(2)}) collective-permute-start(f32[72,512]{1,0:T(8,128)S(1)} %fusion.16), channel_id=1, source_target_pairs={{0,1},{1,0},{2,3},{3,2},{4,5},{5,4},{6,7},{7,6},{8,9},{9,8},{10,11... | collective-permute-start | bytes 442376 | tf_op jit(solution)/shard_map/ppermute | solution.py:14
  106.4 8.4 %collective-permute-start.4 = (f32[72,512]{1,0:T(8,128)S(1)}, f32[72,512]{1,0:T(8,128)S(1)}, u32[]{:S(2)}, u32[]{:S(2)}) collective-permute-start(f32[72,512]{1,0:T(8,128)S(1)} %fusion.12), channel_id=1, source_target_pairs={{0,2},{1,3},{2,0},{3,1},{4,6},{5,7},{6,4},{7,5},{8,10},{9,11},{10,... | collective-permute-start | bytes 442376 | tf_op jit(solution)/shard_map/ppermute | solution.py:14
  115.2 9.9 %collective-permute-start.5 = (f32[72,512]{1,0:T(8,128)S(1)}, f32[72,512]{1,0:T(8,128)S(1)}, u32[]{:S(2)}, u32[]{:S(2)}) collective-permute-start(f32[72,512]{1,0:T(8,128)S(1)} %fusion.8), channel_id=1, source_target_pairs={{0,4},{1,5},{2,6},{3,7},{4,0},{5,1},{6,2},{7,3},{8,12},{9,13},{10,... | collective-permute-start | bytes 442376 | tf_op jit(solution)/shard_map/ppermute | solution.py:14
  121.9 8.2 %collective-permute-start = (f32[72,512]{1,0:T(8,128)S(1)}, f32[72,512]{1,0:T(8,128)S(1)}, u32[]{:S(2)}, u32[]{:S(2)}) collective-permute-start(f32[72,512]{1,0:T(8,128)S(1)} %fusion.18), channel_id=1, source_target_pairs={{0,1},{1,0},{2,3},{3,2},{4,5},{5,4},{6,7},{7,6},{8,9},{9,8},{10,11... | collective-permute-start | bytes 442376 | tf_op jit(solution)/shard_map/ppermute | solution.py:14
  126.0 23.2 %all-to-all-start.10 = ((f32[4,72,512]{2,1,0:T(8,128)}), f32[4,72,512]{2,1,0:T(8,128)S(1)}, u32[]{:S(2)}, u32[]{:S(2)}) async-start(f32[4,72,512]{2,1,0:T(8,128)} %bitcast.40), calls=%async_computation.10 | async-start | bytes 1179648 | tf_op jit(solution)/shard_map/all_to_all | solution.py:60
  130.5 7.4 %collective-permute-start.1 = (f32[72,512]{1,0:T(8,128)S(1)}, f32[72,512]{1,0:T(8,128)S(1)}, u32[]{:S(2)}, u32[]{:S(2)}) collective-permute-start(f32[72,512]{1,0:T(8,128)S(1)} %fusion.14), channel_id=1, source_target_pairs={{0,2},{1,3},{2,0},{3,1},{4,6},{5,7},{6,4},{7,5},{8,10},{9,11},{10,... | collective-permute-start | bytes 442376 | tf_op jit(solution)/shard_map/ppermute | solution.py:14
  138.2 10.0 %collective-permute-start.2 = (f32[72,512]{1,0:T(8,128)S(1)}, f32[72,512]{1,0:T(8,128)S(1)}, u32[]{:S(2)}, u32[]{:S(2)}) collective-permute-start(f32[72,512]{1,0:T(8,128)S(1)} %fusion.10), channel_id=1, source_target_pairs={{0,4},{1,5},{2,6},{3,7},{4,0},{5,1},{6,2},{7,3},{8,12},{9,13},{10,... | collective-permute-start | bytes 442376 | tf_op jit(solution)/shard_map/ppermute | solution.py:14
  149.1 16.7 %all-to-all-start.6 = ((f32[4,72,512]{2,1,0:T(8,128)}), f32[4,72,512]{2,1,0:T(8,128)S(1)}, u32[]{:S(2)}, u32[]{:S(2)}) async-start(f32[4,72,512]{2,1,0:T(8,128)} %bitcast.31), calls=%async_computation.6 | async-start | bytes 1179648 | tf_op jit(solution)/shard_map/all_to_all | solution.py:60
  165.8 12.1 %all-to-all-start.11 = ((f32[2,288,512]{2,1,0:T(8,128)}), f32[2,288,512]{2,1,0:T(8,128)S(1)}, u32[]{:S(2)}, u32[]{:S(2)}) async-start(f32[2,288,512]{2,1,0:T(8,128)} %bitcast.42), calls=%async_computation.11 | async-start | bytes 2359296 | tf_op jit(solution)/shard_map/all_to_all | solution.py:60
  177.9 5.8 %all-to-all-start.7 = ((f32[2,288,512]{2,1,0:T(8,128)}), f32[2,288,512]{2,1,0:T(8,128)S(1)}, u32[]{:S(2)}, u32[]{:S(2)}) async-start(f32[2,288,512]{2,1,0:T(8,128)} %bitcast.120), calls=%async_computation.7 | async-start | bytes 2359296 | tf_op jit(solution)/shard_map/all_to_all | solution.py:60
  182.8 1.1 copy-start.2

commit v7 on v5

--- a/solution.py
+++ b/solution.py
@@ -3,6 +3,7 @@
 import jax
 import jax.numpy as jnp
 from jax import lax
+from jax.experimental import pallas as pl
 from jax.sharding import PartitionSpec as P
 
 inv_four_pi = 1.0 / (4.0 * math.pi)
@@ -77,6 +78,56 @@
     return gather_blocks(gather_blocks(rows, "ylo"), "core")
 
 
+def near_project_kernel(target_ref, source_ref, sketch_ref, probe_ref, order_ref, basis_ref, off_ref, parts_ref):
+    block_count = source_ref.shape[0]
+    probe_count, panels = sketch_ref.shape
+    geometry_rows = source_ref.shape[1] - probe_count
+    target = target_ref[...]
+    near = jnp.zeros((probe_count, panels), jnp.float32)
+    for block in range(block_count):
+        geometry = source_ref[block, 0:geometry_rows, :]
+        distance = jnp.zeros((panels, panels), jnp.float32)
+        for component in range(3):
+            gap = target[:, component : component + 1] - geometry[component : component + 1, :]
+            distance = distance + gap * gap
+        soft = distance + 0.5 * (target[:, 3:4] + geometry[3:4, :])
+        tile = (inv_four_pi * lax.rsqrt(soft)).astype(jnp.bfloat16)
+        scaled = source_ref[block, geometry_rows:, :].astype(jnp.bfloat16)
+        near = near + lax.dot_general(
+            scaled, tile, (((1,), (1,)), ((), ())), preferred_element_type=jnp.float32
+        )
+    off = (sketch_ref[...].astype(jnp.float32) - near).astype(jnp.bfloat16)
+    off_ref[...] = off
+    lanes = lax.broadcasted_iota(jnp.int32, (panels, panels), 1)
+    onehot = (order_ref[...] == lanes).astype(jnp.bfloat16)
+    basis = basis_ref[...]
+    for index, values in enumerate((off, probe_ref[...])):
+        ordered = lax.dot_general(
+            values, onehot, (((1,), (1,)), ((), ())), preferred_element_type=jnp.float32
+        ).astype(jnp.bfloat16)
+        parts_ref[index * probe_count : (index + 1) * probe_count, :] = jnp.dot(
+            ordered, basis, preferred_element_type=jnp.float32
+        )
+
+
+def near_project(target, source, sketch, probe, order, basis):
+    probe_count, panels = sketch.shape
+    width = basis.shape[1]
+    blocks = source.shape[0]
+    flops = 2 * probe_count * panels * (blocks * panels + 2 * panels + 2 * width)
+    bytes_accessed = 4 * source.size + 2 * (3 * sketch.size + basis.size) + 8 * probe_count * width
+    return pl.pallas_call(
+        near_project_kernel,
+        out_shape=(
+            jax.ShapeDtypeStruct((probe_count, panels), jnp.bfloat16),
+            jax.ShapeDtypeStruct((2 * probe_count, width), jnp.float32),
+        ),
+        cost_estimate=pl.CostEstimate(
+            flops=flops, transcendentals=blocks * panels * panels, bytes_accessed=bytes_accessed
+        ),
+    )(target, source, sketch, probe, order, basis)
+
+
 def shards(positions, panel_areas, probe_cols, full_sketch, tree_order, leaf_basis, transfer_mats):
     panels = positions.shape[3]
     probe_count = probe_cols.shape[0]
@@ -86,24 +137,20 @@
     area_row = panel_areas.reshape(1, panels)
     probe_flat = probe_cols.reshape(probe_count, panels)
     scaled = (area_row * probe_flat.astype(jnp.float32)).astype(jnp.bfloat16)
-    sorting = tree_order.reshape(panels)
     basis_flat = leaf_basis.reshape(panels, basis_width)
     level_mats = transfer_mats.reshape(level_count, basis_width, basis_width)
-    probe_part = jnp.dot(
-        jnp.take(probe_flat, sorting, axis=1), basis_flat, preferred_element_type=jnp.float32
+    geometry = jnp.concatenate([coords, area_row, jnp.zeros((4, panels), jnp.float32)], axis=0)
+    outgoing = jnp.concatenate([geometry, scaled.astype(jnp.float32)], axis=0)
+    blocks = gather_blocks(gather_blocks(outgoing, "ylo"), "core")
+    source = blocks.reshape(-1, outgoing.shape[0], panels)
+    offdiag, stacked = near_project(
+        jnp.transpose(geometry),
+        source,
+        full_sketch.reshape(probe_count, panels),
+        probe_flat,
+        tree_order.reshape(panels, 1),
+        basis_flat,
     )
-    outgoing = jnp.concatenate([coords, area_row, scaled.astype(jnp.float32)], axis=0)
-    rows_out = outgoing.shape[0]
-    stacked_blocks = gather_blocks(gather_blocks(outgoing, "ylo"), "core")
-    piece = jnp.transpose(stacked_blocks.reshape(-1, rows_out, panels), (1, 0, 2)).reshape(rows_out, -1)
-    near_sum = near_block(coords, area_row[0], piece[:3], piece[3], piece[4:].astype(jnp.bfloat16))
-    offdiag = (full_sketch.reshape(probe_count, panels).astype(jnp.float32) - near_sum).astype(
-        jnp.bfloat16
-    )
-    sketch_part = jnp.dot(
-        jnp.take(offdiag, sorting, axis=1), basis_flat, preferred_element_type=jnp.float32
-    )
-    stacked = jnp.concatenate([sketch_part, probe_part], axis=0)
     mine = scatter_rows(stacked)
     top = climb_rows(mine, level_mats)
     nested = gather_rows(top).reshape(2, probe_count, basis_width)[None]

time: 172 us -> 175 us (1.017)
  matrix products: 6.14 us -> 1.22 us
  Pallas kernels: 0 us -> 4.76 us
  blocking collectives: 82.4 us -> 84.6 us
    concatenate x1, local copies, waits for them, and re-layouts: 0.92 us -> 8.06 us  [gather_blocks(): return exchange(jnp.concatenate([block] * count, axis=0), axis)]
    dot_general x3 -> x0, matrix products: 4.93 us -> none  [the longest x1 3.07 us: one_block(): lax.dot_general(source_scaled, kernel, (((1,), (1,)), ((), ())), preferre...]
    pallas_call x0 -> x1, Pallas kernels: none -> 4.76 us  [near_project(): pl.pallas_call(near_project_kernel, out_shape=(jax.ShapeDtypeStruct((prob...]
    all_to_all x3 -> x0, local copies, waits for them, and re-layouts: 2.45 us -> none  [exchange(): return lax.all_to_all(value, axis, 0, 0, tiled=True)]
    all_to_all x5, blocking collectives: 82.4 us -> 84.6 us  [exchange(): return lax.all_to_all(value, axis, 0, 0, tiled=True)]
    gather x2 -> x0, local copies, waits for them, and re-layouts: 1.77 us -> none  [the longest x1 0.89 us: shards(): jnp.take(probe_flat, sorting, axis=1)]
where the time goes in v7:
time: 175 us; the launch traced here: 174 us
  blocking collectives  84.6 us (48%)
  waiting for transfers between devices  49.6 us (28%)
  starting transfers between devices  19.7 us (11%)
  local copies, waits for them, and re-layouts  11.6 us (7%)
  Pallas kernels  4.76 us (3%)
  other arithmetic  1.96 us (1%)
    all_to_all x5, blocking collectives, exchange(): return lax.all_to_all(value, axis, 0, 0, tiled=True)  84.6 us
    all_to_all x1, waiting for transfers between devices, exchange(): return lax.all_to_all(value, axis, 0, 0, tiled=True)  25.7 us
    ppermute x3, waiting for transfers between devices, partner(): return lax.ppermute(value, axis, pairs)  23.9 us
    ppermute x3, starting transfers between devices, partner(): return lax.ppermute(value, axis, pairs)  14.1 us
    concatenate x1, local copies, waits for them, and re-layouts, gather_blocks(): return exchange(jnp.concatenate([block] * count, axis=0), axis)  8.06 us
    all_to_all x1, starting transfers between devices, exchange(): return lax.all_to_all(value, axis, 0, 0, tiled=True)  5.55 us
    pallas_call x1, Pallas kernels, near_project(): pl.pallas_call(near_project_kernel, out_shape=(jax.ShapeDtypeStruct((prob...  4.76 us
  transfers between devices with their start and end apart: 4, of which 4 were waited for; matrix products, arithmetic and copies ran while one was open for 1% of the time, Pallas kernels for 0%

profile of v7, /device:TPU:1, one launch (start us, length us, event | category | flops | bytes accessed | tf_op | source)
XLA Modules:
  0.0 174.2 jit_solution(6167108784481542273)
XLA Ops:
  0.6 0.7 copy.13
  1.3 0.9 fusion.11
  2.3 8.1 %concatenate.19 = f32[2336,128]{1,0:T(8,128)} concatenate(f32[3,128]{1,0:T(4,128)S(1)} %bitcast.45, f32[1,128]{1,0:T(1,128)} %bitcast.51, f32[4,128]{1,0:T(4,128)S(1)} %broadcast_in_dim.3, f32[576,128]{1,0:T(8,128)S(1)} %fusion.11, f32[3,128]{1,0:T(4,128)S(1)} %bitcast.46, f32[1,128]{1,0:T(1,128)} %bitcast.52, f32[4,128]{1,0:T(4,128)S(1)} %broadcast_in_dim.3, ...), dimensions={0} | concatenate | bytes 2392064 | tf_op jit(solution)/shard_map/concatenate | solution.py:66
  10.3 0.0 copy-start.1
  10.3 0.0 copy-start.2
  10.3 5.6 %all-to-all-start = ((f32[4,584,128]{2,1,0:T(8,128)}), f32[4,584,128]{2,1,0:T(8,128)S(1)}, u32[]{:S(2)}, u32[]{:S(2)}) async-start(f32[4,584,128]{2,1,0:T(8,128)} %bitcast.4), calls=%async_computation | async-start | bytes 2392064 | tf_op jit(solution)/shard_map/all_to_all | solution.py:61
  15.9 0.0 copy-done.1
  15.9 0.7 copy.9.target_ref
  16.6 0.0 copy-done.2
  16.6 0.7 copy.10.order_ref
  17.4 25.7 %all-to-all-done = f32[4,584,128]{2,1,0:T(8,128)S(1)} async-done(((f32[4,584,128]{2,1,0:T(8,128)}), f32[4,584,128]{2,1,0:T(8,128)S(1)}, u32[]{:S(2)}, u32[]{:S(2)}) %all-to-all-start) | async-done | bytes 1196064 | tf_op jit(solution)/shard_map/all_to_all | solution.py:61
  43.1 0.2 pad_maximum_fusion
  43.2 8.9 %all_to_all.57 = f32[2,2336,128]{2,1,0:T(8,128)} all-to-all(f32[2,2336,128]{2,1,0:T(8,128)S(1)} %bitcast.33), channel_id=1, replica_groups=mesh['ylo'=4,'core'=2,'leaf'=64] {'core'}, dimensions={0} | all-to-all | bytes 4784128 | tf_op jit(solution)/shard_map/all_to_all | solution.py:61
  52.1 4.8 %shard_map.86 = (bf16[576,128]{1,0:T(8,128)(2,1)}, f32[1152,512]{1,0:T(8,128)}) custom-call(f32[128,8]{1,0:T(8,128)} %copy.9.target_ref, f32[8,584,128]{2,1,0:T(8,128)} %bitcast.34, bf16[576,128]{1,0:T(8,128)(2,1)} %bitcast.43, bf16[576,128]{1,0:T(8,128)(2,1)} %bitcast.42, s32[128,1]{1,0:T(8,128)} %copy.10.order_ref, bf16[128,512]{1,0:T(8,128)(2,1)} %bitcast.44), custom_call_target="tpu_custom_call" | custom-call | flops 339738624 | bytes 5324800 | tf_op jit(solution)/shard_map/pallas_call | solution.py:119
  56.8 6.8 %all_to_all.58 = f32[2,576,512]{2,1,0:T(8,128)S(1)} all-to-all(f32[2,576,512]{2,1,0:T(8,128)} %bitcast.41), channel_id=1, replica_groups=mesh['ylo'=4,'core'=2,'leaf'=64] {'core'}, dimensions={0} | all-to-all | bytes 4718592 | tf_op jit(solution)/shard_map/all_to_all | solution.py:61
  63.7 0.2 slice_add_fusion
  63.9 0.0 copy-start
  63.9 30.7 %all_to_all.59 = f32[4,144,512]{2,1,0:T(8,128)S(1)} all-to-all(f32[4,144,512]{2,1,0:T(8,128)S(1)} %bitcast.38), channel_id=1, replica_groups=mesh['ylo'=4,'core'=2,'leaf'=64] {'ylo'}, dimensions={0} | all-to-all | bytes 2359296 | tf_op jit(solution)/shard_map/all_to_all | solution.py:61
  94.7 0.1 reduce_sum.9
  94.8 0.0 copy-done
  94.8 0.4 fusion.4
  95.2 3.1 %collective-permute-start = (f32[144,512]{1,0:T(8,128)S(1)}, f32[144,512]{1,0:T(8,128)S(1)}, u32[]{:S(2)}, u32[]{:S(2)}) collective-permute-start(f32[144,512]{1,0:T(8,128)S(1)} %fusion.4), channel_id=1, source_target_pairs={{0,1},{1,0},{2,3},{3,2},{4,5},{5,4},{6,7},{7,6},{8,9},{9,8},{10,11... | collective-permute-start | bytes 884744 | tf_op jit(solution)/shard_map/ppermute | solution.py:15
  98.3 6.0 %collective-permute-done = f32[144,512]{1,0:T(8,128)S(1)} collective-permute-done((f32[144,512]{1,0:T(8,128)S(1)}, f32[144,512]{1,0:T(8,128)S(1)}, u32[]{:S(2)}, u32[]{:S(2)}) %collective-permute-start) | collective-permute-done | bytes 294944 | tf_op jit(solution)/shard_map/ppermute | solution.py:15
  104.3 0.4 fusion.2
  104.7 4.7 %collective-permute-start.1 = (f32[144,512]{1,0:T(8,128)S(1)}, f32[144,512]{1,0:T(8,128)S(1)}, u32[]{:S(2)}, u32[]{:S(2)}) collective-permute-start(f32[144,512]{1,0:T(8,128)S(1)} %fusion.2), channel_id=1, source_target_pairs={{0,2},{1,3},{2,0},{3,1},{4,6},{5,7},{6,4},{7,5},{8,10},{9,11},{10,... | collective-permute-start | bytes 884744 | tf_op jit(solution)/shard_map/ppermute | solution.py:15
  109.4 5.0 %collective-permute-done.1 = f32[144,512]{1,0:T(8,128)S(1)} collective-permute-done((f32[144,512]{1,0:T(8,128)S(1)}, f32[144,512]{1,0:T(8,128)S(1)}, u32[]{:S(2)}, u32[]{:S(2)}) %collective-permute-start.1) | collective-permute-done | bytes 294944 | tf_op jit(solution)/shard_map/ppermute | solution.py:15
  114.4 0.4 fusion
  114.8 6.3 %collective-permute-start.2 = (f32[144,512]{1,0:T(8,128)S(1)}, f32[144,512]{1,0:T(8,128)S(1)}, u32[]{:S(2)}, u32[]{:S(2)}) collective-permute-start(f32[144,512]{1,0:T(8,128)S(1)} %fusion), channel_id=1, source_target_pairs={{0,4},{1,5},{2,6},{3,7},{4,0},{5,1},{6,2},{7,3},{8,12},{9,13},{10,... | collective-permute-start | bytes 884744 | tf_op jit(solution)/shard_map/ppermute | solution.py:15
  121.2 13.0 %collective-permute-done.2 = f32[144,512]{1,0:T(8,128)S(1)} collective-permute-done((f32[144,512]{1,0:T(8,128)S(1)}, f32[144,512]{1,0:T(8,128)S(1)}, u32[]{:S(2)}, u32[]{:S(2)}) %collective-permute-start.2) | collective-permute-done | bytes 294944 | tf_op jit(solution)/shard_map/ppermute | solution.py:15
  134.2 0.1 pad_maximum_fusion.2
  134.3 31.0 %all_to_all.60 = f32[4,144,512]{2,1,0:T(8,128)S(1)} all-to-all(f32[4,144,512]{2,1,0:T(8,128)S(1)} %bitcast.40), channel_id=1, replica_groups=mesh['ylo'=4,'core'=2,'leaf'=64] {'ylo'}, dimensions={0} | all-to-all | bytes 2359296 | tf_op jit(solution)/shard_map/all_to_all | solution.py:61
  165.3 0.3 pad_maximum_fusion.1
  165.7 7.2 %all_to_all.61 = f32[2,576,512]{2,1,0:T(8,128)S(1)} all-to-all(f32[2,576,512]{2,1,0:T(8,128)S(1)} %bitcast.36), channel_id=1, replica_groups=mesh['ylo'=4,'core'=2,'leaf'=64] {'core'}, dimensions={0} | all-to-all | bytes 4718592 | tf_op jit(solution)/shard_map/all_to_all | solution.py:61
  172.8 1.4 copy.15
  (3 shorter events, 0.1 us)
Async XLA Ops:
  10.3 5.6 %copy-start.1 = (f32[1,1,128]{2,1,0:T(1,128)S(1)}, f32[1,1,128]{2,1,0:T(1,128)}, u32[]{:S(2)}) copy-start(f32[1,1,128]{2,1,0:T(1,128)} %param.8) | copy-start | bytes 1540
  10.3 6.3 %copy-start.2 = (s32[1,1,128]{2,1,0:T(1,128)S(1)}, s32[1,1,128]{2,1,0:T(1,128)}, u32[]{:S(2)}) copy-start(s32[1,1,128]{2,1,0:T(1,128)} %param.11) | copy-start | bytes 1540
  10.3 32.7 %all-to-all-start = ((f32[4,584,128]{2,1,0:T(8,128)}), f32[4,584,128]{2,1,0:T(8,128)S(1)}, u32[]{:S(2)}, u32[]{:S(2)}) async-start(f32[4,584,128]{2,1,0:T(8,128)} %bitcast.4), calls=%async_computation | async-start | bytes 2392064 | tf_op jit(solution)/shard_map/all_to_all | solution.py:61
  63.9 30.9 %copy-start = (bf16[1,3,512,512]{3,2,1,0:T(8,128)(2,1)S(1)}, bf16[1,3,512,512]{3,2,1,0:T(8,128)(2,1)}, u32[]{:S(2)}) copy-start(bf16[1,3,512,512]{3,2,1,0:T(8,128)(2,1)} %param.13) | copy-start | bytes 4718596
  95.2 9.1 %collective-permute-start = (f32[144,512]{1,0:T(8,128)S(1)}, f32[144,512]{1,0:T(8,128)S(1)}, u32[]{:S(2)}, u32[]{:S(2)}) collective-permute-start(f32[144,512]{1,0:T(8,128)S(1)} %fusion.4), channel_id=1, source_target_pairs={{0,1},{1,0},{2,3},{3,2},{4,5},{5,4},{6,7},{7,6},{8,9},{9,8},{10,11... | collective-permute-start | bytes 884744 | tf_op jit(solution)/shard_map/ppermute | solution.py:15
  104.7 9.7 %collective-permute-start.1 = (f32[144,512]{1,0:T(8,128)S(1)}, f32[144,512]{1,0:T(8,128)S(1)}, u32[]{:S(2)}, u32[]{:S(2)}) collective-permute-start(f32[144,512]{1,0:T(8,128)S(1)} %fusion.2), channel_id=1, source_target_pairs={{0,2},{1,3},{2,0},{3,1},{4,6},{5,7},{6,4},{7,5},{8,10},{9,11},{10,... | collective-permute-start | bytes 884744 | tf_op jit(solution)/shard_map/ppermute | solution.py:15
  114.8 19.3 %collective-permute-start.2 = (f32[144,512]{1,0:T(8,128)S(1)}, f32[144,512]{1,0:T(8,128)S(1)}, u32[]{:S(2)}, u32[]{:S(2)}) collective-permute-start(f32[144,512]{1,0:T(8,128)S(1)} %fusion), channel_id=1, source_target_pairs={{0,4},{1,5},{2,6},{3,7},{4,0},{5,1},{6,2},{7,3},{8,12},{9,13},{10,... | collective-permute-start | bytes 884744 | tf_op jit(solution)/shard_map/ppermute | solution.py:15

commit v8 on v7

--- a/solution.py
+++ b/solution.py
@@ -63,7 +63,8 @@
 
 def gather_blocks(block, axis):
     count = lax.axis_size(axis)
-    return exchange(jnp.concatenate([block] * count, axis=0), axis)
+    copies = jnp.broadcast_to(block[None], (count,) + block.shape)
+    return exchange(copies.reshape((count * block.shape[0],) + block.shape[1:]), axis)
 
 
 def scatter_rows(value):

time: 175 us -> 168 us (0.960)
  local copies, waits for them, and re-layouts: 11.6 us -> 5.28 us
    concatenate x1 -> x0, local copies, waits for them, and re-layouts: 8.06 us -> none  [gather_blocks(): return exchange(jnp.concatenate([block] * count, axis=0), axis)]
where the time goes in v8:
time: 168 us
  blocking collectives  84.6 us (50%)
  waiting for transfers between devices  49.5 us (29%)
  starting transfers between devices  19.7 us (12%)
  local copies, waits for them, and re-layouts  5.28 us (3%)
  Pallas kernels  4.76 us (3%)
  other arithmetic  2.03 us (1%)
    all_to_all x5, blocking collectives, exchange(): return lax.all_to_all(value, axis, 0, 0, tiled=True)  84.6 us
    all_to_all x1, waiting for transfers between devices, exchange(): return lax.all_to_all(value, axis, 0, 0, tiled=True)  25.7 us
    ppermute x3, waiting for transfers between devices, partner(): return lax.ppermute(value, axis, pairs)  23.9 us
    ppermute x3, starting transfers between devices, partner(): return lax.ppermute(value, axis, pairs)  14.2 us
    all_to_all x1, starting transfers between devices, exchange(): return lax.all_to_all(value, axis, 0, 0, tiled=True)  5.55 us
    pallas_call x1, Pallas kernels, near_project(): pl.pallas_call(near_project_kernel, out_shape=(jax.ShapeDtypeStruct((prob...  4.76 us
  transfers between devices with their start and end apart: 4, of which 4 were waited for; matrix products, arithmetic and copies ran while one was open for 1% of the time, Pallas kernels for 0%

profile of v8, /device:TPU:1, one launch (start us, length us, event | category | flops | bytes accessed | tf_op | source)
XLA Modules:
  0.0 167.9 jit_solution(9640900003482744629)
XLA Ops:
  0.6 0.7 copy.13
  1.3 0.9 fusion.11
  2.3 0.7 pad_maximum_fusion
  3.0 0.0 copy-start.1
  3.0 1.1 broadcast_in_dim.15
  4.1 0.0 copy-start.2
  4.1 5.6 %all-to-all-start = ((f32[4,584,128]{2,1,0:T(8,128)}), f32[4,584,128]{2,1,0:T(8,128)S(1)}, u32[]{:S(2)}, u32[]{:S(2)}) async-start(f32[4,584,128]{2,1,0:T(8,128)} %broadcast_in_dim.15), calls=%async_computation | async-start | bytes 2392064 | tf_op jit(solution)/shard_map/all_to_all | solution.py:61
  9.6 0.0 copy-done.1
  9.6 0.7 copy.9.target_ref
  10.4 0.0 copy-done.2
  10.4 0.7 copy.10.order_ref
  11.1 25.7 %all-to-all-done = f32[4,584,128]{2,1,0:T(8,128)S(1)} async-done(((f32[4,584,128]{2,1,0:T(8,128)}), f32[4,584,128]{2,1,0:T(8,128)S(1)}, u32[]{:S(2)}, u32[]{:S(2)}) %all-to-all-start) | async-done | bytes 1196064 | tf_op jit(solution)/shard_map/all_to_all | solution.py:61
  36.8 0.2 broadcast_in_dim.34
  36.9 8.9 %all_to_all.39 = f32[2,2336,128]{2,1,0:T(8,128)} all-to-all(f32[2,2336,128]{2,1,0:T(8,128)S(1)} %broadcast_in_dim.34), channel_id=1, replica_groups=mesh['ylo'=4,'core'=2,'leaf'=64] {'core'}, dimensions={0} | all-to-all | bytes 4784128 | tf_op jit(solution)/shard_map/all_to_all | solution.py:61
  45.8 4.8 %shard_map.86 = (bf16[576,128]{1,0:T(8,128)(2,1)}, f32[1152,512]{1,0:T(8,128)}) custom-call(f32[128,8]{1,0:T(8,128)} %copy.9.target_ref, f32[8,584,128]{2,1,0:T(8,128)} %bitcast.29, bf16[576,128]{1,0:T(8,128)(2,1)} %bitcast.36, bf16[576,128]{1,0:T(8,128)(2,1)} %bitcast.35, s32[128,1]{1,0:T(8,128)} %copy.10.order_ref, bf16[128,512]{1,0:T(8,128)(2,1)} %bitcast.37), custom_call_target="tpu_custom_call" | custom-call | flops 339738624 | bytes 5324800 | tf_op jit(solution)/shard_map/pallas_call | solution.py:120
  50.6 6.8 %all_to_all.40 = f32[2,576,512]{2,1,0:T(8,128)S(1)} all-to-all(f32[2,576,512]{2,1,0:T(8,128)} %bitcast.34), channel_id=1, replica_groups=mesh['ylo'=4,'core'=2,'leaf'=64] {'core'}, dimensions={0} | all-to-all | bytes 4718592 | tf_op jit(solution)/shard_map/all_to_all | solution.py:61
  57.4 0.2 slice_add_fusion
  57.7 0.0 copy-start
  57.7 30.7 %all_to_all.41 = f32[4,144,512]{2,1,0:T(8,128)S(1)} all-to-all(f32[4,144,512]{2,1,0:T(8,128)S(1)} %bitcast.32), channel_id=1, replica_groups=mesh['ylo'=4,'core'=2,'leaf'=64] {'ylo'}, dimensions={0} | all-to-all | bytes 2359296 | tf_op jit(solution)/shard_map/all_to_all | solution.py:61
  88.4 0.1 reduce_sum.9
  88.5 0.0 copy-done
  88.5 0.4 fusion.4
  88.9 3.1 %collective-permute-start = (f32[144,512]{1,0:T(8,128)S(1)}, f32[144,512]{1,0:T(8,128)S(1)}, u32[]{:S(2)}, u32[]{:S(2)}) collective-permute-start(f32[144,512]{1,0:T(8,128)S(1)} %fusion.4), channel_id=1, source_target_pairs={{0,1},{1,0},{2,3},{3,2},{4,5},{5,4},{6,7},{7,6},{8,9},{9,8},{10,11... | collective-permute-start | bytes 884744 | tf_op jit(solution)/shard_map/ppermute | solution.py:15
  92.1 5.9 %collective-permute-done = f32[144,512]{1,0:T(8,128)S(1)} collective-permute-done((f32[144,512]{1,0:T(8,128)S(1)}, f32[144,512]{1,0:T(8,128)S(1)}, u32[]{:S(2)}, u32[]{:S(2)}) %collective-permute-start) | collective-permute-done | bytes 294944 | tf_op jit(solution)/shard_map/ppermute | solution.py:15
  98.0 0.4 fusion.2
  98.4 4.7 %collective-permute-start.1 = (f32[144,512]{1,0:T(8,128)S(1)}, f32[144,512]{1,0:T(8,128)S(1)}, u32[]{:S(2)}, u32[]{:S(2)}) collective-permute-start(f32[144,512]{1,0:T(8,128)S(1)} %fusion.2), channel_id=1, source_target_pairs={{0,2},{1,3},{2,0},{3,1},{4,6},{5,7},{6,4},{7,5},{8,10},{9,11},{10,... | collective-permute-start | bytes 884744 | tf_op jit(solution)/shard_map/ppermute | solution.py:15
  103.1 5.0 %collective-permute-done.1 = f32[144,512]{1,0:T(8,128)S(1)} collective-permute-done((f32[144,512]{1,0:T(8,128)S(1)}, f32[144,512]{1,0:T(8,128)S(1)}, u32[]{:S(2)}, u32[]{:S(2)}) %collective-permute-start.1) | collective-permute-done | bytes 294944 | tf_op jit(solution)/shard_map/ppermute | solution.py:15
  108.1 0.4 fusion
  108.5 6.4 %collective-permute-start.2 = (f32[144,512]{1,0:T(8,128)S(1)}, f32[144,512]{1,0:T(8,128)S(1)}, u32[]{:S(2)}, u32[]{:S(2)}) collective-permute-start(f32[144,512]{1,0:T(8,128)S(1)} %fusion), channel_id=1, source_target_pairs={{0,4},{1,5},{2,6},{3,7},{4,0},{5,1},{6,2},{7,3},{8,12},{9,13},{10,... | collective-permute-start | bytes 884744 | tf_op jit(solution)/shard_map/ppermute | solution.py:15
  114.9 12.9 %collective-permute-done.2 = f32[144,512]{1,0:T(8,128)S(1)} collective-permute-done((f32[144,512]{1,0:T(8,128)S(1)}, f32[144,512]{1,0:T(8,128)S(1)}, u32[]{:S(2)}, u32[]{:S(2)}) %collective-permute-start.2) | collective-permute-done | bytes 294944 | tf_op jit(solution)/shard_map/ppermute | solution.py:15
  127.9 0.1 broadcast_in_dim.35
  128.0 30.9 %all_to_all.42 = f32[4,144,512]{2,1,0:T(8,128)S(1)} all-to-all(f32[4,144,512]{2,1,0:T(8,128)S(1)} %broadcast_in_dim.35), channel_id=1, replica_groups=mesh['ylo'=4,'core'=2,'leaf'=64] {'ylo'}, dimensions={0} | all-to-all | bytes 2359296 | tf_op jit(solution)/shard_map/all_to_all | solution.py:61
  158.9 0.3 broadcast_in_dim.37
  159.2 7.2 %all_to_all.43 = f32[2,576,512]{2,1,0:T(8,128)S(1)} all-to-all(f32[2,576,512]{2,1,0:T(8,128)S(1)} %broadcast_in_dim.37), channel_id=1, replica_groups=mesh['ylo'=4,'core'=2,'leaf'=64] {'core'}, dimensions={0} | all-to-all | bytes 4718592 | tf_op jit(solution)/shard_map/all_to_all | solution.py:61
  166.5 1.4 copy.15
  (3 shorter events, 0.1 us)
Async XLA Ops:
  3.0 6.7 %copy-start.1 = (f32[1,1,128]{2,1,0:T(1,128)S(1)}, f32[1,1,128]{2,1,0:T(1,128)}, u32[]{:S(2)}) copy-start(f32[1,1,128]{2,1,0:T(1,128)} %param.8) | copy-start | bytes 1540
  4.1 6.3 %copy-start.2 = (s32[1,1,128]{2,1,0:T(1,128)S(1)}, s32[1,1,128]{2,1,0:T(1,128)}, u32[]{:S(2)}) copy-start(s32[1,1,128]{2,1,0:T(1,128)} %param.11) | copy-start | bytes 1540
  4.1 32.7 %all-to-all-start = ((f32[4,584,128]{2,1,0:T(8,128)}), f32[4,584,128]{2,1,0:T(8,128)S(1)}, u32[]{:S(2)}, u32[]{:S(2)}) async-start(f32[4,584,128]{2,1,0:T(8,128)} %broadcast_in_dim.15), calls=%async_computation | async-start | bytes 2392064 | tf_op jit(solution)/shard_map/all_to_all | solution.py:61
  57.7 30.9 %copy-start = (bf16[1,3,512,512]{3,2,1,0:T(8,128)(2,1)S(1)}, bf16[1,3,512,512]{3,2,1,0:T(8,128)(2,1)}, u32[]{:S(2)}) copy-start(bf16[1,3,512,512]{3,2,1,0:T(8,128)(2,1)} %param.13) | copy-start | bytes 4718596
  88.9 9.1 %collective-permute-start = (f32[144,512]{1,0:T(8,128)S(1)}, f32[144,512]{1,0:T(8,128)S(1)}, u32[]{:S(2)}, u32[]{:S(2)}) collective-permute-start(f32[144,512]{1,0:T(8,128)S(1)} %fusion.4), channel_id=1, source_target_pairs={{0,1},{1,0},{2,3},{3,2},{4,5},{5,4},{6,7},{7,6},{8,9},{9,8},{10,11... | collective-permute-start | bytes 884744 | tf_op jit(solution)/shard_map/ppermute | solution.py:15
  98.4 9.7 %collective-permute-start.1 = (f32[144,512]{1,0:T(8,128)S(1)}, f32[144,512]{1,0:T(8,128)S(1)}, u32[]{:S(2)}, u32[]{:S(2)}) collective-permute-start(f32[144,512]{1,0:T(8,128)S(1)} %fusion.2), channel_id=1, source_target_pairs={{0,2},{1,3},{2,0},{3,1},{4,6},{5,7},{6,4},{7,5},{8,10},{9,11},{10,... | collective-permute-start | bytes 884744 | tf_op jit(solution)/shard_map/ppermute | solution.py:15
  108.5 19.3 %collective-permute-start.2 = (f32[144,512]{1,0:T(8,128)S(1)}, f32[144,512]{1,0:T(8,128)S(1)}, u32[]{:S(2)}, u32[]{:S(2)}) collective-permute-start(f32[144,512]{1,0:T(8,128)S(1)} %fusion), channel_id=1, source_target_pairs={{0,4},{1,5},{2,6},{3,7},{4,0},{5,1},{6,2},{7,3},{8,12},{9,13},{10,... | collective-permute-start | bytes 884744 | tf_op jit(solution)/shard_map/ppermute | solution.py:15

commit v9 on v8

--- a/solution.py
+++ b/solution.py
@@ -50,10 +50,14 @@
     return jnp.dot(current, level_mat.astype(jnp.float32), precision=lax.Precision.HIGHEST)
 
 
+LEVEL_AXES = ("lx0", "lx1", "lyhi")
+
+
 def climb_rows(rows, level_mats):
     for tree_level in range(level_mats.shape[0]):
         projected = project(rows, level_mats[tree_level])
-        rows = projected + partner(projected, "leaf", tree_level)
+        pair = gather_blocks(projected, LEVEL_AXES[tree_level])
+        rows = pair[: projected.shape[0]] + pair[projected.shape[0] :]
     return rows
 
 
@@ -160,19 +164,21 @@
 
 def solution(mesh):
     blk = mesh.shape["blk"]
-    devices = mesh.devices.reshape(blk // 2, 2, mesh.shape["leaf"])
-    split_mesh = jax.sharding.Mesh(devices, ("ylo", "core", "leaf"))
+    leaf = mesh.shape["leaf"]
+    devices = mesh.devices.reshape(blk // 2, 2, leaf // 8, 2, 2, 2)
+    split_mesh = jax.sharding.Mesh(devices, ("ylo", "core", "lz") + LEVEL_AXES[::-1])
     blk_axes = ("ylo", "core")
+    leaf_axes = ("lz",) + LEVEL_AXES[::-1]
     in_specs = (
-        P(None, "leaf", blk_axes, None),
-        P("leaf", blk_axes, None),
-        P(None, "leaf", blk_axes, None),
-        P(None, "leaf", blk_axes, None),
-        P("leaf", blk_axes, None),
-        P("leaf", blk_axes, None, None),
-        P("leaf", None, None, None),
+        P(None, leaf_axes, blk_axes, None),
+        P(leaf_axes, blk_axes, None),
+        P(None, leaf_axes, blk_axes, None),
+        P(None, leaf_axes, blk_axes, None),
+        P(leaf_axes, blk_axes, None),
+        P(leaf_axes, blk_axes, None, None),
+        P(leaf_axes, None, None, None),
     )
-    out_specs = (P(None, "leaf", blk_axes, None), P("leaf", None, None, None))
+    out_specs = (P(None, leaf_axes, blk_axes, None), P(leaf_axes, None, None, None))
     return jax.shard_map(
         shards, mesh=split_mesh, in_specs=in_specs, out_specs=out_specs, check_vma=False
     )

time: 168 us -> 171 us (1.018)
  blocking collectives: 84.6 us -> 125 us
  waiting for transfers between devices: 49.5 us -> 25.7 us
  starting transfers between devices: 19.7 us -> 5.55 us
    all_to_all x5 -> x8, blocking collectives: 84.6 us -> 125 us  [exchange(): return lax.all_to_all(value, axis, 0, 0, tiled=True)]
    ppermute x3 -> x0, waiting for transfers between devices: 23.9 us -> none  [partner(): return lax.ppermute(value, axis, pairs)]
    ppermute x3 -> x0, starting transfers between devices: 14.2 us -> none  [partner(): return lax.ppermute(value, axis, pairs)]
  transfers between devices with their start and end apart: 4 -> 1, of which waited for: 4 -> 1; matrix products, arithmetic and copies ran while one was open for 1% -> 1% of each run, Pallas kernels for 0% -> 0%
where the time goes in v9:
time: 171 us
  blocking collectives  125 us (73%)
  waiting for transfers between devices  25.7 us (15%)
  starting transfers between devices  5.55 us (3%)
  local copies, waits for them, and re-layouts  5.46 us (3%)
  Pallas kernels  4.76 us (3%)
  other arithmetic  2.03 us (1%)
    all_to_all x8, blocking collectives, exchange(): return lax.all_to_all(value, axis, 0, 0, tiled=True)  125 us
    all_to_all x1, waiting for transfers between devices, exchange(): return lax.all_to_all(value, axis, 0, 0, tiled=True)  25.7 us
    all_to_all x1, starting transfers between devices, exchange(): return lax.all_to_all(value, axis, 0, 0, tiled=True)  5.55 us
    pallas_call x1, Pallas kernels, near_project(): pl.pallas_call(near_project_kernel, out_shape=(jax.ShapeDtypeStruct((prob...  4.76 us
  transfers between devices with their start and end apart: 1, of which 1 were waited for; matrix products, arithmetic and copies ran while one was open for 1% of the time, Pallas kernels for 0%

profile of v9, /device:TPU:1, one launch (start us, length us, event | category | flops | bytes accessed | tf_op | source)
XLA Modules:
  0.0 170.6 jit_solution(10867386355672086167)
XLA Ops:
  0.6 0.7 copy.13
  1.3 0.9 fusion.16
  2.3 0.7 pad_maximum_fusion
  3.0 0.0 copy-start.1
  3.0 1.1 broadcast_in_dim.21
  4.1 0.0 copy-start.2
  4.1 5.6 %all-to-all-start = ((f32[4,584,128]{2,1,0:T(8,128)}), f32[4,584,128]{2,1,0:T(8,128)S(1)}, u32[]{:S(2)}, u32[]{:S(2)}) async-start(f32[4,584,128]{2,1,0:T(8,128)} %broadcast_in_dim.21), calls=%async_computation | async-start | bytes 2392064 | tf_op jit(solution)/shard_map/all_to_all | solution.py:65
  9.6 0.0 copy-done.1
  9.6 0.7 copy.9.target_ref
  10.4 0.0 copy-done.2
  10.4 0.7 copy.10.order_ref
  11.1 25.7 %all-to-all-done = f32[4,584,128]{2,1,0:T(8,128)S(1)} async-done(((f32[4,584,128]{2,1,0:T(8,128)}), f32[4,584,128]{2,1,0:T(8,128)S(1)}, u32[]{:S(2)}, u32[]{:S(2)}) %all-to-all-start) | async-done | bytes 1196064 | tf_op jit(solution)/shard_map/all_to_all | solution.py:65
  36.8 0.2 broadcast_in_dim.23
  36.9 8.9 %all_to_all.57 = f32[2,2336,128]{2,1,0:T(8,128)} all-to-all(f32[2,2336,128]{2,1,0:T(8,128)S(1)} %broadcast_in_dim.23), channel_id=1, replica_groups=mesh['ylo'=4,'core'=2,'lz'=8,'lyhi'=2,'lx1'=2,'lx0'=2] {'core'}, dimensions={0} | all-to-all | bytes 4784128 | tf_op jit(solution)/shard_map/all_to_all | solution.py:65
  45.8 4.8 %shard_map.86 = (bf16[576,128]{1,0:T(8,128)(2,1)}, f32[1152,512]{1,0:T(8,128)}) custom-call(f32[128,8]{1,0:T(8,128)} %copy.9.target_ref, f32[8,584,128]{2,1,0:T(8,128)} %bitcast.37, bf16[576,128]{1,0:T(8,128)(2,1)} %bitcast.44, bf16[576,128]{1,0:T(8,128)(2,1)} %bitcast.43, s32[128,1]{1,0:T(8,128)} %copy.10.order_ref, bf16[128,512]{1,0:T(8,128)(2,1)} %bitcast.45), custom_call_target="tpu_custom_call" | custom-call | flops 339738624 | bytes 5324800 | tf_op jit(solution)/shard_map/pallas_call | solution.py:124
  50.6 6.8 %all_to_all.58 = f32[2,576,512]{2,1,0:T(8,128)S(1)} all-to-all(f32[2,576,512]{2,1,0:T(8,128)} %bitcast.42), channel_id=1, replica_groups=mesh['ylo'=4,'core'=2,'lz'=8,'lyhi'=2,'lx1'=2,'lx0'=2] {'core'}, dimensions={0} | all-to-all | bytes 4718592 | tf_op jit(solution)/shard_map/all_to_all | solution.py:65
  57.4 0.2 slice_add_fusion
  57.7 0.0 copy-start
  57.7 30.7 %all_to_all.59 = f32[4,144,512]{2,1,0:T(8,128)S(1)} all-to-all(f32[4,144,512]{2,1,0:T(8,128)S(1)} %bitcast.40), channel_id=1, replica_groups=mesh['ylo'=4,'core'=2,'lz'=8,'lyhi'=2,'lx1'=2,'lx0'=2] {'ylo'}, dimensions={0} | all-to-all | bytes 2359296 | tf_op jit(solution)/shard_map/all_to_all | solution.py:65
  88.4 0.1 reduce_sum.9
  88.5 0.0 copy-done
  88.5 0.4 fusion.4
  88.9 0.1 broadcast_in_dim.24
  89.0 9.7 %all_to_all.60 = f32[2,144,512]{2,1,0:T(8,128)S(1)} all-to-all(f32[2,144,512]{2,1,0:T(8,128)S(1)} %broadcast_in_dim.24), channel_id=1, replica_groups=mesh['ylo'=4,'core'=2,'lz'=8,'lyhi'=2,'lx1'=2,'lx0'=2] {'lx0'}, dimensions={0} | all-to-all | bytes 1179648 | tf_op jit(solution)/shard_map/all_to_all | solution.py:65
  98.7 0.4 fusion.2
  99.1 0.1 broadcast_in_dim.25
  99.2 11.7 %all_to_all.61 = f32[2,144,512]{2,1,0:T(8,128)S(1)} all-to-all(f32[2,144,512]{2,1,0:T(8,128)S(1)} %broadcast_in_dim.25), channel_id=1, replica_groups=mesh['ylo'=4,'core'=2,'lz'=8,'lyhi'=2,'lx1'=2,'lx0'=2] {'lx1'}, dimensions={0} | all-to-all | bytes 1179648 | tf_op jit(solution)/shard_map/all_to_all | solution.py:65
  110.8 0.4 fusion
  111.2 0.1 broadcast_in_dim.26
  111.3 19.2 %all_to_all.62 = f32[2,144,512]{2,1,0:T(8,128)S(1)} all-to-all(f32[2,144,512]{2,1,0:T(8,128)S(1)} %broadcast_in_dim.26), channel_id=1, replica_groups=mesh['ylo'=4,'core'=2,'lz'=8,'lyhi'=2,'lx1'=2,'lx0'=2] {'lyhi'}, dimensions={0} | all-to-all | bytes 1179648 | tf_op jit(solution)/shard_map/all_to_all | solution.py:65
  130.6 0.1 broadcast_in_dim.27
  130.7 30.3 %all_to_all.63 = f32[4,144,512]{2,1,0:T(8,128)S(1)} all-to-all(f32[4,144,512]{2,1,0:T(8,128)S(1)} %broadcast_in_dim.27), channel_id=1, replica_groups=mesh['ylo'=4,'core'=2,'lz'=8,'lyhi'=2,'lx1'=2,'lx0'=2] {'ylo'}, dimensions={0} | all-to-all | bytes 2359296 | tf_op jit(solution)/shard_map/all_to_all | solution.py:65
  161.0 0.3 broadcast_in_dim.58
  161.4 7.9 %all_to_all.64 = f32[2,576,512]{2,1,0:T(8,128)S(1)} all-to-all(f32[2,576,512]{2,1,0:T(8,128)S(1)} %broadcast_in_dim.58), channel_id=1, replica_groups=mesh['ylo'=4,'core'=2,'lz'=8,'lyhi'=2,'lx1'=2,'lx0'=2] {'core'}, dimensions={0} | all-to-all | bytes 4718592 | tf_op jit(solution)/shard_map/all_to_all | solution.py:65
  169.2 1.4 copy.15
  (3 shorter events, 0.1 us)
Async XLA Ops:
  3.0 6.7 %copy-start.1 = (f32[1,1,128]{2,1,0:T(1,128)S(1)}, f32[1,1,128]{2,1,0:T(1,128)}, u32[]{:S(2)}) copy-start(f32[1,1,128]{2,1,0:T(1,128)} %param.8) | copy-start | bytes 1540
  4.1 6.3 %copy-start.2 = (s32[1,1,128]{2,1,0:T(1,128)S(1)}, s32[1,1,128]{2,1,0:T(1,128)}, u32[]{:S(2)}) copy-start(s32[1,1,128]{2,1,0:T(1,128)} %param.11) | copy-start | bytes 1540
  4.1 32.7 %all-to-all-start = ((f32[4,584,128]{2,1,0:T(8,128)}), f32[4,584,128]{2,1,0:T(8,128)S(1)}, u32[]{:S(2)}, u32[]{:S(2)}) async-start(f32[4,584,128]{2,1,0:T(8,128)} %broadcast_in_dim.21), calls=%async_computation | async-start | bytes 2392064 | tf_op jit(solution)/shard_map/all_to_all | solution.py:65
  57.7 30.9 %copy-start = (bf16[1,3,512,512]{3,2,1,0:T(8,128)(2,1)S(1)}, bf16[1,3,512,512]{3,2,1,0:T(8,128)(2,1)}, u32[]{:S(2)}) copy-start(bf16[1,3,512,512]{3,2,1,0:T(8,128)(2,1)} %param.13) | copy-start | bytes 4718596

commit v10 on v9

--- a/solution.py
+++ b/solution.py
@@ -53,11 +53,25 @@
 LEVEL_AXES = ("lx0", "lx1", "lyhi")
 
 
+def mirrored(chunks):
+    return jnp.where(lax.axis_index("lyhi") == 1, chunks[::-1], chunks)
+
+
 def climb_rows(rows, level_mats):
-    for tree_level in range(level_mats.shape[0]):
+    level_count = level_mats.shape[0]
+    for tree_level in range(level_count):
         projected = project(rows, level_mats[tree_level])
-        pair = gather_blocks(projected, LEVEL_AXES[tree_level])
-        rows = pair[: projected.shape[0]] + pair[projected.shape[0] :]
+        if tree_level < level_count - 1:
+            other = lax.ppermute(projected, LEVEL_AXES[tree_level], [(0, 1), (1, 0)])
+        else:
+            count = lax.axis_size("ylo")
+            pairs = [
+                (chip * 2 + half, (count - 1 - chip) * 2 + 1 - half)
+                for chip in range(count)
+                for half in range(2)
+            ]
+            other = lax.ppermute(projected, ("ylo", "lyhi"), pairs)
+        rows = projected + other
     return rows
 
 
@@ -74,13 +88,15 @@
 def scatter_rows(value):
     width = value.shape[1]
     halves = exchange(value, "core").reshape(2, -1, width)
-    summed = halves[0] + halves[1]
     count = lax.axis_size("ylo")
-    return exchange(summed, "ylo").reshape(count, -1, width).sum(axis=0)
+    summed = mirrored((halves[0] + halves[1]).reshape(count, -1, width))
+    return exchange(summed.reshape(-1, width), "ylo").reshape(count, -1, width).sum(axis=0)
 
 
 def gather_rows(rows):
-    return gather_blocks(gather_blocks(rows, "ylo"), "core")
+    count = lax.axis_size("ylo")
+    chips = gather_blocks(rows, "ylo").reshape((count,) + rows.shape)
+    return gather_blocks(mirrored(chips).reshape(-1, rows.shape[1]), "core")
 
 
 def near_project_kernel(target_ref, source_ref, sketch_ref, probe_ref, order_ref, basis_ref, off_ref, parts_ref):

time: 171 us -> 166 us (0.971)
  blocking collectives: 125 us -> 84.2 us
  waiting for transfers between devices: 25.7 us -> 48.6 us
  starting transfers between devices: 5.55 us -> 18.6 us
    all_to_all x8 -> x5, blocking collectives: 125 us -> 84.2 us  [exchange(): return lax.all_to_all(value, axis, 0, 0, tiled=True)]
    ppermute x0 -> x3, waiting for transfers between devices: none -> 23 us  [the longest x1 12 us: climb_rows(): other = lax.ppermute(projected, ('ylo', 'lyhi'), pairs)]
    ppermute x0 -> x3, starting transfers between devices: none -> 13 us  [the longest x2 7.75 us: climb_rows(): other = lax.ppermute(projected, LEVEL_AXES[tree_level], [(0, 1), (1, 0)])]
  transfers between devices with their start and end apart: 1 -> 4, of which waited for: 1 -> 4; matrix products, arithmetic and copies ran while one was open for 1% -> 1% of each run, Pallas kernels for 0% -> 0%
where the time goes in v10:
time: 166 us
  blocking collectives  84.2 us (51%)
  waiting for transfers between devices  48.6 us (29%)
  starting transfers between devices  18.6 us (11%)
  local copies, waits for them, and re-layouts  5.28 us (3%)
  Pallas kernels  4.76 us (3%)
  other arithmetic  2.25 us (1%)
    all_to_all x5, blocking collectives, exchange(): return lax.all_to_all(value, axis, 0, 0, tiled=True)  84.2 us
    all_to_all x1, waiting for transfers between devices, exchange(): return lax.all_to_all(value, axis, 0, 0, tiled=True)  25.7 us
    ppermute x1, waiting for transfers between devices, climb_rows(): other = lax.ppermute(projected, ('ylo', 'lyhi'), pairs)  12 us
    ppermute x2, waiting for transfers between devices, climb_rows(): other = lax.ppermute(projected, LEVEL_AXES[tree_level], [(0, 1), (1, 0)])  11 us
    ppermute x2, starting transfers between devices, climb_rows(): other = lax.ppermute(projected, LEVEL_AXES[tree_level], [(0, 1), (1, 0)])  7.75 us
    all_to_all x1, starting transfers between devices, exchange(): return lax.all_to_all(value, axis, 0, 0, tiled=True)  5.55 us
    ppermute x1, starting transfers between devices, climb_rows(): other = lax.ppermute(projected, ('ylo', 'lyhi'), pairs)  5.26 us
    pallas_call x1, Pallas kernels, near_project(): pl.pallas_call(near_project_kernel, out_shape=(jax.ShapeDtypeStruct((prob...  4.76 us
  transfers between devices with their start and end apart: 4, of which 4 were waited for; matrix products, arithmetic and copies ran while one was open for 1% of the time, Pallas kernels for 0%

profile of v10, /device:TPU:1, one launch (start us, length us, event | category | flops | bytes accessed | tf_op | source)
XLA Modules:
  0.0 165.6 jit_solution(9330953676100405274)
XLA Ops:
  0.6 0.7 copy.13
  1.3 0.9 fusion.11
  2.3 0.7 pad_maximum_fusion
  3.0 1.1 broadcast_in_dim.15
  4.1 0.0 copy-start.1
  4.1 0.0 copy-start.2
  4.1 5.6 %all-to-all-start = ((f32[4,584,128]{2,1,0:T(8,128)}), f32[4,584,128]{2,1,0:T(8,128)S(1)}, u32[]{:S(2)}, u32[]{:S(2)}) async-start(f32[4,584,128]{2,1,0:T(8,128)} %broadcast_in_dim.15), calls=%async_computation | async-start | bytes 2392064 | tf_op jit(solution)/shard_map/all_to_all | solution.py:79
  9.6 0.0 copy-done.1
  9.6 0.7 copy.9.target_ref
  10.4 0.0 copy-done.2
  10.4 0.7 copy.10.order_ref
  11.1 25.7 %all-to-all-done = f32[4,584,128]{2,1,0:T(8,128)S(1)} async-done(((f32[4,584,128]{2,1,0:T(8,128)}), f32[4,584,128]{2,1,0:T(8,128)S(1)}, u32[]{:S(2)}, u32[]{:S(2)}) %all-to-all-start) | async-done | bytes 1196064 | tf_op jit(solution)/shard_map/all_to_all | solution.py:79
  36.8 0.2 broadcast_in_dim.33
  36.9 8.9 %all_to_all.39 = f32[2,2336,128]{2,1,0:T(8,128)} all-to-all(f32[2,2336,128]{2,1,0:T(8,128)S(1)} %broadcast_in_dim.33), channel_id=1, replica_groups=mesh['ylo'=4,'core'=2,'lz'=8,'lyhi'=2,'lx1'=2,'lx0'=2] {'core'}, dimensions={0} | all-to-all | bytes 4784128 | tf_op jit(solution)/shard_map/all_to_all | solution.py:79
  45.8 4.8 %shard_map.86 = (bf16[576,128]{1,0:T(8,128)(2,1)}, f32[1152,512]{1,0:T(8,128)}) custom-call(f32[128,8]{1,0:T(8,128)} %copy.9.target_ref, f32[8,584,128]{2,1,0:T(8,128)} %bitcast.29, bf16[576,128]{1,0:T(8,128)(2,1)} %bitcast.36, bf16[576,128]{1,0:T(8,128)(2,1)} %bitcast.35, s32[128,1]{1,0:T(8,128)} %copy.10.order_ref, bf16[128,512]{1,0:T(8,128)(2,1)} %bitcast.37), custom_call_target="tpu_custom_call" | custom-call | flops 339738624 | bytes 5324800 | tf_op jit(solution)/shard_map/pallas_call | solution.py:140
  50.6 6.8 %all_to_all.40 = f32[2,576,512]{2,1,0:T(8,128)S(1)} all-to-all(f32[2,576,512]{2,1,0:T(8,128)} %bitcast.34), channel_id=1, replica_groups=mesh['ylo'=4,'core'=2,'lz'=8,'lyhi'=2,'lx1'=2,'lx0'=2] {'core'}, dimensions={0} | all-to-all | bytes 4718592 | tf_op jit(solution)/shard_map/all_to_all | solution.py:79
  57.4 0.2 slice_add_fusion
  57.7 0.1 reverse_select_fusion.1
  57.8 0.0 copy-start
  57.8 30.7 %all_to_all.41 = f32[4,144,512]{2,1,0:T(8,128)S(1)} all-to-all(f32[4,144,512]{2,1,0:T(8,128)S(1)} %reverse_select_fusion.1), channel_id=1, replica_groups=mesh['ylo'=4,'core'=2,'lz'=8,'lyhi'=2,'lx1'=2,'lx0'=2] {'ylo'}, dimensions={0} | all-to-all | bytes 2359296 | tf_op jit(solution)/shard_map/all_to_all | solution.py:79
  88.5 0.1 reduce_sum.9
  88.6 0.0 copy-done
  88.7 0.4 fusion.4
  89.1 3.1 %collective-permute-start = (f32[144,512]{1,0:T(8,128)S(1)}, f32[144,512]{1,0:T(8,128)S(1)}, u32[]{:S(2)}, u32[]{:S(2)}) collective-permute-start(f32[144,512]{1,0:T(8,128)S(1)} %fusion.4), channel_id=1, source_target_pairs={{0,1},{1,0},{2,3},{3,2},{4,5},{5,4},{6,7},{7,6},{8,9},{9,8},{10,11... | collective-permute-start | bytes 884744 | tf_op jit(solution)/shard_map/ppermute | solution.py:65
  92.2 6.0 %collective-permute-done = f32[144,512]{1,0:T(8,128)S(1)} collective-permute-done((f32[144,512]{1,0:T(8,128)S(1)}, f32[144,512]{1,0:T(8,128)S(1)}, u32[]{:S(2)}, u32[]{:S(2)}) %collective-permute-start) | collective-permute-done | bytes 294944 | tf_op jit(solution)/shard_map/ppermute | solution.py:65
  98.1 0.4 fusion.2
  98.6 4.6 %collective-permute-start.1 = (f32[144,512]{1,0:T(8,128)S(1)}, f32[144,512]{1,0:T(8,128)S(1)}, u32[]{:S(2)}, u32[]{:S(2)}) collective-permute-start(f32[144,512]{1,0:T(8,128)S(1)} %fusion.2), channel_id=1, source_target_pairs={{0,2},{2,0},{1,3},{3,1},{4,6},{6,4},{5,7},{7,5},{8,10},{10,8},{9,1... | collective-permute-start | bytes 884744 | tf_op jit(solution)/shard_map/ppermute | solution.py:65
  103.2 5.0 %collective-permute-done.1 = f32[144,512]{1,0:T(8,128)S(1)} collective-permute-done((f32[144,512]{1,0:T(8,128)S(1)}, f32[144,512]{1,0:T(8,128)S(1)}, u32[]{:S(2)}, u32[]{:S(2)}) %collective-permute-start.1) | collective-permute-done | bytes 294944 | tf_op jit(solution)/shard_map/ppermute | solution.py:65
  108.2 0.4 fusion
  108.6 5.3 %collective-permute-start.2 = (f32[144,512]{1,0:T(8,128)S(1)}, f32[144,512]{1,0:T(8,128)S(1)}, u32[]{:S(2)}, u32[]{:S(2)}) collective-permute-start(f32[144,512]{1,0:T(8,128)S(1)} %fusion), channel_id=1, source_target_pairs={{0,388},{4,384},{128,260},{132,256},{256,132},{260,128},{384,4},{3... | collective-permute-start | bytes 884744 | tf_op jit(solution)/shard_map/ppermute | solution.py:73
  113.9 12.0 %collective-permute-done.2 = f32[144,512]{1,0:T(8,128)S(1)} collective-permute-done((f32[144,512]{1,0:T(8,128)S(1)}, f32[144,512]{1,0:T(8,128)S(1)}, u32[]{:S(2)}, u32[]{:S(2)}) %collective-permute-start.2) | collective-permute-done | bytes 294944 | tf_op jit(solution)/shard_map/ppermute | solution.py:73
  125.9 0.1 broadcast_in_dim.34
  126.1 30.6 %all_to_all.42 = f32[4,144,512]{2,1,0:T(8,128)S(1)} all-to-all(f32[4,144,512]{2,1,0:T(8,128)S(1)} %broadcast_in_dim.34), channel_id=1, replica_groups=mesh['ylo'=4,'core'=2,'lz'=8,'lyhi'=2,'lx1'=2,'lx0'=2] {'ylo'}, dimensions={0} | all-to-all | bytes 2359296 | tf_op jit(solution)/shard_map/all_to_all | solution.py:79
  156.6 0.1 reverse_select_fusion
  156.8 0.3 broadcast_in_dim.36
  157.1 7.1 %all_to_all.43 = f32[2,576,512]{2,1,0:T(8,128)S(1)} all-to-all(f32[2,576,512]{2,1,0:T(8,128)S(1)} %broadcast_in_dim.36), channel_id=1, replica_groups=mesh['ylo'=4,'core'=2,'lz'=8,'lyhi'=2,'lx1'=2,'lx0'=2] {'core'}, dimensions={0} | all-to-all | bytes 4718592 | tf_op jit(solution)/shard_map/all_to_all | solution.py:79
  164.2 1.4 copy.15
  (3 shorter events, 0.1 us)
Async XLA Ops:
  4.1 5.6 %copy-start.1 = (f32[1,1,128]{2,1,0:T(1,128)S(1)}, f32[1,1,128]{2,1,0:T(1,128)}, u32[]{:S(2)}) copy-start(f32[1,1,128]{2,1,0:T(1,128)} %param.8) | copy-start | bytes 1540
  4.1 6.3 %copy-start.2 = (s32[1,1,128]{2,1,0:T(1,128)S(1)}, s32[1,1,128]{2,1,0:T(1,128)}, u32[]{:S(2)}) copy-start(s32[1,1,128]{2,1,0:T(1,128)} %param.11) | copy-start | bytes 1540
  4.1 32.7 %all-to-all-start = ((f32[4,584,128]{2,1,0:T(8,128)}), f32[4,584,128]{2,1,0:T(8,128)S(1)}, u32[]{:S(2)}, u32[]{:S(2)}) async-start(f32[4,584,128]{2,1,0:T(8,128)} %broadcast_in_dim.15), calls=%async_computation | async-start | bytes 2392064 | tf_op jit(solution)/shard_map/all_to_all | solution.py:79
  57.8 30.9 %copy-start = (bf16[1,3,512,512]{3,2,1,0:T(8,128)(2,1)S(1)}, bf16[1,3,512,512]{3,2,1,0:T(8,128)(2,1)}, u32[]{:S(2)}) copy-start(bf16[1,3,512,512]{3,2,1,0:T(8,128)(2,1)} %param.13) | copy-start | bytes 4718596
  89.1 9.1 %collective-permute-start = (f32[144,512]{1,0:T(8,128)S(1)}, f32[144,512]{1,0:T(8,128)S(1)}, u32[]{:S(2)}, u32[]{:S(2)}) collective-permute-start(f32[144,512]{1,0:T(8,128)S(1)} %fusion.4), channel_id=1, source_target_pairs={{0,1},{1,0},{2,3},{3,2},{4,5},{5,4},{6,7},{7,6},{8,9},{9,8},{10,11... | collective-permute-start | bytes 884744 | tf_op jit(solution)/shard_map/ppermute | solution.py:65
  98.6 9.7 %collective-permute-start.1 = (f32[144,512]{1,0:T(8,128)S(1)}, f32[144,512]{1,0:T(8,128)S(1)}, u32[]{:S(2)}, u32[]{:S(2)}) collective-permute-start(f32[144,512]{1,0:T(8,128)S(1)} %fusion.2), channel_id=1, source_target_pairs={{0,2},{2,0},{1,3},{3,1},{4,6},{6,4},{5,7},{7,5},{8,10},{10,8},{9,1... | collective-permute-start | bytes 884744 | tf_op jit(solution)/shard_map/ppermute | solution.py:65
  108.6 17.2 %collective-permute-start.2 = (f32[144,512]{1,0:T(8,128)S(1)}, f32[144,512]{1,0:T(8,128)S(1)}, u32[]{:S(2)}, u32[]{:S(2)}) collective-permute-start(f32[144,512]{1,0:T(8,128)S(1)} %fusion), channel_id=1, source_target_pairs={{0,388},{4,384},{128,260},{132,256},{256,132},{260,128},{384,4},{3... | collective-permute-start | bytes 884744 | tf_op jit(solution)/shard_map/ppermute | solution.py:73

commit v11 on v10

--- a/solution.py
+++ b/solution.py
@@ -1,3 +1,4 @@
+import functools
 import math
 
 import jax
@@ -99,54 +100,81 @@
     return gather_blocks(mirrored(chips).reshape(-1, rows.shape[1]), "core")
 
 
-def near_project_kernel(target_ref, source_ref, sketch_ref, probe_ref, order_ref, basis_ref, off_ref, parts_ref):
-    block_count = source_ref.shape[0]
-    probe_count, panels = sketch_ref.shape
-    geometry_rows = source_ref.shape[1] - probe_count
-    target = target_ref[...]
-    near = jnp.zeros((probe_count, panels), jnp.float32)
-    for block in range(block_count):
-        geometry = source_ref[block, 0:geometry_rows, :]
-        distance = jnp.zeros((panels, panels), jnp.float32)
-        for component in range(3):
-            gap = target[:, component : component + 1] - geometry[component : component + 1, :]
-            distance = distance + gap * gap
-        soft = distance + 0.5 * (target[:, 3:4] + geometry[3:4, :])
-        tile = (inv_four_pi * lax.rsqrt(soft)).astype(jnp.bfloat16)
-        scaled = source_ref[block, geometry_rows:, :].astype(jnp.bfloat16)
-        near = near + lax.dot_general(
-            scaled, tile, (((1,), (1,)), ((), ())), preferred_element_type=jnp.float32
-        )
-    off = (sketch_ref[...].astype(jnp.float32) - near).astype(jnp.bfloat16)
-    off_ref[...] = off
-    lanes = lax.broadcasted_iota(jnp.int32, (panels, panels), 1)
-    onehot = (order_ref[...] == lanes).astype(jnp.bfloat16)
-    basis = basis_ref[...]
-    for index, values in enumerate((off, probe_ref[...])):
-        ordered = lax.dot_general(
-            values, onehot, (((1,), (1,)), ((), ())), preferred_element_type=jnp.float32
-        ).astype(jnp.bfloat16)
-        parts_ref[index * probe_count : (index + 1) * probe_count, :] = jnp.dot(
-            ordered, basis, preferred_element_type=jnp.float32
-        )
-
-
-def near_project(target, source, sketch, probe, order, basis):
-    probe_count, panels = sketch.shape
+def chip_kernel(layout, recv_ref, own_ref, full_ref, probe_ref, basis_ref, off_ref, parts_ref):
+    blocks_per_core, block_rows, geometry_rows, half = layout
+    panels = own_ref.shape[0]
+    width = basis_ref.shape[1]
+    core = lax.axis_index("core")
+    other = 1 - core
+    base = blocks_per_core * block_rows
+    row0 = pl.multiple_of(core * half, 8)
+    lanes = lax.broadcasted_iota(jnp.int32, (panels, panels), 1).astype(jnp.float32)
+    targets = (own_ref[...], recv_ref[other, base : base + panels, :])
+    sketch_rows = (
+        full_ref[pl.ds(row0, half), :].astype(jnp.float32),
+        recv_ref[other, base + panels : base + panels + half, :],
+    )
+    probe_rows = (
+        probe_ref[pl.ds(row0, half), :],
+        recv_ref[other, base + panels + half : base + panels + 2 * half, :].astype(jnp.bfloat16),
+    )
+    basis_start = base + panels + 2 * half
+    for block in range(2):
+        target = targets[block]
+        near = jnp.zeros((half, panels), jnp.float32)
+        for source_core in range(2):
+            for chip in range(blocks_per_core):
+                start = chip * block_rows
+                geometry = recv_ref[source_core, start : start + geometry_rows, :]
+                distance = jnp.zeros((panels, panels), jnp.float32)
+                for component in range(3):
+                    gap = target[:, component : component + 1] - geometry[component : component + 1, :]
+                    distance = distance + gap * gap
+                soft = distance + 0.5 * (target[:, 3:4] + geometry[3:4, :])
+                tile = (inv_four_pi * lax.rsqrt(soft)).astype(jnp.bfloat16)
+                first = pl.multiple_of(start + geometry_rows + row0, 8)
+                scaled = recv_ref[source_core, pl.ds(first, half), :].astype(jnp.bfloat16)
+                near = near + lax.dot_general(
+                    scaled, tile, (((1,), (1,)), ((), ())), preferred_element_type=jnp.float32
+                )
+        off = (sketch_rows[block] - near).astype(jnp.bfloat16)
+        off_ref[block] = off
+        onehot = (target[:, 4:5] == lanes).astype(jnp.bfloat16)
+        for kind, values in enumerate((off, probe_rows[block])):
+            ordered = lax.dot_general(
+                values, onehot, (((1,), (1,)), ((), ())), preferred_element_type=jnp.float32
+            ).astype(jnp.bfloat16)
+            rows = slice(kind * half, (kind + 1) * half)
+            if block == 0:
+                parts_ref[rows, :] = jnp.dot(
+                    ordered, basis_ref[...], preferred_element_type=jnp.float32
+                )
+            else:
+                for quarter in range(width // panels):
+                    first = basis_start + quarter * panels
+                    basis = recv_ref[other, first : first + panels, :].astype(jnp.bfloat16)
+                    columns = slice(quarter * panels, (quarter + 1) * panels)
+                    parts_ref[rows, columns] = parts_ref[rows, columns] + jnp.dot(
+                        ordered, basis, preferred_element_type=jnp.float32
+                    )
+
+
+def chip_project(layout, recv, own, full, probe, basis):
+    probe_count, panels = full.shape
+    half = probe_count // 2
     width = basis.shape[1]
-    blocks = source.shape[0]
-    flops = 2 * probe_count * panels * (blocks * panels + 2 * panels + 2 * width)
-    bytes_accessed = 4 * source.size + 2 * (3 * sketch.size + basis.size) + 8 * probe_count * width
+    flops = 2 * half * panels * (2 * 2 * layout[0] * panels + 4 * panels + 4 * width)
+    bytes_accessed = 4 * recv.size + 2 * (2 * full.size + basis.size) + 4 * probe_count * width
     return pl.pallas_call(
-        near_project_kernel,
+        functools.partial(chip_kernel, layout),
         out_shape=(
-            jax.ShapeDtypeStruct((probe_count, panels), jnp.bfloat16),
-            jax.ShapeDtypeStruct((2 * probe_count, width), jnp.float32),
+            jax.ShapeDtypeStruct((2, half, panels), jnp.bfloat16),
+            jax.ShapeDtypeStruct((2 * half, width), jnp.float32),
         ),
         cost_estimate=pl.CostEstimate(
-            flops=flops, transcendentals=blocks * panels * panels, bytes_accessed=bytes_accessed
+            flops=flops, transcendentals=4 * layout[0] * panels * panels, bytes_accessed=bytes_accessed
         ),
-    )(target, source, sketch, probe, order, basis)
+    )(recv, own, full, probe, basis)
 
 
 def shards(positions, panel_areas, probe_cols, full_sketch, tree_order, leaf_basis, transfer_mats):
@@ -154,27 +182,68 @@
     probe_count = probe_cols.shape[0]
     basis_width = leaf_basis.shape[3]
     level_count = transfer_mats.shape[1]
+    half = probe_count // 2
     coords = positions.reshape(3, panels)
     area_row = panel_areas.reshape(1, panels)
+    order_row = tree_order.reshape(1, panels).astype(jnp.float32)
     probe_flat = probe_cols.reshape(probe_count, panels)
+    full_flat = full_sketch.reshape(probe_count, panels)
     scaled = (area_row * probe_flat.astype(jnp.float32)).astype(jnp.bfloat16)
     basis_flat = leaf_basis.reshape(panels, basis_width)
     level_mats = transfer_mats.reshape(level_count, basis_width, basis_width)
-    geometry = jnp.concatenate([coords, area_row, jnp.zeros((4, panels), jnp.float32)], axis=0)
+    geometry = jnp.concatenate(
+        [coords, area_row, order_row, jnp.zeros((3, panels), jnp.float32)], axis=0
+    )
     outgoing = jnp.concatenate([geometry, scaled.astype(jnp.float32)], axis=0)
-    blocks = gather_blocks(gather_blocks(outgoing, "ylo"), "core")
-    source = blocks.reshape(-1, outgoing.shape[0], panels)
-    offdiag, stacked = near_project(
-        jnp.transpose(geometry),
-        source,
-        full_sketch.reshape(probe_count, panels),
-        probe_flat,
-        tree_order.reshape(panels, 1),
-        basis_flat,
-    )
-    mine = scatter_rows(stacked)
+    chip_blocks = gather_blocks(outgoing, "ylo")
+    own = jnp.transpose(geometry)
+    own_padded = jnp.pad(own, ((0, 0), (0, panels - own.shape[1])))
+    basis_view = jnp.transpose(
+        basis_flat.astype(jnp.float32).reshape(panels, basis_width // panels, panels), (1, 0, 2)
+    ).reshape(-1, panels)
+    full_wide = full_flat.astype(jnp.float32)
+    probe_wide = probe_flat.astype(jnp.float32)
+    chunks = [
+        jnp.concatenate(
+            [
+                chip_blocks,
+                own_padded,
+                full_wide[index * half : (index + 1) * half],
+                probe_wide[index * half : (index + 1) * half],
+                basis_view,
+            ],
+            axis=0,
+        )
+        for index in range(2)
+    ]
+    recv = exchange(jnp.concatenate(chunks, axis=0), "core").reshape(2, -1, panels)
+    layout = (lax.axis_size("ylo"), outgoing.shape[0], geometry.shape[0], half)
+    off_pair, parts = chip_project(layout, recv, own, full_flat, probe_flat, basis_flat)
+    count = lax.axis_size("ylo")
+    summed = mirrored(parts.reshape(count, -1, basis_width))
+    mine = exchange(summed.reshape(-1, basis_width), "ylo").reshape(count, -1, basis_width).sum(axis=0)
     top = climb_rows(mine, level_mats)
-    nested = gather_rows(top).reshape(2, probe_count, basis_width)[None]
+    chips = gather_blocks(top, "ylo").reshape((count,) + top.shape)
+    half_rows = mirrored(chips).reshape(-1, basis_width)
+    sent_off = off_pair[1].astype(jnp.float32).reshape(-1, basis_width)
+    back = gather_blocks(jnp.concatenate([half_rows, sent_off], axis=0), "core")
+    back = back.reshape(2, -1, basis_width)
+    nested = jnp.stack(
+        [
+            jnp.concatenate([back[0, :half], back[1, :half]], axis=0),
+            jnp.concatenate([back[0, half : 2 * half], back[1, half : 2 * half]], axis=0),
+        ],
+        axis=0,
+    )[None]
+    core = lax.axis_index("core")
+    received = jnp.where(core == 0, back[1, 2 * half :], back[0, 2 * half :])
+    theirs = received.reshape(half, panels).astype(jnp.bfloat16)
+    mine_off = off_pair[0]
+    offdiag = jnp.where(
+        core == 0,
+        jnp.concatenate([mine_off, theirs], axis=0),
+        jnp.concatenate([theirs, mine_off], axis=0),
+    )
     return (offdiag.reshape(probe_count, 1, 1, panels), nested)
 
 

time: 166 us -> 167 us (level)
  blocking collectives: 84.2 us -> 47.7 us
  waiting for transfers between devices: 48.6 us -> 77.7 us
  other arithmetic: 2.25 us -> 6.49 us
  starting transfers between devices: 18.6 us -> 22.1 us
    all_to_all x5 -> x3, blocking collectives: 84.2 us -> 47.7 us  [exchange(): return lax.all_to_all(value, axis, 0, 0, tiled=True)]
    all_to_all x1 -> x2, waiting for transfers between devices: 25.7 us -> 54.7 us  [exchange(): return lax.all_to_all(value, axis, 0, 0, tiled=True)]
    all_to_all x1 -> x2, starting transfers between devices: 5.55 us -> 8.95 us  [exchange(): return lax.all_to_all(value, axis, 0, 0, tiled=True)]
    select_n x2, other arithmetic: 0.22 us -> 2.01 us  [mirrored(): return jnp.where(lax.axis_index('lyhi') == 1, chunks[::-1], chunks)]
  transfers between devices with their start and end apart: 4 -> 5, of which waited for: 4 -> 5; matrix products, arithmetic and copies ran while one was open for 1% -> 0% of each run, Pallas kernels for 0% -> 0%
where the time goes in v11:
time: 167 us; the launch traced here: 166 us
  waiting for transfers between devices  77.7 us (47%)
  blocking collectives  47.7 us (29%)
  starting transfers between devices  22.1 us (13%)
  other arithmetic  6.49 us (4%)
  Pallas kernels  5.22 us (3%)
  local copies, waits for them, and re-layouts  4.87 us (3%)
    all_to_all x2, waiting for transfers between devices, exchange(): return lax.all_to_all(value, axis, 0, 0, tiled=True)  54.7 us
    all_to_all x3, blocking collectives, exchange(): return lax.all_to_all(value, axis, 0, 0, tiled=True)  47.7 us
    ppermute x1, waiting for transfers between devices, climb_rows(): other = lax.ppermute(projected, ('ylo', 'lyhi'), pairs)  12 us
    ppermute x2, waiting for transfers between devices, climb_rows(): other = lax.ppermute(projected, LEVEL_AXES[tree_level], [(0, 1), (1, 0)])  11 us
    all_to_all x2, starting transfers between devices, exchange(): return lax.all_to_all(value, axis, 0, 0, tiled=True)  8.95 us
    ppermute x2, starting transfers between devices, climb_rows(): other = lax.ppermute(projected, LEVEL_AXES[tree_level], [(0, 1), (1, 0)])  7.77 us
    ppermute x1, starting transfers between devices, climb_rows(): other = lax.ppermute(projected, ('ylo', 'lyhi'), pairs)  5.39 us
    pallas_call x1, Pallas kernels, chip_project(): pl.pallas_call(functools.partial(chip_kernel, layout), out_shape=(jax.Sha...  5.22 us
  transfers between devices with their start and end apart: 5, of which 5 were waited for; matrix products, arithmetic and copies ran while one was open for 0% of the time, Pallas kernels for 0%

profile of v11, /device:TPU:1, one launch (start us, length us, event | category | flops | bytes accessed | tf_op | source)
XLA Modules:
  0.0 166.2 jit_solution(17876139205435745835)
XLA Ops:
  0.6 0.7 copy.16
  1.3 0.7 convert_bitcast_fusion
  2.0 0.0 copy-start.6
  2.0 1.0 fusion.11
  2.9 0.0 copy-start.4
  3.0 0.8 concatenate.43
  3.8 0.0 copy-start.1
  3.8 0.0 copy-start.3
  3.8 1.1 broadcast_in_dim.11
  4.9 5.4 %all-to-all-start = ((f32[4,584,128]{2,1,0:T(8,128)}), f32[4,584,128]{2,1,0:T(8,128)S(1)}, u32[]{:S(2)}, u32[]{:S(2)}) async-start(f32[4,584,128]{2,1,0:T(8,128)} %broadcast_in_dim.11), calls=%async_computation | async-start | bytes 2392064 | tf_op jit(solution)/shard_map/all_to_all | solution.py:80
  10.3 0.0 copy-done.6
  10.3 0.1 copy.14.own_ref
  10.4 0.0 copy-done.4
  10.4 0.0 copy-start.2
  10.4 0.1 reshape.176
  10.6 0.0 copy-done.1
  10.6 0.0 copy-done.3
  10.6 26.8 %all-to-all-done = f32[4,584,128]{2,1,0:T(8,128)S(1)} async-done(((f32[4,584,128]{2,1,0:T(8,128)}), f32[4,584,128]{2,1,0:T(8,128)S(1)}, u32[]{:S(2)}, u32[]{:S(2)}) %all-to-all-start) | async-done | bytes 1196064 | tf_op jit(solution)/shard_map/all_to_all | solution.py:80
  37.5 0.1 constant_dynamic-update-slice_fusion.3
  37.6 0.1 constant_dynamic-update-slice_fusion.1
  37.7 0.0 copy-done.2
  37.8 10.0 %all_to_all.36.recv_ref = f32[2,3552,128]{2,1,0:T(8,128)} all-to-all(f32[2,3552,128]{2,1,0:T(8,128)S(1)} %bitcast.51), channel_id=1, replica_groups=mesh['ylo'=4,'core'=2,'lz'=8,'lyhi'=2,'lx1'=2,'lx0'=2] {'core'}, dimensions={0} | all-to-all | bytes 7274496 | tf_op jit(solution)/shard_map/all_to_all | solution.py:80
  47.8 5.2 %shard_map.86 = (bf16[2,288,128]{2,1,0:T(8,128)(2,1)}, f32[576,512]{1,0:T(8,128)}) custom-call(f32[2,3552,128]{2,1,0:T(8,128)} %all_to_all.36.recv_ref, f32[128,8]{1,0:T(8,128)} %copy-done.2, bf16[576,128]{1,0:T(8,128)(2,1)} %bitcast.58, bf16[576,128]{1,0:T(8,128)(2,1)} %bitcast.55, bf16[128,512]{1,0:T(8,128)(2,1)} %bitcast.59), custom_call_target="tpu_custom_call" | custom-call | flops 339738624 | bytes 5242880 | tf_op jit(solution)/shard_map/pallas_call | solution.py:168
  53.1 1.9 %reverse_select_fusion.1 = f32[4,144,512]{2,1,0:T(8,128)S(1)} fusion(f32[4,144,512]{2,1,0:T(8,128)} %bitcast.56, pred[]{:T(512)S(6)} %eq.9), kind=kLoop, calls=%fused_computation.2 | loop fusion | flops 294912 | bytes 2359297 | tf_op jit(solution)/shard_map/jit(_where)/select_n | solution.py:58
  55.0 0.0 copy-start
  55.0 30.7 %all_to_all.37 = f32[4,144,512]{2,1,0:T(8,128)S(1)} all-to-all(f32[4,144,512]{2,1,0:T(8,128)S(1)} %reverse_select_fusion.1), channel_id=1, replica_groups=mesh['ylo'=4,'core'=2,'lz'=8,'lyhi'=2,'lx1'=2,'lx0'=2] {'ylo'}, dimensions={0} | all-to-all | bytes 2359296 | tf_op jit(solution)/shard_map/all_to_all | solution.py:80
  85.7 0.1 reduce_sum.9
  85.8 0.0 copy-done
  85.8 0.4 fusion.4
  86.2 3.1 %collective-permute-start = (f32[144,512]{1,0:T(8,128)S(1)}, f32[144,512]{1,0:T(8,128)S(1)}, u32[]{:S(2)}, u32[]{:S(2)}) collective-permute-start(f32[144,512]{1,0:T(8,128)S(1)} %fusion.4), channel_id=1, source_target_pairs={{0,1},{1,0},{2,3},{3,2},{4,5},{5,4},{6,7},{7,6},{8,9},{9,8},{10,11... | collective-permute-start | bytes 884744 | tf_op jit(solution)/shard_map/ppermute | solution.py:66
  89.4 6.0 %collective-permute-done = f32[144,512]{1,0:T(8,128)S(1)} collective-permute-done((f32[144,512]{1,0:T(8,128)S(1)}, f32[144,512]{1,0:T(8,128)S(1)}, u32[]{:S(2)}, u32[]{:S(2)}) %collective-permute-start) | collective-permute-done | bytes 294944 | tf_op jit(solution)/shard_map/ppermute | solution.py:66
  95.3 0.4 fusion.2
  95.7 4.7 %collective-permute-start.1 = (f32[144,512]{1,0:T(8,128)S(1)}, f32[144,512]{1,0:T(8,128)S(1)}, u32[]{:S(2)}, u32[]{:S(2)}) collective-permute-start(f32[144,512]{1,0:T(8,128)S(1)} %fusion.2), channel_id=1, source_target_pairs={{0,2},{2,0},{1,3},{3,1},{4,6},{6,4},{5,7},{7,5},{8,10},{10,8},{9,1... | collective-permute-start | bytes 884744 | tf_op jit(solution)/shard_map/ppermute | solution.py:66
  100.4 5.0 %collective-permute-done.1 = f32[144,512]{1,0:T(8,128)S(1)} collective-permute-done((f32[144,512]{1,0:T(8,128)S(1)}, f32[144,512]{1,0:T(8,128)S(1)}, u32[]{:S(2)}, u32[]{:S(2)}) %collective-permute-start.1) | collective-permute-done | bytes 294944 | tf_op jit(solution)/shard_map/ppermute | solution.py:66
  105.4 0.4 fusion
  105.8 0.0 copy-start.5
  105.8 5.4 %collective-permute-start.2 = (f32[144,512]{1,0:T(8,128)S(1)}, f32[144,512]{1,0:T(8,128)S(1)}, u32[]{:S(2)}, u32[]{:S(2)}) collective-permute-start(f32[144,512]{1,0:T(8,128)S(1)} %fusion), channel_id=1, source_target_pairs={{0,388},{4,384},{128,260},{132,256},{256,132},{260,128},{384,4},{3... | collective-permute-start | bytes 884744 | tf_op jit(solution)/shard_map/ppermute | solution.py:74
  111.2 12.0 %collective-permute-done.2 = f32[144,512]{1,0:T(8,128)S(1)} collective-permute-done((f32[144,512]{1,0:T(8,128)S(1)}, f32[144,512]{1,0:T(8,128)S(1)}, u32[]{:S(2)}, u32[]{:S(2)}) %collective-permute-start.2) | collective-permute-done | bytes 294944 | tf_op jit(solution)/shard_map/ppermute | solution.py:74
  123.2 1.2 broadcast_in_dim.12
  124.4 3.5 %all-to-all-start.3 = ((f32[4,144,512]{2,1,0:T(8,128)}), f32[4,144,512]{2,1,0:T(8,128)S(1)}, u32[]{:S(2)}, u32[]{:S(2)}) async-start(f32[4,144,512]{2,1,0:T(8,128)} %broadcast_in_dim.12), calls=%async_computation.3 | async-start | bytes 2359296 | tf_op jit(solution)/shard_map/all_to_all | solution.py:80
  127.9 0.0 copy-done.5
  128.0 27.9 %all-to-all-done.3 = f32[4,144,512]{2,1,0:T(8,128)S(1)} async-done(((f32[4,144,512]{2,1,0:T(8,128)}), f32[4,144,512]{2,1,0:T(8,128)S(1)}, u32[]{:S(2)}, u32[]{:S(2)}) %all-to-all-start.3) | async-done | bytes 1179680 | tf_op jit(solution)/shard_map/all_to_all | solution.py:80
  155.9 0.1 reverse_select_fusion
  156.0 0.1 pad_maximum_fusion
  156.1 0.3 broadcast_in_dim.13
  156.5 6.9 %all_to_all.38 = f32[2,648,512]{2,1,0:T(8,128)S(1)} all-to-all(f32[2,648,512]{2,1,0:T(8,128)S(1)} %broadcast_in_dim.13), channel_id=1, replica_groups=mesh['ylo'=4,'core'=2,'lz'=8,'lyhi'=2,'lx1'=2,'lx0'=2] {'core'}, dimensions={0} | all-to-all | bytes 5308416 | tf_op jit(solution)/shard_map/all_to_all | solution.py:80
  163.4 0.1 concatenate.48
  163.5 0.2 slice_bitcast_fusion.3
  163.7 0.2 maximum_bitcast_fusion.1
  163.9 1.6 maximum_bitcast_fusion
  165.5 0.7 maximum_select_fusion
  (17 shorter events, 0.3 us)
Async XLA Ops:
  2.0 8.3 %copy-start.6 = (f32[1,1,128]{2,1,0:T(1,128)S(1)}, f32[1,1,128]{2,1,0:T(1,128)}, u32[]{:S(2)}) copy-start(f32[1,1,128]{2,1,0:T(1,128)} %param.8) | copy-start | bytes 1540
  2.9 7.5 %copy-start.4 = (bf16[1,1,128,512]{3,2,1,0:T(8,128)(2,1)S(1)}, bf16[1,1,128,512]{3,2,1,0:T(8,128)(2,1)}, u32[]{:S(2)}) copy-start(bf16[1,1,128,512]{3,2,1,0:T(8,128)(2,1)} %param.12) | copy-start | bytes 393220
  3.8 6.8 %copy-start.1 = (bf16[576,1,1,128]{3,0,2,1:T(8,128)(2,1)S(1)}, bf16[576,1,1,128]{3,0,2,1:T(8,128)(2,1)}, u32[]{:S(2)}) copy-start(bf16[576,1,1,128]{3,0,2,1:T(8,128)(2,1)} %param.9) | copy-start | bytes 442372
  3.8 6.8 %copy-start.3 = (bf16[576,1,1,128]{3,0,2,1:T(8,128)(2,1)S(1)}, bf16[576,1,1,128]{3,0,2,1:T(8,128)(2,1)}, u32[]{:S(2)}) copy-start(bf16[576,1,1,128]{3,0,2,1:T(8,128)(2,1)} %param.10) | copy-start | bytes 442372
  4.9 32.6 %all-to-all-start = ((f32[4,584,128]{2,1,0:T(8,128)}), f32[4,584,128]{2,1,0:T(8,128)S(1)}, u32[]{:S(2)}, u32[]{:S(2)}) async-start(f32[4,584,128]{2,1,0:T(8,128)} %broadcast_in_dim.11), calls=%async_computation | async-start | bytes 2392064 | tf_op jit(solution)/shard_map/all_to_all | solution.py:80
  10.4 27.3 %copy-start.2 = (f32[128,8]{1,0:T(8,128)}, f32[128,8]{1,0:T(8,128)S(1)}, u32[]{:S(2)}) copy-start(f32[128,8]{1,0:T(8,128)S(1)} %copy.14.own_ref) | copy-start | bytes 12292
  55.0 30.9 %copy-start = (bf16[1,3,512,512]{3,2,1,0:T(8,128)(2,1)S(1)}, bf16[1,3,512,512]{3,2,1,0:T(8,128)(2,1)}, u32[]{:S(2)}) copy-start(bf16[1,3,512,512]{3,2,1,0:T(8,128)(2,1)} %param.13) | copy-start | bytes 4718596
  86.2 9.1 %collective-permute-start = (f32[144,512]{1,0:T(8,128)S(1)}, f32[144,512]{1,0:T(8,128)S(1)}, u32[]{:S(2)}, u32[]{:S(2)}) collective-permute-start(f32[144,512]{1,0:T(8,128)S(1)} %fusion.4), channel_id=1, source_target_pairs={{0,1},{1,0},{2,3},{3,2},{4,5},{5,4},{6,7},{7,6},{8,9},{9,8},{10,11... | collective-permute-start | bytes 884744 | tf_op jit(solution)/shard_map/ppermute | solution.py:66
  95.7 9.7 %collective-permute-start.1 = (f32[144,512]{1,0:T(8,128)S(1)}, f32[144,512]{1,0:T(8,128)S(1)}, u32[]{:S(2)}, u32[]{:S(2)}) collective-permute-start(f32[144,512]{1,0:T(8,128)S(1)} %fusion.2), channel_id=1, source_target_pairs={{0,2},{2,0},{1,3},{3,1},{4,6},{6,4},{5,7},{7,5},{8,10},{10,8},{9,1... | collective-permute-start | bytes 884744 | tf_op jit(solution)/shard_map/ppermute | solution.py:66
  105.8 22.1 %copy-start.5 = (bf16[2,288,128]{2,1,0:T(8,128)(2,1)S(1)}, bf16[2,288,128]{2,1,0:T(8,128)(2,1)}, u32[]{:S(2)}) copy-start(bf16[2,288,128]{2,1,0:T(8,128)(2,1)} %get-tuple-element.4) | copy-start | bytes 442372
  105.8 17.4 %collective-permute-start.2 = (f32[144,512]{1,0:T(8,128)S(1)}, f32[144,512]{1,0:T(8,128)S(1)}, u32[]{:S(2)}, u32[]{:S(2)}) collective-permute-start(f32[144,512]{1,0:T(8,128)S(1)} %fusion), channel_id=1, source_target_pairs={{0,388},{4,384},{128,260},{132,256},{256,132},{260,128},{384,4},{3... | collective-permute-start | bytes 884744 | tf_op jit(solution)/shard_map/ppermute | solution.py:74
  124.4 31.5 %all-to-all-start.3 = ((f32[4,144,512]{2,1,0:T(8,128)}), f32[4,144,512]{2,1,0:T(8,128)S(1)}, u32[]{:S(2)}, u32[]{:S(2)}) async-start(f32[4,144,512]{2,1,0:T(8,128)} %broadcast_in_dim.12), calls=%async_computation.3 | async-start | bytes 2359296 | tf_op jit(solution)/shard_map/all_to_all | solution.py:80

commit v12 on v11

--- a/solution.py
+++ b/solution.py
@@ -119,6 +119,9 @@
         recv_ref[other, base + panels + half : base + panels + 2 * half, :].astype(jnp.bfloat16),
     )
     basis_start = base + panels + 2 * half
+    mirror = lax.axis_index("lyhi")
+    pieces = blocks_per_core // 2
+    piece_rows = half // pieces
     for block in range(2):
         target = targets[block]
         near = jnp.zeros((half, panels), jnp.float32)
@@ -144,19 +147,23 @@
             ordered = lax.dot_general(
                 values, onehot, (((1,), (1,)), ((), ())), preferred_element_type=jnp.float32
             ).astype(jnp.bfloat16)
-            rows = slice(kind * half, (kind + 1) * half)
-            if block == 0:
-                parts_ref[rows, :] = jnp.dot(
-                    ordered, basis_ref[...], preferred_element_type=jnp.float32
-                )
-            else:
-                for quarter in range(width // panels):
-                    first = basis_start + quarter * panels
-                    basis = recv_ref[other, first : first + panels, :].astype(jnp.bfloat16)
-                    columns = slice(quarter * panels, (quarter + 1) * panels)
-                    parts_ref[rows, columns] = parts_ref[rows, columns] + jnp.dot(
-                        ordered, basis, preferred_element_type=jnp.float32
+            for sub in range(pieces):
+                piece = kind * pieces + sub
+                target_piece = piece + mirror * (2 * pieces - 1 - 2 * piece)
+                rows = pl.ds(pl.multiple_of(target_piece * piece_rows, 8), piece_rows)
+                values_rows = ordered[sub * piece_rows : (sub + 1) * piece_rows]
+                if block == 0:
+                    parts_ref[rows, :] = jnp.dot(
+                        values_rows, basis_ref[...], preferred_element_type=jnp.float32
                     )
+                else:
+                    for quarter in range(width // panels):
+                        first = basis_start + quarter * panels
+                        basis = recv_ref[other, first : first + panels, :].astype(jnp.bfloat16)
+                        columns = pl.ds(quarter * panels, panels)
+                        parts_ref[rows, columns] = parts_ref[rows, columns] + jnp.dot(
+                            values_rows, basis, preferred_element_type=jnp.float32
+                        )
 
 
 def chip_project(layout, recv, own, full, probe, basis):
@@ -220,8 +227,7 @@
     layout = (lax.axis_size("ylo"), outgoing.shape[0], geometry.shape[0], half)
     off_pair, parts = chip_project(layout, recv, own, full_flat, probe_flat, basis_flat)
     count = lax.axis_size("ylo")
-    summed = mirrored(parts.reshape(count, -1, basis_width))
-    mine = exchange(summed.reshape(-1, basis_width), "ylo").reshape(count, -1, basis_width).sum(axis=0)
+    mine = exchange(parts, "ylo").reshape(count, -1, basis_width).sum(axis=0)
     top = climb_rows(mine, level_mats)
     chips = gather_blocks(top, "ylo").reshape((count,) + top.shape)
     half_rows = mirrored(chips).reshape(-1, basis_width)

time: 167 us -> 166 us (level)
  other arithmetic: 6.49 us -> 4.59 us
    select_n x2 -> x1, other arithmetic: 2.01 us -> 0.11 us  [mirrored(): return jnp.where(lax.axis_index('lyhi') == 1, chunks[::-1], chunks)]
where the time goes in v12:
time: 166 us
  waiting for transfers between devices  78.1 us (47%)
  blocking collectives  48.9 us (29%)
  starting transfers between devices  21.8 us (13%)
  Pallas kernels  5.4 us (3%)
  local copies, waits for them, and re-layouts  4.86 us (3%)
  other arithmetic  4.59 us (3%)
    all_to_all x2, waiting for transfers between devices, exchange(): return lax.all_to_all(value, axis, 0, 0, tiled=True)  54.7 us
    all_to_all x3, blocking collectives, exchange(): return lax.all_to_all(value, axis, 0, 0, tiled=True)  48.9 us
    ppermute x1, waiting for transfers between devices, climb_rows(): other = lax.ppermute(projected, ('ylo', 'lyhi'), pairs)  12.1 us
    ppermute x2, waiting for transfers between devices, climb_rows(): other = lax.ppermute(projected, LEVEL_AXES[tree_level], [(0, 1), (1, 0)])  11.2 us
    all_to_all x2, starting transfers between devices, exchange(): return lax.all_to_all(value, axis, 0, 0, tiled=True)  8.95 us
    ppermute x2, starting transfers between devices, climb_rows(): other = lax.ppermute(projected, LEVEL_AXES[tree_level], [(0, 1), (1, 0)])  7.76 us
    pallas_call x1, Pallas kernels, chip_project(): pl.pallas_call(functools.partial(chip_kernel, layout), out_shape=(jax.Sha...  5.4 us
    ppermute x1, starting transfers between devices, climb_rows(): other = lax.ppermute(projected, ('ylo', 'lyhi'), pairs)  5.12 us
  transfers between devices with their start and end apart: 5, of which 5 were waited for; matrix products, arithmetic and copies ran while one was open for 0% of the time, Pallas kernels for 0%

profile of v12, /device:TPU:1, one launch (start us, length us, event | category | flops | bytes accessed | tf_op | source)
XLA Modules:
  0.0 165.8 jit_solution(3365449373494050470)
XLA Ops:
  0.6 0.7 copy.16
  1.3 0.7 convert_bitcast_fusion
  2.0 0.0 copy-start.6
  2.0 1.0 fusion.11
  2.9 0.0 copy-start.4
  3.0 0.8 concatenate.43
  3.8 0.0 copy-start.1
  3.8 0.0 copy-start.3
  3.8 1.1 broadcast_in_dim.11
  4.9 5.4 %all-to-all-start = ((f32[4,584,128]{2,1,0:T(8,128)}), f32[4,584,128]{2,1,0:T(8,128)S(1)}, u32[]{:S(2)}, u32[]{:S(2)}) async-start(f32[4,584,128]{2,1,0:T(8,128)} %broadcast_in_dim.11), calls=%async_computation | async-start | bytes 2392064 | tf_op jit(solution)/shard_map/all_to_all | solution.py:80
  10.3 0.0 copy-done.6
  10.3 0.1 copy.14.own_ref
  10.4 0.0 copy-done.4
  10.4 0.0 copy-start.2
  10.4 0.1 reshape.170
  10.6 0.0 copy-done.1
  10.6 0.0 copy-done.3
  10.6 26.8 %all-to-all-done = f32[4,584,128]{2,1,0:T(8,128)S(1)} async-done(((f32[4,584,128]{2,1,0:T(8,128)}), f32[4,584,128]{2,1,0:T(8,128)S(1)}, u32[]{:S(2)}, u32[]{:S(2)}) %all-to-all-start) | async-done | bytes 1196064 | tf_op jit(solution)/shard_map/all_to_all | solution.py:80
  37.5 0.1 constant_dynamic-update-slice_fusion.3
  37.6 0.1 constant_dynamic-update-slice_fusion.1
  37.7 0.0 copy-done.2
  37.8 10.0 %all_to_all.39.recv_ref = f32[2,3552,128]{2,1,0:T(8,128)} all-to-all(f32[2,3552,128]{2,1,0:T(8,128)S(1)} %bitcast.51), channel_id=1, replica_groups=mesh['ylo'=4,'core'=2,'lz'=8,'lyhi'=2,'lx1'=2,'lx0'=2] {'core'}, dimensions={0} | all-to-all | bytes 7274496 | tf_op jit(solution)/shard_map/all_to_all | solution.py:80
  47.8 5.4 %shard_map.86 = (bf16[2,288,128]{2,1,0:T(8,128)(2,1)}, f32[576,512]{1,0:T(8,128)}) custom-call(f32[2,3552,128]{2,1,0:T(8,128)} %all_to_all.39.recv_ref, f32[128,8]{1,0:T(8,128)} %copy-done.2, bf16[576,128]{1,0:T(8,128)(2,1)} %bitcast.58, bf16[576,128]{1,0:T(8,128)(2,1)} %bitcast.55, bf16[128,512]{1,0:T(8,128)(2,1)} %bitcast.59), custom_call_target="tpu_custom_call" | custom-call | flops 339738624 | bytes 5242880 | tf_op jit(solution)/shard_map/pallas_call | solution.py:175
  53.2 0.0 copy-start
  53.2 31.9 %all_to_all.40 = f32[4,144,512]{2,1,0:T(8,128)S(1)} all-to-all(f32[4,144,512]{2,1,0:T(8,128)} %bitcast.56), channel_id=1, replica_groups=mesh['ylo'=4,'core'=2,'lz'=8,'lyhi'=2,'lx1'=2,'lx0'=2] {'ylo'}, dimensions={0} | all-to-all | bytes 2359296 | tf_op jit(solution)/shard_map/all_to_all | solution.py:80
  85.1 0.1 reduce_sum.9
  85.3 0.0 copy-done
  85.3 0.4 fusion.4
  85.7 3.1 %collective-permute-start = (f32[144,512]{1,0:T(8,128)S(1)}, f32[144,512]{1,0:T(8,128)S(1)}, u32[]{:S(2)}, u32[]{:S(2)}) collective-permute-start(f32[144,512]{1,0:T(8,128)S(1)} %fusion.4), channel_id=1, source_target_pairs={{0,1},{1,0},{2,3},{3,2},{4,5},{5,4},{6,7},{7,6},{8,9},{9,8},{10,11... | collective-permute-start | bytes 884744 | tf_op jit(solution)/shard_map/ppermute | solution.py:66
  88.8 6.1 %collective-permute-done = f32[144,512]{1,0:T(8,128)S(1)} collective-permute-done((f32[144,512]{1,0:T(8,128)S(1)}, f32[144,512]{1,0:T(8,128)S(1)}, u32[]{:S(2)}, u32[]{:S(2)}) %collective-permute-start) | collective-permute-done | bytes 294944 | tf_op jit(solution)/shard_map/ppermute | solution.py:66
  94.9 0.4 fusion.2
  95.3 4.7 %collective-permute-start.1 = (f32[144,512]{1,0:T(8,128)S(1)}, f32[144,512]{1,0:T(8,128)S(1)}, u32[]{:S(2)}, u32[]{:S(2)}) collective-permute-start(f32[144,512]{1,0:T(8,128)S(1)} %fusion.2), channel_id=1, source_target_pairs={{0,2},{2,0},{1,3},{3,1},{4,6},{6,4},{5,7},{7,5},{8,10},{10,8},{9,1... | collective-permute-start | bytes 884744 | tf_op jit(solution)/shard_map/ppermute | solution.py:66
  99.9 5.1 %collective-permute-done.1 = f32[144,512]{1,0:T(8,128)S(1)} collective-permute-done((f32[144,512]{1,0:T(8,128)S(1)}, f32[144,512]{1,0:T(8,128)S(1)}, u32[]{:S(2)}, u32[]{:S(2)}) %collective-permute-start.1) | collective-permute-done | bytes 294944 | tf_op jit(solution)/shard_map/ppermute | solution.py:66
  105.1 0.4 fusion
  105.5 0.0 copy-start.5
  105.5 5.1 %collective-permute-start.2 = (f32[144,512]{1,0:T(8,128)S(1)}, f32[144,512]{1,0:T(8,128)S(1)}, u32[]{:S(2)}, u32[]{:S(2)}) collective-permute-start(f32[144,512]{1,0:T(8,128)S(1)} %fusion), channel_id=1, source_target_pairs={{0,388},{4,384},{128,260},{132,256},{256,132},{260,128},{384,4},{3... | collective-permute-start | bytes 884744 | tf_op jit(solution)/shard_map/ppermute | solution.py:74
  110.6 12.1 %collective-permute-done.2 = f32[144,512]{1,0:T(8,128)S(1)} collective-permute-done((f32[144,512]{1,0:T(8,128)S(1)}, f32[144,512]{1,0:T(8,128)S(1)}, u32[]{:S(2)}, u32[]{:S(2)}) %collective-permute-start.2) | collective-permute-done | bytes 294944 | tf_op jit(solution)/shard_map/ppermute | solution.py:74
  122.8 1.2 broadcast_in_dim.12
  124.0 3.5 %all-to-all-start.3 = ((f32[4,144,512]{2,1,0:T(8,128)}), f32[4,144,512]{2,1,0:T(8,128)S(1)}, u32[]{:S(2)}, u32[]{:S(2)}) async-start(f32[4,144,512]{2,1,0:T(8,128)} %broadcast_in_dim.12), calls=%async_computation.3 | async-start | bytes 2359296 | tf_op jit(solution)/shard_map/all_to_all | solution.py:80
  127.5 0.0 copy-done.5
  127.6 27.9 %all-to-all-done.3 = f32[4,144,512]{2,1,0:T(8,128)S(1)} async-done(((f32[4,144,512]{2,1,0:T(8,128)}), f32[4,144,512]{2,1,0:T(8,128)S(1)}, u32[]{:S(2)}, u32[]{:S(2)}) %all-to-all-start.3) | async-done | bytes 1179680 | tf_op jit(solution)/shard_map/all_to_all | solution.py:80
  155.5 0.1 reverse_select_fusion
  155.6 0.1 pad_maximum_fusion
  155.7 0.3 broadcast_in_dim.13
  156.1 6.9 %all_to_all.41 = f32[2,648,512]{2,1,0:T(8,128)S(1)} all-to-all(f32[2,648,512]{2,1,0:T(8,128)S(1)} %broadcast_in_dim.13), channel_id=1, replica_groups=mesh['ylo'=4,'core'=2,'lz'=8,'lyhi'=2,'lx1'=2,'lx0'=2] {'core'}, dimensions={0} | all-to-all | bytes 5308416 | tf_op jit(solution)/shard_map/all_to_all | solution.py:80
  163.0 0.1 concatenate.48
  163.1 0.2 slice_bitcast_fusion.3
  163.3 0.2 maximum_bitcast_fusion.1
  163.5 1.6 maximum_bitcast_fusion
  165.1 0.7 maximum_select_fusion
  (17 shorter events, 0.3 us)
Async XLA Ops:
  2.0 8.3 %copy-start.6 = (f32[1,1,128]{2,1,0:T(1,128)S(1)}, f32[1,1,128]{2,1,0:T(1,128)}, u32[]{:S(2)}) copy-start(f32[1,1,128]{2,1,0:T(1,128)} %param.8) | copy-start | bytes 1540
  2.9 7.5 %copy-start.4 = (bf16[1,1,128,512]{3,2,1,0:T(8,128)(2,1)S(1)}, bf16[1,1,128,512]{3,2,1,0:T(8,128)(2,1)}, u32[]{:S(2)}) copy-start(bf16[1,1,128,512]{3,2,1,0:T(8,128)(2,1)} %param.12) | copy-start | bytes 393220
  3.8 6.8 %copy-start.1 = (bf16[576,1,1,128]{3,0,2,1:T(8,128)(2,1)S(1)}, bf16[576,1,1,128]{3,0,2,1:T(8,128)(2,1)}, u32[]{:S(2)}) copy-start(bf16[576,1,1,128]{3,0,2,1:T(8,128)(2,1)} %param.9) | copy-start | bytes 442372
  3.8 6.8 %copy-start.3 = (bf16[576,1,1,128]{3,0,2,1:T(8,128)(2,1)S(1)}, bf16[576,1,1,128]{3,0,2,1:T(8,128)(2,1)}, u32[]{:S(2)}) copy-start(bf16[576,1,1,128]{3,0,2,1:T(8,128)(2,1)} %param.10) | copy-start | bytes 442372
  4.9 32.6 %all-to-all-start = ((f32[4,584,128]{2,1,0:T(8,128)}), f32[4,584,128]{2,1,0:T(8,128)S(1)}, u32[]{:S(2)}, u32[]{:S(2)}) async-start(f32[4,584,128]{2,1,0:T(8,128)} %broadcast_in_dim.11), calls=%async_computation | async-start | bytes 2392064 | tf_op jit(solution)/shard_map/all_to_all | solution.py:80
  10.4 27.3 %copy-start.2 = (f32[128,8]{1,0:T(8,128)}, f32[128,8]{1,0:T(8,128)S(1)}, u32[]{:S(2)}) copy-start(f32[128,8]{1,0:T(8,128)S(1)} %copy.14.own_ref) | copy-start | bytes 12292
  53.2 32.0 %copy-start = (bf16[1,3,512,512]{3,2,1,0:T(8,128)(2,1)S(1)}, bf16[1,3,512,512]{3,2,1,0:T(8,128)(2,1)}, u32[]{:S(2)}) copy-start(bf16[1,3,512,512]{3,2,1,0:T(8,128)(2,1)} %param.13) | copy-start | bytes 4718596
  85.7 9.2 %collective-permute-start = (f32[144,512]{1,0:T(8,128)S(1)}, f32[144,512]{1,0:T(8,128)S(1)}, u32[]{:S(2)}, u32[]{:S(2)}) collective-permute-start(f32[144,512]{1,0:T(8,128)S(1)} %fusion.4), channel_id=1, source_target_pairs={{0,1},{1,0},{2,3},{3,2},{4,5},{5,4},{6,7},{7,6},{8,9},{9,8},{10,11... | collective-permute-start | bytes 884744 | tf_op jit(solution)/shard_map/ppermute | solution.py:66
  95.3 9.8 %collective-permute-start.1 = (f32[144,512]{1,0:T(8,128)S(1)}, f32[144,512]{1,0:T(8,128)S(1)}, u32[]{:S(2)}, u32[]{:S(2)}) collective-permute-start(f32[144,512]{1,0:T(8,128)S(1)} %fusion.2), channel_id=1, source_target_pairs={{0,2},{2,0},{1,3},{3,1},{4,6},{6,4},{5,7},{7,5},{8,10},{10,8},{9,1... | collective-permute-start | bytes 884744 | tf_op jit(solution)/shard_map/ppermute | solution.py:66
  105.5 22.0 %copy-start.5 = (bf16[2,288,128]{2,1,0:T(8,128)(2,1)S(1)}, bf16[2,288,128]{2,1,0:T(8,128)(2,1)}, u32[]{:S(2)}) copy-start(bf16[2,288,128]{2,1,0:T(8,128)(2,1)} %get-tuple-element.4) | copy-start | bytes 442372
  105.5 17.3 %collective-permute-start.2 = (f32[144,512]{1,0:T(8,128)S(1)}, f32[144,512]{1,0:T(8,128)S(1)}, u32[]{:S(2)}, u32[]{:S(2)}) collective-permute-start(f32[144,512]{1,0:T(8,128)S(1)} %fusion), channel_id=1, source_target_pairs={{0,388},{4,384},{128,260},{132,256},{256,132},{260,128},{384,4},{3... | collective-permute-start | bytes 884744 | tf_op jit(solution)/shard_map/ppermute | solution.py:74
  124.0 31.5 %all-to-all-start.3 = ((f32[4,144,512]{2,1,0:T(8,128)}), f32[4,144,512]{2,1,0:T(8,128)S(1)}, u32[]{:S(2)}, u32[]{:S(2)}) async-start(f32[4,144,512]{2,1,0:T(8,128)} %broadcast_in_dim.12), calls=%async_computation.3 | async-start | bytes 2359296 | tf_op jit(solution)/shard_map/all_to_all | solution.py:80

commit v13 on v9

--- a/solution.py
+++ b/solution.py
@@ -53,12 +53,27 @@
 LEVEL_AXES = ("lx0", "lx1", "lyhi")
 
 
+def mirrored(chunks):
+    return jnp.where(lax.axis_index("lyhi") == 1, chunks[::-1], chunks)
+
+
 def climb_rows(rows, level_mats):
     for tree_level in range(level_mats.shape[0]):
         projected = project(rows, level_mats[tree_level])
-        pair = gather_blocks(projected, LEVEL_AXES[tree_level])
-        rows = pair[: projected.shape[0]] + pair[projected.shape[0] :]
+        other = lax.ppermute(projected, LEVEL_AXES[tree_level], [(0, 1), (1, 0)])
+        rows = projected + other
     return rows
+
+
+def ring_shift(rows, sources):
+    count = lax.axis_size("ylo")
+    ring = 2 * count
+
+    def index(place):
+        return (place % count) * 2 + place // count
+
+    pairs = [(index(sources(place) % ring), index(place)) for place in range(ring)]
+    return lax.ppermute(rows, ("ylo", "lyhi"), pairs)
 
 
 def exchange(value, axis):
@@ -74,13 +89,21 @@
 def scatter_rows(value):
     width = value.shape[1]
     halves = exchange(value, "core").reshape(2, -1, width)
+    count = lax.axis_size("ylo")
     summed = halves[0] + halves[1]
+    return exchange(summed, "ylo").reshape(count, -1, width).sum(axis=0)
+
+
+def gather_rows(rows):
     count = lax.axis_size("ylo")
-    return exchange(summed, "ylo").reshape(count, -1, width).sum(axis=0)
-
-
-def gather_rows(rows):
-    return gather_blocks(gather_blocks(rows, "ylo"), "core")
+    from_left = ring_shift(rows, lambda place: place - 1)
+    from_right = ring_shift(rows, lambda place: place + 1)
+    far = ring_shift(rows, lambda place: place + 2 if place % 2 == 0 else place - 2)
+    by_offset = jnp.stack([rows, from_right, far, from_left], axis=0)
+    doubled = jnp.concatenate([by_offset, by_offset], axis=0)
+    chip = lax.axis_index("ylo")
+    chips = lax.dynamic_slice_in_dim(doubled, (count - chip) % count, count, axis=0)
+    return gather_blocks(chips.reshape(-1, rows.shape[1]), "core")
 
 
 def near_project_kernel(target_ref, source_ref, sketch_ref, probe_ref, order_ref, basis_ref, off_ref, parts_ref):

time: 171 us -> 158 us (0.924)
  blocking collectives: 125 us -> 53.3 us
  waiting for transfers between devices: 25.7 us -> 61.4 us
  starting transfers between devices: 5.55 us -> 28 us
    all_to_all x8 -> x4, blocking collectives: 125 us -> 53.3 us  [exchange(): return lax.all_to_all(value, axis, 0, 0, tiled=True)]
    ppermute x0 -> x6, waiting for transfers between devices: none -> 35.7 us  [the longest x3 23.9 us: climb_rows(): other = lax.ppermute(projected, LEVEL_AXES[tree_level], [(0, 1), (1, 0)])]
    ppermute x0 -> x6, starting transfers between devices: none -> 22.6 us  [the longest x3 14.1 us: climb_rows(): other = lax.ppermute(projected, LEVEL_AXES[tree_level], [(0, 1), (1, 0)])]
  transfers between devices with their start and end apart: 1 -> 7, of which waited for: 1 -> 6; matrix products, arithmetic and copies ran while one was open for 1% -> 1% of each run, Pallas kernels for 0% -> 0%
where the time goes in v13:
time: 158 us; the launch traced here: 157 us
  waiting for transfers between devices  61.4 us (39%)
  blocking collectives  53.3 us (34%)
  starting transfers between devices  28 us (18%)
  local copies, waits for them, and re-layouts  5.39 us (3%)
  Pallas kernels  4.76 us (3%)
  other arithmetic  2.05 us (1%)
    all_to_all x4, blocking collectives, exchange(): return lax.all_to_all(value, axis, 0, 0, tiled=True)  53.3 us
    all_to_all x1, waiting for transfers between devices, exchange(): return lax.all_to_all(value, axis, 0, 0, tiled=True)  25.7 us
    ppermute x3, waiting for transfers between devices, climb_rows(): other = lax.ppermute(projected, LEVEL_AXES[tree_level], [(0, 1), (1, 0)])  23.9 us
    ppermute x3, starting transfers between devices, climb_rows(): other = lax.ppermute(projected, LEVEL_AXES[tree_level], [(0, 1), (1, 0)])  14.1 us
    ppermute x3, waiting for transfers between devices, ring_shift(): return lax.ppermute(rows, ('ylo', 'lyhi'), pairs)  11.8 us
    ppermute x3, starting transfers between devices, ring_shift(): return lax.ppermute(rows, ('ylo', 'lyhi'), pairs)  8.47 us
    all_to_all x1, starting transfers between devices, exchange(): return lax.all_to_all(value, axis, 0, 0, tiled=True)  5.42 us
    pallas_call x1, Pallas kernels, near_project(): pl.pallas_call(near_project_kernel, out_shape=(jax.ShapeDtypeStruct((prob...  4.76 us
  transfers between devices with their start and end apart: 7, of which 6 were waited for; matrix products, arithmetic and copies ran while one was open for 1% of the time, Pallas kernels for 0%

profile of v13, /device:TPU:1, one launch (start us, length us, event | category | flops | bytes accessed | tf_op | source)
XLA Modules:
  0.0 157.0 jit_solution(8836120699888960747)
XLA Ops:
  0.6 0.7 copy.13
  1.3 0.0 copy-start.1
  1.3 1.0 fusion.11
  2.3 0.0 copy-start.2
  2.3 0.7 pad_maximum_fusion
  3.0 1.1 broadcast_in_dim.25
  4.1 5.4 %all-to-all-start = ((f32[4,584,128]{2,1,0:T(8,128)}), f32[4,584,128]{2,1,0:T(8,128)S(1)}, u32[]{:S(2)}, u32[]{:S(2)}) async-start(f32[4,584,128]{2,1,0:T(8,128)} %broadcast_in_dim.25), calls=%async_computation | async-start | bytes 2392064 | tf_op jit(solution)/shard_map/all_to_all | solution.py:80
  9.5 0.0 copy-done.1
  9.5 0.7 copy.9.target_ref
  10.2 0.0 copy-done.2
  10.2 0.7 copy.10.order_ref
  11.0 25.7 %all-to-all-done = f32[4,584,128]{2,1,0:T(8,128)S(1)} async-done(((f32[4,584,128]{2,1,0:T(8,128)}), f32[4,584,128]{2,1,0:T(8,128)S(1)}, u32[]{:S(2)}, u32[]{:S(2)}) %all-to-all-start) | async-done | bytes 1196064 | tf_op jit(solution)/shard_map/all_to_all | solution.py:80
  36.7 0.2 broadcast_in_dim.27
  36.8 8.9 %all_to_all.33 = f32[2,2336,128]{2,1,0:T(8,128)} all-to-all(f32[2,2336,128]{2,1,0:T(8,128)S(1)} %broadcast_in_dim.27), channel_id=1, replica_groups=mesh['ylo'=4,'core'=2,'lz'=8,'lyhi'=2,'lx1'=2,'lx0'=2] {'core'}, dimensions={0} | all-to-all | bytes 4784128 | tf_op jit(solution)/shard_map/all_to_all | solution.py:80
  45.7 4.8 %shard_map.86 = (bf16[576,128]{1,0:T(8,128)(2,1)}, f32[1152,512]{1,0:T(8,128)}) custom-call(f32[128,8]{1,0:T(8,128)} %copy.9.target_ref, f32[8,584,128]{2,1,0:T(8,128)} %bitcast.41, bf16[576,128]{1,0:T(8,128)(2,1)} %bitcast.48, bf16[576,128]{1,0:T(8,128)(2,1)} %bitcast.47, s32[128,1]{1,0:T(8,128)} %copy.10.order_ref, bf16[128,512]{1,0:T(8,128)(2,1)} %bitcast.49), custom_call_target="tpu_custom_call" | custom-call | flops 339738624 | bytes 5324800 | tf_op jit(solution)/shard_map/pallas_call | solution.py:147
  50.4 6.9 %all_to_all.34 = f32[2,576,512]{2,1,0:T(8,128)S(1)} all-to-all(f32[2,576,512]{2,1,0:T(8,128)} %bitcast.46), channel_id=1, replica_groups=mesh['ylo'=4,'core'=2,'lz'=8,'lyhi'=2,'lx1'=2,'lx0'=2] {'core'}, dimensions={0} | all-to-all | bytes 4718592 | tf_op jit(solution)/shard_map/all_to_all | solution.py:80
  57.3 0.2 slice_add_fusion
  57.5 0.0 copy-start
  57.6 30.7 %all_to_all.35 = f32[4,144,512]{2,1,0:T(8,128)S(1)} all-to-all(f32[4,144,512]{2,1,0:T(8,128)S(1)} %bitcast.45), channel_id=1, replica_groups=mesh['ylo'=4,'core'=2,'lz'=8,'lyhi'=2,'lx1'=2,'lx0'=2] {'ylo'}, dimensions={0} | all-to-all | bytes 2359296 | tf_op jit(solution)/shard_map/all_to_all | solution.py:80
  88.3 0.1 reduce_sum.9
  88.4 0.0 copy-done
  88.4 0.4 fusion.4
  88.8 3.1 %collective-permute-start = (f32[144,512]{1,0:T(8,128)S(1)}, f32[144,512]{1,0:T(8,128)S(1)}, u32[]{:S(2)}, u32[]{:S(2)}) collective-permute-start(f32[144,512]{1,0:T(8,128)S(1)} %fusion.4), channel_id=1, source_target_pairs={{0,1},{1,0},{2,3},{3,2},{4,5},{5,4},{6,7},{7,6},{8,9},{9,8},{10,11... | collective-permute-start | bytes 884744 | tf_op jit(solution)/shard_map/ppermute | solution.py:63
  92.0 6.0 %collective-permute-done = f32[144,512]{1,0:T(8,128)S(1)} collective-permute-done((f32[144,512]{1,0:T(8,128)S(1)}, f32[144,512]{1,0:T(8,128)S(1)}, u32[]{:S(2)}, u32[]{:S(2)}) %collective-permute-start) | collective-permute-done | bytes 294944 | tf_op jit(solution)/shard_map/ppermute | solution.py:63
  97.9 0.4 fusion.2
  98.3 4.6 %collective-permute-start.1 = (f32[144,512]{1,0:T(8,128)S(1)}, f32[144,512]{1,0:T(8,128)S(1)}, u32[]{:S(2)}, u32[]{:S(2)}) collective-permute-start(f32[144,512]{1,0:T(8,128)S(1)} %fusion.2), channel_id=1, source_target_pairs={{0,2},{2,0},{1,3},{3,1},{4,6},{6,4},{5,7},{7,5},{8,10},{10,8},{9,1... | collective-permute-start | bytes 884744 | tf_op jit(solution)/shard_map/ppermute | solution.py:63
  103.0 5.0 %collective-permute-done.1 = f32[144,512]{1,0:T(8,128)S(1)} collective-permute-done((f32[144,512]{1,0:T(8,128)S(1)}, f32[144,512]{1,0:T(8,128)S(1)}, u32[]{:S(2)}, u32[]{:S(2)}) %collective-permute-start.1) | collective-permute-done | bytes 294944 | tf_op jit(solution)/shard_map/ppermute | solution.py:63
  108.0 0.4 fusion
  108.4 6.4 %collective-permute-start.2 = (f32[144,512]{1,0:T(8,128)S(1)}, f32[144,512]{1,0:T(8,128)S(1)}, u32[]{:S(2)}, u32[]{:S(2)}) collective-permute-start(f32[144,512]{1,0:T(8,128)S(1)} %fusion), channel_id=1, source_target_pairs={{0,4},{4,0},{1,5},{5,1},{2,6},{6,2},{3,7},{7,3},{8,12},{12,8},{9,1... | collective-permute-start | bytes 884744 | tf_op jit(solution)/shard_map/ppermute | solution.py:63
  114.8 13.0 %collective-permute-done.2 = f32[144,512]{1,0:T(8,128)S(1)} collective-permute-done((f32[144,512]{1,0:T(8,128)S(1)}, f32[144,512]{1,0:T(8,128)S(1)}, u32[]{:S(2)}, u32[]{:S(2)}) %collective-permute-start.2) | collective-permute-done | bytes 294944 | tf_op jit(solution)/shard_map/ppermute | solution.py:63
  127.7 0.1 bitcast_dynamic-update-slice_fusion.6
  127.8 3.3 %collective-permute-start.3 = (f32[144,512]{1,0:T(8,128)S(1)}, f32[144,512]{1,0:T(8,128)S(1)}, u32[]{:S(2)}, u32[]{:S(2)}) collective-permute-start(f32[144,512]{1,0:T(8,128)S(1)} %get-tuple-element.7), channel_id=1, source_target_pairs={{128,0},{256,128},{384,256},{4,384},{132,4},{260,132},{388,260},{0... | collective-permute-start | bytes 884744 | tf_op jit(solution)/shard_map/ppermute | solution.py:76
  131.1 1.9 %collective-permute-start.4 = (f32[144,512]{1,0:T(8,128)S(1)}, f32[144,512]{1,0:T(8,128)S(1)}, u32[]{:S(2)}, u32[]{:S(2)}) collective-permute-start(f32[144,512]{1,0:T(8,128)S(1)} %get-tuple-element.7), channel_id=1, source_target_pairs={{256,0},{388,128},{4,256},{128,384},{260,4},{384,132},{0,260},{132... | collective-permute-start | bytes 884744 | tf_op jit(solution)/shard_map/ppermute | solution.py:76
  133.0 3.3 %collective-permute-start.5 = (f32[144,512]{1,0:T(8,128)S(1)}, f32[144,512]{1,0:T(8,128)S(1)}, u32[]{:S(2)}, u32[]{:S(2)}) collective-permute-start(f32[144,512]{1,0:T(8,128)S(1)} %get-tuple-element.7), channel_id=1, source_target_pairs={{388,0},{0,128},{128,256},{256,384},{384,4},{4,132},{132,260},{260... | collective-permute-start | bytes 884744 | tf_op jit(solution)/shard_map/ppermute | solution.py:76
  136.3 0.0 collective-permute-done.3
  136.3 5.4 %collective-permute-done.4 = f32[144,512]{1,0:T(8,128)S(1)} collective-permute-done((f32[144,512]{1,0:T(8,128)S(1)}, f32[144,512]{1,0:T(8,128)S(1)}, u32[]{:S(2)}, u32[]{:S(2)}) %collective-permute-start.4) | collective-permute-done | bytes 294944 | tf_op jit(solution)/shard_map/ppermute | solution.py:76
  141.8 6.3 %collective-permute-done.5 = f32[144,512]{1,0:T(8,128)S(1)} collective-permute-done((f32[144,512]{1,0:T(8,128)S(1)}, f32[144,512]{1,0:T(8,128)S(1)}, u32[]{:S(2)}, u32[]{:S(2)}) %collective-permute-start.5) | collective-permute-done | bytes 294944 | tf_op jit(solution)/shard_map/ppermute | solution.py:76
  148.3 0.1 constant_dynamic-slice_fusion
  148.4 0.3 broadcast_in_dim.29
  148.7 6.9 %all_to_all.36 = f32[2,576,512]{2,1,0:T(8,128)S(1)} all-to-all(f32[2,576,512]{2,1,0:T(8,128)S(1)} %broadcast_in_dim.29), channel_id=1, replica_groups=mesh['ylo'=4,'core'=2,'lz'=8,'lyhi'=2,'lx1'=2,'lx0'=2] {'core'}, dimensions={0} | all-to-all | bytes 4718592 | tf_op jit(solution)/shard_map/all_to_all | solution.py:80
  155.6 1.4 copy.22
  (9 shorter events, 0.2 us)
Async XLA Ops:
  1.3 8.2 %copy-start.1 = (f32[1,1,128]{2,1,0:T(1,128)S(1)}, f32[1,1,128]{2,1,0:T(1,128)}, u32[]{:S(2)}) copy-start(f32[1,1,128]{2,1,0:T(1,128)} %param.8) | copy-start | bytes 1540
  2.3 8.0 %copy-start.2 = (s32[1,1,128]{2,1,0:T(1,128)S(1)}, s32[1,1,128]{2,1,0:T(1,128)}, u32[]{:S(2)}) copy-start(s32[1,1,128]{2,1,0:T(1,128)} %param.11) | copy-start | bytes 1540
  4.1 32.6 %all-to-all-start = ((f32[4,584,128]{2,1,0:T(8,128)}), f32[4,584,128]{2,1,0:T(8,128)S(1)}, u32[]{:S(2)}, u32[]{:S(2)}) async-start(f32[4,584,128]{2,1,0:T(8,128)} %broadcast_in_dim.25), calls=%async_computation | async-start | bytes 2392064 | tf_op jit(solution)/shard_map/all_to_all | solution.py:80
  57.5 30.9 %copy-start = (bf16[1,3,512,512]{3,2,1,0:T(8,128)(2,1)S(1)}, bf16[1,3,512,512]{3,2,1,0:T(8,128)(2,1)}, u32[]{:S(2)}) copy-start(bf16[1,3,512,512]{3,2,1,0:T(8,128)(2,1)} %param.13) | copy-start | bytes 4718596
  88.8 9.1 %collective-permute-start = (f32[144,512]{1,0:T(8,128)S(1)}, f32[144,512]{1,0:T(8,128)S(1)}, u32[]{:S(2)}, u32[]{:S(2)}) collective-permute-start(f32[144,512]{1,0:T(8,128)S(1)} %fusion.4), channel_id=1, source_target_pairs={{0,1},{1,0},{2,3},{3,2},{4,5},{5,4},{6,7},{7,6},{8,9},{9,8},{10,11... | collective-permute-start | bytes 884744 | tf_op jit(solution)/shard_map/ppermute | solution.py:63
  98.3 9.7 %collective-permute-start.1 = (f32[144,512]{1,0:T(8,128)S(1)}, f32[144,512]{1,0:T(8,128)S(1)}, u32[]{:S(2)}, u32[]{:S(2)}) collective-permute-start(f32[144,512]{1,0:T(8,128)S(1)} %fusion.2), channel_id=1, source_target_pairs={{0,2},{2,0},{1,3},{3,1},{4,6},{6,4},{5,7},{7,5},{8,10},{10,8},{9,1... | collective-permute-start | bytes 884744 | tf_op jit(solution)/shard_map/ppermute | solution.py:63
  108.4 19.3 %collective-permute-start.2 = (f32[144,512]{1,0:T(8,128)S(1)}, f32[144,512]{1,0:T(8,128)S(1)}, u32[]{:S(2)}, u32[]{:S(2)}) collective-permute-start(f32[144,512]{1,0:T(8,128)S(1)} %fusion), channel_id=1, source_target_pairs={{0,4},{4,0},{1,5},{5,1},{2,6},{6,2},{3,7},{7,3},{8,12},{12,8},{9,1... | collective-permute-start | bytes 884744 | tf_op jit(solution)/shard_map/ppermute | solution.py:63
  127.8 8.5 %collective-permute-start.3 = (f32[144,512]{1,0:T(8,128)S(1)}, f32[144,512]{1,0:T(8,128)S(1)}, u32[]{:S(2)}, u32[]{:S(2)}) collective-permute-start(f32[144,512]{1,0:T(8,128)S(1)} %get-tuple-element.7), channel_id=1, source_target_pairs={{128,0},{256,128},{384,256},{4,384},{132,4},{260,132},{388,260},{0... | collective-permute-start | bytes 884744 | tf_op jit(solution)/shard_map/ppermute | solution.py:76
  131.1 10.7 %collective-permute-start.4 = (f32[144,512]{1,0:T(8,128)S(1)}, f32[144,512]{1,0:T(8,128)S(1)}, u32[]{:S(2)}, u32[]{:S(2)}) collective-permute-start(f32[144,512]{1,0:T(8,128)S(1)} %get-tuple-element.7), channel_id=1, source_target_pairs={{256,0},{388,128},{4,256},{128,384},{260,4},{384,132},{0,260},{132... | collective-permute-start | bytes 884744 | tf_op jit(solution)/shard_map/ppermute | solution.py:76
  133.0 15.1 %collective-permute-start.5 = (f32[144,512]{1,0:T(8,128)S(1)}, f32[144,512]{1,0:T(8,128)S(1)}, u32[]{:S(2)}, u32[]{:S(2)}) collective-permute-start(f32[144,512]{1,0:T(8,128)S(1)} %get-tuple-element.7), channel_id=1, source_target_pairs={{388,0},{0,128},{128,256},{256,384},{384,4},{4,132},{132,260},{260... | collective-permute-start | bytes 884744 | tf_op jit(solution)/shard_map/ppermute | solution.py:76

commit v14 on v11

--- a/solution.py
+++ b/solution.py
@@ -59,21 +59,33 @@
 
 
 def climb_rows(rows, level_mats):
-    level_count = level_mats.shape[0]
-    for tree_level in range(level_count):
+    for tree_level in range(level_mats.shape[0]):
         projected = project(rows, level_mats[tree_level])
-        if tree_level < level_count - 1:
-            other = lax.ppermute(projected, LEVEL_AXES[tree_level], [(0, 1), (1, 0)])
-        else:
-            count = lax.axis_size("ylo")
-            pairs = [
-                (chip * 2 + half, (count - 1 - chip) * 2 + 1 - half)
-                for chip in range(count)
-                for half in range(2)
-            ]
-            other = lax.ppermute(projected, ("ylo", "lyhi"), pairs)
+        other = lax.ppermute(projected, LEVEL_AXES[tree_level], [(0, 1), (1, 0)])
         rows = projected + other
     return rows
+
+
+def ring_shift(rows, sources):
+    count = lax.axis_size("ylo")
+    ring = 2 * count
+
+    def index(place):
+        return (place % count) * 2 + place // count
+
+    pairs = [(index(sources(place) % ring), index(place)) for place in range(ring)]
+    return lax.ppermute(rows, ("ylo", "lyhi"), pairs)
+
+
+def ring_gather(rows):
+    count = lax.axis_size("ylo")
+    from_left = ring_shift(rows, lambda place: place - 1)
+    from_right = ring_shift(rows, lambda place: place + 1)
+    far = ring_shift(rows, lambda place: place + 2 if place % 2 == 0 else place - 2)
+    by_offset = jnp.stack([rows, from_right, far, from_left], axis=0)
+    doubled = jnp.concatenate([by_offset, by_offset], axis=0)
+    chip = lax.axis_index("ylo")
+    return lax.dynamic_slice_in_dim(doubled, (count - chip) % count, count, axis=0)
 
 
 def exchange(value, axis):
@@ -220,11 +232,9 @@
     layout = (lax.axis_size("ylo"), outgoing.shape[0], geometry.shape[0], half)
     off_pair, parts = chip_project(layout, recv, own, full_flat, probe_flat, basis_flat)
     count = lax.axis_size("ylo")
-    summed = mirrored(parts.reshape(count, -1, basis_width))
-    mine = exchange(summed.reshape(-1, basis_width), "ylo").reshape(count, -1, basis_width).sum(axis=0)
+    mine = exchange(parts, "ylo").reshape(count, -1, basis_width).sum(axis=0)
     top = climb_rows(mine, level_mats)
-    chips = gather_blocks(top, "ylo").reshape((count,) + top.shape)
-    half_rows = mirrored(chips).reshape(-1, basis_width)
+    half_rows = ring_gather(top).reshape(-1, basis_width)
     sent_off = off_pair[1].astype(jnp.float32).reshape(-1, basis_width)
     back = gather_blocks(jnp.concatenate([half_rows, sent_off], axis=0), "core")
     back = back.reshape(2, -1, basis_width)

time: 167 us -> 156 us (0.934)
  waiting for transfers between devices: 77.7 us -> 63.2 us
  starting transfers between devices: 22.1 us -> 27.2 us
    all_to_all x2 -> x1, waiting for transfers between devices: 54.7 us -> 26.8 us  [exchange(): return lax.all_to_all(value, axis, 0, 0, tiled=True)]
    ppermute x2 -> x3, waiting for transfers between devices: 11 us -> 24.4 us  [climb_rows(): other = lax.ppermute(projected, LEVEL_AXES[tree_level], [(0, 1), (1, 0)])]
    ppermute x2 -> x3, starting transfers between devices: 7.77 us -> 14.1 us  [climb_rows(): other = lax.ppermute(projected, LEVEL_AXES[tree_level], [(0, 1), (1, 0)])]
    all_to_all x2 -> x1, starting transfers between devices: 8.95 us -> 5.42 us  [exchange(): return lax.all_to_all(value, axis, 0, 0, tiled=True)]
    ppermute x1 -> x3, starting transfers between devices: 5.39 us -> 7.7 us  [ring_shift(): return lax.ppermute(rows, ('ylo', 'lyhi'), pairs)]
    select_n x2 -> x0, other arithmetic: 2.01 us -> none  [mirrored(): return jnp.where(lax.axis_index('lyhi') == 1, chunks[::-1], chunks)]
    ppermute x1 -> x3, waiting for transfers between devices: 12 us -> 11.9 us  [ring_shift(): return lax.ppermute(rows, ('ylo', 'lyhi'), pairs)]
  transfers between devices with their start and end apart: 5 -> 7, of which waited for: 5 -> 6; matrix products, arithmetic and copies ran while one was open for 0% -> 1% of each run, Pallas kernels for 0% -> 0%
where the time goes in v14:
time: 156 us
  waiting for transfers between devices  63.2 us (41%)
  blocking collectives  48.9 us (31%)
  starting transfers between devices  27.2 us (17%)
  Pallas kernels  5.22 us (3%)
  other arithmetic  5.11 us (3%)
  local copies, waits for them, and re-layouts  3.98 us (3%)
    all_to_all x3, blocking collectives, exchange(): return lax.all_to_all(value, axis, 0, 0, tiled=True)  48.9 us
    all_to_all x1, waiting for transfers between devices, exchange(): return lax.all_to_all(value, axis, 0, 0, tiled=True)  26.8 us
    ppermute x3, waiting for transfers between devices, climb_rows(): other = lax.ppermute(projected, LEVEL_AXES[tree_level], [(0, 1), (1, 0)])  24.4 us
    ppermute x3, starting transfers between devices, climb_rows(): other = lax.ppermute(projected, LEVEL_AXES[tree_level], [(0, 1), (1, 0)])  14.1 us
    ppermute x3, waiting for transfers between devices, ring_shift(): return lax.ppermute(rows, ('ylo', 'lyhi'), pairs)  11.9 us
    ppermute x3, starting transfers between devices, ring_shift(): return lax.ppermute(rows, ('ylo', 'lyhi'), pairs)  7.7 us
    all_to_all x1, starting transfers between devices, exchange(): return lax.all_to_all(value, axis, 0, 0, tiled=True)  5.42 us
    pallas_call x1, Pallas kernels, chip_project(): pl.pallas_call(functools.partial(chip_kernel, layout), out_shape=(jax.Sha...  5.22 us
  transfers between devices with their start and end apart: 7, of which 6 were waited for; matrix products, arithmetic and copies ran while one was open for 1% of the time, Pallas kernels for 0%

profile of v14, /device:TPU:1, one launch (start us, length us, event | category | flops | bytes accessed | tf_op | source)
XLA Modules:
  0.0 155.9 jit_solution(14546314517661600566)
XLA Ops:
  0.6 0.7 copy.16
  1.3 0.7 convert_bitcast_fusion
  2.0 0.0 copy-start.7
  2.0 1.0 fusion.11
  2.9 0.0 copy-start.4
  3.0 0.8 concatenate.47
  3.8 0.0 copy-start.1
  3.8 0.0 copy-start.3
  3.8 1.1 broadcast_in_dim.9
  4.9 5.4 %all-to-all-start = ((f32[4,584,128]{2,1,0:T(8,128)}), f32[4,584,128]{2,1,0:T(8,128)S(1)}, u32[]{:S(2)}, u32[]{:S(2)}) async-start(f32[4,584,128]{2,1,0:T(8,128)} %broadcast_in_dim.9), calls=%async_computation | async-start | bytes 2392064 | tf_op jit(solution)/shard_map/all_to_all | solution.py:92
  10.3 0.0 copy-done.7
  10.3 0.1 copy.14.own_ref
  10.4 0.0 copy-done.4
  10.4 0.0 copy-start.2
  10.4 0.1 reshape.162
  10.6 0.0 copy-done.1
  10.6 0.0 copy-done.3
  10.6 26.8 %all-to-all-done = f32[4,584,128]{2,1,0:T(8,128)S(1)} async-done(((f32[4,584,128]{2,1,0:T(8,128)}), f32[4,584,128]{2,1,0:T(8,128)S(1)}, u32[]{:S(2)}, u32[]{:S(2)}) %all-to-all-start) | async-done | bytes 1196064 | tf_op jit(solution)/shard_map/all_to_all | solution.py:92
  37.5 0.1 constant_dynamic-update-slice_fusion.3
  37.6 0.1 constant_dynamic-update-slice_fusion.1
  37.7 0.0 copy-done.2
  37.8 10.0 %all_to_all.33.recv_ref = f32[2,3552,128]{2,1,0:T(8,128)} all-to-all(f32[2,3552,128]{2,1,0:T(8,128)S(1)} %bitcast.63), channel_id=1, replica_groups=mesh['ylo'=4,'core'=2,'lz'=8,'lyhi'=2,'lx1'=2,'lx0'=2] {'core'}, dimensions={0} | all-to-all | bytes 7274496 | tf_op jit(solution)/shard_map/all_to_all | solution.py:92
  47.8 5.2 %shard_map.86 = (bf16[2,288,128]{2,1,0:T(8,128)(2,1)}, f32[576,512]{1,0:T(8,128)}) custom-call(f32[2,3552,128]{2,1,0:T(8,128)} %all_to_all.33.recv_ref, f32[128,8]{1,0:T(8,128)} %copy-done.2, bf16[576,128]{1,0:T(8,128)(2,1)} %bitcast.70, bf16[576,128]{1,0:T(8,128)(2,1)} %bitcast.67, bf16[128,512]{1,0:T(8,128)(2,1)} %bitcast.71), custom_call_target="tpu_custom_call" | custom-call | flops 339738624 | bytes 5242880 | tf_op jit(solution)/shard_map/pallas_call | solution.py:180
  53.0 0.0 copy-start
  53.0 31.9 %all_to_all.34 = f32[4,144,512]{2,1,0:T(8,128)S(1)} all-to-all(f32[4,144,512]{2,1,0:T(8,128)} %bitcast.68), channel_id=1, replica_groups=mesh['ylo'=4,'core'=2,'lz'=8,'lyhi'=2,'lx1'=2,'lx0'=2] {'ylo'}, dimensions={0} | all-to-all | bytes 2359296 | tf_op jit(solution)/shard_map/all_to_all | solution.py:92
  85.0 0.1 reduce_sum.9
  85.1 0.0 copy-done
  85.1 0.0 copy-start.6
  85.1 0.4 fusion.4
  85.5 3.1 %collective-permute-start = (f32[144,512]{1,0:T(8,128)S(1)}, f32[144,512]{1,0:T(8,128)S(1)}, u32[]{:S(2)}, u32[]{:S(2)}) collective-permute-start(f32[144,512]{1,0:T(8,128)S(1)} %fusion.4), channel_id=1, source_target_pairs={{0,1},{1,0},{2,3},{3,2},{4,5},{5,4},{6,7},{7,6},{8,9},{9,8},{10,11... | collective-permute-start | bytes 884744 | tf_op jit(solution)/shard_map/ppermute | solution.py:64
  88.6 6.1 %collective-permute-done = f32[144,512]{1,0:T(8,128)S(1)} collective-permute-done((f32[144,512]{1,0:T(8,128)S(1)}, f32[144,512]{1,0:T(8,128)S(1)}, u32[]{:S(2)}, u32[]{:S(2)}) %collective-permute-start) | collective-permute-done | bytes 294944 | tf_op jit(solution)/shard_map/ppermute | solution.py:64
  94.7 0.4 fusion.2
  95.1 4.6 %collective-permute-start.1 = (f32[144,512]{1,0:T(8,128)S(1)}, f32[144,512]{1,0:T(8,128)S(1)}, u32[]{:S(2)}, u32[]{:S(2)}) collective-permute-start(f32[144,512]{1,0:T(8,128)S(1)} %fusion.2), channel_id=1, source_target_pairs={{0,2},{2,0},{1,3},{3,1},{4,6},{6,4},{5,7},{7,5},{8,10},{10,8},{9,1... | collective-permute-start | bytes 884744 | tf_op jit(solution)/shard_map/ppermute | solution.py:64
  99.7 5.1 %collective-permute-done.1 = f32[144,512]{1,0:T(8,128)S(1)} collective-permute-done((f32[144,512]{1,0:T(8,128)S(1)}, f32[144,512]{1,0:T(8,128)S(1)}, u32[]{:S(2)}, u32[]{:S(2)}) %collective-permute-start.1) | collective-permute-done | bytes 294944 | tf_op jit(solution)/shard_map/ppermute | solution.py:64
  104.9 0.4 fusion
  105.3 6.3 %collective-permute-start.2 = (f32[144,512]{1,0:T(8,128)S(1)}, f32[144,512]{1,0:T(8,128)S(1)}, u32[]{:S(2)}, u32[]{:S(2)}) collective-permute-start(f32[144,512]{1,0:T(8,128)S(1)} %fusion), channel_id=1, source_target_pairs={{0,4},{4,0},{1,5},{5,1},{2,6},{6,2},{3,7},{7,3},{8,12},{12,8},{9,1... | collective-permute-start | bytes 884744 | tf_op jit(solution)/shard_map/ppermute | solution.py:64
  111.7 13.2 %collective-permute-done.2 = f32[144,512]{1,0:T(8,128)S(1)} collective-permute-done((f32[144,512]{1,0:T(8,128)S(1)}, f32[144,512]{1,0:T(8,128)S(1)}, u32[]{:S(2)}, u32[]{:S(2)}) %collective-permute-start.2) | collective-permute-done | bytes 294944 | tf_op jit(solution)/shard_map/ppermute | solution.py:64
  124.9 2.8 %collective-permute-start.3 = (f32[144,512]{1,0:T(8,128)S(1)}, f32[144,512]{1,0:T(8,128)S(1)}, u32[]{:S(2)}, u32[]{:S(2)}) collective-permute-start(f32[144,512]{1,0:T(8,128)S(1)} %get-tuple-element.7), channel_id=1, source_target_pairs={{128,0},{256,128},{384,256},{4,384},{132,4},{260,132},{388,260},{0... | collective-permute-start | bytes 884744 | tf_op jit(solution)/shard_map/ppermute | solution.py:77
  127.7 1.9 %collective-permute-start.4 = (f32[144,512]{1,0:T(8,128)S(1)}, f32[144,512]{1,0:T(8,128)S(1)}, u32[]{:S(2)}, u32[]{:S(2)}) collective-permute-start(f32[144,512]{1,0:T(8,128)S(1)} %get-tuple-element.7), channel_id=1, source_target_pairs={{256,0},{388,128},{4,256},{128,384},{260,4},{384,132},{0,260},{132... | collective-permute-start | bytes 884744 | tf_op jit(solution)/shard_map/ppermute | solution.py:77
  129.6 0.0 copy-done.6
  129.6 0.6 slice_bitcast_fusion.4
  130.3 3.0 %collective-permute-start.5 = (f32[144,512]{1,0:T(8,128)S(1)}, f32[144,512]{1,0:T(8,128)S(1)}, u32[]{:S(2)}, u32[]{:S(2)}) collective-permute-start(f32[144,512]{1,0:T(8,128)S(1)} %get-tuple-element.7), channel_id=1, source_target_pairs={{388,0},{0,128},{128,256},{256,384},{384,4},{4,132},{132,260},{260... | collective-permute-start | bytes 884744 | tf_op jit(solution)/shard_map/ppermute | solution.py:77
  133.3 0.0 collective-permute-done.3
  133.4 4.7 %collective-permute-done.4 = f32[144,512]{1,0:T(8,128)S(1)} collective-permute-done((f32[144,512]{1,0:T(8,128)S(1)}, f32[144,512]{1,0:T(8,128)S(1)}, u32[]{:S(2)}, u32[]{:S(2)}) %collective-permute-start.4) | collective-permute-done | bytes 294944 | tf_op jit(solution)/shard_map/ppermute | solution.py:77
  138.1 7.2 %collective-permute-done.5 = f32[144,512]{1,0:T(8,128)S(1)} collective-permute-done((f32[144,512]{1,0:T(8,128)S(1)}, f32[144,512]{1,0:T(8,128)S(1)}, u32[]{:S(2)}, u32[]{:S(2)}) %collective-permute-start.5) | collective-permute-done | bytes 294944 | tf_op jit(solution)/shard_map/ppermute | solution.py:77
  145.5 0.1 constant_dynamic-slice_fusion
  145.6 0.1 pad_maximum_fusion
  145.7 0.3 broadcast_in_dim.20
  146.0 7.0 %all_to_all.35 = f32[2,648,512]{2,1,0:T(8,128)S(1)} all-to-all(f32[2,648,512]{2,1,0:T(8,128)S(1)} %broadcast_in_dim.20), channel_id=1, replica_groups=mesh['ylo'=4,'core'=2,'lz'=8,'lyhi'=2,'lx1'=2,'lx0'=2] {'core'}, dimensions={0} | all-to-all | bytes 5308416 | tf_op jit(solution)/shard_map/all_to_all | solution.py:92
  153.1 0.1 concatenate.53
  153.2 0.2 slice_bitcast_fusion.3
  153.4 0.2 maximum_bitcast_fusion.1
  153.6 0.0 copy-start.5
  153.6 1.6 %maximum_bitcast_fusion = f32[1,2,576,512]{3,2,1,0:T(8,128)} fusion(f32[1,576,512]{2,1,0:T(8,128)S(1)} %get-tuple-element.15, f32[1,576,512]{2,1,0:T(8,128)S(1)} %get-tuple-element.14), kind=kLoop, calls=%fused_computation | loop fusion | flops 589824 | bytes 4718592 | tf_op jit(solution)/shard_map/broadcast_in_dim | solution.py:241
  155.2 0.0 copy-done.5
  155.2 0.7 maximum_select_fusion
  (23 shorter events, 0.4 us)
Async XLA Ops:
  2.0 8.3 %copy-start.7 = (f32[1,1,128]{2,1,0:T(1,128)S(1)}, f32[1,1,128]{2,1,0:T(1,128)}, u32[]{:S(2)}) copy-start(f32[1,1,128]{2,1,0:T(1,128)} %param.8) | copy-start | bytes 1540
  2.9 7.5 %copy-start.4 = (bf16[1,1,128,512]{3,2,1,0:T(8,128)(2,1)S(1)}, bf16[1,1,128,512]{3,2,1,0:T(8,128)(2,1)}, u32[]{:S(2)}) copy-start(bf16[1,1,128,512]{3,2,1,0:T(8,128)(2,1)} %param.12) | copy-start | bytes 393220
  3.8 6.8 %copy-start.1 = (bf16[576,1,1,128]{3,0,2,1:T(8,128)(2,1)S(1)}, bf16[576,1,1,128]{3,0,2,1:T(8,128)(2,1)}, u32[]{:S(2)}) copy-start(bf16[576,1,1,128]{3,0,2,1:T(8,128)(2,1)} %param.9) | copy-start | bytes 442372
  3.8 6.8 %copy-start.3 = (bf16[576,1,1,128]{3,0,2,1:T(8,128)(2,1)S(1)}, bf16[576,1,1,128]{3,0,2,1:T(8,128)(2,1)}, u32[]{:S(2)}) copy-start(bf16[576,1,1,128]{3,0,2,1:T(8,128)(2,1)} %param.10) | copy-start | bytes 442372
  4.9 32.6 %all-to-all-start = ((f32[4,584,128]{2,1,0:T(8,128)}), f32[4,584,128]{2,1,0:T(8,128)S(1)}, u32[]{:S(2)}, u32[]{:S(2)}) async-start(f32[4,584,128]{2,1,0:T(8,128)} %broadcast_in_dim.9), calls=%async_computation | async-start | bytes 2392064 | tf_op jit(solution)/shard_map/all_to_all | solution.py:92
  10.4 27.3 %copy-start.2 = (f32[128,8]{1,0:T(8,128)}, f32[128,8]{1,0:T(8,128)S(1)}, u32[]{:S(2)}) copy-start(f32[128,8]{1,0:T(8,128)S(1)} %copy.14.own_ref) | copy-start | bytes 12292
  53.0 32.0 %copy-start = (bf16[1,3,512,512]{3,2,1,0:T(8,128)(2,1)S(1)}, bf16[1,3,512,512]{3,2,1,0:T(8,128)(2,1)}, u32[]{:S(2)}) copy-start(bf16[1,3,512,512]{3,2,1,0:T(8,128)(2,1)} %param.13) | copy-start | bytes 4718596
  85.1 44.6 %copy-start.6 = (bf16[2,288,128]{2,1,0:T(8,128)(2,1)S(1)}, bf16[2,288,128]{2,1,0:T(8,128)(2,1)}, u32[]{:S(2)}) copy-start(bf16[2,288,128]{2,1,0:T(8,128)(2,1)} %get-tuple-element.4) | copy-start | bytes 442372
  85.5 9.2 %collective-permute-start = (f32[144,512]{1,0:T(8,128)S(1)}, f32[144,512]{1,0:T(8,128)S(1)}, u32[]{:S(2)}, u32[]{:S(2)}) collective-permute-start(f32[144,512]{1,0:T(8,128)S(1)} %fusion.4), channel_id=1, source_target_pairs={{0,1},{1,0},{2,3},{3,2},{4,5},{5,4},{6,7},{7,6},{8,9},{9,8},{10,11... | collective-permute-start | bytes 884744 | tf_op jit(solution)/shard_map/ppermute | solution.py:64
  95.1 9.8 %collective-permute-start.1 = (f32[144,512]{1,0:T(8,128)S(1)}, f32[144,512]{1,0:T(8,128)S(1)}, u32[]{:S(2)}, u32[]{:S(2)}) collective-permute-start(f32[144,512]{1,0:T(8,128)S(1)} %fusion.2), channel_id=1, source_target_pairs={{0,2},{2,0},{1,3},{3,1},{4,6},{6,4},{5,7},{7,5},{8,10},{10,8},{9,1... | collective-permute-start | bytes 884744 | tf_op jit(solution)/shard_map/ppermute | solution.py:64
  105.3 19.6 %collective-permute-start.2 = (f32[144,512]{1,0:T(8,128)S(1)}, f32[144,512]{1,0:T(8,128)S(1)}, u32[]{:S(2)}, u32[]{:S(2)}) collective-permute-start(f32[144,512]{1,0:T(8,128)S(1)} %fusion), channel_id=1, source_target_pairs={{0,4},{4,0},{1,5},{5,1},{2,6},{6,2},{3,7},{7,3},{8,12},{12,8},{9,1... | collective-permute-start | bytes 884744 | tf_op jit(solution)/shard_map/ppermute | solution.py:64
  124.9 8.4 %collective-permute-start.3 = (f32[144,512]{1,0:T(8,128)S(1)}, f32[144,512]{1,0:T(8,128)S(1)}, u32[]{:S(2)}, u32[]{:S(2)}) collective-permute-start(f32[144,512]{1,0:T(8,128)S(1)} %get-tuple-element.7), channel_id=1, source_target_pairs={{128,0},{256,128},{384,256},{4,384},{132,4},{260,132},{388,260},{0... | collective-permute-start | bytes 884744 | tf_op jit(solution)/shard_map/ppermute | solution.py:77
  127.7 10.4 %collective-permute-start.4 = (f32[144,512]{1,0:T(8,128)S(1)}, f32[144,512]{1,0:T(8,128)S(1)}, u32[]{:S(2)}, u32[]{:S(2)}) collective-permute-start(f32[144,512]{1,0:T(8,128)S(1)} %get-tuple-element.7), channel_id=1, source_target_pairs={{256,0},{388,128},{4,256},{128,384},{260,4},{384,132},{0,260},{132... | collective-permute-start | bytes 884744 | tf_op jit(solution)/shard_map/ppermute | solution.py:77
  130.3 15.0 %collective-permute-start.5 = (f32[144,512]{1,0:T(8,128)S(1)}, f32[144,512]{1,0:T(8,128)S(1)}, u32[]{:S(2)}, u32[]{:S(2)}) collective-permute-start(f32[144,512]{1,0:T(8,128)S(1)} %get-tuple-element.7), channel_id=1, source_target_pairs={{388,0},{0,128},{128,256},{256,384},{384,4},{4,132},{132,260},{260... | collective-permute-start | bytes 884744 | tf_op jit(solution)/shard_map/ppermute | solution.py:77
  153.6 1.6 %copy-start.5 = (bf16[288,1,1,128]{3,0,2,1:T(8,128)(2,1)S(1)}, bf16[288,1,1,128]{3,0,2,1:T(8,128)(2,1)}, u32[]{:S(2)}) copy-start(bf16[288,1,1,128]{3,0,2,1:T(8,128)(2,1)} %get-tuple-element.12) | copy-start | bytes 221188

commit v15 on v14

--- a/solution.py
+++ b/solution.py
@@ -232,7 +232,13 @@
     layout = (lax.axis_size("ylo"), outgoing.shape[0], geometry.shape[0], half)
     off_pair, parts = chip_project(layout, recv, own, full_flat, probe_flat, basis_flat)
     count = lax.axis_size("ylo")
-    mine = exchange(parts, "ylo").reshape(count, -1, basis_width).sum(axis=0)
+    chip = lax.axis_index("ylo")
+    pieces = parts.reshape(count, -1, basis_width)
+    mine = lax.dynamic_index_in_dim(pieces, chip, keepdims=False)
+    for step in range(1, count):
+        outgoing = lax.dynamic_index_in_dim(pieces, (chip + step) % count, keepdims=False)
+        pairs = [(source, (source + step) % count) for source in range(count)]
+        mine = mine + lax.ppermute(outgoing, "ylo", pairs)
     top = climb_rows(mine, level_mats)
     half_rows = ring_gather(top).reshape(-1, basis_width)
     sent_off = off_pair[1].astype(jnp.float32).reshape(-1, basis_width)

time: 156 us -> 157 us (level)
  blocking collectives: 48.9 us -> 16.9 us
  starting transfers between devices: 27.2 us -> 46.9 us
  waiting for transfers between devices: 63.2 us -> 74.1 us
    all_to_all x3 -> x2, blocking collectives: 48.9 us -> 16.9 us  [exchange(): return lax.all_to_all(value, axis, 0, 0, tiled=True)]
    ppermute x0 -> x3, waiting for transfers between devices: none -> 20.2 us  [shards(): mine = mine + lax.ppermute(outgoing, 'ylo', pairs)]
    ppermute x3, starting transfers between devices: 7.7 us -> 20 us  [ring_shift(): return lax.ppermute(rows, ('ylo', 'lyhi'), pairs)]
    ppermute x3, waiting for transfers between devices: 24.4 us -> 16.6 us  [climb_rows(): other = lax.ppermute(projected, LEVEL_AXES[tree_level], [(0, 1), (1, 0)])]
    ppermute x0 -> x3, starting transfers between devices: none -> 7.2 us  [shards(): mine = mine + lax.ppermute(outgoing, 'ylo', pairs)]
  transfers between devices with their start and end apart: 7 -> 10, of which waited for: 6 -> 8; matrix products, arithmetic and copies ran while one was open for 1% -> 1% of each run, Pallas kernels for 0% -> 0%
where the time goes in v15:
time: 157 us
  waiting for transfers between devices  74.1 us (47%)
  starting transfers between devices  46.9 us (30%)
  blocking collectives  16.9 us (11%)
  Pallas kernels  5.33 us (3%)
  local copies, waits for them, and re-layouts  5.18 us (3%)
  other arithmetic  5 us (3%)
  matrix products  2.18 us (1%)
    all_to_all x1, waiting for transfers between devices, exchange(): return lax.all_to_all(value, axis, 0, 0, tiled=True)  26.8 us
    ppermute x3, waiting for transfers between devices, shards(): mine = mine + lax.ppermute(outgoing, 'ylo', pairs)  20.2 us
    ppermute x3, starting transfers between devices, ring_shift(): return lax.ppermute(rows, ('ylo', 'lyhi'), pairs)  20 us
    all_to_all x2, blocking collectives, exchange(): return lax.all_to_all(value, axis, 0, 0, tiled=True)  16.9 us
    ppermute x3, waiting for transfers between devices, climb_rows(): other = lax.ppermute(projected, LEVEL_AXES[tree_level], [(0, 1), (1, 0)])  16.6 us
    ppermute x3, starting transfers between devices, climb_rows(): other = lax.ppermute(projected, LEVEL_AXES[tree_level], [(0, 1), (1, 0)])  14.3 us
    ppermute x3, waiting for transfers between devices, ring_shift(): return lax.ppermute(rows, ('ylo', 'lyhi'), pairs)  10.5 us
    ppermute x3, starting transfers between devices, shards(): mine = mine + lax.ppermute(outgoing, 'ylo', pairs)  7.2 us
  transfers between devices with their start and end apart: 10, of which 8 were waited for; matrix products, arithmetic and copies ran while one was open for 1% of the time, Pallas kernels for 0%

profile of v15, /device:TPU:1, one launch (start us, length us, event | category | flops | bytes accessed | tf_op | source)
XLA Modules:
  0.0 156.8 jit_solution(14035512895786193501)
XLA Ops:
  0.6 0.7 copy.16
  1.3 0.7 convert_bitcast_fusion
  2.0 0.9 fusion.15
  2.9 0.0 copy-start.7
  2.9 0.0 copy-start.4
  3.0 0.8 concatenate.47
  3.8 0.0 copy-start.1
  3.8 0.0 copy-start.3
  3.8 1.1 broadcast_in_dim.9
  4.9 5.4 %all-to-all-start = ((f32[4,584,128]{2,1,0:T(8,128)}), f32[4,584,128]{2,1,0:T(8,128)S(1)}, u32[]{:S(2)}, u32[]{:S(2)}) async-start(f32[4,584,128]{2,1,0:T(8,128)} %broadcast_in_dim.9), calls=%async_computation | async-start | bytes 2392064 | tf_op jit(solution)/shard_map/all_to_all | solution.py:92
  10.3 0.0 copy-done.7
  10.3 0.1 copy.14.own_ref
  10.4 0.0 copy-done.4
  10.4 0.0 copy-start.2
  10.4 0.1 reshape.162
  10.6 0.0 copy-done.1
  10.6 0.0 copy-done.3
  10.7 26.8 %all-to-all-done = f32[4,584,128]{2,1,0:T(8,128)S(1)} async-done(((f32[4,584,128]{2,1,0:T(8,128)}), f32[4,584,128]{2,1,0:T(8,128)S(1)}, u32[]{:S(2)}, u32[]{:S(2)}) %all-to-all-start) | async-done | bytes 1196064 | tf_op jit(solution)/shard_map/all_to_all | solution.py:92
  37.5 0.1 constant_dynamic-update-slice_fusion.3
  37.6 0.1 constant_dynamic-update-slice_fusion.1
  37.7 0.0 copy-done.2
  37.8 10.0 %all_to_all.24.recv_ref = f32[2,3552,128]{2,1,0:T(8,128)} all-to-all(f32[2,3552,128]{2,1,0:T(8,128)S(1)} %bitcast.75), channel_id=1, replica_groups=mesh['ylo'=4,'core'=2,'lz'=8,'lyhi'=2,'lx1'=2,'lx0'=2] {'core'}, dimensions={0} | all-to-all | bytes 7274496 | tf_op jit(solution)/shard_map/all_to_all | solution.py:92
  47.8 0.0 copy-start
  47.8 5.3 %shard_map.86 = (bf16[2,288,128]{2,1,0:T(8,128)(2,1)}, f32[576,512]{1,0:T(8,128)}) custom-call(f32[2,3552,128]{2,1,0:T(8,128)} %all_to_all.24.recv_ref, f32[128,8]{1,0:T(8,128)} %copy-done.2, bf16[576,128]{1,0:T(8,128)(2,1)} %bitcast.83, bf16[576,128]{1,0:T(8,128)(2,1)} %bitcast.79, bf16[128,512]{1,0:T(8,128)(2,1)} %bitcast.84), custom_call_target="tpu_custom_call" | custom-call | flops 339738624 | bytes 5242880 | tf_op jit(solution)/shard_map/pallas_call | solution.py:180
  53.2 1.2 dynamic-slice_bitcast_fusion.2
  54.4 3.1 %collective-permute-start.2 = (f32[144,512]{1,0:T(8,128)S(1)}, f32[144,512]{1,0:T(8,128)S(1)}, u32[]{:S(2)}, u32[]{:S(2)}) collective-permute-start(f32[144,512]{1,0:T(8,128)S(1)} %get-tuple-element.13), channel_id=1, source_target_pairs={{0,384},{128,0},{256,128},{384,256},{1,385},{129,1},{257,129},{385... | collective-permute-start | bytes 884744 | tf_op jit(solution)/shard_map/ppermute | solution.py:241
  57.5 1.9 %collective-permute-start.1 = (f32[144,512]{1,0:T(8,128)S(1)}, f32[144,512]{1,0:T(8,128)S(1)}, u32[]{:S(2)}, u32[]{:S(2)}) collective-permute-start(f32[144,512]{1,0:T(8,128)S(1)} %get-tuple-element.14), channel_id=1, source_target_pairs={{0,256},{128,384},{256,0},{384,128},{1,257},{129,385},{257,1},{385... | collective-permute-start | bytes 884744 | tf_op jit(solution)/shard_map/ppermute | solution.py:241
  59.4 2.2 %collective-permute-start = (f32[144,512]{1,0:T(8,128)S(1)}, f32[144,512]{1,0:T(8,128)S(1)}, u32[]{:S(2)}, u32[]{:S(2)}) collective-permute-start(f32[144,512]{1,0:T(8,128)S(1)} %get-tuple-element.12), channel_id=1, source_target_pairs={{0,128},{128,256},{256,384},{384,0},{1,129},{129,257},{257,385},{3... | collective-permute-start | bytes 884744 | tf_op jit(solution)/shard_map/ppermute | solution.py:241
  61.6 4.5 %collective-permute-done.2 = f32[144,512]{1,0:T(8,128)S(1)} collective-permute-done((f32[144,512]{1,0:T(8,128)S(1)}, f32[144,512]{1,0:T(8,128)S(1)}, u32[]{:S(2)}, u32[]{:S(2)}) %collective-permute-start.2) | collective-permute-done | bytes 294944 | tf_op jit(solution)/shard_map/ppermute | solution.py:241
  66.1 15.7 %collective-permute-done.1 = f32[144,512]{1,0:T(8,128)S(1)} collective-permute-done((f32[144,512]{1,0:T(8,128)S(1)}, f32[144,512]{1,0:T(8,128)S(1)}, u32[]{:S(2)}, u32[]{:S(2)}) %collective-permute-start.1) | collective-permute-done | bytes 294944 | tf_op jit(solution)/shard_map/ppermute | solution.py:241
  81.8 0.0 collective-permute-done
  81.8 0.0 copy-done
  81.8 1.4 fusion.4
  83.2 0.0 copy-start.6
  83.2 3.3 %collective-permute-start.3 = (f32[144,512]{1,0:T(8,128)S(1)}, f32[144,512]{1,0:T(8,128)S(1)}, u32[]{:S(2)}, u32[]{:S(2)}) collective-permute-start(f32[144,512]{1,0:T(8,128)S(1)} %fusion.4), channel_id=1, source_target_pairs={{0,1},{1,0},{2,3},{3,2},{4,5},{5,4},{6,7},{7,6},{8,9},{9,8},{10,11... | collective-permute-start | bytes 884744 | tf_op jit(solution)/shard_map/ppermute | solution.py:64
  86.5 6.3 %collective-permute-done.3 = f32[144,512]{1,0:T(8,128)S(1)} collective-permute-done((f32[144,512]{1,0:T(8,128)S(1)}, f32[144,512]{1,0:T(8,128)S(1)}, u32[]{:S(2)}, u32[]{:S(2)}) %collective-permute-start.3) | collective-permute-done | bytes 294944 | tf_op jit(solution)/shard_map/ppermute | solution.py:64
  92.7 0.4 fusion.2
  93.1 4.7 %collective-permute-start.4 = (f32[144,512]{1,0:T(8,128)S(1)}, f32[144,512]{1,0:T(8,128)S(1)}, u32[]{:S(2)}, u32[]{:S(2)}) collective-permute-start(f32[144,512]{1,0:T(8,128)S(1)} %fusion.2), channel_id=1, source_target_pairs={{0,2},{2,0},{1,3},{3,1},{4,6},{6,4},{5,7},{7,5},{8,10},{10,8},{9,1... | collective-permute-start | bytes 884744 | tf_op jit(solution)/shard_map/ppermute | solution.py:64
  97.8 5.3 %collective-permute-done.4 = f32[144,512]{1,0:T(8,128)S(1)} collective-permute-done((f32[144,512]{1,0:T(8,128)S(1)}, f32[144,512]{1,0:T(8,128)S(1)}, u32[]{:S(2)}, u32[]{:S(2)}) %collective-permute-start.4) | collective-permute-done | bytes 294944 | tf_op jit(solution)/shard_map/ppermute | solution.py:64
  103.1 0.4 fusion
  103.5 6.4 %collective-permute-start.5 = (f32[144,512]{1,0:T(8,128)S(1)}, f32[144,512]{1,0:T(8,128)S(1)}, u32[]{:S(2)}, u32[]{:S(2)}) collective-permute-start(f32[144,512]{1,0:T(8,128)S(1)} %fusion), channel_id=1, source_target_pairs={{0,4},{4,0},{1,5},{5,1},{2,6},{6,2},{3,7},{7,3},{8,12},{12,8},{9,1... | collective-permute-start | bytes 884744 | tf_op jit(solution)/shard_map/ppermute | solution.py:64
  109.9 5.0 %collective-permute-done.5 = f32[144,512]{1,0:T(8,128)S(1)} collective-permute-done((f32[144,512]{1,0:T(8,128)S(1)}, f32[144,512]{1,0:T(8,128)S(1)}, u32[]{:S(2)}, u32[]{:S(2)}) %collective-permute-start.5) | collective-permute-done | bytes 294944 | tf_op jit(solution)/shard_map/ppermute | solution.py:64
  114.9 4.0 %collective-permute-start.6 = (f32[144,512]{1,0:T(8,128)S(1)}, f32[144,512]{1,0:T(8,128)S(1)}, u32[]{:S(2)}, u32[]{:S(2)}) collective-permute-start(f32[144,512]{1,0:T(8,128)S(1)} %get-tuple-element.7), channel_id=1, source_target_pairs={{128,0},{256,128},{384,256},{4,384},{132,4},{260,132},{388,260},{0... | collective-permute-start | bytes 884744 | tf_op jit(solution)/shard_map/ppermute | solution.py:77
  119.0 14.1 %collective-permute-start.7 = (f32[144,512]{1,0:T(8,128)S(1)}, f32[144,512]{1,0:T(8,128)S(1)}, u32[]{:S(2)}, u32[]{:S(2)}) collective-permute-start(f32[144,512]{1,0:T(8,128)S(1)} %get-tuple-element.7), channel_id=1, source_target_pairs={{256,0},{388,128},{4,256},{128,384},{260,4},{384,132},{0,260},{132... | collective-permute-start | bytes 884744 | tf_op jit(solution)/shard_map/ppermute | solution.py:77
  133.1 0.0 copy-done.6
  133.1 0.6 slice_bitcast_fusion.4
  133.8 1.9 %collective-permute-start.8 = (f32[144,512]{1,0:T(8,128)S(1)}, f32[144,512]{1,0:T(8,128)S(1)}, u32[]{:S(2)}, u32[]{:S(2)}) collective-permute-start(f32[144,512]{1,0:T(8,128)S(1)} %get-tuple-element.7), channel_id=1, source_target_pairs={{388,0},{0,128},{128,256},{256,384},{384,4},{4,132},{132,260},{260... | collective-permute-start | bytes 884744 | tf_op jit(solution)/shard_map/ppermute | solution.py:77
  135.7 0.0 collective-permute-done.6
  135.7 6.3 %collective-permute-done.7 = f32[144,512]{1,0:T(8,128)S(1)} collective-permute-done((f32[144,512]{1,0:T(8,128)S(1)}, f32[144,512]{1,0:T(8,128)S(1)}, u32[]{:S(2)}, u32[]{:S(2)}) %collective-permute-start.7) | collective-permute-done | bytes 294944 | tf_op jit(solution)/shard_map/ppermute | solution.py:77
  142.0 4.2 %collective-permute-done.8 = f32[144,512]{1,0:T(8,128)S(1)} collective-permute-done((f32[144,512]{1,0:T(8,128)S(1)}, f32[144,512]{1,0:T(8,128)S(1)}, u32[]{:S(2)}, u32[]{:S(2)}) %collective-permute-start.8) | collective-permute-done | bytes 294944 | tf_op jit(solution)/shard_map/ppermute | solution.py:77
  146.4 0.1 constant_dynamic-slice_fusion
  146.5 0.1 pad_maximum_fusion
  146.7 0.3 broadcast_in_dim.20
  147.0 0.0 copy-start.5
  147.0 6.9 %all_to_all.25 = f32[2,648,512]{2,1,0:T(8,128)S(1)} all-to-all(f32[2,648,512]{2,1,0:T(8,128)S(1)} %broadcast_in_dim.20), channel_id=1, replica_groups=mesh['ylo'=4,'core'=2,'lz'=8,'lyhi'=2,'lx1'=2,'lx0'=2] {'core'}, dimensions={0} | all-to-all | bytes 5308416 | tf_op jit(solution)/shard_map/all_to_all | solution.py:92
  154.0 0.1 concatenate.53
  154.0 0.0 copy-done.5
  154.0 0.7 maximum_select_fusion
  154.7 0.2 slice_bitcast_fusion.3
  154.9 0.2 maximum_bitcast_fusion.1
  155.2 1.6 %maximum_bitcast_fusion = f32[1,2,576,512]{3,2,1,0:T(8,128)} fusion(f32[1,576,512]{2,1,0:T(8,128)S(1)} %get-tuple-element.18, f32[1,576,512]{2,1,0:T(8,128)S(1)} %get-tuple-element.17), kind=kLoop, calls=%fused_computation | loop fusion | flops 589824 | bytes 4718592 | tf_op jit(solution)/shard_map/broadcast_in_dim | solution.py:247
  (23 shorter events, 0.4 us)
Async XLA Ops:
  2.9 7.4 %copy-start.7 = (f32[1,1,128]{2,1,0:T(1,128)S(1)}, f32[1,1,128]{2,1,0:T(1,128)}, u32[]{:S(2)}) copy-start(f32[1,1,128]{2,1,0:T(1,128)} %param.8) | copy-start | bytes 1540
  2.9 7.5 %copy-start.4 = (bf16[1,1,128,512]{3,2,1,0:T(8,128)(2,1)S(1)}, bf16[1,1,128,512]{3,2,1,0:T(8,128)(2,1)}, u32[]{:S(2)}) copy-start(bf16[1,1,128,512]{3,2,1,0:T(8,128)(2,1)} %param.12) | copy-start | bytes 393220
  3.8 6.8 %copy-start.1 = (bf16[576,1,1,128]{3,0,2,1:T(8,128)(2,1)S(1)}, bf16[576,1,1,128]{3,0,2,1:T(8,128)(2,1)}, u32[]{:S(2)}) copy-start(bf16[576,1,1,128]{3,0,2,1:T(8,128)(2,1)} %param.9) | copy-start | bytes 442372
  3.8 6.8 %copy-start.3 = (bf16[576,1,1,128]{3,0,2,1:T(8,128)(2,1)S(1)}, bf16[576,1,1,128]{3,0,2,1:T(8,128)(2,1)}, u32[]{:S(2)}) copy-start(bf16[576,1,1,128]{3,0,2,1:T(8,128)(2,1)} %param.10) | copy-start | bytes 442372
  4.9 32.6 %all-to-all-start = ((f32[4,584,128]{2,1,0:T(8,128)}), f32[4,584,128]{2,1,0:T(8,128)S(1)}, u32[]{:S(2)}, u32[]{:S(2)}) async-start(f32[4,584,128]{2,1,0:T(8,128)} %broadcast_in_dim.9), calls=%async_computation | async-start | bytes 2392064 | tf_op jit(solution)/shard_map/all_to_all | solution.py:92
  10.4 27.3 %copy-start.2 = (f32[128,8]{1,0:T(8,128)}, f32[128,8]{1,0:T(8,128)S(1)}, u32[]{:S(2)}) copy-start(f32[128,8]{1,0:T(8,128)S(1)} %copy.14.own_ref) | copy-start | bytes 12292
  47.8 34.0 %copy-start = (bf16[1,3,512,512]{3,2,1,0:T(8,128)(2,1)S(1)}, bf16[1,3,512,512]{3,2,1,0:T(8,128)(2,1)}, u32[]{:S(2)}) copy-start(bf16[1,3,512,512]{3,2,1,0:T(8,128)(2,1)} %param.13) | copy-start | bytes 4718596
  54.4 11.8 %collective-permute-start.2 = (f32[144,512]{1,0:T(8,128)S(1)}, f32[144,512]{1,0:T(8,128)S(1)}, u32[]{:S(2)}, u32[]{:S(2)}) collective-permute-start(f32[144,512]{1,0:T(8,128)S(1)} %get-tuple-element.13), channel_id=1, source_target_pairs={{0,384},{128,0},{256,128},{384,256},{1,385},{129,1},{257,129},{385... | collective-permute-start | bytes 884744 | tf_op jit(solution)/shard_map/ppermute | solution.py:241
  57.5 24.4 %collective-permute-start.1 = (f32[144,512]{1,0:T(8,128)S(1)}, f32[144,512]{1,0:T(8,128)S(1)}, u32[]{:S(2)}, u32[]{:S(2)}) collective-permute-start(f32[144,512]{1,0:T(8,128)S(1)} %get-tuple-element.14), channel_id=1, source_target_pairs={{0,256},{128,384},{256,0},{384,128},{1,257},{129,385},{257,1},{385... | collective-permute-start | bytes 884744 | tf_op jit(solution)/shard_map/ppermute | solution.py:241
  59.4 22.4 %collective-permute-start = (f32[144,512]{1,0:T(8,128)S(1)}, f32[144,512]{1,0:T(8,128)S(1)}, u32[]{:S(2)}, u32[]{:S(2)}) collective-permute-start(f32[144,512]{1,0:T(8,128)S(1)} %get-tuple-element.12), channel_id=1, source_target_pairs={{0,128},{128,256},{256,384},{384,0},{1,129},{129,257},{257,385},{3... | collective-permute-start | bytes 884744 | tf_op jit(solution)/shard_map/ppermute | solution.py:241
  83.2 49.9 %copy-start.6 = (bf16[2,288,128]{2,1,0:T(8,128)(2,1)S(1)}, bf16[2,288,128]{2,1,0:T(8,128)(2,1)}, u32[]{:S(2)}) copy-start(bf16[2,288,128]{2,1,0:T(8,128)(2,1)} %get-tuple-element.4) | copy-start | bytes 442372
  83.2 9.5 %collective-permute-start.3 = (f32[144,512]{1,0:T(8,128)S(1)}, f32[144,512]{1,0:T(8,128)S(1)}, u32[]{:S(2)}, u32[]{:S(2)}) collective-permute-start(f32[144,512]{1,0:T(8,128)S(1)} %fusion.4), channel_id=1, source_target_pairs={{0,1},{1,0},{2,3},{3,2},{4,5},{5,4},{6,7},{7,6},{8,9},{9,8},{10,11... | collective-permute-start | bytes 884744 | tf_op jit(solution)/shard_map/ppermute | solution.py:64
  93.1 10.0 %collective-permute-start.4 = (f32[144,512]{1,0:T(8,128)S(1)}, f32[144,512]{1,0:T(8,128)S(1)}, u32[]{:S(2)}, u32[]{:S(2)}) collective-permute-start(f32[144,512]{1,0:T(8,128)S(1)} %fusion.2), channel_id=1, source_target_pairs={{0,2},{2,0},{1,3},{3,1},{4,6},{6,4},{5,7},{7,5},{8,10},{10,8},{9,1... | collective-permute-start | bytes 884744 | tf_op jit(solution)/shard_map/ppermute | solution.py:64
  103.5 11.4 %collective-permute-start.5 = (f32[144,512]{1,0:T(8,128)S(1)}, f32[144,512]{1,0:T(8,128)S(1)}, u32[]{:S(2)}, u32[]{:S(2)}) collective-permute-start(f32[144,512]{1,0:T(8,128)S(1)} %fusion), channel_id=1, source_target_pairs={{0,4},{4,0},{1,5},{5,1},{2,6},{6,2},{3,7},{7,3},{8,12},{12,8},{9,1... | collective-permute-start | bytes 884744 | tf_op jit(solution)/shard_map/ppermute | solution.py:64
  114.9 20.8 %collective-permute-start.6 = (f32[144,512]{1,0:T(8,128)S(1)}, f32[144,512]{1,0:T(8,128)S(1)}, u32[]{:S(2)}, u32[]{:S(2)}) collective-permute-start(f32[144,512]{1,0:T(8,128)S(1)} %get-tuple-element.7), channel_id=1, source_target_pairs={{128,0},{256,128},{384,256},{4,384},{132,4},{260,132},{388,260},{0... | collective-permute-start | bytes 884744 | tf_op jit(solution)/shard_map/ppermute | solution.py:77
  119.0 23.0 %collective-permute-start.7 = (f32[144,512]{1,0:T(8,128)S(1)}, f32[144,512]{1,0:T(8,128)S(1)}, u32[]{:S(2)}, u32[]{:S(2)}) collective-permute-start(f32[144,512]{1,0:T(8,128)S(1)} %get-tuple-element.7), channel_id=1, source_target_pairs={{256,0},{388,128},{4,256},{128,384},{260,4},{384,132},{0,260},{132... | collective-permute-start | bytes 884744 | tf_op jit(solution)/shard_map/ppermute | solution.py:77
  133.8 12.5 %collective-permute-start.8 = (f32[144,512]{1,0:T(8,128)S(1)}, f32[144,512]{1,0:T(8,128)S(1)}, u32[]{:S(2)}, u32[]{:S(2)}) collective-permute-start(f32[144,512]{1,0:T(8,128)S(1)} %get-tuple-element.7), channel_id=1, source_target_pairs={{388,0},{0,128},{128,256},{256,384},{384,4},{4,132},{132,260},{260... | collective-permute-start | bytes 884744 | tf_op jit(solution)/shard_map/ppermute | solution.py:77
  147.0 7.0 %copy-start.5 = (bf16[288,1,1,128]{3,0,2,1:T(8,128)(2,1)S(1)}, bf16[288,1,1,128]{3,0,2,1:T(8,128)(2,1)}, u32[]{:S(2)}) copy-start(bf16[288,1,1,128]{3,0,2,1:T(8,128)(2,1)} %get-tuple-element.15) | copy-start | bytes 221188

commit v16 on v14

--- a/solution.py
+++ b/solution.py
@@ -112,7 +112,7 @@
     return gather_blocks(mirrored(chips).reshape(-1, rows.shape[1]), "core")
 
 
-def chip_kernel(layout, recv_ref, own_ref, full_ref, probe_ref, basis_ref, off_ref, parts_ref):
+def chip_kernel(layout, recv_ref, extra_ref, own_ref, full_ref, probe_ref, basis_ref, off_ref, parts_ref):
     blocks_per_core, block_rows, geometry_rows, half = layout
     panels = own_ref.shape[0]
     width = basis_ref.shape[1]
@@ -121,16 +121,16 @@
     base = blocks_per_core * block_rows
     row0 = pl.multiple_of(core * half, 8)
     lanes = lax.broadcasted_iota(jnp.int32, (panels, panels), 1).astype(jnp.float32)
-    targets = (own_ref[...], recv_ref[other, base : base + panels, :])
+    targets = (own_ref[...], extra_ref[0:panels, :])
     sketch_rows = (
         full_ref[pl.ds(row0, half), :].astype(jnp.float32),
-        recv_ref[other, base + panels : base + panels + half, :],
+        extra_ref[panels : panels + half, :],
     )
     probe_rows = (
         probe_ref[pl.ds(row0, half), :],
-        recv_ref[other, base + panels + half : base + panels + 2 * half, :].astype(jnp.bfloat16),
-    )
-    basis_start = base + panels + 2 * half
+        extra_ref[panels + half : panels + 2 * half, :].astype(jnp.bfloat16),
+    )
+    basis_start = panels + 2 * half
     for block in range(2):
         target = targets[block]
         near = jnp.zeros((half, panels), jnp.float32)
@@ -164,19 +164,19 @@
             else:
                 for quarter in range(width // panels):
                     first = basis_start + quarter * panels
-                    basis = recv_ref[other, first : first + panels, :].astype(jnp.bfloat16)
+                    basis = extra_ref[first : first + panels, :].astype(jnp.bfloat16)
                     columns = slice(quarter * panels, (quarter + 1) * panels)
                     parts_ref[rows, columns] = parts_ref[rows, columns] + jnp.dot(
                         ordered, basis, preferred_element_type=jnp.float32
                     )
 
 
-def chip_project(layout, recv, own, full, probe, basis):
+def chip_project(layout, recv, extra, own, full, probe, basis):
     probe_count, panels = full.shape
     half = probe_count // 2
     width = basis.shape[1]
     flops = 2 * half * panels * (2 * 2 * layout[0] * panels + 4 * panels + 4 * width)
-    bytes_accessed = 4 * recv.size + 2 * (2 * full.size + basis.size) + 4 * probe_count * width
+    bytes_accessed = 4 * (recv.size + extra.size) + 2 * (2 * full.size + basis.size) + 4 * probe_count * width
     return pl.pallas_call(
         functools.partial(chip_kernel, layout),
         out_shape=(
@@ -186,7 +186,7 @@
         cost_estimate=pl.CostEstimate(
             flops=flops, transcendentals=4 * layout[0] * panels * panels, bytes_accessed=bytes_accessed
         ),
-    )(recv, own, full, probe, basis)
+    )(recv, extra, own, full, probe, basis)
 
 
 def shards(positions, panel_areas, probe_cols, full_sketch, tree_order, leaf_basis, transfer_mats):
@@ -215,22 +215,20 @@
     ).reshape(-1, panels)
     full_wide = full_flat.astype(jnp.float32)
     probe_wide = probe_flat.astype(jnp.float32)
-    chunks = [
-        jnp.concatenate(
-            [
-                chip_blocks,
-                own_padded,
-                full_wide[index * half : (index + 1) * half],
-                probe_wide[index * half : (index + 1) * half],
-                basis_view,
-            ],
-            axis=0,
-        )
-        for index in range(2)
-    ]
-    recv = exchange(jnp.concatenate(chunks, axis=0), "core").reshape(2, -1, panels)
+    other_half = (1 - lax.axis_index("core")) * half
+    extra = jnp.concatenate(
+        [
+            own_padded,
+            lax.dynamic_slice_in_dim(full_wide, other_half, half, axis=0),
+            lax.dynamic_slice_in_dim(probe_wide, other_half, half, axis=0),
+            basis_view,
+        ],
+        axis=0,
+    )
+    extra = lax.ppermute(extra, "core", [(0, 1), (1, 0)])
+    recv = gather_blocks(chip_blocks, "core").reshape(2, -1, panels)
     layout = (lax.axis_size("ylo"), outgoing.shape[0], geometry.shape[0], half)
-    off_pair, parts = chip_project(layout, recv, own, full_flat, probe_flat, basis_flat)
+    off_pair, parts = chip_project(layout, recv, extra, own, full_flat, probe_flat, basis_flat)
     count = lax.axis_size("ylo")
     mine = exchange(parts, "ylo").reshape(count, -1, basis_width).sum(axis=0)
     top = climb_rows(mine, level_mats)

time: 156 us -> 158 us (1.013)
  starting transfers between devices: 27.2 us -> 40.6 us
  blocking collectives: 48.9 us -> 39.1 us
  waiting for transfers between devices: 63.2 us -> 58 us
  local copies, waits for them, and re-layouts: 3.98 us -> 6.77 us
    all_to_all x3 -> x2, blocking collectives: 48.9 us -> 39.1 us  [exchange(): return lax.all_to_all(value, axis, 0, 0, tiled=True)]
    ppermute x0 -> x1, starting transfers between devices: none -> 6.91 us  [shards(): extra = lax.ppermute(extra, 'core', [(0, 1), (1, 0)])]
    all_to_all x1 -> x2, starting transfers between devices: 5.42 us -> 11.9 us  [exchange(): return lax.all_to_all(value, axis, 0, 0, tiled=True)]
    all_to_all x1 -> x2, waiting for transfers between devices: 26.8 us -> 21.7 us  [exchange(): return lax.all_to_all(value, axis, 0, 0, tiled=True)]
    broadcast_in_dim x2 -> x3, local copies, waits for them, and re-layouts: 1.42 us -> 3.01 us  [gather_blocks(): copies = jnp.broadcast_to(block[None], (count,) + block.shape)]
  transfers between devices with their start and end apart: 7 -> 9, of which waited for: 6 -> 7; matrix products, arithmetic and copies ran while one was open for 1% -> 2% of each run, Pallas kernels for 0% -> 0%
where the time goes in v16:
time: 158 us
  waiting for transfers between devices  58 us (37%)
  starting transfers between devices  40.6 us (26%)
  blocking collectives  39.1 us (25%)
  local copies, waits for them, and re-layouts  6.77 us (4%)
  other arithmetic  5.99 us (4%)
  Pallas kernels  5 us (3%)
    all_to_all x2, blocking collectives, exchange(): return lax.all_to_all(value, axis, 0, 0, tiled=True)  39.1 us
    ppermute x3, waiting for transfers between devices, climb_rows(): other = lax.ppermute(projected, LEVEL_AXES[tree_level], [(0, 1), (1, 0)])  24.4 us
    all_to_all x2, waiting for transfers between devices, exchange(): return lax.all_to_all(value, axis, 0, 0, tiled=True)  21.7 us
    ppermute x3, starting transfers between devices, climb_rows(): other = lax.ppermute(projected, LEVEL_AXES[tree_level], [(0, 1), (1, 0)])  14.1 us
    ppermute x3, waiting for transfers between devices, ring_shift(): return lax.ppermute(rows, ('ylo', 'lyhi'), pairs)  11.9 us
    all_to_all x2, starting transfers between devices, exchange(): return lax.all_to_all(value, axis, 0, 0, tiled=True)  11.9 us
    ppermute x3, starting transfers between devices, ring_shift(): return lax.ppermute(rows, ('ylo', 'lyhi'), pairs)  7.69 us
    ppermute x1, starting transfers between devices, shards(): extra = lax.ppermute(extra, 'core', [(0, 1), (1, 0)])  6.91 us
  transfers between devices with their start and end apart: 9, of which 7 were waited for; matrix products, arithmetic and copies ran while one was open for 2% of the time, Pallas kernels for 0%

profile of v16, /device:TPU:1, one launch (start us, length us, event | category | flops | bytes accessed | tf_op | source)
XLA Modules:
  0.0 157.7 jit_solution(10730731391711130531)
XLA Ops:
  0.6 0.7 convert_bitcast_fusion
  1.3 0.7 copy.15
  2.0 0.9 fusion.13
  2.9 0.0 copy-start.9
  2.9 0.0 copy-start.5
  3.0 0.8 concatenate.47
  3.8 0.0 copy-start.6
  3.8 0.0 copy-start.2
  3.8 1.1 broadcast_in_dim.13
  4.9 5.4 %all-to-all-start = ((f32[4,584,128]{2,1,0:T(8,128)}), f32[4,584,128]{2,1,0:T(8,128)S(1)}, u32[]{:S(2)}, u32[]{:S(2)}) async-start(f32[4,584,128]{2,1,0:T(8,128)} %broadcast_in_dim.13), calls=%async_computation | async-start | bytes 2392064 | tf_op jit(solution)/shard_map/all_to_all | solution.py:92
  10.3 0.0 copy-done.9
  10.3 0.1 copy.13.own_ref
  10.4 0.0 copy-done.5
  10.4 0.0 copy-start.4
  10.4 0.1 reshape.166
  10.6 0.0 copy-done.6
  10.6 0.0 copy-done.2
  10.7 0.9 fusion.1
  11.6 6.9 %collective-permute-start = (f32[1216,128]{1,0:T(8,128)}, f32[1216,128]{1,0:T(8,128)S(1)}, u32[]{:S(2)}, u32[]{:S(2)}) collective-permute-start(f32[1216,128]{1,0:T(8,128)} %fusion.1), channel_id=1, source_target_pairs={{0,64},{64,0},{1,65},{65,1},{2,66},{66,2},{3,67},{67,3},{4,68},{68... | collective-permute-start | bytes 1867784 | tf_op jit(solution)/shard_map/ppermute | solution.py:228
  18.5 19.0 %all-to-all-done = f32[4,584,128]{2,1,0:T(8,128)S(1)} async-done(((f32[4,584,128]{2,1,0:T(8,128)}), f32[4,584,128]{2,1,0:T(8,128)S(1)}, u32[]{:S(2)}, u32[]{:S(2)}) %all-to-all-start) | async-done | bytes 1196064 | tf_op jit(solution)/shard_map/all_to_all | solution.py:92
  37.5 1.6 %broadcast_in_dim.29 = f32[2,2336,128]{2,1,0:T(8,128)} broadcast(f32[2336,128]{1,0:T(8,128)S(1)} %bitcast.60), dimensions={1,2} | broadcast | bytes 3588096 | tf_op jit(solution)/shard_map/broadcast_in_dim | solution.py:97
  39.1 0.0 copy-done.4
  39.1 6.5 %all-to-all-start.1 = ((f32[2,2336,128]{2,1,0:T(8,128)}), f32[2,2336,128]{2,1,0:T(8,128)S(1)}, u32[]{:S(2)}, u32[]{:S(2)}) async-start(f32[2,2336,128]{2,1,0:T(8,128)} %broadcast_in_dim.29), calls=%async_computation.1 | async-start | bytes 4784128 | tf_op jit(solution)/shard_map/all_to_all | solution.py:92
  45.6 0.0 collective-permute-done.extra_ref
  45.6 0.0 copy-start.3
  45.6 2.7 %all-to-all-done.1.recv_ref = f32[2,2336,128]{2,1,0:T(8,128)S(1)} async-done(((f32[2,2336,128]{2,1,0:T(8,128)}), f32[2,2336,128]{2,1,0:T(8,128)S(1)}, u32[]{:S(2)}, u32[]{:S(2)}) %all-to-all-start.1) | async-done | bytes 2392096 | tf_op jit(solution)/shard_map/all_to_all | solution.py:92
  48.3 0.0 copy-start
  48.3 0.0 copy-done.3
  48.3 1.4 copy-done
  49.7 5.0 %shard_map.86 = (bf16[2,288,128]{2,1,0:T(8,128)(2,1)}, f32[576,512]{1,0:T(8,128)}) custom-call(f32[2,2336,128]{2,1,0:T(8,128)} %copy-done, f32[1216,128]{1,0:T(8,128)} %copy-done.3, f32[128,8]{1,0:T(8,128)} %copy-done.4, bf16[576,128]{1,0:T(8,128)(2,1)} %bitcast.66, bf16[576,128]{1,0:T(8,128)(2,1)} %bitcast.62, bf16[128,512]{1,0:T(8,128)(2,1)} %bitcast.65), custom_call_target="tpu_custom_call" | custom-call | flops 339738624 | bytes 4620288 | tf_op jit(solution)/shard_map/pallas_call | solution.py:180
  54.7 0.0 copy-start.1
  54.7 31.9 %all_to_all.27 = f32[4,144,512]{2,1,0:T(8,128)S(1)} all-to-all(f32[4,144,512]{2,1,0:T(8,128)} %bitcast.63), channel_id=1, replica_groups=mesh['ylo'=4,'core'=2,'lz'=8,'lyhi'=2,'lx1'=2,'lx0'=2] {'ylo'}, dimensions={0} | all-to-all | bytes 2359296 | tf_op jit(solution)/shard_map/all_to_all | solution.py:92
  86.6 0.1 reduce_sum.9
  86.7 0.0 copy-done.1
  86.7 0.0 copy-start.8
  86.8 0.4 fusion.6
  87.2 3.1 %collective-permute-start.1 = (f32[144,512]{1,0:T(8,128)S(1)}, f32[144,512]{1,0:T(8,128)S(1)}, u32[]{:S(2)}, u32[]{:S(2)}) collective-permute-start(f32[144,512]{1,0:T(8,128)S(1)} %fusion.6), channel_id=1, source_target_pairs={{0,1},{1,0},{2,3},{3,2},{4,5},{5,4},{6,7},{7,6},{8,9},{9,8},{10,11... | collective-permute-start | bytes 884744 | tf_op jit(solution)/shard_map/ppermute | solution.py:64
  90.3 6.1 %collective-permute-done.1 = f32[144,512]{1,0:T(8,128)S(1)} collective-permute-done((f32[144,512]{1,0:T(8,128)S(1)}, f32[144,512]{1,0:T(8,128)S(1)}, u32[]{:S(2)}, u32[]{:S(2)}) %collective-permute-start.1) | collective-permute-done | bytes 294944 | tf_op jit(solution)/shard_map/ppermute | solution.py:64
  96.4 0.4 fusion.4
  96.8 4.7 %collective-permute-start.2 = (f32[144,512]{1,0:T(8,128)S(1)}, f32[144,512]{1,0:T(8,128)S(1)}, u32[]{:S(2)}, u32[]{:S(2)}) collective-permute-start(f32[144,512]{1,0:T(8,128)S(1)} %fusion.4), channel_id=1, source_target_pairs={{0,2},{2,0},{1,3},{3,1},{4,6},{6,4},{5,7},{7,5},{8,10},{10,8},{9,1... | collective-permute-start | bytes 884744 | tf_op jit(solution)/shard_map/ppermute | solution.py:64
  101.4 5.1 %collective-permute-done.2 = f32[144,512]{1,0:T(8,128)S(1)} collective-permute-done((f32[144,512]{1,0:T(8,128)S(1)}, f32[144,512]{1,0:T(8,128)S(1)}, u32[]{:S(2)}, u32[]{:S(2)}) %collective-permute-start.2) | collective-permute-done | bytes 294944 | tf_op jit(solution)/shard_map/ppermute | solution.py:64
  106.6 0.4 fusion.2
  107.0 6.4 %collective-permute-start.3 = (f32[144,512]{1,0:T(8,128)S(1)}, f32[144,512]{1,0:T(8,128)S(1)}, u32[]{:S(2)}, u32[]{:S(2)}) collective-permute-start(f32[144,512]{1,0:T(8,128)S(1)} %fusion.2), channel_id=1, source_target_pairs={{0,4},{4,0},{1,5},{5,1},{2,6},{6,2},{3,7},{7,3},{8,12},{12,8},{9,1... | collective-permute-start | bytes 884744 | tf_op jit(solution)/shard_map/ppermute | solution.py:64
  113.3 13.2 %collective-permute-done.3 = f32[144,512]{1,0:T(8,128)S(1)} collective-permute-done((f32[144,512]{1,0:T(8,128)S(1)}, f32[144,512]{1,0:T(8,128)S(1)}, u32[]{:S(2)}, u32[]{:S(2)}) %collective-permute-start.3) | collective-permute-done | bytes 294944 | tf_op jit(solution)/shard_map/ppermute | solution.py:64
  126.6 2.8 %collective-permute-start.4 = (f32[144,512]{1,0:T(8,128)S(1)}, f32[144,512]{1,0:T(8,128)S(1)}, u32[]{:S(2)}, u32[]{:S(2)}) collective-permute-start(f32[144,512]{1,0:T(8,128)S(1)} %get-tuple-element.7), channel_id=1, source_target_pairs={{128,0},{256,128},{384,256},{4,384},{132,4},{260,132},{388,260},{0... | collective-permute-start | bytes 884744 | tf_op jit(solution)/shard_map/ppermute | solution.py:77
  129.4 1.9 %collective-permute-start.5 = (f32[144,512]{1,0:T(8,128)S(1)}, f32[144,512]{1,0:T(8,128)S(1)}, u32[]{:S(2)}, u32[]{:S(2)}) collective-permute-start(f32[144,512]{1,0:T(8,128)S(1)} %get-tuple-element.7), channel_id=1, source_target_pairs={{256,0},{388,128},{4,256},{128,384},{260,4},{384,132},{0,260},{132... | collective-permute-start | bytes 884744 | tf_op jit(solution)/shard_map/ppermute | solution.py:77
  131.3 0.0 copy-done.8
  131.3 0.6 slice_bitcast_fusion.4
  132.0 3.0 %collective-permute-start.6 = (f32[144,512]{1,0:T(8,128)S(1)}, f32[144,512]{1,0:T(8,128)S(1)}, u32[]{:S(2)}, u32[]{:S(2)}) collective-permute-start(f32[144,512]{1,0:T(8,128)S(1)} %get-tuple-element.7), channel_id=1, source_target_pairs={{388,0},{0,128},{128,256},{256,384},{384,4},{4,132},{132,260},{260... | collective-permute-start | bytes 884744 | tf_op jit(solution)/shard_map/ppermute | solution.py:77
  135.0 0.0 collective-permute-done.4
  135.1 4.7 %collective-permute-done.5 = f32[144,512]{1,0:T(8,128)S(1)} collective-permute-done((f32[144,512]{1,0:T(8,128)S(1)}, f32[144,512]{1,0:T(8,128)S(1)}, u32[]{:S(2)}, u32[]{:S(2)}) %collective-permute-start.5) | collective-permute-done | bytes 294944 | tf_op jit(solution)/shard_map/ppermute | solution.py:77
  139.8 7.2 %collective-permute-done.6 = f32[144,512]{1,0:T(8,128)S(1)} collective-permute-done((f32[144,512]{1,0:T(8,128)S(1)}, f32[144,512]{1,0:T(8,128)S(1)}, u32[]{:S(2)}, u32[]{:S(2)}) %collective-permute-start.6) | collective-permute-done | bytes 294944 | tf_op jit(solution)/shard_map/ppermute | solution.py:77
  147.1 0.1 constant_dynamic-slice_fusion
  147.3 0.1 pad_maximum_fusion
  147.4 0.3 broadcast_in_dim.30
  147.7 0.0 copy-start.7
  147.7 7.2 %all_to_all.28 = f32[2,648,512]{2,1,0:T(8,128)S(1)} all-to-all(f32[2,648,512]{2,1,0:T(8,128)S(1)} %broadcast_in_dim.30), channel_id=1, replica_groups=mesh['ylo'=4,'core'=2,'lz'=8,'lyhi'=2,'lx1'=2,'lx0'=2] {'core'}, dimensions={0} | all-to-all | bytes 5308416 | tf_op jit(solution)/shard_map/all_to_all | solution.py:92
  154.9 0.1 concatenate.53
  155.0 0.0 copy-done.7
  155.0 0.7 maximum_select_fusion
  155.7 0.2 slice_bitcast_fusion.3
  155.9 0.2 maximum_bitcast_fusion.1
  156.1 1.6 %maximum_bitcast_fusion = f32[1,2,576,512]{3,2,1,0:T(8,128)} fusion(f32[1,576,512]{2,1,0:T(8,128)S(1)} %get-tuple-element.15, f32[1,576,512]{2,1,0:T(8,128)S(1)} %get-tuple-element.14), kind=kLoop, calls=%fused_computation | loop fusion | flops 589824 | bytes 4718592 | tf_op jit(solution)/shard_map/broadcast_in_dim | solution.py:239
  (16 shorter events, 0.3 us)
Async XLA Ops:
  2.9 7.4 %copy-start.9 = (f32[1,1,128]{2,1,0:T(1,128)S(1)}, f32[1,1,128]{2,1,0:T(1,128)}, u32[]{:S(2)}) copy-start(f32[1,1,128]{2,1,0:T(1,128)} %param.8) | copy-start | bytes 1540
  2.9 7.5 %copy-start.5 = (bf16[1,1,128,512]{3,2,1,0:T(8,128)(2,1)S(1)}, bf16[1,1,128,512]{3,2,1,0:T(8,128)(2,1)}, u32[]{:S(2)}) copy-start(bf16[1,1,128,512]{3,2,1,0:T(8,128)(2,1)} %param.12) | copy-start | bytes 393220
  3.8 6.8 %copy-start.6 = (bf16[576,1,1,128]{3,0,2,1:T(8,128)(2,1)S(1)}, bf16[576,1,1,128]{3,0,2,1:T(8,128)(2,1)}, u32[]{:S(2)}) copy-start(bf16[576,1,1,128]{3,0,2,1:T(8,128)(2,1)} %param.10) | copy-start | bytes 442372
  3.8 6.8 %copy-start.2 = (bf16[576,1,1,128]{3,0,2,1:T(8,128)(2,1)S(1)}, bf16[576,1,1,128]{3,0,2,1:T(8,128)(2,1)}, u32[]{:S(2)}) copy-start(bf16[576,1,1,128]{3,0,2,1:T(8,128)(2,1)} %param.9) | copy-start | bytes 442372
  4.9 32.6 %all-to-all-start = ((f32[4,584,128]{2,1,0:T(8,128)}), f32[4,584,128]{2,1,0:T(8,128)S(1)}, u32[]{:S(2)}, u32[]{:S(2)}) async-start(f32[4,584,128]{2,1,0:T(8,128)} %broadcast_in_dim.13), calls=%async_computation | async-start | bytes 2392064 | tf_op jit(solution)/shard_map/all_to_all | solution.py:92
  10.4 28.6 %copy-start.4 = (f32[128,8]{1,0:T(8,128)}, f32[128,8]{1,0:T(8,128)S(1)}, u32[]{:S(2)}) copy-start(f32[128,8]{1,0:T(8,128)S(1)} %copy.13.own_ref) | copy-start | bytes 12292
  11.6 34.0 %collective-permute-start = (f32[1216,128]{1,0:T(8,128)}, f32[1216,128]{1,0:T(8,128)S(1)}, u32[]{:S(2)}, u32[]{:S(2)}) collective-permute-start(f32[1216,128]{1,0:T(8,128)} %fusion.1), channel_id=1, source_target_pairs={{0,64},{64,0},{1,65},{65,1},{2,66},{66,2},{3,67},{67,3},{4,68},{68... | collective-permute-start | bytes 1867784 | tf_op jit(solution)/shard_map/ppermute | solution.py:228
  39.1 9.2 %all-to-all-start.1 = ((f32[2,2336,128]{2,1,0:T(8,128)}), f32[2,2336,128]{2,1,0:T(8,128)S(1)}, u32[]{:S(2)}, u32[]{:S(2)}) async-start(f32[2,2336,128]{2,1,0:T(8,128)} %broadcast_in_dim.29), calls=%async_computation.1 | async-start | bytes 4784128 | tf_op jit(solution)/shard_map/all_to_all | solution.py:92
  45.6 2.7 %copy-start.3 = (f32[1216,128]{1,0:T(8,128)}, f32[1216,128]{1,0:T(8,128)S(1)}, u32[]{:S(2)}) copy-start(f32[1216,128]{1,0:T(8,128)S(1)} %collective-permute-done.extra_ref) | copy-start | bytes 1867780
  48.3 1.4 copy-start
  54.7 32.0 %copy-start.1 = (bf16[1,3,512,512]{3,2,1,0:T(8,128)(2,1)S(1)}, bf16[1,3,512,512]{3,2,1,0:T(8,128)(2,1)}, u32[]{:S(2)}) copy-start(bf16[1,3,512,512]{3,2,1,0:T(8,128)(2,1)} %param.13) | copy-start | bytes 4718596
  86.7 44.6 %copy-start.8 = (bf16[2,288,128]{2,1,0:T(8,128)(2,1)S(1)}, bf16[2,288,128]{2,1,0:T(8,128)(2,1)}, u32[]{:S(2)}) copy-start(bf16[2,288,128]{2,1,0:T(8,128)(2,1)} %get-tuple-element.4) | copy-start | bytes 442372
  87.2 9.2 %collective-permute-start.1 = (f32[144,512]{1,0:T(8,128)S(1)}, f32[144,512]{1,0:T(8,128)S(1)}, u32[]{:S(2)}, u32[]{:S(2)}) collective-permute-start(f32[144,512]{1,0:T(8,128)S(1)} %fusion.6), channel_id=1, source_target_pairs={{0,1},{1,0},{2,3},{3,2},{4,5},{5,4},{6,7},{7,6},{8,9},{9,8},{10,11... | collective-permute-start | bytes 884744 | tf_op jit(solution)/shard_map/ppermute | solution.py:64
  96.8 9.8 %collective-permute-start.2 = (f32[144,512]{1,0:T(8,128)S(1)}, f32[144,512]{1,0:T(8,128)S(1)}, u32[]{:S(2)}, u32[]{:S(2)}) collective-permute-start(f32[144,512]{1,0:T(8,128)S(1)} %fusion.4), channel_id=1, source_target_pairs={{0,2},{2,0},{1,3},{3,1},{4,6},{6,4},{5,7},{7,5},{8,10},{10,8},{9,1... | collective-permute-start | bytes 884744 | tf_op jit(solution)/shard_map/ppermute | solution.py:64
  107.0 19.6 %collective-permute-start.3 = (f32[144,512]{1,0:T(8,128)S(1)}, f32[144,512]{1,0:T(8,128)S(1)}, u32[]{:S(2)}, u32[]{:S(2)}) collective-permute-start(f32[144,512]{1,0:T(8,128)S(1)} %fusion.2), channel_id=1, source_target_pairs={{0,4},{4,0},{1,5},{5,1},{2,6},{6,2},{3,7},{7,3},{8,12},{12,8},{9,1... | collective-permute-start | bytes 884744 | tf_op jit(solution)/shard_map/ppermute | solution.py:64
  126.6 8.4 %collective-permute-start.4 = (f32[144,512]{1,0:T(8,128)S(1)}, f32[144,512]{1,0:T(8,128)S(1)}, u32[]{:S(2)}, u32[]{:S(2)}) collective-permute-start(f32[144,512]{1,0:T(8,128)S(1)} %get-tuple-element.7), channel_id=1, source_target_pairs={{128,0},{256,128},{384,256},{4,384},{132,4},{260,132},{388,260},{0... | collective-permute-start | bytes 884744 | tf_op jit(solution)/shard_map/ppermute | solution.py:77
  129.4 10.4 %collective-permute-start.5 = (f32[144,512]{1,0:T(8,128)S(1)}, f32[144,512]{1,0:T(8,128)S(1)}, u32[]{:S(2)}, u32[]{:S(2)}) collective-permute-start(f32[144,512]{1,0:T(8,128)S(1)} %get-tuple-element.7), channel_id=1, source_target_pairs={{256,0},{388,128},{4,256},{128,384},{260,4},{384,132},{0,260},{132... | collective-permute-start | bytes 884744 | tf_op jit(solution)/shard_map/ppermute | solution.py:77
  132.0 15.0 %collective-permute-start.6 = (f32[144,512]{1,0:T(8,128)S(1)}, f32[144,512]{1,0:T(8,128)S(1)}, u32[]{:S(2)}, u32[]{:S(2)}) collective-permute-start(f32[144,512]{1,0:T(8,128)S(1)} %get-tuple-element.7), channel_id=1, source_target_pairs={{388,0},{0,128},{128,256},{256,384},{384,4},{4,132},{132,260},{260... | collective-permute-start | bytes 884744 | tf_op jit(solution)/shard_map/ppermute | solution.py:77
  147.7 7.3 %copy-start.7 = (bf16[288,1,1,128]{3,0,2,1:T(8,128)(2,1)S(1)}, bf16[288,1,1,128]{3,0,2,1:T(8,128)(2,1)}, u32[]{:S(2)}) copy-start(bf16[288,1,1,128]{3,0,2,1:T(8,128)(2,1)} %get-tuple-element.12) | copy-start | bytes 221188

commit v17 on v14

--- a/solution.py
+++ b/solution.py
@@ -207,7 +207,15 @@
         [coords, area_row, order_row, jnp.zeros((3, panels), jnp.float32)], axis=0
     )
     outgoing = jnp.concatenate([geometry, scaled.astype(jnp.float32)], axis=0)
-    chip_blocks = gather_blocks(outgoing, "ylo")
+    chip_count = lax.axis_size("ylo")
+    copies = jnp.concatenate(
+        [
+            jnp.broadcast_to(geometry[None], (chip_count,) + geometry.shape),
+            jnp.broadcast_to(scaled[None], (chip_count,) + scaled.shape).astype(jnp.float32),
+        ],
+        axis=1,
+    )
+    chip_blocks = exchange(copies.reshape(-1, panels), "ylo")
     own = jnp.transpose(geometry)
     own_padded = jnp.pad(own, ((0, 0), (0, panels - own.shape[1])))
     basis_view = jnp.transpose(

time: 156 us -> 157 us (level)
  other arithmetic: 5.11 us -> 6.91 us
  local copies, waits for them, and re-layouts: 3.98 us -> 2.23 us
    concatenate x0 -> x2, other arithmetic: none -> 1.83 us  [the longest x1 1.1 us: shards(): jnp.concatenate([jnp.broadcast_to(geometry[None], (chip_count,) + geometr...]
where the time goes in v17:
time: 157 us; the launch traced here: 156 us
  waiting for transfers between devices  63.1 us (40%)
  blocking collectives  49 us (31%)
  starting transfers between devices  27.4 us (17%)
  other arithmetic  6.91 us (4%)
  Pallas kernels  5.22 us (3%)
  local copies, waits for them, and re-layouts  2.23 us (1%)
    all_to_all x3, blocking collectives, exchange(): return lax.all_to_all(value, axis, 0, 0, tiled=True)  49 us
    all_to_all x1, waiting for transfers between devices, exchange(): return lax.all_to_all(value, axis, 0, 0, tiled=True)  26.9 us
    ppermute x3, waiting for transfers between devices, climb_rows(): other = lax.ppermute(projected, LEVEL_AXES[tree_level], [(0, 1), (1, 0)])  24.4 us
    ppermute x3, starting transfers between devices, climb_rows(): other = lax.ppermute(projected, LEVEL_AXES[tree_level], [(0, 1), (1, 0)])  14.1 us
    ppermute x3, waiting for transfers between devices, ring_shift(): return lax.ppermute(rows, ('ylo', 'lyhi'), pairs)  11.9 us
    ppermute x3, starting transfers between devices, ring_shift(): return lax.ppermute(rows, ('ylo', 'lyhi'), pairs)  7.74 us
    all_to_all x1, starting transfers between devices, exchange(): return lax.all_to_all(value, axis, 0, 0, tiled=True)  5.55 us
    pallas_call x1, Pallas kernels, chip_project(): pl.pallas_call(functools.partial(chip_kernel, layout), out_shape=(jax.Sha...  5.22 us
  transfers between devices with their start and end apart: 7, of which 6 were waited for; matrix products, arithmetic and copies ran while one was open for 1% of the time, Pallas kernels for 0%

profile of v17, /device:TPU:1, one launch (start us, length us, event | category | flops | bytes accessed | tf_op | source)
XLA Modules:
  0.0 156.1 jit_solution(244977247402346907)
XLA Ops:
  0.6 0.7 copy.18
  1.3 0.7 convert_bitcast_fusion
  2.0 0.1 pad.22.clone
  2.0 0.9 fusion.11
  3.0 0.7 maximum_maximum_fusion
  3.7 0.1 broadcast_in_dim.12
  3.8 0.0 copy-start.4
  3.8 0.0 copy-start.1
  3.8 1.1 pad_maximum_fusion.1
  4.9 0.0 copy-start.3
  4.9 5.6 %all-to-all-start = ((f32[4,584,128]{2,1,0:T(8,128)}), f32[4,584,128]{2,1,0:T(8,128)S(1)}, u32[]{:S(2)}, u32[]{:S(2)}) async-start(f32[4,584,128]{2,1,0:T(8,128)} %pad_maximum_fusion.1), calls=%async_computation | async-start | bytes 2392064 | tf_op jit(solution)/shard_map/all_to_all | solution.py:92
  10.5 0.1 copy.14
  10.6 0.0 copy-done.4
  10.6 0.0 copy-start.2
  10.6 0.1 reshape.186
  10.7 0.0 copy-done.1
  10.8 0.0 copy-done.3
  10.8 26.9 %all-to-all-done = f32[4,584,128]{2,1,0:T(8,128)S(1)} async-done(((f32[4,584,128]{2,1,0:T(8,128)}), f32[4,584,128]{2,1,0:T(8,128)S(1)}, u32[]{:S(2)}, u32[]{:S(2)}) %all-to-all-start) | async-done | bytes 1196064 | tf_op jit(solution)/shard_map/all_to_all | solution.py:92
  37.7 0.1 constant_dynamic-update-slice_fusion.3
  37.8 0.1 constant_dynamic-update-slice_fusion.1
  37.9 0.0 copy-done.2
  38.0 10.0 %all_to_all.33.recv_ref = f32[2,3552,128]{2,1,0:T(8,128)} all-to-all(f32[2,3552,128]{2,1,0:T(8,128)S(1)} %bitcast.62), channel_id=1, replica_groups=mesh['ylo'=4,'core'=2,'lz'=8,'lyhi'=2,'lx1'=2,'lx0'=2] {'core'}, dimensions={0} | all-to-all | bytes 7274496 | tf_op jit(solution)/shard_map/all_to_all | solution.py:92
  48.0 5.2 %shard_map.86 = (bf16[2,288,128]{2,1,0:T(8,128)(2,1)}, f32[576,512]{1,0:T(8,128)}) custom-call(f32[2,3552,128]{2,1,0:T(8,128)} %all_to_all.33.recv_ref, f32[128,8]{1,0:T(8,128)} %bitcast.70, bf16[576,128]{1,0:T(8,128)(2,1)} %bitcast.72, bf16[576,128]{1,0:T(8,128)(2,1)} %bitcast.66, bf16[128,512]{1,0:T(8,128)(2,1)} %bitcast.73), custom_call_target="tpu_custom_call" | custom-call | flops 339738624 | bytes 5242880 | tf_op jit(solution)/shard_map/pallas_call | solution.py:180
  53.2 0.0 copy-start
  53.2 31.9 %all_to_all.34 = f32[4,144,512]{2,1,0:T(8,128)S(1)} all-to-all(f32[4,144,512]{2,1,0:T(8,128)} %bitcast.67), channel_id=1, replica_groups=mesh['ylo'=4,'core'=2,'lz'=8,'lyhi'=2,'lx1'=2,'lx0'=2] {'ylo'}, dimensions={0} | all-to-all | bytes 2359296 | tf_op jit(solution)/shard_map/all_to_all | solution.py:92
  85.1 0.1 reduce_sum.9
  85.2 0.0 copy-done
  85.3 0.0 copy-start.6
  85.3 0.4 fusion.4
  85.7 3.1 %collective-permute-start = (f32[144,512]{1,0:T(8,128)S(1)}, f32[144,512]{1,0:T(8,128)S(1)}, u32[]{:S(2)}, u32[]{:S(2)}) collective-permute-start(f32[144,512]{1,0:T(8,128)S(1)} %fusion.4), channel_id=1, source_target_pairs={{0,1},{1,0},{2,3},{3,2},{4,5},{5,4},{6,7},{7,6},{8,9},{9,8},{10,11... | collective-permute-start | bytes 884744 | tf_op jit(solution)/shard_map/ppermute | solution.py:64
  88.8 6.1 %collective-permute-done = f32[144,512]{1,0:T(8,128)S(1)} collective-permute-done((f32[144,512]{1,0:T(8,128)S(1)}, f32[144,512]{1,0:T(8,128)S(1)}, u32[]{:S(2)}, u32[]{:S(2)}) %collective-permute-start) | collective-permute-done | bytes 294944 | tf_op jit(solution)/shard_map/ppermute | solution.py:64
  94.9 0.4 fusion.2
  95.3 4.7 %collective-permute-start.1 = (f32[144,512]{1,0:T(8,128)S(1)}, f32[144,512]{1,0:T(8,128)S(1)}, u32[]{:S(2)}, u32[]{:S(2)}) collective-permute-start(f32[144,512]{1,0:T(8,128)S(1)} %fusion.2), channel_id=1, source_target_pairs={{0,2},{2,0},{1,3},{3,1},{4,6},{6,4},{5,7},{7,5},{8,10},{10,8},{9,1... | collective-permute-start | bytes 884744 | tf_op jit(solution)/shard_map/ppermute | solution.py:64
  99.9 5.1 %collective-permute-done.1 = f32[144,512]{1,0:T(8,128)S(1)} collective-permute-done((f32[144,512]{1,0:T(8,128)S(1)}, f32[144,512]{1,0:T(8,128)S(1)}, u32[]{:S(2)}, u32[]{:S(2)}) %collective-permute-start.1) | collective-permute-done | bytes 294944 | tf_op jit(solution)/shard_map/ppermute | solution.py:64
  105.1 0.4 fusion
  105.5 6.4 %collective-permute-start.2 = (f32[144,512]{1,0:T(8,128)S(1)}, f32[144,512]{1,0:T(8,128)S(1)}, u32[]{:S(2)}, u32[]{:S(2)}) collective-permute-start(f32[144,512]{1,0:T(8,128)S(1)} %fusion), channel_id=1, source_target_pairs={{0,4},{4,0},{1,5},{5,1},{2,6},{6,2},{3,7},{7,3},{8,12},{12,8},{9,1... | collective-permute-start | bytes 884744 | tf_op jit(solution)/shard_map/ppermute | solution.py:64
  111.8 13.2 %collective-permute-done.2 = f32[144,512]{1,0:T(8,128)S(1)} collective-permute-done((f32[144,512]{1,0:T(8,128)S(1)}, f32[144,512]{1,0:T(8,128)S(1)}, u32[]{:S(2)}, u32[]{:S(2)}) %collective-permute-start.2) | collective-permute-done | bytes 294944 | tf_op jit(solution)/shard_map/ppermute | solution.py:64
  125.1 2.8 %collective-permute-start.3 = (f32[144,512]{1,0:T(8,128)S(1)}, f32[144,512]{1,0:T(8,128)S(1)}, u32[]{:S(2)}, u32[]{:S(2)}) collective-permute-start(f32[144,512]{1,0:T(8,128)S(1)} %get-tuple-element.7), channel_id=1, source_target_pairs={{128,0},{256,128},{384,256},{4,384},{132,4},{260,132},{388,260},{0... | collective-permute-start | bytes 884744 | tf_op jit(solution)/shard_map/ppermute | solution.py:77
  127.9 1.9 %collective-permute-start.4 = (f32[144,512]{1,0:T(8,128)S(1)}, f32[144,512]{1,0:T(8,128)S(1)}, u32[]{:S(2)}, u32[]{:S(2)}) collective-permute-start(f32[144,512]{1,0:T(8,128)S(1)} %get-tuple-element.7), channel_id=1, source_target_pairs={{256,0},{388,128},{4,256},{128,384},{260,4},{384,132},{0,260},{132... | collective-permute-start | bytes 884744 | tf_op jit(solution)/shard_map/ppermute | solution.py:77
  129.8 0.0 copy-done.6
  129.8 0.6 slice_bitcast_fusion.4
  130.5 3.0 %collective-permute-start.5 = (f32[144,512]{1,0:T(8,128)S(1)}, f32[144,512]{1,0:T(8,128)S(1)}, u32[]{:S(2)}, u32[]{:S(2)}) collective-permute-start(f32[144,512]{1,0:T(8,128)S(1)} %get-tuple-element.7), channel_id=1, source_target_pairs={{388,0},{0,128},{128,256},{256,384},{384,4},{4,132},{132,260},{260... | collective-permute-start | bytes 884744 | tf_op jit(solution)/shard_map/ppermute | solution.py:77
  133.5 0.0 collective-permute-done.3
  133.6 4.7 %collective-permute-done.4 = f32[144,512]{1,0:T(8,128)S(1)} collective-permute-done((f32[144,512]{1,0:T(8,128)S(1)}, f32[144,512]{1,0:T(8,128)S(1)}, u32[]{:S(2)}, u32[]{:S(2)}) %collective-permute-start.4) | collective-permute-done | bytes 294944 | tf_op jit(solution)/shard_map/ppermute | solution.py:77
  138.3 7.1 %collective-permute-done.5 = f32[144,512]{1,0:T(8,128)S(1)} collective-permute-done((f32[144,512]{1,0:T(8,128)S(1)}, f32[144,512]{1,0:T(8,128)S(1)}, u32[]{:S(2)}, u32[]{:S(2)}) %collective-permute-start.5) | collective-permute-done | bytes 294944 | tf_op jit(solution)/shard_map/ppermute | solution.py:77
  145.6 0.1 constant_dynamic-slice_fusion
  145.7 0.1 pad_maximum_fusion
  145.8 0.3 broadcast_in_dim.13
  146.2 7.1 %all_to_all.35 = f32[2,648,512]{2,1,0:T(8,128)S(1)} all-to-all(f32[2,648,512]{2,1,0:T(8,128)S(1)} %broadcast_in_dim.13), channel_id=1, replica_groups=mesh['ylo'=4,'core'=2,'lz'=8,'lyhi'=2,'lx1'=2,'lx0'=2] {'core'}, dimensions={0} | all-to-all | bytes 5308416 | tf_op jit(solution)/shard_map/all_to_all | solution.py:92
  153.2 0.1 concatenate.52
  153.3 0.2 slice_bitcast_fusion.3
  153.5 0.2 maximum_bitcast_fusion.1
  153.7 0.0 copy-start.5
  153.8 1.6 %maximum_bitcast_fusion = f32[1,2,576,512]{3,2,1,0:T(8,128)} fusion(f32[1,576,512]{2,1,0:T(8,128)S(1)} %get-tuple-element.15, f32[1,576,512]{2,1,0:T(8,128)S(1)} %get-tuple-element.14), kind=kLoop, calls=%fused_computation | loop fusion | flops 589824 | bytes 4718592 | tf_op jit(solution)/shard_map/broadcast_in_dim | solution.py:249
  155.4 0.0 copy-done.5
  155.4 0.7 maximum_select_fusion
  (23 shorter events, 0.4 us)
Async XLA Ops:
  3.8 6.8 %copy-start.4 = (bf16[1,1,128,512]{3,2,1,0:T(8,128)(2,1)S(1)}, bf16[1,1,128,512]{3,2,1,0:T(8,128)(2,1)}, u32[]{:S(2)}) copy-start(bf16[1,1,128,512]{3,2,1,0:T(8,128)(2,1)} %param.12) | copy-start | bytes 393220
  3.8 6.9 %copy-start.1 = (bf16[576,1,1,128]{3,0,2,1:T(8,128)(2,1)S(1)}, bf16[576,1,1,128]{3,0,2,1:T(8,128)(2,1)}, u32[]{:S(2)}) copy-start(bf16[576,1,1,128]{3,0,2,1:T(8,128)(2,1)} %param.9) | copy-start | bytes 442372
  4.9 5.8 %copy-start.3 = (bf16[576,1,1,128]{3,0,2,1:T(8,128)(2,1)S(1)}, bf16[576,1,1,128]{3,0,2,1:T(8,128)(2,1)}, u32[]{:S(2)}) copy-start(bf16[576,1,1,128]{3,0,2,1:T(8,128)(2,1)} %param.10) | copy-start | bytes 442372
  4.9 32.7 %all-to-all-start = ((f32[4,584,128]{2,1,0:T(8,128)}), f32[4,584,128]{2,1,0:T(8,128)S(1)}, u32[]{:S(2)}, u32[]{:S(2)}) async-start(f32[4,584,128]{2,1,0:T(8,128)} %pad_maximum_fusion.1), calls=%async_computation | async-start | bytes 2392064 | tf_op jit(solution)/shard_map/all_to_all | solution.py:92
  10.6 27.3 %copy-start.2 = (f32[8,128]{0,1:T(8,128)}, f32[8,128]{0,1:T(8,128)S(1)}, u32[]{:S(2)}) copy-start(f32[8,128]{0,1:T(8,128)S(1)} %copy.14) | copy-start | bytes 12292
  53.2 32.0 %copy-start = (bf16[1,3,512,512]{3,2,1,0:T(8,128)(2,1)S(1)}, bf16[1,3,512,512]{3,2,1,0:T(8,128)(2,1)}, u32[]{:S(2)}) copy-start(bf16[1,3,512,512]{3,2,1,0:T(8,128)(2,1)} %param.13) | copy-start | bytes 4718596
  85.3 44.6 %copy-start.6 = (bf16[2,288,128]{2,1,0:T(8,128)(2,1)S(1)}, bf16[2,288,128]{2,1,0:T(8,128)(2,1)}, u32[]{:S(2)}) copy-start(bf16[2,288,128]{2,1,0:T(8,128)(2,1)} %get-tuple-element.4) | copy-start | bytes 442372
  85.7 9.2 %collective-permute-start = (f32[144,512]{1,0:T(8,128)S(1)}, f32[144,512]{1,0:T(8,128)S(1)}, u32[]{:S(2)}, u32[]{:S(2)}) collective-permute-start(f32[144,512]{1,0:T(8,128)S(1)} %fusion.4), channel_id=1, source_target_pairs={{0,1},{1,0},{2,3},{3,2},{4,5},{5,4},{6,7},{7,6},{8,9},{9,8},{10,11... | collective-permute-start | bytes 884744 | tf_op jit(solution)/shard_map/ppermute | solution.py:64
  95.3 9.8 %collective-permute-start.1 = (f32[144,512]{1,0:T(8,128)S(1)}, f32[144,512]{1,0:T(8,128)S(1)}, u32[]{:S(2)}, u32[]{:S(2)}) collective-permute-start(f32[144,512]{1,0:T(8,128)S(1)} %fusion.2), channel_id=1, source_target_pairs={{0,2},{2,0},{1,3},{3,1},{4,6},{6,4},{5,7},{7,5},{8,10},{10,8},{9,1... | collective-permute-start | bytes 884744 | tf_op jit(solution)/shard_map/ppermute | solution.py:64
  105.5 19.6 %collective-permute-start.2 = (f32[144,512]{1,0:T(8,128)S(1)}, f32[144,512]{1,0:T(8,128)S(1)}, u32[]{:S(2)}, u32[]{:S(2)}) collective-permute-start(f32[144,512]{1,0:T(8,128)S(1)} %fusion), channel_id=1, source_target_pairs={{0,4},{4,0},{1,5},{5,1},{2,6},{6,2},{3,7},{7,3},{8,12},{12,8},{9,1... | collective-permute-start | bytes 884744 | tf_op jit(solution)/shard_map/ppermute | solution.py:64
  125.1 8.5 %collective-permute-start.3 = (f32[144,512]{1,0:T(8,128)S(1)}, f32[144,512]{1,0:T(8,128)S(1)}, u32[]{:S(2)}, u32[]{:S(2)}) collective-permute-start(f32[144,512]{1,0:T(8,128)S(1)} %get-tuple-element.7), channel_id=1, source_target_pairs={{128,0},{256,128},{384,256},{4,384},{132,4},{260,132},{388,260},{0... | collective-permute-start | bytes 884744 | tf_op jit(solution)/shard_map/ppermute | solution.py:77
  127.9 10.4 %collective-permute-start.4 = (f32[144,512]{1,0:T(8,128)S(1)}, f32[144,512]{1,0:T(8,128)S(1)}, u32[]{:S(2)}, u32[]{:S(2)}) collective-permute-start(f32[144,512]{1,0:T(8,128)S(1)} %get-tuple-element.7), channel_id=1, source_target_pairs={{256,0},{388,128},{4,256},{128,384},{260,4},{384,132},{0,260},{132... | collective-permute-start | bytes 884744 | tf_op jit(solution)/shard_map/ppermute | solution.py:77
  130.5 14.9 %collective-permute-start.5 = (f32[144,512]{1,0:T(8,128)S(1)}, f32[144,512]{1,0:T(8,128)S(1)}, u32[]{:S(2)}, u32[]{:S(2)}) collective-permute-start(f32[144,512]{1,0:T(8,128)S(1)} %get-tuple-element.7), channel_id=1, source_target_pairs={{388,0},{0,128},{128,256},{256,384},{384,4},{4,132},{132,260},{260... | collective-permute-start | bytes 884744 | tf_op jit(solution)/shard_map/ppermute | solution.py:77
  153.7 1.6 %copy-start.5 = (bf16[288,1,1,128]{3,0,2,1:T(8,128)(2,1)S(1)}, bf16[288,1,1,128]{3,0,2,1:T(8,128)(2,1)}, u32[]{:S(2)}) copy-start(bf16[288,1,1,128]{3,0,2,1:T(8,128)(2,1)} %get-tuple-element.12) | copy-start | bytes 221188
